TPU v7x, 768 devices: a whole 4x8x12 slice. The times are simulated.
768 devices in a mesh: depth: 32 (over y, z_hi), chan: 24 (over x, z_lo, core).
Axes of the slice: x: 4, y: 8, z: 12 (z_hi: 4, z_lo: 3; z = z_hi * 3 + z_lo), core: 2. Of those that a mesh axis runs over, the one named last changes fastest.
Arguments:
- volume: bfloat16 [1, 32, 384, 1024], P(None, 'depth', 'chan'), may hold values from -6 to 6
- kernel: bfloat16 [384, 3, 3, 3, 384], P('chan'), may hold values from -0.09375 to 0.09375
- cotangent: bfloat16 [1, 32, 384, 1024], P(None, 'depth', 'chan'), may hold values from -6 to 6
Outputs:
- activated: bfloat16 [1, 32, 384, 1024], P(None, 'depth', 'chan')
- grad_volume: bfloat16 [1, 32, 384, 1024], P(None, 'depth', 'chan')
- grad_kernel: float32 [384, 3, 3, 3, 384], P('chan')
All inputs are finite; a program needn't handle non-finite values.
Results may differ from a plain program's by a relative error of at most 0.0049.
Values may be sent and summed in bfloat16 or wider, within the bound.
No kernel may reach another device: no remote copies, remote signals or barrier semaphores. Data moves between devices by JAX's collectives and lax.ppermute only.
A program may use at most 32 MiB of HBM per device.

v0:
```python
import math

import jax
import jax.numpy as jnp
from jax import lax
from jax.sharding import PartitionSpec as P

DEPTH = 32
SIDE = 32
UNIV = 1


def extended_2(block, sides, width):
    for axis, dim in sides:
        count = lax.axis_size(axis)
        forward = [(i, i + 1) for i in range(count - 1)]
        forward.append((count - 1, 0))
        backward = [(target, source) for source, target in forward]
        low = lax.ppermute(
            lax.slice_in_dim(block, block.shape[dim] - width, None, axis=dim), axis, forward
        )
        high = lax.ppermute(lax.slice_in_dim(block, 0, width, axis=dim), axis, backward)
        block = jnp.concatenate([low, block, high], axis=dim)
    return block


def roll_plane(plane_data, row_step, col_step):
    if col_step != 0:
        columns = lax.broadcasted_iota(jnp.int32, plane_data.shape, plane_data.ndim - 1) % SIDE
        edge_col = 0 if col_step > 0 else SIDE - 1
        wrapped = jnp.roll(plane_data, col_step - col_step * SIDE, axis=-1)
        plain = jnp.roll(plane_data, col_step, axis=-1)
        plane_data = jnp.where(columns == edge_col, wrapped, plain)
    if row_step != 0:
        plane_data = jnp.roll(plane_data, row_step * SIDE, axis=-1)
    return plane_data


def tap_matrix(kernel, depth_tap):
    return jnp.transpose(kernel[:, depth_tap], (1, 2, 0, 3)).reshape(-1, kernel.shape[4])


def body(volume, kernel, cotangent):
    universes = volume.shape[0]
    planes = volume.shape[1]
    cell_count = volume.shape[3]
    out_panel = kernel.shape[0]
    gathered = lax.all_gather(volume, "chan", axis=2, tiled=True)
    extended = extended_2(gathered, (("depth", 1),), 1)
    preact = jnp.zeros((universes, planes, out_panel, cell_count), jnp.float32)
    for depth_tap in range(3):
        source = extended[:, depth_tap : depth_tap + planes]
        product = jnp.einsum(
            "ki,upic->upkc",
            tap_matrix(kernel, depth_tap),
            source,
            preferred_element_type=jnp.float32,
        )
        product = product.reshape(universes, planes, 3, 3, out_panel, cell_count)
        for row_tap in range(3):
            for col_tap in range(3):
                preact = preact + roll_plane(
                    product[:, :, row_tap, col_tap], 1 - row_tap, 1 - col_tap
                )
    activated = jax.nn.silu(preact).astype(jnp.bfloat16)
    sigmoid_pre = jax.nn.sigmoid(preact)
    grad_pre = (
        cotangent.astype(jnp.float32) * sigmoid_pre * (1.0 + preact * (1.0 - sigmoid_pre))
    ).astype(jnp.bfloat16)
    rimmed = extended_2(grad_pre, (("depth", 1),), 1)
    stacked = jnp.concatenate(
        [
            roll_plane(rimmed, row_tap - 1, col_tap - 1)
            for row_tap in range(3)
            for col_tap in range(3)
        ],
        axis=2,
    )
    central = extended[:, 1 : 1 + planes]
    kernel_terms = []
    for depth_tap in range(3):
        grad_slice = stacked[:, 2 - depth_tap : 2 - depth_tap + planes]
        tap_grad = jnp.einsum(
            "upic,upkc->ki", central, grad_slice, preferred_element_type=jnp.float32
        )
        kernel_terms.append(jnp.transpose(tap_grad.reshape(3, 3, out_panel, -1), (2, 0, 1, 3)))
    local_grad = jnp.stack(kernel_terms, axis=1)
    grad_scale = 1.0 / math.sqrt(UNIV * DEPTH * SIDE * SIDE)
    grad_kernel = lax.psum(local_grad, "depth") * grad_scale
    partial_sum = jnp.zeros((universes, planes, extended.shape[2], cell_count), jnp.float32)
    for depth_tap in range(3):
        grad_slice = stacked[:, 2 - depth_tap : 2 - depth_tap + planes]
        partial_sum = partial_sum + jnp.einsum(
            "upkc,ki->upic",
            grad_slice,
            tap_matrix(kernel, depth_tap),
            preferred_element_type=jnp.float32,
        )
    grad_volume = lax.psum_scatter(partial_sum, "chan", scatter_dimension=2, tiled=True).astype(
        jnp.bfloat16
    )
    return (activated, grad_volume, grad_kernel)


def solution(mesh):
    placed = (
        P(None, "depth", "chan", None),
        P("chan", None, None, None, None),
        P(None, "depth", "chan", None),
    )
    return jax.shard_map(
        body,
        mesh=mesh,
        in_specs=placed,
        out_specs=(
            P(None, "depth", "chan", None),
            P(None, "depth", "chan", None),
            P("chan", None, None, None, None),
        ),
        check_vma=False,
    )
```

profile of v0, /device:TPU:2, one launch (start us, length us, event | category | flops | bytes accessed | tf_op | source)
XLA Modules:
  0.0 504.2 jit_solution(299417376217394076)
XLA Ops:
  7.2 36.0 %all_gather.3 = bf16[1,1,384,1024]{3,2,1,0:T(8,128)(2,1)S(1)} all-gather(bf16[1,1,16,1024]{3,2,1,0:T(8,128)(2,1)} %param.3), channel_id=1, replica_groups=mesh['depth'=32,'chan'=24] {'chan'}, dimensions={2}, use_global_device_ids=true | all-gather | bytes 819200 | tf_op jit(solution)/shard_map/all_gather | solution.py:48
  43.2 7.0 %collective-permute-start = (bf16[1,1,384,1024]{3,2,1,0:T(8,128)(2,1)S(1)}, bf16[1,1,384,1024]{3,2,1,0:T(8,128)(2,1)}, u32[]{:S(2)}, u32[]{:S(2)}) collective-permute-start(bf16[1,1,384,1024]{3,2,1,0:T(8,128)(2,1)S(1)} %all_gather.3), channel_id=1, source_target_pairs={{0,24},{24,48},{48,72},{72,96},{96,120},{120,144},{144,168},{168,1... | collective-permute-start | bytes 2359304 | tf_op jit(solution)/shard_map/ppermute | solution.py:19
  50.2 4.8 collective-permute-start.1
  55.0 1.0 fusion.68
  56.0 0.3 fusion.5
  56.4 0.7 slice.736
  57.2 0.7 slice.764
  57.9 0.6 slice.765
  58.5 0.7 slice.766
  59.2 0.7 slice.776
  59.9 0.7 slice.748
  60.7 0.7 slice.746
  61.3 0.6 slice.749
  62.1 0.7 slice.761
  62.9 0.7 slice.771
  63.6 0.6 slice.772
  64.2 0.7 slice.743
  64.8 1.4 dynamic-slice
  66.9 38.5 %collective-permute-done = bf16[1,1,384,1024]{3,2,1,0:T(8,128)(2,1)} collective-permute-done((bf16[1,1,384,1024]{3,2,1,0:T(8,128)(2,1)S(1)}, bf16[1,1,384,1024]{3,2,1,0:T(8,128)(2,1)}, u32[]{:S(2)}, u32[]{:S(2)}) %collective-permute-start) | collective-permute-done | bytes 786464 | tf_op jit(solution)/shard_map/ppermute | solution.py:19
  105.4 1.4 fusion.7
  107.1 0.9 collective-permute-done.1
  108.0 0.3 fusion.3
  108.6 0.2 fusion.24
  109.3 0.2 fusion.31
  110.3 0.1 fusion.33
  112.1 0.4 multiply_convert_fusion
  112.6 2.8 collective-permute-start.2
  115.4 8.1 %collective-permute-start.3 = (bf16[1,1,16,1024]{3,2,1,0:T(8,128)(2,1)S(1)}, bf16[1,1,16,1024]{3,2,1,0:T(8,128)(2,1)S(1)}, u32[]{:S(2)}, u32[]{:S(2)}) collective-permute-start(bf16[1,1,16,1024]{3,2,1,0:T(8,128)(2,1)S(1)} %get-tuple-element.9), channel_id=1, source_target_pairs={{24,0},{48,24},{72,48},{96,72},{120,96},{144,120},{168,144},{192,1... | collective-permute-start | bytes 98312 | tf_op jit(solution)/shard_map/ppermute | solution.py:22
  123.5 0.6 multiply_convert_fusion.1
  124.2 0.9 collective-permute-done.3
  125.1 0.1 fusion.76
  125.2 0.1 fusion.77
  125.5 0.1 fusion.15
  125.6 0.1 fusion.74
  126.6 0.1 maximum_dynamic-update-slice_fusion.1
  126.8 1.6 fusion.10
  128.5 1.7 fusion.12
  130.1 0.4 convolution_bitcast_fusion
  130.5 0.4 convolution_bitcast_fusion.1
  130.9 0.4 convolution_bitcast_fusion.2
  131.3 0.9 pad_maximum_fusion
  132.3 0.7 copy-done
  133.0 2.0 add_bitcast_fusion
  135.0 1.2 copy.7
  136.2 313.7 %all-reduce.5 = bf16[1,1,384,1024]{3,1,0,2:T(2,128)(2,1)S(1)} all-reduce(f32[1,1,384,1024]{3,1,0,2:T(1,128)S(1)} %copy.7), channel_id=2, replica_groups=mesh['depth'=32,'chan'=24] {'chan'}, use_global_device_ids=true, to_apply=%region_0.1.clone | all-reduce | flops 393216 | bytes 2359296
  449.9 0.6 copy.8
  450.6 44.8 %all-reduce.4.cloned.1.call-done = f32[16,3,3,3,384]{4,0,3,2,1:T(8,128)} async-done(((f32[16,3,3,3,384]{4,0,3,2,1:T(8,128)}), f32[16,3,3,3,384]{4,0,3,2,1:T(8,128)}) %all-reduce.4.cloned.1.call-update) | async-done | bytes 663568 | tf_op jit(solution)/shard_map/psum | solution.py:89
  495.4 2.0 broadcast_multiply_fusion
  (124 shorter events, 4.9 us)
Async XLA Ops:
  7.2 488.2 %all-reduce.4.cloned.1.call-start = ((), (), s32[]{:S(2)}) async-start(), calls=%async_computation | async-start | bytes 1327104 | tf_op jit(solution)/shard_map/psum | solution.py:89
  43.2 62.3 %collective-permute-start = (bf16[1,1,384,1024]{3,2,1,0:T(8,128)(2,1)S(1)}, bf16[1,1,384,1024]{3,2,1,0:T(8,128)(2,1)}, u32[]{:S(2)}, u32[]{:S(2)}) collective-permute-start(bf16[1,1,384,1024]{3,2,1,0:T(8,128)(2,1)S(1)} %all_gather.3), channel_id=1, source_target_pairs={{0,24},{24,48},{48,72},{72,96},{96,120},{120,144},{144,168},{168,1... | collective-permute-start | bytes 2359304 | tf_op jit(solution)/shard_map/ppermute | solution.py:19
  50.2 57.9 %collective-permute-start.1 = (bf16[1,1,384,1024]{3,2,1,0:T(8,128)(2,1)S(1)}, bf16[1,1,384,1024]{3,2,1,0:T(8,128)(2,1)S(1)}, u32[]{:S(2)}, u32[]{:S(2)}) collective-permute-start(bf16[1,1,384,1024]{3,2,1,0:T(8,128)(2,1)S(1)} %all_gather.3), channel_id=1, source_target_pairs={{24,0},{48,24},{72,48},{96,72},{120,96},{144,120},{168,144},{192,1... | collective-permute-start | bytes 2359304 | tf_op jit(solution)/shard_map/ppermute | solution.py:22
  106.9 1.6 copy-start.6
  106.9 1.6 copy-start.7
  107.0 1.6 copy-start.13
  107.0 1.6 copy-start.14
  108.3 1.0 copy-start.5
  108.6 1.7 copy-start.4
  108.6 1.7 copy-start.11
  108.6 1.7 copy-start.12
  109.6 2.5 copy-start.2
  109.6 2.5 copy-start.3
  109.6 2.5 copy-start.8
  109.6 2.5 copy-start.9
  109.6 2.5 copy-start.10
  112.6 11.6 %collective-permute-start.2 = (bf16[1,1,16,1024]{3,2,1,0:T(8,128)(2,1)S(1)}, bf16[1,1,16,1024]{3,2,1,0:T(8,128)(2,1)S(1)}, u32[]{:S(2)}, u32[]{:S(2)}) collective-permute-start(bf16[1,1,16,1024]{3,2,1,0:T(8,128)(2,1)S(1)} %get-tuple-element.9), channel_id=1, source_target_pairs={{0,24},{24,48},{48,72},{72,96},{96,120},{120,144},{144,168},{168,1... | collective-permute-start | bytes 98312 | tf_op jit(solution)/shard_map/ppermute | solution.py:19
  115.4 9.7 %collective-permute-start.3 = (bf16[1,1,16,1024]{3,2,1,0:T(8,128)(2,1)S(1)}, bf16[1,1,16,1024]{3,2,1,0:T(8,128)(2,1)S(1)}, u32[]{:S(2)}, u32[]{:S(2)}) collective-permute-start(bf16[1,1,16,1024]{3,2,1,0:T(8,128)(2,1)S(1)} %get-tuple-element.9), channel_id=1, source_target_pairs={{24,0},{48,24},{72,48},{96,72},{120,96},{144,120},{168,144},{192,1... | collective-permute-start | bytes 98312 | tf_op jit(solution)/shard_map/ppermute | solution.py:22
  126.8 4.6 copy-start.1
  131.3 1.6 copy-start
Sparse Core Ops, SparseCore 0:
  132.4 362.9 all-reduce.3
where the time goes:
time: 505 us; the launch traced here: 504 us
  blocking collectives  350 us (69%)
  waiting for transfers between devices  85.1 us (17%)
  starting transfers between devices  22.8 us (5%)
  local copies, waits for them, and re-layouts  17.6 us (3%)
  between operations  15.3 us (3%)
  matrix products  8.54 us (2%)
  other arithmetic  5.11 us (1%)
    unnamed x1, blocking collectives  314 us
    psum x1, waiting for transfers between devices, body(): grad_kernel = lax.psum(local_grad, 'depth') * grad_scale  44.8 us
    ppermute x2, waiting for transfers between devices, extended_2(): lax.ppermute(lax.slice_in_dim(block, block.shape[dim] - width, None, axis...  38.5 us
    all_gather x1, blocking collectives, body(): gathered = lax.all_gather(volume, 'chan', axis=2, tiled=True)  36 us
    ppermute x2, starting transfers between devices, extended_2(): lax.ppermute(lax.slice_in_dim(block, 0, width, axis=dim), axis, backward)  13 us
  transfers between devices with their start and end apart: 5, of which 4 were waited for; matrix products, arithmetic and copies ran while one was open for 3% of the time, Pallas kernels for 0%

commit v1 on v0

v1 whole, which is shorter than its diff:
```python
import math

import jax
import jax.numpy as jnp
from jax import lax
from jax.sharding import PartitionSpec as P

DEPTH = 32
SIDE = 32
UNIV = 1
TAPS = 27


def roll_plane(plane_data, row_step, col_step):
    if col_step != 0:
        columns = lax.broadcasted_iota(jnp.int32, plane_data.shape, plane_data.ndim - 1) % SIDE
        edge_col = 0 if col_step > 0 else SIDE - 1
        wrapped = jnp.roll(plane_data, col_step - col_step * SIDE, axis=-1)
        plain = jnp.roll(plane_data, col_step, axis=-1)
        plane_data = jnp.where(columns == edge_col, wrapped, plain)
    if row_step != 0:
        plane_data = jnp.roll(plane_data, row_step * SIDE, axis=-1)
    return plane_data


def spread(block, axis):
    count = lax.axis_size(axis)
    return lax.all_to_all(jnp.broadcast_to(block[None], (count,) + block.shape), axis, 0, 0)


def rolled_sum(product, sign):
    product = product.reshape(3, 3, 3, -1, product.shape[-1])
    sums = []
    for depth_tap in range(3):
        total = None
        for row_tap in range(3):
            for col_tap in range(3):
                term = roll_plane(
                    product[depth_tap, row_tap, col_tap], sign * (1 - row_tap), sign * (1 - col_tap)
                )
                total = term if total is None else total + term
        sums.append(total)
    return sums


def body(volume, kernel, cotangent):
    ch_local = volume.shape[2]
    cells = volume.shape[3]
    chans = lax.axis_size("chan")
    depths = lax.axis_size("depth")
    ring = [(i, (i + 1) % depths) for i in range(depths)]
    back = [(b, a) for a, b in ring]

    gathered = spread(volume.reshape(ch_local, cells), "chan").reshape(-1, cells)
    k4 = kernel.reshape(ch_local, TAPS, chans, ch_local)
    k_in = lax.all_to_all(
        jnp.transpose(k4, (2, 0, 1, 3)).reshape(chans, ch_local, TAPS * ch_local), "chan", 0, 0
    ).reshape(chans * ch_local, TAPS * ch_local)
    k_rows = jnp.transpose(kernel.reshape(ch_local, TAPS, -1), (1, 0, 2)).reshape(TAPS * ch_local, -1)

    product = jnp.dot(k_rows, gathered, preferred_element_type=jnp.float32)
    up, mid, down = rolled_sum(product, 1)
    preact = mid + lax.ppermute(up, "depth", ring) + lax.ppermute(down, "depth", back)
    sig = jax.nn.sigmoid(preact)
    activated = (preact * sig).astype(jnp.bfloat16)
    cot = cotangent.reshape(ch_local, cells).astype(jnp.float32)
    grad_pre = (cot * sig * (1.0 + preact * (1.0 - sig))).astype(jnp.bfloat16)

    grad_above = lax.ppermute(grad_pre, "depth", back)
    grad_below = lax.ppermute(grad_pre, "depth", ring)
    stacked = jnp.concatenate(
        [
            roll_plane(plane, row_tap - 1, col_tap - 1)
            for plane in (grad_above, grad_pre, grad_below)
            for row_tap in range(3)
            for col_tap in range(3)
        ],
        axis=0,
    )
    local = lax.dot_general(
        stacked, gathered, (((1,), (1,)), ((), ())), preferred_element_type=jnp.float32
    )
    pieces = local.astype(jnp.bfloat16).reshape(TAPS, ch_local, -1)
    pieces = jnp.concatenate(
        [pieces, jnp.zeros((depths - TAPS,) + pieces.shape[1:], pieces.dtype)], axis=0
    )
    terms = lax.all_to_all(pieces, "depth", 0, 0)
    grad_scale = 1.0 / math.sqrt(UNIV * DEPTH * SIDE * SIDE)
    tap_total = jnp.sum(terms.astype(jnp.float32), axis=0) * grad_scale
    all_taps = spread(tap_total.astype(jnp.bfloat16), "depth")[:TAPS]
    grad_kernel = jnp.transpose(all_taps.astype(jnp.float32), (1, 0, 2)).reshape(kernel.shape)

    grad_all = spread(grad_pre, "chan").reshape(-1, cells)
    back_product = lax.dot_general(
        k_in, grad_all, (((0,), (0,)), ((), ())), preferred_element_type=jnp.float32
    )
    low, same, high = rolled_sum(back_product, -1)
    grad_volume = (
        same + lax.ppermute(low, "depth", back) + lax.ppermute(high, "depth", ring)
    ).astype(jnp.bfloat16)
    return (activated.reshape(volume.shape), grad_volume.reshape(volume.shape), grad_kernel)


def solution(mesh):
    placed = (
        P(None, "depth", "chan", None),
        P("chan", None, None, None, None),
        P(None, "depth", "chan", None),
    )
    return jax.shard_map(
        body,
        mesh=mesh,
        in_specs=placed,
        out_specs=(
            P(None, "depth", "chan", None),
            P(None, "depth", "chan", None),
            P("chan", None, None, None, None),
        ),
        check_vma=False,
    )
```

time: 505 us -> 179 us (0.35)
  the two profiles are of different devices: /device:TPU:2 before, /device:TPU:1 now
where the time goes in v1:
time: 179 us; the launch traced here: 178 us
  starting transfers between devices  73.6 us (41%)
  waiting for transfers between devices  39.3 us (22%)
  local copies, waits for them, and re-layouts  26.5 us (15%)
  blocking collectives  25.7 us (14%)
  other arithmetic  9.94 us (6%)
  matrix products  1.92 us (1%)
    all_to_all x3, starting transfers between devices, spread(): lax.all_to_all(jnp.broadcast_to(block[None], (count,) + block.shape), axi...  35.4 us
    all_to_all x3, waiting for transfers between devices, spread(): lax.all_to_all(jnp.broadcast_to(block[None], (count,) + block.shape), axi...  31 us
    all_to_all x1, blocking collectives, body(): terms = lax.all_to_all(pieces, 'depth', 0, 0)  25.7 us
    ppermute x1, starting transfers between devices, body(): lax.ppermute(down, 'depth', back)  10.7 us
    ppermute x1, starting transfers between devices, body(): grad_above = lax.ppermute(grad_pre, 'depth', back)  8.75 us
    ppermute x1, waiting for transfers between devices, body(): lax.ppermute(high, 'depth', ring)  7.06 us
    ppermute x1, starting transfers between devices, body(): lax.ppermute(low, 'depth', back)  5.47 us
    ppermute x1, starting transfers between devices, body(): lax.ppermute(high, 'depth', ring)  4.94 us
  transfers between devices with their start and end apart: 10, of which 4 were waited for; matrix products, arithmetic and copies ran while one was open for 14% of the time, Pallas kernels for 0%

profile of v1, /device:TPU:1, one launch (start us, length us, event | category | flops | bytes accessed | tf_op | source)
XLA Modules:
  0.0 178.2 jit_solution(906620762882741635)
XLA Ops:
  0.6 1.8 %broadcast_in_dim.9 = bf16[24,16,1024]{2,1,0:T(8,128)(2,1)} broadcast(bf16[16,1024]{1,0:T(8,128)(2,1)} %bitcast.282), dimensions={1,2} | broadcast | bytes 819200 | tf_op jit(solution)/shard_map/broadcast_in_dim | solution.py:28
  2.5 14.1 %all-to-all-start = ((bf16[24,16,1024]{2,1,0:T(8,128)(2,1)}), bf16[24,16,1024]{2,1,0:T(8,128)(2,1)S(1)}, u32[]{:S(2)}, u32[]{:S(2)}) async-start(bf16[24,16,1024]{2,1,0:T(8,128)(2,1)} %broadcast_in_dim.9), calls=%async_computation | async-start | bytes 1572864 | tf_op jit(solution)/shard_map/all_to_all | solution.py:28
  16.6 15.9 %all-to-all-done = bf16[24,16,1024]{2,1,0:T(8,128)(2,1)S(1)} async-done(((bf16[24,16,1024]{2,1,0:T(8,128)(2,1)}), bf16[24,16,1024]{2,1,0:T(8,128)(2,1)S(1)}, u32[]{:S(2)}, u32[]{:S(2)}) %all-to-all-start) | async-done | bytes 786464 | tf_op jit(solution)/shard_map/all_to_all | solution.py:28
  32.5 0.6 fusion
  33.1 0.7 slice_bitcast_fusion.52
  34.2 0.8 slice_bitcast_fusion.53
  36.3 0.1 slice.1527
  36.4 0.1 slice.1515
  36.9 0.8 fusion.22
  38.2 0.8 fusion.43
  39.2 0.8 fusion.20
  40.5 0.8 fusion.57
  41.3 10.7 %collective-permute-start.1 = (f32[16,1024]{1,0:T(8,128)}, f32[16,1024]{1,0:T(8,128)}, u32[]{:S(2)}, u32[]{:S(2)}) collective-permute-start(f32[16,1024]{1,0:T(8,128)} %fusion.57), channel_id=1, source_target_pairs={{24,0},{48,24},{72,48},{96,72},{120,96},{144,120},{168,144},{192,1... | collective-permute-start | bytes 196616 | tf_op jit(solution)/shard_map/ppermute | solution.py:63
  52.0 0.8 fusion.53
  52.8 1.9 %collective-permute-start = (f32[16,1024]{1,0:T(8,128)}, f32[16,1024]{1,0:T(8,128)}, u32[]{:S(2)}, u32[]{:S(2)}) collective-permute-start(f32[16,1024]{1,0:T(8,128)} %fusion.53), channel_id=1, source_target_pairs={{0,24},{24,48},{48,72},{72,96},{96,120},{120,144},{144,168},{168,1... | collective-permute-start | bytes 196616 | tf_op jit(solution)/shard_map/ppermute | solution.py:63
  54.7 3.2 %reshape.54 = bf16[16,27,24,16]{3,2,0,1:T(8,128)(2,1)S(1)} reshape(bf16[16,3,3,3,384]{4,0,3,2,1:T(8,128)(2,1)} %param.4) | data formatting | bytes 663552 | tf_op jit(solution)/shard_map/reshape | solution.py:55
  57.9 2.4 %copy.9 = bf16[24,16,27,16]{0,3,2,1:T(8,128)(2,1)} copy(bf16[24,16,27,16]{3,0,1,2:T(8,128)(2,1)S(1)} %bitcast.217) | data formatting | bytes 663552 | tf_op jit(solution)/shard_map/transpose | solution.py:57
  60.4 2.8 %copy.10 = bf16[24,16,432]{2,1,0:T(8,128)(2,1)} copy(bf16[24,16,432]{0,2,1:T(8,128)(2,1)} %bitcast.223) | data formatting | bytes 663552 | tf_op jit(solution)/shard_map/reshape | solution.py:57
  63.2 4.5 %all-to-all-start.2 = ((bf16[24,16,432]{2,1,0:T(8,128)(2,1)}), bf16[24,16,432]{2,1,0:T(8,128)(2,1)S(1)}, u32[]{:S(2)}, u32[]{:S(2)}) async-start(bf16[24,16,432]{2,1,0:T(8,128)(2,1)} %copy.10), calls=%async_computation.2 | async-start | bytes 786432 | tf_op jit(solution)/shard_map/all_to_all | solution.py:56
  68.6 1.1 fusion.92
  69.8 1.9 %collective-permute-start.5 = (bf16[16,1024]{1,0:T(8,128)(2,1)S(1)}, bf16[16,1024]{1,0:T(8,128)(2,1)S(1)}, u32[]{:S(2)}, u32[]{:S(2)}) collective-permute-start(bf16[16,1024]{1,0:T(8,128)(2,1)S(1)} %get-tuple-element.3), channel_id=1, source_target_pairs={{0,24},{24,48},{48,72},{72,96},{96,120},{120,144},{144,168},{168,1... | collective-permute-start | bytes 98312 | tf_op jit(solution)/shard_map/ppermute | solution.py:70
  72.1 8.8 %collective-permute-start.4 = (bf16[16,1024]{1,0:T(8,128)(2,1)S(1)}, bf16[16,1024]{1,0:T(8,128)(2,1)S(1)}, u32[]{:S(2)}, u32[]{:S(2)}) collective-permute-start(bf16[16,1024]{1,0:T(8,128)(2,1)S(1)} %get-tuple-element.3), channel_id=1, source_target_pairs={{24,0},{48,24},{72,48},{96,72},{120,96},{144,120},{168,144},{192,1... | collective-permute-start | bytes 98312 | tf_op jit(solution)/shard_map/ppermute | solution.py:69
  80.8 1.2 collective-permute-done.5
  82.7 0.1 fusion.2
  83.4 0.1 fusion.3
  85.7 0.6 convolution_convert_fusion
  86.4 25.7 %all_to_all.25 = bf16[32,16,384]{2,1,0:T(8,128)(2,1)S(1)} all-to-all(bf16[32,16,384]{2,1,0:T(8,128)(2,1)S(1)} %concatenate.595), channel_id=1, replica_groups=mesh['depth'=32,'chan'=24] {'depth'}, dimensions={0} | all-to-all | bytes 786432 | tf_op jit(solution)/shard_map/all_to_all | solution.py:87
  112.1 1.0 broadcast_in_dim.10
  113.1 14.1 %all-to-all-start.1 = ((bf16[24,16,1024]{2,1,0:T(8,128)(2,1)}), bf16[24,16,1024]{2,1,0:T(8,128)(2,1)S(1)}, u32[]{:S(2)}, u32[]{:S(2)}) async-start(bf16[24,16,1024]{2,1,0:T(8,128)(2,1)} %broadcast_in_dim.10), calls=%async_computation.1 | async-start | bytes 1572864 | tf_op jit(solution)/shard_map/all_to_all | solution.py:28
  127.2 0.6 fusion.93
  127.9 15.1 %all-to-all-done.1 = bf16[24,16,1024]{2,1,0:T(8,128)(2,1)S(1)} async-done(((bf16[24,16,1024]{2,1,0:T(8,128)(2,1)}), bf16[24,16,1024]{2,1,0:T(8,128)(2,1)S(1)}, u32[]{:S(2)}, u32[]{:S(2)}) %all-to-all-start.1) | async-done | bytes 786464 | tf_op jit(solution)/shard_map/all_to_all | solution.py:28
  143.0 0.8 broadcast_in_dim.11
  143.8 7.2 %all-to-all-start.4 = ((bf16[32,16,384]{2,1,0:T(8,128)(2,1)}), bf16[32,16,384]{2,1,0:T(8,128)(2,1)S(1)}, u32[]{:S(2)}, u32[]{:S(2)}) async-start(bf16[32,16,384]{2,1,0:T(8,128)(2,1)} %broadcast_in_dim.11), calls=%async_computation.4 | async-start | bytes 786432 | tf_op jit(solution)/shard_map/all_to_all | solution.py:28
  151.0 0.7 fusion.130
  152.2 0.7 slice.1555
  152.9 0.7 slice.1551
  153.7 0.1 slice_bitcast_fusion.26
  155.8 0.2 fusion.34
  155.9 0.7 slice.1536
  157.2 0.2 fusion.32
  157.6 0.2 fusion.13
  158.6 0.2 fusion.78
  158.8 4.9 %collective-permute-start.3 = (f32[16,1024]{1,0:T(8,128)S(1)}, f32[16,1024]{1,0:T(8,128)S(1)}, u32[]{:S(2)}, u32[]{:S(2)}) collective-permute-start(f32[16,1024]{1,0:T(8,128)S(1)} %fusion.78), channel_id=1, source_target_pairs={{0,24},{24,48},{48,72},{72,96},{96,120},{120,144},{144,168},{168,1... | collective-permute-start | bytes 196616 | tf_op jit(solution)/shard_map/ppermute | solution.py:99
  163.7 0.2 fusion.72
  163.9 5.5 %collective-permute-start.2 = (f32[16,1024]{1,0:T(8,128)S(1)}, f32[16,1024]{1,0:T(8,128)S(1)}, u32[]{:S(2)}, u32[]{:S(2)}) collective-permute-start(f32[16,1024]{1,0:T(8,128)S(1)} %fusion.72), channel_id=1, source_target_pairs={{24,0},{48,24},{72,48},{96,72},{120,96},{144,120},{168,144},{192,1... | collective-permute-start | bytes 196616 | tf_op jit(solution)/shard_map/ppermute | solution.py:99
  169.4 0.9 slice_convert_fusion
  170.3 7.1 %collective-permute-done.3 = f32[16,1024]{1,0:T(8,128)S(1)} collective-permute-done((f32[16,1024]{1,0:T(8,128)S(1)}, f32[16,1024]{1,0:T(8,128)S(1)}, u32[]{:S(2)}, u32[]{:S(2)}) %collective-permute-start.3) | collective-permute-done | bytes 65568 | tf_op jit(solution)/shard_map/ppermute | solution.py:99
  177.4 0.8 fusion.94
  (252 shorter events, 12.1 us)
Async XLA Ops:
  0.6 31.8 %copy-start.1 = (bf16[16,3,3,3,384]{4,0,3,2,1:T(8,128)(2,1)S(1)}, bf16[16,3,3,3,384]{4,0,3,2,1:T(8,128)(2,1)}, u32[]{:S(2)}) copy-start(bf16[16,3,3,3,384]{4,0,3,2,1:T(8,128)(2,1)} %param.4) | copy-start | bytes 995332
  2.5 30.0 %all-to-all-start = ((bf16[24,16,1024]{2,1,0:T(8,128)(2,1)}), bf16[24,16,1024]{2,1,0:T(8,128)(2,1)S(1)}, u32[]{:S(2)}, u32[]{:S(2)}) async-start(bf16[24,16,1024]{2,1,0:T(8,128)(2,1)} %broadcast_in_dim.9), calls=%async_computation | async-start | bytes 1572864 | tf_op jit(solution)/shard_map/all_to_all | solution.py:28
  33.1 18.9 %copy-start = (f32[3,3,3,16,1024]{4,3,2,1,0:T(8,128)}, f32[3,3,3,16,1024]{4,3,2,1,0:T(8,128)S(1)}, u32[]{:S(2)}) copy-start(f32[3,3,3,16,1024]{4,3,2,1,0:T(8,128)S(1)} %fusion) | copy-start | bytes 5308420
  41.3 27.3 %collective-permute-start.1 = (f32[16,1024]{1,0:T(8,128)}, f32[16,1024]{1,0:T(8,128)}, u32[]{:S(2)}, u32[]{:S(2)}) collective-permute-start(f32[16,1024]{1,0:T(8,128)} %fusion.57), channel_id=1, source_target_pairs={{24,0},{48,24},{72,48},{96,72},{120,96},{144,120},{168,144},{192,1... | collective-permute-start | bytes 196616 | tf_op jit(solution)/shard_map/ppermute | solution.py:63
  52.8 15.8 %collective-permute-start = (f32[16,1024]{1,0:T(8,128)}, f32[16,1024]{1,0:T(8,128)}, u32[]{:S(2)}, u32[]{:S(2)}) collective-permute-start(f32[16,1024]{1,0:T(8,128)} %fusion.53), channel_id=1, source_target_pairs={{0,24},{24,48},{48,72},{72,96},{96,120},{120,144},{144,168},{168,1... | collective-permute-start | bytes 196616 | tf_op jit(solution)/shard_map/ppermute | solution.py:63
  60.3 7.4 %copy-start.2 = (f32[16,1024]{1,0:T(8,128)S(1)}, f32[16,1024]{1,0:T(8,128)}, u32[]{:S(2)}) copy-start(f32[16,1024]{1,0:T(8,128)} %get-tuple-element.51) | copy-start | bytes 196612
  60.3 7.7 %copy-start.4 = (f32[16,1024]{1,0:T(8,128)S(1)}, f32[16,1024]{1,0:T(8,128)}, u32[]{:S(2)}) copy-start(f32[16,1024]{1,0:T(8,128)} %get-tuple-element.47) | copy-start | bytes 196612
  60.3 7.8 %copy-start.8 = (f32[16,1024]{1,0:T(8,128)S(1)}, f32[16,1024]{1,0:T(8,128)}, u32[]{:S(2)}) copy-start(f32[16,1024]{1,0:T(8,128)} %get-tuple-element.139) | copy-start | bytes 196612
  60.4 7.9 %copy-start.7 = (f32[16,1024]{1,0:T(8,128)S(1)}, f32[16,1024]{1,0:T(8,128)}, u32[]{:S(2)}) copy-start(f32[16,1024]{1,0:T(8,128)} %get-tuple-element.140) | copy-start | bytes 196612
  60.4 8.0 %copy-start.3 = (f32[16,1024]{1,0:T(8,128)S(1)}, f32[16,1024]{1,0:T(8,128)}, u32[]{:S(2)}) copy-start(f32[16,1024]{1,0:T(8,128)} %get-tuple-element.48) | copy-start | bytes 196612
  60.4 8.0 %copy-start.5 = (f32[16,1024]{1,0:T(8,128)S(1)}, f32[16,1024]{1,0:T(8,128)}, u32[]{:S(2)}) copy-start(f32[16,1024]{1,0:T(8,128)} %get-tuple-element.131) | copy-start | bytes 196612
  60.4 8.1 %copy-start.6 = (f32[16,1024]{1,0:T(8,128)S(1)}, f32[16,1024]{1,0:T(8,128)}, u32[]{:S(2)}) copy-start(f32[16,1024]{1,0:T(8,128)} %get-tuple-element.135) | copy-start | bytes 196612
  60.4 8.2 %copy-start.12 = (bf16[1,1,16,1024]{3,2,1,0:T(8,128)(2,1)S(1)}, bf16[1,1,16,1024]{3,2,1,0:T(8,128)(2,1)}, u32[]{:S(2)}) copy-start(bf16[1,1,16,1024]{3,2,1,0:T(8,128)(2,1)} %param.5) | copy-start | bytes 98308
  63.2 23.2 %all-to-all-start.2 = ((bf16[24,16,432]{2,1,0:T(8,128)(2,1)}), bf16[24,16,432]{2,1,0:T(8,128)(2,1)S(1)}, u32[]{:S(2)}, u32[]{:S(2)}) async-start(bf16[24,16,432]{2,1,0:T(8,128)(2,1)} %copy.10), calls=%async_computation.2 | async-start | bytes 786432 | tf_op jit(solution)/shard_map/all_to_all | solution.py:56
  69.8 12.2 %collective-permute-start.5 = (bf16[16,1024]{1,0:T(8,128)(2,1)S(1)}, bf16[16,1024]{1,0:T(8,128)(2,1)S(1)}, u32[]{:S(2)}, u32[]{:S(2)}) collective-permute-start(bf16[16,1024]{1,0:T(8,128)(2,1)S(1)} %get-tuple-element.3), channel_id=1, source_target_pairs={{0,24},{24,48},{48,72},{72,96},{96,120},{120,144},{144,168},{168,1... | collective-permute-start | bytes 98312 | tf_op jit(solution)/shard_map/ppermute | solution.py:70
  72.1 10.1 %collective-permute-start.4 = (bf16[16,1024]{1,0:T(8,128)(2,1)S(1)}, bf16[16,1024]{1,0:T(8,128)(2,1)S(1)}, u32[]{:S(2)}, u32[]{:S(2)}) collective-permute-start(bf16[16,1024]{1,0:T(8,128)(2,1)S(1)} %get-tuple-element.3), channel_id=1, source_target_pairs={{24,0},{48,24},{72,48},{96,72},{120,96},{144,120},{168,144},{192,1... | collective-permute-start | bytes 98312 | tf_op jit(solution)/shard_map/ppermute | solution.py:69
  113.1 29.9 %all-to-all-start.1 = ((bf16[24,16,1024]{2,1,0:T(8,128)(2,1)}), bf16[24,16,1024]{2,1,0:T(8,128)(2,1)S(1)}, u32[]{:S(2)}, u32[]{:S(2)}) async-start(bf16[24,16,1024]{2,1,0:T(8,128)(2,1)} %broadcast_in_dim.10), calls=%async_computation.1 | async-start | bytes 1572864 | tf_op jit(solution)/shard_map/all_to_all | solution.py:28
  143.8 25.6 %all-to-all-start.4 = ((bf16[32,16,384]{2,1,0:T(8,128)(2,1)}), bf16[32,16,384]{2,1,0:T(8,128)(2,1)S(1)}, u32[]{:S(2)}, u32[]{:S(2)}) async-start(bf16[32,16,384]{2,1,0:T(8,128)(2,1)} %broadcast_in_dim.11), calls=%async_computation.4 | async-start | bytes 786432 | tf_op jit(solution)/shard_map/all_to_all | solution.py:28
  157.7 19.6 %copy-start.9 = (f32[16,993]{1,0:T(8,128)S(1)}, f32[16,993]{1,0:T(8,128)}, u32[]{:S(2)}) copy-start(f32[16,993]{1,0:T(8,128)} %slice.1555) | copy-start | bytes 190660
  157.7 19.6 %copy-start.10 = (f32[16,1023]{1,0:T(8,128)S(1)}, f32[16,1023]{1,0:T(8,128)}, u32[]{:S(2)}) copy-start(f32[16,1023]{1,0:T(8,128)} %slice.1551) | copy-start | bytes 196420
  157.8 19.6 %copy-start.11 = (f32[16,992]{1,0:T(8,128)S(1)}, f32[16,992]{1,0:T(8,128)}, u32[]{:S(2)}) copy-start(f32[16,992]{1,0:T(8,128)} %slice.1536) | copy-start | bytes 190468
  158.8 18.6 %collective-permute-start.3 = (f32[16,1024]{1,0:T(8,128)S(1)}, f32[16,1024]{1,0:T(8,128)S(1)}, u32[]{:S(2)}, u32[]{:S(2)}) collective-permute-start(f32[16,1024]{1,0:T(8,128)S(1)} %fusion.78), channel_id=1, source_target_pairs={{0,24},{24,48},{48,72},{72,96},{96,120},{120,144},{144,168},{168,1... | collective-permute-start | bytes 196616 | tf_op jit(solution)/shard_map/ppermute | solution.py:99
  163.9 13.4 %collective-permute-start.2 = (f32[16,1024]{1,0:T(8,128)S(1)}, f32[16,1024]{1,0:T(8,128)S(1)}, u32[]{:S(2)}, u32[]{:S(2)}) collective-permute-start(f32[16,1024]{1,0:T(8,128)S(1)} %fusion.72), channel_id=1, source_target_pairs={{24,0},{48,24},{72,48},{96,72},{120,96},{144,120},{168,144},{192,1... | collective-permute-start | bytes 196616 | tf_op jit(solution)/shard_map/ppermute | solution.py:99

commit v2 on v1

v2 whole, which is shorter than its diff:
```python
import functools
import math

import jax
import jax.numpy as jnp
from jax import lax
from jax.experimental import pallas as pl
from jax.experimental.pallas import tpu as pltpu
from jax.sharding import Mesh
from jax.sharding import PartitionSpec as P

DEPTH = 32
SIDE = 32
UNIV = 1
TAPS = 27
VMEM_LIMIT = 48 * 1024 * 1024
DEP = ("y", "zh")
CHIPS = ("x", "zl")
CHAN = ("x", "zl", "core")


def shift_cells(plane, row_step, col_step):
    cells = plane.shape[-1]
    if col_step:
        columns = lax.broadcasted_iota(jnp.int32, plane.shape, 1) % SIDE
        edge = 0 if col_step > 0 else SIDE - 1
        plain = pltpu.roll(plane, col_step % cells, 1)
        wrapped = pltpu.roll(plane, (col_step - col_step * SIDE) % cells, 1)
        plane = jnp.where(columns == edge, wrapped, plain)
    if row_step:
        plane = pltpu.roll(plane, (row_step * SIDE) % cells, 1)
    return plane


def merge_cores(core_ref, mine_ref, other_ref, x_ref):
    first = core_ref[0] == 0
    mine, other = mine_ref[...], other_ref[...]
    x_ref[:, 0] = jnp.where(first, mine, other)
    x_ref[:, 1] = jnp.where(first, other, mine)
    return x_ref[...].reshape(-1, x_ref.shape[-1])


def conv_kernel(core_ref, w_ref, mine_ref, other_ref, *refs, sign):
    outs, x_ref = refs[:3], refs[3]
    rows = outs[0].shape[0]
    x = merge_cores(core_ref, mine_ref, other_ref, x_ref)
    for depth_tap in range(3):
        w = w_ref[depth_tap * 9 * rows : (depth_tap + 1) * 9 * rows, :]
        product = jnp.dot(w, x, preferred_element_type=jnp.float32)
        total = None
        for col_tap in range(3):
            part = None
            for row_tap in range(3):
                at = (row_tap * 3 + col_tap) * rows
                term = shift_cells(product[at : at + rows], sign * (1 - row_tap), 0)
                part = term if part is None else part + term
            part = shift_cells(part, 0, sign * (1 - col_tap))
            total = part if total is None else total + part
        outs[depth_tap][...] = total


def merged_specs(count):
    smem = pl.BlockSpec(memory_space=pltpu.SMEM)
    return [smem] + [pl.BlockSpec(memory_space=pltpu.VMEM)] * count


def merged_scratch(mine):
    return [pltpu.VMEM((mine.shape[0], 2) + mine.shape[1:], mine.dtype)]


def conv(core, weights, mine, other, sign):
    rows = weights.shape[0] // TAPS
    cells = mine.shape[-1]
    return pl.pallas_call(
        functools.partial(conv_kernel, sign=sign),
        out_shape=[jax.ShapeDtypeStruct((rows, cells), jnp.float32)] * 3,
        in_specs=merged_specs(3),
        scratch_shapes=merged_scratch(mine),
        compiler_params=pltpu.CompilerParams(vmem_limit_bytes=VMEM_LIMIT),
        name="conv",
    )(core, weights, mine, other)


def wgrad_kernel(core_ref, above_ref, own_ref, below_ref, mine_ref, other_ref, out_ref, x_ref):
    rows = own_ref.shape[0]
    x = merge_cores(core_ref, mine_ref, other_ref, x_ref)
    for depth_tap, ref in enumerate((above_ref, own_ref, below_ref)):
        plane = ref[...].astype(jnp.float32)
        moved = [shift_cells(plane, 0, col_tap - 1) for col_tap in range(3)]
        stack = jnp.concatenate(
            [
                shift_cells(moved[col_tap], row_tap - 1, 0).astype(jnp.bfloat16)
                for row_tap in range(3)
                for col_tap in range(3)
            ],
            axis=0,
        )
        grad = lax.dot_general(
            stack, x, (((1,), (1,)), ((), ())), preferred_element_type=jnp.float32
        )
        out_ref[depth_tap * 9 : depth_tap * 9 + 9] = grad.astype(jnp.bfloat16).reshape(9, rows, -1)
    out_ref[TAPS:] = jnp.zeros((out_ref.shape[0] - TAPS,) + out_ref.shape[1:], out_ref.dtype)


def wgrad(core, above, own, below, mine, other, slots):
    rows = own.shape[0]
    chans = 2 * mine.shape[0] * mine.shape[1]
    return pl.pallas_call(
        wgrad_kernel,
        out_shape=jax.ShapeDtypeStruct((slots, rows, chans), jnp.bfloat16),
        in_specs=merged_specs(5),
        scratch_shapes=merged_scratch(mine),
        compiler_params=pltpu.CompilerParams(vmem_limit_bytes=VMEM_LIMIT),
        name="wgrad",
    )(core, above, own, below, mine, other)


def act_kernel(mid_ref, low_ref, high_ref, cot_ref, act_ref, grad_ref):
    preact = mid_ref[...] + low_ref[...] + high_ref[...]
    sig = jax.nn.sigmoid(preact)
    act_ref[...] = (preact * sig).astype(jnp.bfloat16)
    cot = cot_ref[...].astype(jnp.float32)
    grad_ref[...] = (cot * sig * (1.0 + preact * (1.0 - sig))).astype(jnp.bfloat16)


def activate(mid, low, high, cot):
    shape = jax.ShapeDtypeStruct(mid.shape, jnp.bfloat16)
    return pl.pallas_call(
        act_kernel,
        out_shape=[shape, shape],
        compiler_params=pltpu.CompilerParams(vmem_limit_bytes=VMEM_LIMIT),
        name="activate",
    )(mid, low, high, cot)


def total_kernel(terms_ref, out_ref, *, scale):
    total = jnp.sum(terms_ref[...].astype(jnp.float32), axis=0) * scale
    out_ref[...] = jnp.broadcast_to(total.astype(jnp.bfloat16)[None], out_ref.shape)


def total_spread(terms, scale, copies):
    return pl.pallas_call(
        functools.partial(total_kernel, scale=scale),
        out_shape=jax.ShapeDtypeStruct((copies,) + terms.shape[1:], jnp.bfloat16),
        compiler_params=pltpu.CompilerParams(vmem_limit_bytes=VMEM_LIMIT),
        name="total",
    )(terms)


def swap_cores(blocks):
    return lax.ppermute(blocks, "core", [(0, 1), (1, 0)])


def body(volume, kernel, cotangent):
    rows = volume.shape[2]
    cells = volume.shape[3]
    chips = lax.axis_size(CHIPS)
    chans = lax.axis_size(CHAN)
    depths = lax.axis_size(DEP)
    ring = [(i, (i + 1) % depths) for i in range(depths)]
    back = [(b, a) for a, b in ring]
    core = lax.axis_index("core").astype(jnp.int32).reshape(1)
    own = volume.reshape(rows, cells)
    cot = cotangent.reshape(rows, cells)

    def copies(block):
        return jnp.broadcast_to(block[None], (chips, rows, cells))

    mine = lax.all_to_all(copies(own), CHIPS, 0, 0)
    k_rows = jnp.transpose(kernel.reshape(rows, TAPS, -1), (1, 0, 2)).reshape(TAPS * rows, -1)
    pieces = jnp.transpose(k_rows).reshape(chans, rows, TAPS * rows)
    mine, pieces, k_rows, cot = lax.optimization_barrier((mine, pieces, k_rows, cot))
    other = swap_cores(mine)
    k_in = lax.all_to_all(pieces, CHAN, 0, 0)

    up, mid, down = conv(core, k_rows, mine, other, 1)
    low = lax.ppermute(up, DEP, ring)
    high = lax.ppermute(down, DEP, back)
    activated, grad_pre = activate(mid, low, high, cot)
    grad_pre, k_in = lax.optimization_barrier((grad_pre, k_in))

    grad_above = lax.ppermute(grad_pre, DEP, back)
    grad_below = lax.ppermute(grad_pre, DEP, ring)
    grad_mine = lax.all_to_all(copies(grad_pre), CHIPS, 0, 0)
    wide = wgrad(core, grad_above, grad_pre, grad_below, mine, other, depths)
    wide, grad_mine = lax.optimization_barrier((wide, grad_mine))
    terms = lax.all_to_all(wide, DEP, 0, 0)

    k_cols = jnp.transpose(k_in.reshape(chans, rows, TAPS, rows), (2, 1, 0, 3))
    k_cols = k_cols.reshape(TAPS * rows, chans * rows)
    grad_other = swap_cores(grad_mine)
    to_low, same, to_high = conv(core, k_cols, grad_mine, grad_other, -1)
    terms, same = lax.optimization_barrier((terms, same))
    from_high = lax.ppermute(to_low, DEP, back)
    from_low = lax.ppermute(to_high, DEP, ring)
    grad_volume = (same + from_high + from_low).astype(jnp.bfloat16)

    scale = 1.0 / math.sqrt(UNIV * DEPTH * SIDE * SIDE)
    all_taps = lax.all_to_all(total_spread(terms, scale, depths), DEP, 0, 0)[:TAPS]
    grad_kernel = jnp.transpose(all_taps.astype(jnp.float32), (1, 0, 2)).reshape(kernel.shape)
    return (activated.reshape(volume.shape), grad_volume.reshape(volume.shape), grad_kernel)


def solution(mesh):
    fine = Mesh(mesh.devices.reshape(8, 4, 4, 3, 2), ("y", "zh", "x", "zl", "core"))
    field = P(None, DEP, CHAN, None)
    weight = P(CHAN, None, None, None, None)
    return jax.shard_map(
        body,
        mesh=fine,
        in_specs=(field, weight, field),
        out_specs=(field, field, weight),
        check_vma=False,
    )
```

time: 179 us -> 141 us (0.79)
  the two profiles are of different devices: /device:TPU:1 before, /device:TPU:130 now
where the time goes in v2:
time: 141 us; the launch traced here: 140 us
  starting transfers between devices  76.1 us (54%)
  waiting for transfers between devices  43.9 us (31%)
  local copies, waits for them, and re-layouts  12.4 us (9%)
  Pallas kernels  5.27 us (4%)
  other arithmetic  1.51 us (1%)
    all_to_all x1, starting transfers between devices, body(): mine = lax.all_to_all(copies(own), CHIPS, 0, 0)  11.2 us
    ppermute x1, waiting for transfers between devices, body(): from_low = lax.ppermute(to_high, DEP, ring)  10.3 us
    all_to_all x1, waiting for transfers between devices, body(): terms = lax.all_to_all(wide, DEP, 0, 0)  9.25 us
    ppermute x1, starting transfers between devices, body(): low = lax.ppermute(up, DEP, ring)  8.38 us
    ppermute x1, waiting for transfers between devices, body(): grad_below = lax.ppermute(grad_pre, DEP, ring)  7.56 us
    all_to_all x1, starting transfers between devices, body(): terms = lax.all_to_all(wide, DEP, 0, 0)  7.4 us
    all_to_all x1, starting transfers between devices, body(): k_in = lax.all_to_all(pieces, CHAN, 0, 0)  7.22 us
    ppermute x1, starting transfers between devices, body(): from_low = lax.ppermute(to_high, DEP, ring)  6.71 us
  transfers between devices with their start and end apart: 13, of which 10 were waited for; matrix products, arithmetic and copies ran while one was open for 8% of the time, Pallas kernels for 3%

profile of v2, /device:TPU:130, one launch (start us, length us, event | category | flops | bytes accessed | tf_op | source)
XLA Modules:
  0.0 139.9 jit_solution(14712235564732286629)
XLA Ops:
  0.6 0.0 copy-start
  0.6 0.0 copy-start.1
  0.7 1.6 %broadcast_in_dim.14 = bf16[12,16,1024]{2,1,0:T(8,128)(2,1)} broadcast(bf16[16,1024]{1,0:T(8,128)(2,1)} %bitcast.27), dimensions={1,2} | broadcast | bytes 425984 | tf_op jit(solution)/shard_map/broadcast_in_dim | solution.py:167
  2.2 11.2 %all-to-all-start = ((bf16[12,16,1024]{2,1,0:T(8,128)(2,1)}), bf16[12,16,1024]{2,1,0:T(8,128)(2,1)S(1)}, u32[]{:S(2)}, u32[]{:S(2)}) async-start(bf16[12,16,1024]{2,1,0:T(8,128)(2,1)} %broadcast_in_dim.14), calls=%async_computation | async-start | bytes 786432 | tf_op jit(solution)/shard_map/all_to_all | solution.py:169
  13.4 1.9 %copy.6 = bf16[384,432]{1,0:T(8,128)(2,1)} copy(bf16[384,432]{0,1:T(8,128)(2,1)} %bitcast.22) | data formatting | bytes 663552 | tf_op jit(solution)/shard_map/transpose | solution.py:171
  15.3 4.1 %all-to-all-done.mine_ref = bf16[12,16,1024]{2,1,0:T(8,128)(2,1)S(1)} async-done(((bf16[12,16,1024]{2,1,0:T(8,128)(2,1)}), bf16[12,16,1024]{2,1,0:T(8,128)(2,1)S(1)}, u32[]{:S(2)}, u32[]{:S(2)}) %all-to-all-start) | async-done | bytes 393248 | tf_op jit(solution)/shard_map/all_to_all | solution.py:169
  19.4 7.2 %all-to-all-start.1 = ((bf16[24,16,432]{2,1,0:T(8,128)(2,1)}), bf16[24,16,432]{2,1,0:T(8,128)(2,1)S(1)}, u32[]{:S(2)}, u32[]{:S(2)}) async-start(bf16[24,16,432]{2,1,0:T(8,128)(2,1)} %bitcast.6), calls=%async_computation.1 | async-start | bytes 786432 | tf_op jit(solution)/shard_map/all_to_all | solution.py:174
  26.6 2.1 %collective-permute-start = (bf16[12,16,1024]{2,1,0:T(8,128)(2,1)S(1)}, bf16[12,16,1024]{2,1,0:T(8,128)(2,1)S(1)}, u32[]{:S(2)}, u32[]{:S(2)}) collective-permute-start(bf16[12,16,1024]{2,1,0:T(8,128)(2,1)S(1)} %all-to-all-done.mine_ref), channel_id=1, source_target_pairs={{0,1},{1,0},{2,3},{3,2},{4,5},{5,4},{6,7},{7,6},{8,9},{9,8},{10,11... | collective-permute-start | bytes 1179656 | tf_op jit(solution)/shard_map/ppermute | solution.py:151
  28.7 1.5 %collective-permute-done.other_ref = bf16[12,16,1024]{2,1,0:T(8,128)(2,1)S(1)} collective-permute-done((bf16[12,16,1024]{2,1,0:T(8,128)(2,1)S(1)}, bf16[12,16,1024]{2,1,0:T(8,128)(2,1)S(1)}, u32[]{:S(2)}, u32[]{:S(2)}) %collective-permute-start) | collective-permute-done | bytes 393248 | tf_op jit(solution)/shard_map/ppermute | solution.py:151
  30.2 0.0 copy-done
  30.2 0.9 conv.2
  31.1 8.4 %collective-permute-start.1 = (f32[16,1024]{1,0:T(8,128)S(1)}, f32[16,1024]{1,0:T(8,128)S(1)}, u32[]{:S(2)}, u32[]{:S(2)}) collective-permute-start(f32[16,1024]{1,0:T(8,128)S(1)} %get-tuple-element.24), channel_id=1, source_target_pairs={{0,24},{24,48},{48,72},{72,96},{96,120},{120,144},{144,168},{168,1... | collective-permute-start | bytes 196616 | tf_op jit(solution)/shard_map/ppermute | solution.py:177
  39.5 6.1 %collective-permute-start.2 = (f32[16,1024]{1,0:T(8,128)S(1)}, f32[16,1024]{1,0:T(8,128)S(1)}, u32[]{:S(2)}, u32[]{:S(2)}) collective-permute-start(f32[16,1024]{1,0:T(8,128)S(1)} %get-tuple-element.25), channel_id=1, source_target_pairs={{24,0},{48,24},{72,48},{96,72},{120,96},{144,120},{168,144},{192,1... | collective-permute-start | bytes 196616 | tf_op jit(solution)/shard_map/ppermute | solution.py:178
  45.6 3.2 %collective-permute-done.1.low_ref = f32[16,1024]{1,0:T(8,128)S(1)} collective-permute-done((f32[16,1024]{1,0:T(8,128)S(1)}, f32[16,1024]{1,0:T(8,128)S(1)}, u32[]{:S(2)}, u32[]{:S(2)}) %collective-permute-start.1) | collective-permute-done | bytes 65568 | tf_op jit(solution)/shard_map/ppermute | solution.py:177
  48.8 2.5 %collective-permute-done.2.high_ref = f32[16,1024]{1,0:T(8,128)S(1)} collective-permute-done((f32[16,1024]{1,0:T(8,128)S(1)}, f32[16,1024]{1,0:T(8,128)S(1)}, u32[]{:S(2)}, u32[]{:S(2)}) %collective-permute-start.2) | collective-permute-done | bytes 65568 | tf_op jit(solution)/shard_map/ppermute | solution.py:178
  51.3 0.0 copy-done.1
  51.3 0.6 activate.1
  51.9 0.0 all-to-all-done.1
  51.9 0.0 copy-start.2
  51.9 0.8 broadcast_in_dim.15
  52.8 6.6 %all-to-all-start.2 = ((bf16[12,16,1024]{2,1,0:T(8,128)(2,1)}), bf16[12,16,1024]{2,1,0:T(8,128)(2,1)S(1)}, u32[]{:S(2)}, u32[]{:S(2)}) async-start(bf16[12,16,1024]{2,1,0:T(8,128)(2,1)} %broadcast_in_dim.15), calls=%async_computation.2 | async-start | bytes 786432 | tf_op jit(solution)/shard_map/all_to_all | solution.py:184
  59.4 6.5 %collective-permute-start.3 = (bf16[16,1024]{1,0:T(8,128)(2,1)S(1)}, bf16[16,1024]{1,0:T(8,128)(2,1)S(1)}, u32[]{:S(2)}, u32[]{:S(2)}) collective-permute-start(bf16[16,1024]{1,0:T(8,128)(2,1)S(1)} %get-tuple-element.30.own_ref), channel_id=1, source_target_pairs={{24,0},{48,24},{72,48},{96,72},{120,96},{144,120},{168,144},{192,1... | collective-permute-start | bytes 98312 | tf_op jit(solution)/shard_map/ppermute | solution.py:182
  66.0 2.3 %collective-permute-start.4 = (bf16[16,1024]{1,0:T(8,128)(2,1)S(1)}, bf16[16,1024]{1,0:T(8,128)(2,1)S(1)}, u32[]{:S(2)}, u32[]{:S(2)}) collective-permute-start(bf16[16,1024]{1,0:T(8,128)(2,1)S(1)} %get-tuple-element.30.own_ref), channel_id=1, source_target_pairs={{0,24},{24,48},{48,72},{72,96},{96,120},{120,144},{144,168},{168,1... | collective-permute-start | bytes 98312 | tf_op jit(solution)/shard_map/ppermute | solution.py:183
  68.3 1.8 %collective-permute-done.3.above_ref = bf16[16,1024]{1,0:T(8,128)(2,1)S(1)} collective-permute-done((bf16[16,1024]{1,0:T(8,128)(2,1)S(1)}, bf16[16,1024]{1,0:T(8,128)(2,1)S(1)}, u32[]{:S(2)}, u32[]{:S(2)}) %collective-permute-start.3) | collective-permute-done | bytes 32800 | tf_op jit(solution)/shard_map/ppermute | solution.py:182
  70.0 7.6 %collective-permute-done.4.below_ref = bf16[16,1024]{1,0:T(8,128)(2,1)S(1)} collective-permute-done((bf16[16,1024]{1,0:T(8,128)(2,1)S(1)}, bf16[16,1024]{1,0:T(8,128)(2,1)S(1)}, u32[]{:S(2)}, u32[]{:S(2)}) %collective-permute-start.4) | collective-permute-done | bytes 32800 | tf_op jit(solution)/shard_map/ppermute | solution.py:183
  77.6 2.0 %wgrad.1 = bf16[32,16,384]{2,1,0:T(8,128)(2,1)} custom-call(s32[1]{0:T(128)} %bitcast.core_ref, bf16[16,1024]{1,0:T(8,128)(2,1)S(1)} %collective-permute-done.3.above_ref, bf16[16,1024]{1,0:T(8,128)(2,1)S(1)} %get-tuple-element.30.own_ref, bf16[16,1024]{1,0:T(8,128)(2,1)S(1)} %collective-permute-done.4.below_ref, ...), custom_call_target="tpu_custom_call" | custom-call | tf_op jit(solution)/shard_map/wgrad/pallas_call | solution.py:108
  79.6 0.0 all-to-all-done.2.mine_ref
  79.6 0.0 copy-done.2
  79.6 7.4 %all-to-all-start.3 = ((bf16[32,16,384]{2,1,0:T(8,128)(2,1)}), bf16[32,16,384]{2,1,0:T(8,128)(2,1)S(1)}, u32[]{:S(2)}, u32[]{:S(2)}) async-start(bf16[32,16,384]{2,1,0:T(8,128)(2,1)} %wgrad.1), calls=%async_computation.3 | async-start | bytes 786432 | tf_op jit(solution)/shard_map/all_to_all | solution.py:187
  87.0 1.9 %collective-permute-start.5 = (bf16[12,16,1024]{2,1,0:T(8,128)(2,1)S(1)}, bf16[12,16,1024]{2,1,0:T(8,128)(2,1)S(1)}, u32[]{:S(2)}, u32[]{:S(2)}) collective-permute-start(bf16[12,16,1024]{2,1,0:T(8,128)(2,1)S(1)} %all-to-all-done.2.mine_ref), channel_id=1, source_target_pairs={{0,1},{1,0},{2,3},{3,2},{4,5},{5,4},{6,7},{7,6},{8,9},{9,8},{10,11... | collective-permute-start | bytes 1179656 | tf_op jit(solution)/shard_map/ppermute | solution.py:151
  88.9 1.9 %copy.7 = bf16[24,16,432]{0,2,1:T(8,128)(2,1)S(1)} copy(bf16[24,16,432]{2,1,0:T(8,128)(2,1)} %copy-done.2) | data formatting | bytes 663552 | tf_op jit(solution)/shard_map/optimization_barrier | solution.py:180
  90.8 2.6 %copy.8 = bf16[27,16,24,16]{3,2,1,0:T(8,128)(2,1)} copy(bf16[27,16,24,16]{2,3,0,1:T(8,128)(2,1)S(1)} %bitcast.25) | data formatting | bytes 663552 | tf_op jit(solution)/shard_map/transpose | solution.py:189
  93.4 3.6 %reshape.48.w_ref = bf16[432,384]{1,0:T(8,128)(2,1)S(1)} reshape(bf16[27,16,24,16]{3,2,1,0:T(8,128)(2,1)} %copy.8) | data formatting | bytes 663552 | tf_op jit(solution)/shard_map/reshape | solution.py:190
  97.0 0.0 collective-permute-done.5.other_ref
  97.0 0.9 conv.3
  97.9 9.2 %all-to-all-done.3.terms_ref = bf16[32,16,384]{2,1,0:T(8,128)(2,1)S(1)} async-done(((bf16[32,16,384]{2,1,0:T(8,128)(2,1)}), bf16[32,16,384]{2,1,0:T(8,128)(2,1)S(1)}, u32[]{:S(2)}, u32[]{:S(2)}) %all-to-all-start.3) | async-done | bytes 393248 | tf_op jit(solution)/shard_map/all_to_all | solution.py:187
  107.2 0.8 total.1
  108.0 5.4 %all-to-all-start.4 = ((bf16[32,16,384]{2,1,0:T(8,128)(2,1)}), bf16[32,16,384]{2,1,0:T(8,128)(2,1)S(1)}, u32[]{:S(2)}, u32[]{:S(2)}) async-start(bf16[32,16,384]{2,1,0:T(8,128)(2,1)} %total.1), calls=%async_computation.4 | async-start | bytes 786432 | tf_op jit(solution)/shard_map/all_to_all | solution.py:199
  113.4 6.7 %collective-permute-start.7 = (f32[16,1024]{1,0:T(8,128)S(1)}, f32[16,1024]{1,0:T(8,128)S(1)}, u32[]{:S(2)}, u32[]{:S(2)}) collective-permute-start(f32[16,1024]{1,0:T(8,128)S(1)} %get-tuple-element.37), channel_id=1, source_target_pairs={{0,24},{24,48},{48,72},{72,96},{96,120},{120,144},{144,168},{168,1... | collective-permute-start | bytes 196616 | tf_op jit(solution)/shard_map/ppermute | solution.py:195
  120.2 4.3 %collective-permute-start.6 = (f32[16,1024]{1,0:T(8,128)S(1)}, f32[16,1024]{1,0:T(8,128)S(1)}, u32[]{:S(2)}, u32[]{:S(2)}) collective-permute-start(f32[16,1024]{1,0:T(8,128)S(1)} %get-tuple-element.36), channel_id=1, source_target_pairs={{24,0},{48,24},{72,48},{96,72},{120,96},{144,120},{168,144},{192,1... | collective-permute-start | bytes 196616 | tf_op jit(solution)/shard_map/ppermute | solution.py:194
  124.4 10.3 %collective-permute-done.7 = f32[16,1024]{1,0:T(8,128)S(1)} collective-permute-done((f32[16,1024]{1,0:T(8,128)S(1)}, f32[16,1024]{1,0:T(8,128)S(1)}, u32[]{:S(2)}, u32[]{:S(2)}) %collective-permute-start.7) | collective-permute-done | bytes 65568 | tf_op jit(solution)/shard_map/ppermute | solution.py:195
  134.7 0.6 collective-permute-done.6
  135.3 0.6 fusion
  136.0 3.1 %all-to-all-done.4 = bf16[32,16,384]{2,1,0:T(8,128)(2,1)S(1)} async-done(((bf16[32,16,384]{2,1,0:T(8,128)(2,1)}), bf16[32,16,384]{2,1,0:T(8,128)(2,1)S(1)}, u32[]{:S(2)}, u32[]{:S(2)}) %all-to-all-start.4) | async-done | bytes 393248 | tf_op jit(solution)/shard_map/all_to_all | solution.py:199
  139.0 0.9 slice_convert_fusion
Async XLA Ops:
  0.6 29.6 %copy-start = (bf16[16,3,3,3,384]{4,0,3,2,1:T(8,128)(2,1)S(1)}, bf16[16,3,3,3,384]{4,0,3,2,1:T(8,128)(2,1)}, u32[]{:S(2)}) copy-start(bf16[16,3,3,3,384]{4,0,3,2,1:T(8,128)(2,1)} %param.4) | copy-start | bytes 995332
  0.6 50.6 %copy-start.1 = (bf16[1,1,16,1024]{3,2,1,0:T(8,128)(2,1)S(1)}, bf16[1,1,16,1024]{3,2,1,0:T(8,128)(2,1)}, u32[]{:S(2)}) copy-start(bf16[1,1,16,1024]{3,2,1,0:T(8,128)(2,1)} %param.5) | copy-start | bytes 98308
  2.2 17.1 %all-to-all-start = ((bf16[12,16,1024]{2,1,0:T(8,128)(2,1)}), bf16[12,16,1024]{2,1,0:T(8,128)(2,1)S(1)}, u32[]{:S(2)}, u32[]{:S(2)}) async-start(bf16[12,16,1024]{2,1,0:T(8,128)(2,1)} %broadcast_in_dim.14), calls=%async_computation | async-start | bytes 786432 | tf_op jit(solution)/shard_map/all_to_all | solution.py:169
  19.4 32.6 %all-to-all-start.1 = ((bf16[24,16,432]{2,1,0:T(8,128)(2,1)}), bf16[24,16,432]{2,1,0:T(8,128)(2,1)S(1)}, u32[]{:S(2)}, u32[]{:S(2)}) async-start(bf16[24,16,432]{2,1,0:T(8,128)(2,1)} %bitcast.6), calls=%async_computation.1 | async-start | bytes 786432 | tf_op jit(solution)/shard_map/all_to_all | solution.py:174
  26.6 3.6 %collective-permute-start = (bf16[12,16,1024]{2,1,0:T(8,128)(2,1)S(1)}, bf16[12,16,1024]{2,1,0:T(8,128)(2,1)S(1)}, u32[]{:S(2)}, u32[]{:S(2)}) collective-permute-start(bf16[12,16,1024]{2,1,0:T(8,128)(2,1)S(1)} %all-to-all-done.mine_ref), channel_id=1, source_target_pairs={{0,1},{1,0},{2,3},{3,2},{4,5},{5,4},{6,7},{7,6},{8,9},{9,8},{10,11... | collective-permute-start | bytes 1179656 | tf_op jit(solution)/shard_map/ppermute | solution.py:151
  31.1 17.7 %collective-permute-start.1 = (f32[16,1024]{1,0:T(8,128)S(1)}, f32[16,1024]{1,0:T(8,128)S(1)}, u32[]{:S(2)}, u32[]{:S(2)}) collective-permute-start(f32[16,1024]{1,0:T(8,128)S(1)} %get-tuple-element.24), channel_id=1, source_target_pairs={{0,24},{24,48},{48,72},{72,96},{96,120},{120,144},{144,168},{168,1... | collective-permute-start | bytes 196616 | tf_op jit(solution)/shard_map/ppermute | solution.py:177
  39.5 11.8 %collective-permute-start.2 = (f32[16,1024]{1,0:T(8,128)S(1)}, f32[16,1024]{1,0:T(8,128)S(1)}, u32[]{:S(2)}, u32[]{:S(2)}) collective-permute-start(f32[16,1024]{1,0:T(8,128)S(1)} %get-tuple-element.25), channel_id=1, source_target_pairs={{24,0},{48,24},{72,48},{96,72},{120,96},{144,120},{168,144},{192,1... | collective-permute-start | bytes 196616 | tf_op jit(solution)/shard_map/ppermute | solution.py:178
  51.9 27.7 %copy-start.2 = (bf16[24,16,432]{2,1,0:T(8,128)(2,1)}, bf16[24,16,432]{2,1,0:T(8,128)(2,1)S(1)}, u32[]{:S(2)}) copy-start(bf16[24,16,432]{2,1,0:T(8,128)(2,1)S(1)} %all-to-all-done.1) | copy-start | bytes 995332
  52.8 26.8 %all-to-all-start.2 = ((bf16[12,16,1024]{2,1,0:T(8,128)(2,1)}), bf16[12,16,1024]{2,1,0:T(8,128)(2,1)S(1)}, u32[]{:S(2)}, u32[]{:S(2)}) async-start(bf16[12,16,1024]{2,1,0:T(8,128)(2,1)} %broadcast_in_dim.15), calls=%async_computation.2 | async-start | bytes 786432 | tf_op jit(solution)/shard_map/all_to_all | solution.py:184
  59.4 10.6 %collective-permute-start.3 = (bf16[16,1024]{1,0:T(8,128)(2,1)S(1)}, bf16[16,1024]{1,0:T(8,128)(2,1)S(1)}, u32[]{:S(2)}, u32[]{:S(2)}) collective-permute-start(bf16[16,1024]{1,0:T(8,128)(2,1)S(1)} %get-tuple-element.30.own_ref), channel_id=1, source_target_pairs={{24,0},{48,24},{72,48},{96,72},{120,96},{144,120},{168,144},{192,1... | collective-permute-start | bytes 98312 | tf_op jit(solution)/shard_map/ppermute | solution.py:182
  66.0 11.6 %collective-permute-start.4 = (bf16[16,1024]{1,0:T(8,128)(2,1)S(1)}, bf16[16,1024]{1,0:T(8,128)(2,1)S(1)}, u32[]{:S(2)}, u32[]{:S(2)}) collective-permute-start(bf16[16,1024]{1,0:T(8,128)(2,1)S(1)} %get-tuple-element.30.own_ref), channel_id=1, source_target_pairs={{0,24},{24,48},{48,72},{72,96},{96,120},{120,144},{144,168},{168,1... | collective-permute-start | bytes 98312 | tf_op jit(solution)/shard_map/ppermute | solution.py:183
  79.6 27.6 %all-to-all-start.3 = ((bf16[32,16,384]{2,1,0:T(8,128)(2,1)}), bf16[32,16,384]{2,1,0:T(8,128)(2,1)S(1)}, u32[]{:S(2)}, u32[]{:S(2)}) async-start(bf16[32,16,384]{2,1,0:T(8,128)(2,1)} %wgrad.1), calls=%async_computation.3 | async-start | bytes 786432 | tf_op jit(solution)/shard_map/all_to_all | solution.py:187
  87.0 10.0 %collective-permute-start.5 = (bf16[12,16,1024]{2,1,0:T(8,128)(2,1)S(1)}, bf16[12,16,1024]{2,1,0:T(8,128)(2,1)S(1)}, u32[]{:S(2)}, u32[]{:S(2)}) collective-permute-start(bf16[12,16,1024]{2,1,0:T(8,128)(2,1)S(1)} %all-to-all-done.2.mine_ref), channel_id=1, source_target_pairs={{0,1},{1,0},{2,3},{3,2},{4,5},{5,4},{6,7},{7,6},{8,9},{9,8},{10,11... | collective-permute-start | bytes 1179656 | tf_op jit(solution)/shard_map/ppermute | solution.py:151
  108.0 31.0 %all-to-all-start.4 = ((bf16[32,16,384]{2,1,0:T(8,128)(2,1)}), bf16[32,16,384]{2,1,0:T(8,128)(2,1)S(1)}, u32[]{:S(2)}, u32[]{:S(2)}) async-start(bf16[32,16,384]{2,1,0:T(8,128)(2,1)} %total.1), calls=%async_computation.4 | async-start | bytes 786432 | tf_op jit(solution)/shard_map/all_to_all | solution.py:199
  113.4 21.3 %collective-permute-start.7 = (f32[16,1024]{1,0:T(8,128)S(1)}, f32[16,1024]{1,0:T(8,128)S(1)}, u32[]{:S(2)}, u32[]{:S(2)}) collective-permute-start(f32[16,1024]{1,0:T(8,128)S(1)} %get-tuple-element.37), channel_id=1, source_target_pairs={{0,24},{24,48},{48,72},{72,96},{96,120},{120,144},{144,168},{168,1... | collective-permute-start | bytes 196616 | tf_op jit(solution)/shard_map/ppermute | solution.py:195
  120.2 15.2 %collective-permute-start.6 = (f32[16,1024]{1,0:T(8,128)S(1)}, f32[16,1024]{1,0:T(8,128)S(1)}, u32[]{:S(2)}, u32[]{:S(2)}) collective-permute-start(f32[16,1024]{1,0:T(8,128)S(1)} %get-tuple-element.36), channel_id=1, source_target_pairs={{24,0},{48,24},{72,48},{96,72},{120,96},{144,120},{168,144},{192,1... | collective-permute-start | bytes 196616 | tf_op jit(solution)/shard_map/ppermute | solution.py:194

commit v3 on v2

--- a/solution.py
+++ b/solution.py
@@ -81,38 +81,57 @@
     )(core, weights, mine, other)
 
 
-def wgrad_kernel(core_ref, above_ref, own_ref, below_ref, mine_ref, other_ref, out_ref, x_ref):
+def grads_kernel(
+    place_ref, k_ref, above_ref, own_ref, below_ref, mine_ref, other_ref,
+    wide_ref, keep_ref, send_ref, x_ref, stack_ref,
+):
     rows = own_ref.shape[0]
-    x = merge_cores(core_ref, mine_ref, other_ref, x_ref)
+    x = merge_cores(place_ref, mine_ref, other_ref, x_ref)
     for depth_tap, ref in enumerate((above_ref, own_ref, below_ref)):
         plane = ref[...].astype(jnp.float32)
         moved = [shift_cells(plane, 0, col_tap - 1) for col_tap in range(3)]
-        stack = jnp.concatenate(
-            [
-                shift_cells(moved[col_tap], row_tap - 1, 0).astype(jnp.bfloat16)
-                for row_tap in range(3)
-                for col_tap in range(3)
-            ],
-            axis=0,
+        for row_tap in range(3):
+            for col_tap in range(3):
+                at = ((depth_tap * 3 + row_tap) * 3 + col_tap) * rows
+                stack_ref[at : at + rows, :] = shift_cells(moved[col_tap], row_tap - 1, 0).astype(
+                    jnp.bfloat16
+                )
+        at = depth_tap * 9 * rows
+        grad = lax.dot_general(
+            stack_ref[at : at + 9 * rows, :],
+            x,
+            (((1,), (1,)), ((), ())),
+            preferred_element_type=jnp.float32,
         )
-        grad = lax.dot_general(
-            stack, x, (((1,), (1,)), ((), ())), preferred_element_type=jnp.float32
-        )
-        out_ref[depth_tap * 9 : depth_tap * 9 + 9] = grad.astype(jnp.bfloat16).reshape(9, rows, -1)
-    out_ref[TAPS:] = jnp.zeros((out_ref.shape[0] - TAPS,) + out_ref.shape[1:], out_ref.dtype)
-
-
-def wgrad(core, above, own, below, mine, other, slots):
-    rows = own.shape[0]
+        wide_ref[depth_tap * 9 : depth_tap * 9 + 9] = grad.astype(jnp.bfloat16).reshape(9, rows, -1)
+    wide_ref[TAPS:] = jnp.zeros((wide_ref.shape[0] - TAPS,) + wide_ref.shape[1:], wide_ref.dtype)
+
+    partial = lax.dot_general(
+        k_ref[...], stack_ref[...], (((0,), (0,)), ((), ())), preferred_element_type=jnp.float32
+    ).astype(jnp.bfloat16)
+    first = place_ref[0] == 0
+    for x_at in range(4):
+        for z_at in range(3):
+            x_slot = x_at ^ place_ref[1]
+            z_slot = lax.rem(z_at - place_ref[2] + 3, 3)
+            at = (x_at * 3 + z_at) * 2 * rows
+            even, odd = partial[at : at + rows], partial[at + rows : at + 2 * rows]
+            keep_ref[x_slot, z_slot] = jnp.where(first, even, odd)
+            send_ref[x_slot, z_slot] = jnp.where(first, odd, even)
+
+
+def grads(place, k_rows, above, own, below, mine, other, slots):
+    rows, cells = own.shape
     chans = 2 * mine.shape[0] * mine.shape[1]
-    return pl.pallas_call(
-        wgrad_kernel,
-        out_shape=jax.ShapeDtypeStruct((slots, rows, chans), jnp.bfloat16),
-        in_specs=merged_specs(5),
-        scratch_shapes=merged_scratch(mine),
-        compiler_params=pltpu.CompilerParams(vmem_limit_bytes=VMEM_LIMIT),
-        name="wgrad",
-    )(core, above, own, below, mine, other)
+    half = jax.ShapeDtypeStruct((4, 3, rows, cells), jnp.bfloat16)
+    return pl.pallas_call(
+        grads_kernel,
+        out_shape=[jax.ShapeDtypeStruct((slots, rows, chans), jnp.bfloat16), half, half],
+        in_specs=merged_specs(6),
+        scratch_shapes=merged_scratch(mine) + [pltpu.VMEM((TAPS * rows, cells), jnp.bfloat16)],
+        compiler_params=pltpu.CompilerParams(vmem_limit_bytes=VMEM_LIMIT),
+        name="grads",
+    )(place, k_rows, above, own, below, mine, other)
 
 
 def act_kernel(mid_ref, low_ref, high_ref, cot_ref, act_ref, grad_ref):
@@ -155,11 +174,10 @@
     rows = volume.shape[2]
     cells = volume.shape[3]
     chips = lax.axis_size(CHIPS)
-    chans = lax.axis_size(CHAN)
     depths = lax.axis_size(DEP)
     ring = [(i, (i + 1) % depths) for i in range(depths)]
     back = [(b, a) for a, b in ring]
-    core = lax.axis_index("core").astype(jnp.int32).reshape(1)
+    place = jnp.stack([lax.axis_index(name) for name in ("core", "x", "zl")]).astype(jnp.int32)
     own = volume.reshape(rows, cells)
     cot = cotangent.reshape(rows, cells)
 
@@ -168,32 +186,29 @@
 
     mine = lax.all_to_all(copies(own), CHIPS, 0, 0)
     k_rows = jnp.transpose(kernel.reshape(rows, TAPS, -1), (1, 0, 2)).reshape(TAPS * rows, -1)
-    pieces = jnp.transpose(k_rows).reshape(chans, rows, TAPS * rows)
-    mine, pieces, k_rows, cot = lax.optimization_barrier((mine, pieces, k_rows, cot))
+    mine, k_rows, cot, place = lax.optimization_barrier((mine, k_rows, cot, place))
     other = swap_cores(mine)
-    k_in = lax.all_to_all(pieces, CHAN, 0, 0)
-
-    up, mid, down = conv(core, k_rows, mine, other, 1)
+
+    up, mid, down = conv(place, k_rows, mine, other, 1)
     low = lax.ppermute(up, DEP, ring)
     high = lax.ppermute(down, DEP, back)
     activated, grad_pre = activate(mid, low, high, cot)
-    grad_pre, k_in = lax.optimization_barrier((grad_pre, k_in))
 
     grad_above = lax.ppermute(grad_pre, DEP, back)
     grad_below = lax.ppermute(grad_pre, DEP, ring)
-    grad_mine = lax.all_to_all(copies(grad_pre), CHIPS, 0, 0)
-    wide = wgrad(core, grad_above, grad_pre, grad_below, mine, other, depths)
-    wide, grad_mine = lax.optimization_barrier((wide, grad_mine))
+    wide, keep, send = grads(place, k_rows, grad_above, grad_pre, grad_below, mine, other, depths)
     terms = lax.all_to_all(wide, DEP, 0, 0)
 
-    k_cols = jnp.transpose(k_in.reshape(chans, rows, TAPS, rows), (2, 1, 0, 3))
-    k_cols = k_cols.reshape(TAPS * rows, chans * rows)
-    grad_other = swap_cores(grad_mine)
-    to_low, same, to_high = conv(core, k_cols, grad_mine, grad_other, -1)
-    terms, same = lax.optimization_barrier((terms, same))
-    from_high = lax.ppermute(to_low, DEP, back)
-    from_low = lax.ppermute(to_high, DEP, ring)
-    grad_volume = (same + from_high + from_low).astype(jnp.bfloat16)
+    total = keep.astype(jnp.float32) + swap_cores(send).astype(jnp.float32)
+    total = total.reshape(2, 2, 3, rows, cells)
+    step = lax.ppermute(total[:, 1].astype(jnp.bfloat16), "x", [(i, i ^ 1) for i in range(4)])
+    total = total[:, 0] + step.astype(jnp.float32)
+    terms, total = lax.optimization_barrier((terms, total))
+    step = lax.ppermute(total[1].astype(jnp.bfloat16), "x", [(i, i ^ 2) for i in range(4)])
+    total = total[0] + step.astype(jnp.float32)
+    after = lax.ppermute(total[1], "zl", [(i, (i + 1) % 3) for i in range(3)])
+    before = lax.ppermute(total[2], "zl", [(i, (i + 2) % 3) for i in range(3)])
+    grad_volume = (total[0] + after + before).astype(jnp.bfloat16)
 
     scale = 1.0 / math.sqrt(UNIV * DEPTH * SIDE * SIDE)
     all_taps = lax.all_to_all(total_spread(terms, scale, depths), DEP, 0, 0)[:TAPS]

time: 141 us -> 132 us (0.936)
  the two profiles are of different devices: /device:TPU:130 before, /device:TPU:1 now
where the time goes in v3:
time: 132 us; the launch traced here: 131 us
  starting transfers between devices  73.4 us (56%)
  waiting for transfers between devices  47.5 us (36%)
  Pallas kernels  5.88 us (4%)
  other arithmetic  1.76 us (1%)
  local copies, waits for them, and re-layouts  1.6 us (1%)
    ppermute x2, starting transfers between devices, swap_cores(): return lax.ppermute(blocks, 'core', [(0, 1), (1, 0)])  13.1 us
    all_to_all x1, waiting for transfers between devices, body(): terms = lax.all_to_all(wide, DEP, 0, 0)  12.2 us
    all_to_all x1, starting transfers between devices, body(): terms = lax.all_to_all(wide, DEP, 0, 0)  11.3 us
    all_to_all x1, starting transfers between devices, body(): mine = lax.all_to_all(copies(own), CHIPS, 0, 0)  8.63 us
    all_to_all x1, waiting for transfers between devices, body(): mine = lax.all_to_all(copies(own), CHIPS, 0, 0)  8.26 us
    ppermute x1, starting transfers between devices, body(): high = lax.ppermute(down, DEP, back)  7.28 us
    ppermute x1, starting transfers between devices, body(): low = lax.ppermute(up, DEP, ring)  6.88 us
    ppermute x1, waiting for transfers between devices, body(): lax.ppermute(total[:, 1].astype(jnp.bfloat16), 'x', [(i, i ^ 1) for i in...  6.17 us
  transfers between devices with their start and end apart: 13, of which 11 were waited for; matrix products, arithmetic and copies ran while one was open for 1% of the time, Pallas kernels for 0%

profile of v3, /device:TPU:1, one launch (start us, length us, event | category | flops | bytes accessed | tf_op | source)
XLA Modules:
  0.0 131.0 jit_solution(14122611082766442324)
XLA Ops:
  0.6 1.5 %broadcast_in_dim.8 = bf16[12,16,1024]{2,1,0:T(8,128)(2,1)} broadcast(bf16[16,1024]{1,0:T(8,128)(2,1)} %bitcast.47), dimensions={1,2} | broadcast | bytes 425984 | tf_op jit(solution)/shard_map/broadcast_in_dim | solution.py:185
  2.2 0.0 copy-start
  2.2 8.6 %all-to-all-start = ((bf16[12,16,1024]{2,1,0:T(8,128)(2,1)}), bf16[12,16,1024]{2,1,0:T(8,128)(2,1)S(1)}, u32[]{:S(2)}, u32[]{:S(2)}) async-start(bf16[12,16,1024]{2,1,0:T(8,128)(2,1)} %broadcast_in_dim.8), calls=%async_computation | async-start | bytes 786432 | tf_op jit(solution)/shard_map/all_to_all | solution.py:187
  10.8 0.1 pad_add_fusion.core_ref.place_ref
  10.9 8.3 %all-to-all-done.mine_ref = bf16[12,16,1024]{2,1,0:T(8,128)(2,1)S(1)} async-done(((bf16[12,16,1024]{2,1,0:T(8,128)(2,1)}), bf16[12,16,1024]{2,1,0:T(8,128)(2,1)S(1)}, u32[]{:S(2)}, u32[]{:S(2)}) %all-to-all-start) | async-done | bytes 393248 | tf_op jit(solution)/shard_map/all_to_all | solution.py:187
  19.2 0.0 copy-start.1
  19.2 8.7 %collective-permute-start = (bf16[12,16,1024]{2,1,0:T(8,128)(2,1)S(1)}, bf16[12,16,1024]{2,1,0:T(8,128)(2,1)S(1)}, u32[]{:S(2)}, u32[]{:S(2)}) collective-permute-start(bf16[12,16,1024]{2,1,0:T(8,128)(2,1)S(1)} %all-to-all-done.mine_ref), channel_id=1, source_target_pairs={{0,1},{1,0},{2,3},{3,2},{4,5},{5,4},{6,7},{7,6},{8,9},{9,8},{10,11... | collective-permute-start | bytes 1179656 | tf_op jit(solution)/shard_map/ppermute | solution.py:170
  27.9 1.3 %collective-permute-done.other_ref = bf16[12,16,1024]{2,1,0:T(8,128)(2,1)S(1)} collective-permute-done((bf16[12,16,1024]{2,1,0:T(8,128)(2,1)S(1)}, bf16[12,16,1024]{2,1,0:T(8,128)(2,1)S(1)}, u32[]{:S(2)}, u32[]{:S(2)}) %collective-permute-start) | collective-permute-done | bytes 393248 | tf_op jit(solution)/shard_map/ppermute | solution.py:170
  29.2 0.0 copy-done
  29.2 1.5 %conv.1 = (f32[16,1024]{1,0:T(8,128)S(1)}, f32[16,1024]{1,0:T(8,128)S(1)}, f32[16,1024]{1,0:T(8,128)S(1)}) custom-call(s32[3]{0:T(128)S(1)} %pad_add_fusion.core_ref.place_ref, bf16[432,384]{1,0:T(8,128)(2,1)S(1)} %bitcast.41, bf16[12,16,1024]{2,1,0:T(8,128)(2,1)S(1)} %all-to-all-done.mine_ref, bf16[12,16,1024]{2,1,0:T(8,128)(2,1)S(1)} %collective-permute-done.other_ref), custom_call_target="tpu_custom_call" | custom-call | tf_op jit(solution)/shard_map/conv/pallas_call | solution.py:74
  30.6 6.9 %collective-permute-start.1 = (f32[16,1024]{1,0:T(8,128)S(1)}, f32[16,1024]{1,0:T(8,128)S(1)}, u32[]{:S(2)}, u32[]{:S(2)}) collective-permute-start(f32[16,1024]{1,0:T(8,128)S(1)} %get-tuple-element.21), channel_id=1, source_target_pairs={{0,24},{24,48},{48,72},{72,96},{96,120},{120,144},{144,168},{168,1... | collective-permute-start | bytes 196616 | tf_op jit(solution)/shard_map/ppermute | solution.py:193
  37.5 7.3 %collective-permute-start.2 = (f32[16,1024]{1,0:T(8,128)S(1)}, f32[16,1024]{1,0:T(8,128)S(1)}, u32[]{:S(2)}, u32[]{:S(2)}) collective-permute-start(f32[16,1024]{1,0:T(8,128)S(1)} %get-tuple-element.22), channel_id=1, source_target_pairs={{24,0},{48,24},{72,48},{96,72},{120,96},{144,120},{168,144},{192,1... | collective-permute-start | bytes 196616 | tf_op jit(solution)/shard_map/ppermute | solution.py:194
  44.8 0.2 collective-permute-done.1.low_ref
  45.0 4.3 %collective-permute-done.2.high_ref = f32[16,1024]{1,0:T(8,128)S(1)} collective-permute-done((f32[16,1024]{1,0:T(8,128)S(1)}, f32[16,1024]{1,0:T(8,128)S(1)}, u32[]{:S(2)}, u32[]{:S(2)}) %collective-permute-start.2) | collective-permute-done | bytes 65568 | tf_op jit(solution)/shard_map/ppermute | solution.py:194
  49.3 0.0 copy-done.1
  49.3 0.6 activate.1
  50.0 5.6 %collective-permute-start.4 = (bf16[16,1024]{1,0:T(8,128)(2,1)S(1)}, bf16[16,1024]{1,0:T(8,128)(2,1)S(1)}, u32[]{:S(2)}, u32[]{:S(2)}) collective-permute-start(bf16[16,1024]{1,0:T(8,128)(2,1)S(1)} %get-tuple-element.25.own_ref), channel_id=1, source_target_pairs={{0,24},{24,48},{48,72},{72,96},{96,120},{120,144},{144,168},{168,1... | collective-permute-start | bytes 98312 | tf_op jit(solution)/shard_map/ppermute | solution.py:198
  55.6 4.8 %collective-permute-start.3 = (bf16[16,1024]{1,0:T(8,128)(2,1)S(1)}, bf16[16,1024]{1,0:T(8,128)(2,1)S(1)}, u32[]{:S(2)}, u32[]{:S(2)}) collective-permute-start(bf16[16,1024]{1,0:T(8,128)(2,1)S(1)} %get-tuple-element.25.own_ref), channel_id=1, source_target_pairs={{24,0},{48,24},{72,48},{96,72},{120,96},{144,120},{168,144},{192,1... | collective-permute-start | bytes 98312 | tf_op jit(solution)/shard_map/ppermute | solution.py:197
  60.4 0.0 collective-permute-done.4.below_ref
  60.4 1.7 %collective-permute-done.3.above_ref = bf16[16,1024]{1,0:T(8,128)(2,1)S(1)} collective-permute-done((bf16[16,1024]{1,0:T(8,128)(2,1)S(1)}, bf16[16,1024]{1,0:T(8,128)(2,1)S(1)}, u32[]{:S(2)}, u32[]{:S(2)}) %collective-permute-start.3) | collective-permute-done | bytes 32800 | tf_op jit(solution)/shard_map/ppermute | solution.py:197
  62.0 3.0 %grads.1 = (bf16[32,16,384]{2,1,0:T(8,128)(2,1)}, bf16[4,3,16,1024]{3,2,1,0:T(8,128)(2,1)S(1)}, bf16[4,3,16,1024]{3,2,1,0:T(8,128)(2,1)S(1)}) custom-call(s32[3]{0:T(128)S(1)} %pad_add_fusion.core_ref.place_ref, bf16[432,384]{1,0:T(8,128)(2,1)S(1)} %bitcast.42, bf16[16,1024]{1,0:T(8,128)(2,1)S(1)} %collective-permute-done.3.above_ref, ...), custom_call_target="tpu_custom_call" | custom-call | tf_op jit(solution)/shard_map/grads/pallas_call | solution.py:127
  65.0 4.4 %collective-permute-start.5 = (bf16[4,3,16,1024]{3,2,1,0:T(8,128)(2,1)S(1)}, bf16[4,3,16,1024]{3,2,1,0:T(8,128)(2,1)S(1)}, u32[]{:S(2)}, u32[]{:S(2)}) collective-permute-start(bf16[4,3,16,1024]{3,2,1,0:T(8,128)(2,1)S(1)} %get-tuple-element.28), channel_id=1, source_target_pairs={{0,1},{1,0},{2,3},{3,2},{4,5},{5,4},{6,7},{7,6},{8,9},{9,8},{10,11... | collective-permute-start | bytes 1179656 | tf_op jit(solution)/shard_map/ppermute | solution.py:170
  69.4 11.3 %all-to-all-start.1 = ((bf16[32,16,384]{2,1,0:T(8,128)(2,1)}), bf16[32,16,384]{2,1,0:T(8,128)(2,1)S(1)}, u32[]{:S(2)}, u32[]{:S(2)}) async-start(bf16[32,16,384]{2,1,0:T(8,128)(2,1)} %get-tuple-element.26), calls=%async_computation.1 | async-start | bytes 786432 | tf_op jit(solution)/shard_map/all_to_all | solution.py:200
  80.8 0.0 collective-permute-done.5
  80.8 0.1 convert_add_fusion
  80.9 1.9 %collective-permute-start.6 = (bf16[2,3,16,1024]{3,2,1,0:T(8,128)(2,1)S(1)}, bf16[2,3,16,1024]{3,2,1,0:T(8,128)(2,1)S(1)}, u32[]{:S(2)}, u32[]{:S(2)}) collective-permute-start(bf16[2,3,16,1024]{3,2,1,0:T(8,128)(2,1)S(1)} %fusion.1), channel_id=1, source_target_pairs={{0,6},{6,0},{12,18},{18,12},{1,7},{7,1},{13,19},{19,13},{2,8},{8,2... | collective-permute-start | bytes 589832 | tf_op jit(solution)/shard_map/ppermute | solution.py:204
  82.8 6.2 %collective-permute-done.6 = bf16[2,3,16,1024]{3,2,1,0:T(8,128)(2,1)S(1)} collective-permute-done((bf16[2,3,16,1024]{3,2,1,0:T(8,128)(2,1)S(1)}, bf16[2,3,16,1024]{3,2,1,0:T(8,128)(2,1)S(1)}, u32[]{:S(2)}, u32[]{:S(2)}) %collective-permute-start.6) | collective-permute-done | bytes 196640 | tf_op jit(solution)/shard_map/ppermute | solution.py:204
  89.1 12.2 %all-to-all-done.1.terms_ref = bf16[32,16,384]{2,1,0:T(8,128)(2,1)S(1)} async-done(((bf16[32,16,384]{2,1,0:T(8,128)(2,1)}), bf16[32,16,384]{2,1,0:T(8,128)(2,1)S(1)}, u32[]{:S(2)}, u32[]{:S(2)}) %all-to-all-start.1) | async-done | bytes 393248 | tf_op jit(solution)/shard_map/all_to_all | solution.py:200
  101.2 0.8 total.1
  102.1 5.8 %all-to-all-start.2 = ((bf16[32,16,384]{2,1,0:T(8,128)(2,1)}), bf16[32,16,384]{2,1,0:T(8,128)(2,1)S(1)}, u32[]{:S(2)}, u32[]{:S(2)}) async-start(bf16[32,16,384]{2,1,0:T(8,128)(2,1)} %total.1), calls=%async_computation.2 | async-start | bytes 786432 | tf_op jit(solution)/shard_map/all_to_all | solution.py:214
  107.9 1.9 %collective-permute-start.7 = (bf16[3,16,1024]{2,1,0:T(8,128)(2,1)S(1)}, bf16[3,16,1024]{2,1,0:T(8,128)(2,1)S(1)}, u32[]{:S(2)}, u32[]{:S(2)}) collective-permute-start(bf16[3,16,1024]{2,1,0:T(8,128)(2,1)S(1)} %fusion.2), channel_id=1, source_target_pairs={{0,12},{6,18},{12,0},{18,6},{1,13},{7,19},{13,1},{19,7},{2,14},{8,... | collective-permute-start | bytes 294920 | tf_op jit(solution)/shard_map/ppermute | solution.py:207
  109.8 4.9 %collective-permute-done.7 = bf16[3,16,1024]{2,1,0:T(8,128)(2,1)S(1)} collective-permute-done((bf16[3,16,1024]{2,1,0:T(8,128)(2,1)S(1)}, bf16[3,16,1024]{2,1,0:T(8,128)(2,1)S(1)}, u32[]{:S(2)}, u32[]{:S(2)}) %collective-permute-start.7) | collective-permute-done | bytes 98336 | tf_op jit(solution)/shard_map/ppermute | solution.py:207
  114.8 1.9 %collective-permute-start.8 = (f32[16,1024]{1,0:T(8,128)S(1)}, f32[16,1024]{1,0:T(8,128)S(1)}, u32[]{:S(2)}, u32[]{:S(2)}) collective-permute-start(f32[16,1024]{1,0:T(8,128)S(1)} %get-tuple-element.31), channel_id=1, source_target_pairs={{0,2},{2,4},{4,0},{1,3},{3,5},{5,1},{6,8},{8,10},{10,6},{7,9},{9,1... | collective-permute-start | bytes 196616 | tf_op jit(solution)/shard_map/ppermute | solution.py:209
  116.7 4.3 %collective-permute-start.9 = (f32[16,1024]{1,0:T(8,128)S(1)}, f32[16,1024]{1,0:T(8,128)S(1)}, u32[]{:S(2)}, u32[]{:S(2)}) collective-permute-start(f32[16,1024]{1,0:T(8,128)S(1)} %get-tuple-element.32), channel_id=1, source_target_pairs={{0,4},{2,0},{4,2},{1,5},{3,1},{5,3},{6,10},{8,6},{10,8},{7,11},{9,... | collective-permute-start | bytes 196616 | tf_op jit(solution)/shard_map/ppermute | solution.py:210
  121.0 3.6 %collective-permute-done.8 = f32[16,1024]{1,0:T(8,128)S(1)} collective-permute-done((f32[16,1024]{1,0:T(8,128)S(1)}, f32[16,1024]{1,0:T(8,128)S(1)}, u32[]{:S(2)}, u32[]{:S(2)}) %collective-permute-start.8) | collective-permute-done | bytes 65568 | tf_op jit(solution)/shard_map/ppermute | solution.py:209
  124.6 1.5 %collective-permute-done.9 = f32[16,1024]{1,0:T(8,128)S(1)} collective-permute-done((f32[16,1024]{1,0:T(8,128)S(1)}, f32[16,1024]{1,0:T(8,128)S(1)}, u32[]{:S(2)}, u32[]{:S(2)}) %collective-permute-start.9) | collective-permute-done | bytes 65568 | tf_op jit(solution)/shard_map/ppermute | solution.py:210
  126.1 0.6 fusion.6
  126.7 3.4 %all-to-all-done.2 = bf16[32,16,384]{2,1,0:T(8,128)(2,1)S(1)} async-done(((bf16[32,16,384]{2,1,0:T(8,128)(2,1)}), bf16[32,16,384]{2,1,0:T(8,128)(2,1)S(1)}, u32[]{:S(2)}, u32[]{:S(2)}) %all-to-all-start.2) | async-done | bytes 393248 | tf_op jit(solution)/shard_map/all_to_all | solution.py:214
  130.1 0.9 slice_convert_fusion
  (5 shorter events, 0.1 us)
Async XLA Ops:
  2.2 27.0 %copy-start = (bf16[16,3,3,3,384]{4,0,3,2,1:T(8,128)(2,1)S(1)}, bf16[16,3,3,3,384]{4,0,3,2,1:T(8,128)(2,1)}, u32[]{:S(2)}) copy-start(bf16[16,3,3,3,384]{4,0,3,2,1:T(8,128)(2,1)} %param.4) | copy-start | bytes 995332
  2.2 17.0 %all-to-all-start = ((bf16[12,16,1024]{2,1,0:T(8,128)(2,1)}), bf16[12,16,1024]{2,1,0:T(8,128)(2,1)S(1)}, u32[]{:S(2)}, u32[]{:S(2)}) async-start(bf16[12,16,1024]{2,1,0:T(8,128)(2,1)} %broadcast_in_dim.8), calls=%async_computation | async-start | bytes 786432 | tf_op jit(solution)/shard_map/all_to_all | solution.py:187
  19.2 30.1 %copy-start.1 = (bf16[1,1,16,1024]{3,2,1,0:T(8,128)(2,1)S(1)}, bf16[1,1,16,1024]{3,2,1,0:T(8,128)(2,1)}, u32[]{:S(2)}) copy-start(bf16[1,1,16,1024]{3,2,1,0:T(8,128)(2,1)} %param.5) | copy-start | bytes 98308
  19.2 10.0 %collective-permute-start = (bf16[12,16,1024]{2,1,0:T(8,128)(2,1)S(1)}, bf16[12,16,1024]{2,1,0:T(8,128)(2,1)S(1)}, u32[]{:S(2)}, u32[]{:S(2)}) collective-permute-start(bf16[12,16,1024]{2,1,0:T(8,128)(2,1)S(1)} %all-to-all-done.mine_ref), channel_id=1, source_target_pairs={{0,1},{1,0},{2,3},{3,2},{4,5},{5,4},{6,7},{7,6},{8,9},{9,8},{10,11... | collective-permute-start | bytes 1179656 | tf_op jit(solution)/shard_map/ppermute | solution.py:170
  30.6 14.4 %collective-permute-start.1 = (f32[16,1024]{1,0:T(8,128)S(1)}, f32[16,1024]{1,0:T(8,128)S(1)}, u32[]{:S(2)}, u32[]{:S(2)}) collective-permute-start(f32[16,1024]{1,0:T(8,128)S(1)} %get-tuple-element.21), channel_id=1, source_target_pairs={{0,24},{24,48},{48,72},{72,96},{96,120},{120,144},{144,168},{168,1... | collective-permute-start | bytes 196616 | tf_op jit(solution)/shard_map/ppermute | solution.py:193
  37.5 11.8 %collective-permute-start.2 = (f32[16,1024]{1,0:T(8,128)S(1)}, f32[16,1024]{1,0:T(8,128)S(1)}, u32[]{:S(2)}, u32[]{:S(2)}) collective-permute-start(f32[16,1024]{1,0:T(8,128)S(1)} %get-tuple-element.22), channel_id=1, source_target_pairs={{24,0},{48,24},{72,48},{96,72},{120,96},{144,120},{168,144},{192,1... | collective-permute-start | bytes 196616 | tf_op jit(solution)/shard_map/ppermute | solution.py:194
  50.0 10.4 %collective-permute-start.4 = (bf16[16,1024]{1,0:T(8,128)(2,1)S(1)}, bf16[16,1024]{1,0:T(8,128)(2,1)S(1)}, u32[]{:S(2)}, u32[]{:S(2)}) collective-permute-start(bf16[16,1024]{1,0:T(8,128)(2,1)S(1)} %get-tuple-element.25.own_ref), channel_id=1, source_target_pairs={{0,24},{24,48},{48,72},{72,96},{96,120},{120,144},{144,168},{168,1... | collective-permute-start | bytes 98312 | tf_op jit(solution)/shard_map/ppermute | solution.py:198
  55.6 6.5 %collective-permute-start.3 = (bf16[16,1024]{1,0:T(8,128)(2,1)S(1)}, bf16[16,1024]{1,0:T(8,128)(2,1)S(1)}, u32[]{:S(2)}, u32[]{:S(2)}) collective-permute-start(bf16[16,1024]{1,0:T(8,128)(2,1)S(1)} %get-tuple-element.25.own_ref), channel_id=1, source_target_pairs={{24,0},{48,24},{72,48},{96,72},{120,96},{144,120},{168,144},{192,1... | collective-permute-start | bytes 98312 | tf_op jit(solution)/shard_map/ppermute | solution.py:197
  65.0 15.8 %collective-permute-start.5 = (bf16[4,3,16,1024]{3,2,1,0:T(8,128)(2,1)S(1)}, bf16[4,3,16,1024]{3,2,1,0:T(8,128)(2,1)S(1)}, u32[]{:S(2)}, u32[]{:S(2)}) collective-permute-start(bf16[4,3,16,1024]{3,2,1,0:T(8,128)(2,1)S(1)} %get-tuple-element.28), channel_id=1, source_target_pairs={{0,1},{1,0},{2,3},{3,2},{4,5},{5,4},{6,7},{7,6},{8,9},{9,8},{10,11... | collective-permute-start | bytes 1179656 | tf_op jit(solution)/shard_map/ppermute | solution.py:170
  69.4 31.8 %all-to-all-start.1 = ((bf16[32,16,384]{2,1,0:T(8,128)(2,1)}), bf16[32,16,384]{2,1,0:T(8,128)(2,1)S(1)}, u32[]{:S(2)}, u32[]{:S(2)}) async-start(bf16[32,16,384]{2,1,0:T(8,128)(2,1)} %get-tuple-element.26), calls=%async_computation.1 | async-start | bytes 786432 | tf_op jit(solution)/shard_map/all_to_all | solution.py:200
  80.9 8.1 %collective-permute-start.6 = (bf16[2,3,16,1024]{3,2,1,0:T(8,128)(2,1)S(1)}, bf16[2,3,16,1024]{3,2,1,0:T(8,128)(2,1)S(1)}, u32[]{:S(2)}, u32[]{:S(2)}) collective-permute-start(bf16[2,3,16,1024]{3,2,1,0:T(8,128)(2,1)S(1)} %fusion.1), channel_id=1, source_target_pairs={{0,6},{6,0},{12,18},{18,12},{1,7},{7,1},{13,19},{19,13},{2,8},{8,2... | collective-permute-start | bytes 589832 | tf_op jit(solution)/shard_map/ppermute | solution.py:204
  102.1 28.1 %all-to-all-start.2 = ((bf16[32,16,384]{2,1,0:T(8,128)(2,1)}), bf16[32,16,384]{2,1,0:T(8,128)(2,1)S(1)}, u32[]{:S(2)}, u32[]{:S(2)}) async-start(bf16[32,16,384]{2,1,0:T(8,128)(2,1)} %total.1), calls=%async_computation.2 | async-start | bytes 786432 | tf_op jit(solution)/shard_map/all_to_all | solution.py:214
  107.9 6.9 %collective-permute-start.7 = (bf16[3,16,1024]{2,1,0:T(8,128)(2,1)S(1)}, bf16[3,16,1024]{2,1,0:T(8,128)(2,1)S(1)}, u32[]{:S(2)}, u32[]{:S(2)}) collective-permute-start(bf16[3,16,1024]{2,1,0:T(8,128)(2,1)S(1)} %fusion.2), channel_id=1, source_target_pairs={{0,12},{6,18},{12,0},{18,6},{1,13},{7,19},{13,1},{19,7},{2,14},{8,... | collective-permute-start | bytes 294920 | tf_op jit(solution)/shard_map/ppermute | solution.py:207
  114.8 9.8 %collective-permute-start.8 = (f32[16,1024]{1,0:T(8,128)S(1)}, f32[16,1024]{1,0:T(8,128)S(1)}, u32[]{:S(2)}, u32[]{:S(2)}) collective-permute-start(f32[16,1024]{1,0:T(8,128)S(1)} %get-tuple-element.31), channel_id=1, source_target_pairs={{0,2},{2,4},{4,0},{1,3},{3,5},{5,1},{6,8},{8,10},{10,6},{7,9},{9,1... | collective-permute-start | bytes 196616 | tf_op jit(solution)/shard_map/ppermute | solution.py:209
  116.7 9.4 %collective-permute-start.9 = (f32[16,1024]{1,0:T(8,128)S(1)}, f32[16,1024]{1,0:T(8,128)S(1)}, u32[]{:S(2)}, u32[]{:S(2)}) collective-permute-start(f32[16,1024]{1,0:T(8,128)S(1)} %get-tuple-element.32), channel_id=1, source_target_pairs={{0,4},{2,0},{4,2},{1,5},{3,1},{5,3},{6,10},{8,6},{10,8},{7,11},{9,... | collective-permute-start | bytes 196616 | tf_op jit(solution)/shard_map/ppermute | solution.py:210

commit v4 on v3

--- a/solution.py
+++ b/solution.py
@@ -13,6 +13,7 @@
 SIDE = 32
 UNIV = 1
 TAPS = 27
+LANES = 128
 VMEM_LIMIT = 48 * 1024 * 1024
 DEP = ("y", "zh")
 CHIPS = ("x", "zl")
@@ -86,6 +87,8 @@
     wide_ref, keep_ref, send_ref, x_ref, stack_ref,
 ):
     rows = own_ref.shape[0]
+    slots, per = wide_ref.shape[:2]
+    columns = x_ref.shape[0] * x_ref.shape[1] * x_ref.shape[2] // LANES
     x = merge_cores(place_ref, mine_ref, other_ref, x_ref)
     for depth_tap, ref in enumerate((above_ref, own_ref, below_ref)):
         plane = ref[...].astype(jnp.float32)
@@ -103,8 +106,15 @@
             (((1,), (1,)), ((), ())),
             preferred_element_type=jnp.float32,
         )
-        wide_ref[depth_tap * 9 : depth_tap * 9 + 9] = grad.astype(jnp.bfloat16).reshape(9, rows, -1)
-    wide_ref[TAPS:] = jnp.zeros((wide_ref.shape[0] - TAPS,) + wide_ref.shape[1:], wide_ref.dtype)
+        grad = grad.astype(jnp.bfloat16)
+        for tap in range(9):
+            for column in range(columns):
+                unit = (depth_tap * 9 + tap) * columns + column
+                wide_ref[unit // per, unit % per] = grad[
+                    tap * rows : (tap + 1) * rows, column * LANES : (column + 1) * LANES
+                ]
+    for unit in range(TAPS * columns, slots * per):
+        wide_ref[unit // per, unit % per] = jnp.zeros((rows, LANES), jnp.bfloat16)
 
     partial = lax.dot_general(
         k_ref[...], stack_ref[...], (((0,), (0,)), ((), ())), preferred_element_type=jnp.float32
@@ -123,10 +133,11 @@
 def grads(place, k_rows, above, own, below, mine, other, slots):
     rows, cells = own.shape
     chans = 2 * mine.shape[0] * mine.shape[1]
+    per = -(-TAPS * chans // (LANES * slots))
     half = jax.ShapeDtypeStruct((4, 3, rows, cells), jnp.bfloat16)
     return pl.pallas_call(
         grads_kernel,
-        out_shape=[jax.ShapeDtypeStruct((slots, rows, chans), jnp.bfloat16), half, half],
+        out_shape=[jax.ShapeDtypeStruct((slots, per, rows, LANES), jnp.bfloat16), half, half],
         in_specs=merged_specs(6),
         scratch_shapes=merged_scratch(mine) + [pltpu.VMEM((TAPS * rows, cells), jnp.bfloat16)],
         compiler_params=pltpu.CompilerParams(vmem_limit_bytes=VMEM_LIMIT),
@@ -164,6 +175,25 @@
         compiler_params=pltpu.CompilerParams(vmem_limit_bytes=VMEM_LIMIT),
         name="total",
     )(terms)
+
+
+def unpack_kernel(units_ref, out_ref):
+    per = units_ref.shape[1]
+    columns = out_ref.shape[2] // LANES
+    for tap in range(TAPS):
+        for column in range(columns):
+            unit = tap * columns + column
+            block = units_ref[unit // per, unit % per].astype(jnp.float32)
+            out_ref[tap, :, column * LANES : (column + 1) * LANES] = block
+
+
+def unpack(units, chans):
+    return pl.pallas_call(
+        unpack_kernel,
+        out_shape=jax.ShapeDtypeStruct((TAPS, units.shape[2], chans), jnp.float32),
+        compiler_params=pltpu.CompilerParams(vmem_limit_bytes=VMEM_LIMIT),
+        name="unpack",
+    )(units)
 
 
 def swap_cores(blocks):
@@ -196,23 +226,26 @@
 
     grad_above = lax.ppermute(grad_pre, DEP, back)
     grad_below = lax.ppermute(grad_pre, DEP, ring)
-    wide, keep, send = grads(place, k_rows, grad_above, grad_pre, grad_below, mine, other, depths)
-    terms = lax.all_to_all(wide, DEP, 0, 0)
+    ys, zs, xs = lax.axis_size("y"), lax.axis_size("zh"), lax.axis_size("x")
+    wide, keep, send = grads(place, k_rows, grad_above, grad_pre, grad_below, mine, other, ys)
+    scale = 1.0 / math.sqrt(UNIV * DEPTH * SIDE * SIDE)
+    over_y = lax.all_to_all(wide, "y", 0, 0)
 
     total = keep.astype(jnp.float32) + swap_cores(send).astype(jnp.float32)
-    total = total.reshape(2, 2, 3, rows, cells)
-    step = lax.ppermute(total[:, 1].astype(jnp.bfloat16), "x", [(i, i ^ 1) for i in range(4)])
-    total = total[:, 0] + step.astype(jnp.float32)
-    terms, total = lax.optimization_barrier((terms, total))
-    step = lax.ppermute(total[1].astype(jnp.bfloat16), "x", [(i, i ^ 2) for i in range(4)])
-    total = total[0] + step.astype(jnp.float32)
+    over_y, total = lax.optimization_barrier((over_y, total))
+    over_z = lax.all_to_all(total_spread(over_y, 1.0, zs), "zh", 0, 0)
+    steps = [
+        lax.ppermute(total[away].astype(jnp.bfloat16), "x", [(i, i ^ away) for i in range(xs)])
+        for away in range(1, xs)
+    ]
+    total = total[0] + sum(step.astype(jnp.float32) for step in steps)
+    over_z, total = lax.optimization_barrier((over_z, total))
+    units = lax.all_to_all(total_spread(over_z, scale, ys), "y", 0, 0)
     after = lax.ppermute(total[1], "zl", [(i, (i + 1) % 3) for i in range(3)])
     before = lax.ppermute(total[2], "zl", [(i, (i + 2) % 3) for i in range(3)])
     grad_volume = (total[0] + after + before).astype(jnp.bfloat16)
-
-    scale = 1.0 / math.sqrt(UNIV * DEPTH * SIDE * SIDE)
-    all_taps = lax.all_to_all(total_spread(terms, scale, depths), DEP, 0, 0)[:TAPS]
-    grad_kernel = jnp.transpose(all_taps.astype(jnp.float32), (1, 0, 2)).reshape(kernel.shape)
+    all_taps = unpack(units, kernel.shape[-1])
+    grad_kernel = jnp.transpose(all_taps, (1, 0, 2)).reshape(kernel.shape)
     return (activated.reshape(volume.shape), grad_volume.reshape(volume.shape), grad_kernel)
 
 

time: 132 us -> 128 us (0.970)
  the two profiles are of different devices: /device:TPU:1 before, /device:TPU:4 now
where the time goes in v4:
time: 128 us; the launch traced here: 127 us
  starting transfers between devices  76.4 us (60%)
  waiting for transfers between devices  39.8 us (31%)
  Pallas kernels  7.41 us (6%)
  local copies, waits for them, and re-layouts  1.59 us (1%)
    all_to_all x1, waiting for transfers between devices, body(): over_y = lax.all_to_all(wide, 'y', 0, 0)  14.5 us
    all_to_all x1, starting transfers between devices, body(): mine = lax.all_to_all(copies(own), CHIPS, 0, 0)  13.1 us
    ppermute x3, starting transfers between devices, body(): lax.ppermute(total[away].astype(jnp.bfloat16), 'x', [(i, i ^ away) for i...  9.82 us
    ppermute x1, starting transfers between devices, body(): high = lax.ppermute(down, DEP, back)  7.28 us
    ppermute x1, starting transfers between devices, body(): low = lax.ppermute(up, DEP, ring)  7.2 us
    all_to_all x1, starting transfers between devices, body(): over_y = lax.all_to_all(wide, 'y', 0, 0)  7.01 us
    all_to_all x1, starting transfers between devices, body(): over_z = lax.all_to_all(total_spread(over_y, 1.0, zs), 'zh', 0, 0)  6.48 us
    all_to_all x1, waiting for transfers between devices, body(): mine = lax.all_to_all(copies(own), CHIPS, 0, 0)  6.46 us
  transfers between devices with their start and end apart: 15, of which 11 were waited for; matrix products, arithmetic and copies ran while one was open for 1% of the time, Pallas kernels for 0%

profile of v4, /device:TPU:4, one launch (start us, length us, event | category | flops | bytes accessed | tf_op | source)
XLA Modules:
  0.0 126.9 jit_solution(4997725527831173377)
XLA Ops:
  0.6 1.5 %broadcast_in_dim.8 = bf16[12,16,1024]{2,1,0:T(8,128)(2,1)} broadcast(bf16[16,1024]{1,0:T(8,128)(2,1)} %bitcast.40), dimensions={1,2} | broadcast | bytes 425984 | tf_op jit(solution)/shard_map/broadcast_in_dim | solution.py:215
  2.2 0.0 copy-start
  2.2 13.1 %all-to-all-start = ((bf16[12,16,1024]{2,1,0:T(8,128)(2,1)}), bf16[12,16,1024]{2,1,0:T(8,128)(2,1)S(1)}, u32[]{:S(2)}, u32[]{:S(2)}) async-start(bf16[12,16,1024]{2,1,0:T(8,128)(2,1)} %broadcast_in_dim.8), calls=%async_computation | async-start | bytes 786432 | tf_op jit(solution)/shard_map/all_to_all | solution.py:217
  15.3 0.1 pad_add_fusion.core_ref.place_ref
  15.4 6.5 %all-to-all-done.mine_ref = bf16[12,16,1024]{2,1,0:T(8,128)(2,1)S(1)} async-done(((bf16[12,16,1024]{2,1,0:T(8,128)(2,1)}), bf16[12,16,1024]{2,1,0:T(8,128)(2,1)S(1)}, u32[]{:S(2)}, u32[]{:S(2)}) %all-to-all-start) | async-done | bytes 393248 | tf_op jit(solution)/shard_map/all_to_all | solution.py:217
  21.8 0.0 copy-start.1
  21.8 2.0 %collective-permute-start = (bf16[12,16,1024]{2,1,0:T(8,128)(2,1)S(1)}, bf16[12,16,1024]{2,1,0:T(8,128)(2,1)S(1)}, u32[]{:S(2)}, u32[]{:S(2)}) collective-permute-start(bf16[12,16,1024]{2,1,0:T(8,128)(2,1)S(1)} %all-to-all-done.mine_ref), channel_id=1, source_target_pairs={{0,1},{1,0},{2,3},{3,2},{4,5},{5,4},{6,7},{7,6},{8,9},{9,8},{10,11... | collective-permute-start | bytes 1179656 | tf_op jit(solution)/shard_map/ppermute | solution.py:200
  23.9 1.7 %collective-permute-done.other_ref = bf16[12,16,1024]{2,1,0:T(8,128)(2,1)S(1)} collective-permute-done((bf16[12,16,1024]{2,1,0:T(8,128)(2,1)S(1)}, bf16[12,16,1024]{2,1,0:T(8,128)(2,1)S(1)}, u32[]{:S(2)}, u32[]{:S(2)}) %collective-permute-start) | collective-permute-done | bytes 393248 | tf_op jit(solution)/shard_map/ppermute | solution.py:200
  25.6 0.0 copy-done
  25.6 1.4 %conv.1 = (f32[16,1024]{1,0:T(8,128)S(1)}, f32[16,1024]{1,0:T(8,128)S(1)}, f32[16,1024]{1,0:T(8,128)S(1)}) custom-call(s32[3]{0:T(128)S(1)} %pad_add_fusion.core_ref.place_ref, bf16[432,384]{1,0:T(8,128)(2,1)S(1)} %bitcast.36, bf16[12,16,1024]{2,1,0:T(8,128)(2,1)S(1)} %all-to-all-done.mine_ref, bf16[12,16,1024]{2,1,0:T(8,128)(2,1)S(1)} %collective-permute-done.other_ref), custom_call_target="tpu_custom_call" | custom-call | tf_op jit(solution)/shard_map/conv/pallas_call | solution.py:75
  27.0 7.2 %collective-permute-start.1 = (f32[16,1024]{1,0:T(8,128)S(1)}, f32[16,1024]{1,0:T(8,128)S(1)}, u32[]{:S(2)}, u32[]{:S(2)}) collective-permute-start(f32[16,1024]{1,0:T(8,128)S(1)} %get-tuple-element.23), channel_id=1, source_target_pairs={{0,24},{24,48},{48,72},{72,96},{96,120},{120,144},{144,168},{168,1... | collective-permute-start | bytes 196616 | tf_op jit(solution)/shard_map/ppermute | solution.py:223
  34.2 7.3 %collective-permute-start.2 = (f32[16,1024]{1,0:T(8,128)S(1)}, f32[16,1024]{1,0:T(8,128)S(1)}, u32[]{:S(2)}, u32[]{:S(2)}) collective-permute-start(f32[16,1024]{1,0:T(8,128)S(1)} %get-tuple-element.24), channel_id=1, source_target_pairs={{24,0},{48,24},{72,48},{96,72},{120,96},{144,120},{168,144},{192,1... | collective-permute-start | bytes 196616 | tf_op jit(solution)/shard_map/ppermute | solution.py:224
  41.5 0.7 collective-permute-done.1.low_ref
  42.2 3.8 %collective-permute-done.2.high_ref = f32[16,1024]{1,0:T(8,128)S(1)} collective-permute-done((f32[16,1024]{1,0:T(8,128)S(1)}, f32[16,1024]{1,0:T(8,128)S(1)}, u32[]{:S(2)}, u32[]{:S(2)}) %collective-permute-start.2) | collective-permute-done | bytes 65568 | tf_op jit(solution)/shard_map/ppermute | solution.py:224
  45.9 0.0 copy-done.1
  45.9 0.6 activate.1
  46.6 5.8 %collective-permute-start.4 = (bf16[16,1024]{1,0:T(8,128)(2,1)S(1)}, bf16[16,1024]{1,0:T(8,128)(2,1)S(1)}, u32[]{:S(2)}, u32[]{:S(2)}) collective-permute-start(bf16[16,1024]{1,0:T(8,128)(2,1)S(1)} %get-tuple-element.27.own_ref), channel_id=1, source_target_pairs={{0,24},{24,48},{48,72},{72,96},{96,120},{120,144},{144,168},{168,1... | collective-permute-start | bytes 98312 | tf_op jit(solution)/shard_map/ppermute | solution.py:228
  52.4 5.6 %collective-permute-start.3 = (bf16[16,1024]{1,0:T(8,128)(2,1)S(1)}, bf16[16,1024]{1,0:T(8,128)(2,1)S(1)}, u32[]{:S(2)}, u32[]{:S(2)}) collective-permute-start(bf16[16,1024]{1,0:T(8,128)(2,1)S(1)} %get-tuple-element.27.own_ref), channel_id=1, source_target_pairs={{24,0},{48,24},{72,48},{96,72},{120,96},{144,120},{168,144},{192,1... | collective-permute-start | bytes 98312 | tf_op jit(solution)/shard_map/ppermute | solution.py:227
  58.0 0.0 collective-permute-done.4.below_ref
  58.0 2.1 %collective-permute-done.3.above_ref = bf16[16,1024]{1,0:T(8,128)(2,1)S(1)} collective-permute-done((bf16[16,1024]{1,0:T(8,128)(2,1)S(1)}, bf16[16,1024]{1,0:T(8,128)(2,1)S(1)}, u32[]{:S(2)}, u32[]{:S(2)}) %collective-permute-start.3) | collective-permute-done | bytes 32800 | tf_op jit(solution)/shard_map/ppermute | solution.py:227
  60.1 3.0 %grads.1 = (bf16[8,11,16,128]{3,2,1,0:T(8,128)(2,1)}, bf16[4,3,16,1024]{3,2,1,0:T(8,128)(2,1)S(1)}, bf16[4,3,16,1024]{3,2,1,0:T(8,128)(2,1)S(1)}) custom-call(s32[3]{0:T(128)S(1)} %pad_add_fusion.core_ref.place_ref, bf16[432,384]{1,0:T(8,128)(2,1)S(1)} %bitcast.37, bf16[16,1024]{1,0:T(8,128)(2,1)S(1)} %collective-permute-done.3.above_ref, ...), custom_call_target="tpu_custom_call" | custom-call | tf_op jit(solution)/shard_map/grads/pallas_call | solution.py:138
  63.1 1.9 %collective-permute-start.5 = (bf16[4,3,16,1024]{3,2,1,0:T(8,128)(2,1)S(1)}, bf16[4,3,16,1024]{3,2,1,0:T(8,128)(2,1)S(1)}, u32[]{:S(2)}, u32[]{:S(2)}) collective-permute-start(bf16[4,3,16,1024]{3,2,1,0:T(8,128)(2,1)S(1)} %get-tuple-element.30), channel_id=1, source_target_pairs={{0,1},{1,0},{2,3},{3,2},{4,5},{5,4},{6,7},{7,6},{8,9},{9,8},{10,11... | collective-permute-start | bytes 1179656 | tf_op jit(solution)/shard_map/ppermute | solution.py:200
  65.0 7.0 %all-to-all-start.1 = ((bf16[8,11,16,128]{3,2,1,0:T(8,128)(2,1)}), bf16[8,11,16,128]{3,2,1,0:T(8,128)(2,1)S(1)}, u32[]{:S(2)}, u32[]{:S(2)}) async-start(bf16[8,11,16,128]{3,2,1,0:T(8,128)(2,1)} %get-tuple-element.28), calls=%async_computation.1 | async-start | bytes 720896 | tf_op jit(solution)/shard_map/all_to_all | solution.py:232
  72.0 0.0 collective-permute-done.5
  72.0 0.1 convert_add_fusion
  72.1 14.5 %all-to-all-done.1.terms_ref = bf16[8,11,16,128]{3,2,1,0:T(8,128)(2,1)S(1)} async-done(((bf16[8,11,16,128]{3,2,1,0:T(8,128)(2,1)}), bf16[8,11,16,128]{3,2,1,0:T(8,128)(2,1)S(1)}, u32[]{:S(2)}, u32[]{:S(2)}) %all-to-all-start.1) | async-done | bytes 360480 | tf_op jit(solution)/shard_map/all_to_all | solution.py:232
  86.7 0.7 total.2
  87.4 6.5 %all-to-all-start.2 = ((bf16[4,11,16,128]{3,2,1,0:T(8,128)(2,1)}), bf16[4,11,16,128]{3,2,1,0:T(8,128)(2,1)S(1)}, u32[]{:S(2)}, u32[]{:S(2)}) async-start(bf16[4,11,16,128]{3,2,1,0:T(8,128)(2,1)} %total.2), calls=%async_computation.2 | async-start | bytes 360448 | tf_op jit(solution)/shard_map/all_to_all | solution.py:236
  94.0 3.7 %collective-permute-start.6 = (bf16[3,16,1024]{2,1,0:T(8,128)(2,1)S(1)}, bf16[3,16,1024]{2,1,0:T(8,128)(2,1)S(1)}, u32[]{:S(2)}, u32[]{:S(2)}) collective-permute-start(bf16[3,16,1024]{2,1,0:T(8,128)(2,1)S(1)} %get-tuple-element.35), channel_id=1, source_target_pairs={{0,6},{6,0},{12,18},{18,12},{1,7},{7,1},{13,19},{19,13},{2,8},{8,2... | collective-permute-start | bytes 294920 | tf_op jit(solution)/shard_map/ppermute | solution.py:238
  97.7 3.6 %collective-permute-start.8 = (bf16[3,16,1024]{2,1,0:T(8,128)(2,1)S(1)}, bf16[3,16,1024]{2,1,0:T(8,128)(2,1)S(1)}, u32[]{:S(2)}, u32[]{:S(2)}) collective-permute-start(bf16[3,16,1024]{2,1,0:T(8,128)(2,1)S(1)} %get-tuple-element.36), channel_id=1, source_target_pairs={{0,18},{6,12},{12,6},{18,0},{1,19},{7,13},{13,7},{19,1},{2,20},{8,... | collective-permute-start | bytes 294920 | tf_op jit(solution)/shard_map/ppermute | solution.py:238
  101.3 2.5 %collective-permute-start.7 = (bf16[3,16,1024]{2,1,0:T(8,128)(2,1)S(1)}, bf16[3,16,1024]{2,1,0:T(8,128)(2,1)S(1)}, u32[]{:S(2)}, u32[]{:S(2)}) collective-permute-start(bf16[3,16,1024]{2,1,0:T(8,128)(2,1)S(1)} %get-tuple-element.37), channel_id=1, source_target_pairs={{0,12},{6,18},{12,0},{18,6},{1,13},{7,19},{13,1},{19,7},{2,14},{8,... | collective-permute-start | bytes 294920 | tf_op jit(solution)/shard_map/ppermute | solution.py:238
  103.8 0.0 collective-permute-done.6
  103.8 0.4 collective-permute-done.8
  104.2 5.1 %collective-permute-done.7 = bf16[3,16,1024]{2,1,0:T(8,128)(2,1)S(1)} collective-permute-done((bf16[3,16,1024]{2,1,0:T(8,128)(2,1)S(1)}, bf16[3,16,1024]{2,1,0:T(8,128)(2,1)S(1)}, u32[]{:S(2)}, u32[]{:S(2)}) %collective-permute-start.7) | collective-permute-done | bytes 98336 | tf_op jit(solution)/shard_map/ppermute | solution.py:238
  109.3 0.1 bitcast_add_fusion
  109.4 0.0 all-to-all-done.2.terms_ref
  109.4 0.8 total.3
  110.2 3.4 %all-to-all-start.3 = ((bf16[8,11,16,128]{3,2,1,0:T(8,128)(2,1)}), bf16[8,11,16,128]{3,2,1,0:T(8,128)(2,1)S(1)}, u32[]{:S(2)}, u32[]{:S(2)}) async-start(bf16[8,11,16,128]{3,2,1,0:T(8,128)(2,1)} %total.3), calls=%async_computation.3 | async-start | bytes 720896 | tf_op jit(solution)/shard_map/all_to_all | solution.py:243
  113.6 1.9 %collective-permute-start.9 = (f32[16,1024]{1,0:T(8,128)S(1)}, f32[16,1024]{1,0:T(8,128)S(1)}, u32[]{:S(2)}, u32[]{:S(2)}) collective-permute-start(f32[16,1024]{1,0:T(8,128)S(1)} %get-tuple-element.38), channel_id=1, source_target_pairs={{0,2},{2,4},{4,0},{1,3},{3,5},{5,1},{6,8},{8,10},{10,6},{7,9},{9,1... | collective-permute-start | bytes 196616 | tf_op jit(solution)/shard_map/ppermute | solution.py:244
  115.6 4.8 %collective-permute-start.10 = (f32[16,1024]{1,0:T(8,128)S(1)}, f32[16,1024]{1,0:T(8,128)S(1)}, u32[]{:S(2)}, u32[]{:S(2)}) collective-permute-start(f32[16,1024]{1,0:T(8,128)S(1)} %get-tuple-element.39), channel_id=1, source_target_pairs={{0,4},{2,0},{4,2},{1,5},{3,1},{5,3},{6,10},{8,6},{10,8},{7,11},{9,... | collective-permute-start | bytes 196616 | tf_op jit(solution)/shard_map/ppermute | solution.py:245
  120.4 0.3 collective-permute-done.9
  120.7 1.6 %collective-permute-done.10 = f32[16,1024]{1,0:T(8,128)S(1)} collective-permute-done((f32[16,1024]{1,0:T(8,128)S(1)}, f32[16,1024]{1,0:T(8,128)S(1)}, u32[]{:S(2)}, u32[]{:S(2)}) %collective-permute-start.10) | collective-permute-done | bytes 65568 | tf_op jit(solution)/shard_map/ppermute | solution.py:245
  122.3 0.6 fusion.2
  122.9 3.1 %all-to-all-done.3.units_ref = bf16[8,11,16,128]{3,2,1,0:T(8,128)(2,1)S(1)} async-done(((bf16[8,11,16,128]{3,2,1,0:T(8,128)(2,1)}), bf16[8,11,16,128]{3,2,1,0:T(8,128)(2,1)S(1)}, u32[]{:S(2)}, u32[]{:S(2)}) %all-to-all-start.3) | async-done | bytes 360480 | tf_op jit(solution)/shard_map/all_to_all | solution.py:243
  126.0 0.9 unpack.1
  (3 shorter events, 0.1 us)
Async XLA Ops:
  2.2 23.4 %copy-start = (bf16[16,3,3,3,384]{4,0,3,2,1:T(8,128)(2,1)S(1)}, bf16[16,3,3,3,384]{4,0,3,2,1:T(8,128)(2,1)}, u32[]{:S(2)}) copy-start(bf16[16,3,3,3,384]{4,0,3,2,1:T(8,128)(2,1)} %param.4) | copy-start | bytes 995332
  2.2 19.6 %all-to-all-start = ((bf16[12,16,1024]{2,1,0:T(8,128)(2,1)}), bf16[12,16,1024]{2,1,0:T(8,128)(2,1)S(1)}, u32[]{:S(2)}, u32[]{:S(2)}) async-start(bf16[12,16,1024]{2,1,0:T(8,128)(2,1)} %broadcast_in_dim.8), calls=%async_computation | async-start | bytes 786432 | tf_op jit(solution)/shard_map/all_to_all | solution.py:217
  21.8 24.1 %copy-start.1 = (bf16[1,1,16,1024]{3,2,1,0:T(8,128)(2,1)S(1)}, bf16[1,1,16,1024]{3,2,1,0:T(8,128)(2,1)}, u32[]{:S(2)}) copy-start(bf16[1,1,16,1024]{3,2,1,0:T(8,128)(2,1)} %param.5) | copy-start | bytes 98308
  21.8 3.7 %collective-permute-start = (bf16[12,16,1024]{2,1,0:T(8,128)(2,1)S(1)}, bf16[12,16,1024]{2,1,0:T(8,128)(2,1)S(1)}, u32[]{:S(2)}, u32[]{:S(2)}) collective-permute-start(bf16[12,16,1024]{2,1,0:T(8,128)(2,1)S(1)} %all-to-all-done.mine_ref), channel_id=1, source_target_pairs={{0,1},{1,0},{2,3},{3,2},{4,5},{5,4},{6,7},{7,6},{8,9},{9,8},{10,11... | collective-permute-start | bytes 1179656 | tf_op jit(solution)/shard_map/ppermute | solution.py:200
  27.0 15.2 %collective-permute-start.1 = (f32[16,1024]{1,0:T(8,128)S(1)}, f32[16,1024]{1,0:T(8,128)S(1)}, u32[]{:S(2)}, u32[]{:S(2)}) collective-permute-start(f32[16,1024]{1,0:T(8,128)S(1)} %get-tuple-element.23), channel_id=1, source_target_pairs={{0,24},{24,48},{48,72},{72,96},{96,120},{120,144},{144,168},{168,1... | collective-permute-start | bytes 196616 | tf_op jit(solution)/shard_map/ppermute | solution.py:223
  34.2 11.7 %collective-permute-start.2 = (f32[16,1024]{1,0:T(8,128)S(1)}, f32[16,1024]{1,0:T(8,128)S(1)}, u32[]{:S(2)}, u32[]{:S(2)}) collective-permute-start(f32[16,1024]{1,0:T(8,128)S(1)} %get-tuple-element.24), channel_id=1, source_target_pairs={{24,0},{48,24},{72,48},{96,72},{120,96},{144,120},{168,144},{192,1... | collective-permute-start | bytes 196616 | tf_op jit(solution)/shard_map/ppermute | solution.py:224
  46.6 11.4 %collective-permute-start.4 = (bf16[16,1024]{1,0:T(8,128)(2,1)S(1)}, bf16[16,1024]{1,0:T(8,128)(2,1)S(1)}, u32[]{:S(2)}, u32[]{:S(2)}) collective-permute-start(bf16[16,1024]{1,0:T(8,128)(2,1)S(1)} %get-tuple-element.27.own_ref), channel_id=1, source_target_pairs={{0,24},{24,48},{48,72},{72,96},{96,120},{120,144},{144,168},{168,1... | collective-permute-start | bytes 98312 | tf_op jit(solution)/shard_map/ppermute | solution.py:228
  52.4 7.7 %collective-permute-start.3 = (bf16[16,1024]{1,0:T(8,128)(2,1)S(1)}, bf16[16,1024]{1,0:T(8,128)(2,1)S(1)}, u32[]{:S(2)}, u32[]{:S(2)}) collective-permute-start(bf16[16,1024]{1,0:T(8,128)(2,1)S(1)} %get-tuple-element.27.own_ref), channel_id=1, source_target_pairs={{24,0},{48,24},{72,48},{96,72},{120,96},{144,120},{168,144},{192,1... | collective-permute-start | bytes 98312 | tf_op jit(solution)/shard_map/ppermute | solution.py:227
  63.1 8.9 %collective-permute-start.5 = (bf16[4,3,16,1024]{3,2,1,0:T(8,128)(2,1)S(1)}, bf16[4,3,16,1024]{3,2,1,0:T(8,128)(2,1)S(1)}, u32[]{:S(2)}, u32[]{:S(2)}) collective-permute-start(bf16[4,3,16,1024]{3,2,1,0:T(8,128)(2,1)S(1)} %get-tuple-element.30), channel_id=1, source_target_pairs={{0,1},{1,0},{2,3},{3,2},{4,5},{5,4},{6,7},{7,6},{8,9},{9,8},{10,11... | collective-permute-start | bytes 1179656 | tf_op jit(solution)/shard_map/ppermute | solution.py:200
  65.0 21.7 %all-to-all-start.1 = ((bf16[8,11,16,128]{3,2,1,0:T(8,128)(2,1)}), bf16[8,11,16,128]{3,2,1,0:T(8,128)(2,1)S(1)}, u32[]{:S(2)}, u32[]{:S(2)}) async-start(bf16[8,11,16,128]{3,2,1,0:T(8,128)(2,1)} %get-tuple-element.28), calls=%async_computation.1 | async-start | bytes 720896 | tf_op jit(solution)/shard_map/all_to_all | solution.py:232
  87.4 22.0 %all-to-all-start.2 = ((bf16[4,11,16,128]{3,2,1,0:T(8,128)(2,1)}), bf16[4,11,16,128]{3,2,1,0:T(8,128)(2,1)S(1)}, u32[]{:S(2)}, u32[]{:S(2)}) async-start(bf16[4,11,16,128]{3,2,1,0:T(8,128)(2,1)} %total.2), calls=%async_computation.2 | async-start | bytes 360448 | tf_op jit(solution)/shard_map/all_to_all | solution.py:236
  94.0 9.8 %collective-permute-start.6 = (bf16[3,16,1024]{2,1,0:T(8,128)(2,1)S(1)}, bf16[3,16,1024]{2,1,0:T(8,128)(2,1)S(1)}, u32[]{:S(2)}, u32[]{:S(2)}) collective-permute-start(bf16[3,16,1024]{2,1,0:T(8,128)(2,1)S(1)} %get-tuple-element.35), channel_id=1, source_target_pairs={{0,6},{6,0},{12,18},{18,12},{1,7},{7,1},{13,19},{19,13},{2,8},{8,2... | collective-permute-start | bytes 294920 | tf_op jit(solution)/shard_map/ppermute | solution.py:238
  97.7 6.5 %collective-permute-start.8 = (bf16[3,16,1024]{2,1,0:T(8,128)(2,1)S(1)}, bf16[3,16,1024]{2,1,0:T(8,128)(2,1)S(1)}, u32[]{:S(2)}, u32[]{:S(2)}) collective-permute-start(bf16[3,16,1024]{2,1,0:T(8,128)(2,1)S(1)} %get-tuple-element.36), channel_id=1, source_target_pairs={{0,18},{6,12},{12,6},{18,0},{1,19},{7,13},{13,7},{19,1},{2,20},{8,... | collective-permute-start | bytes 294920 | tf_op jit(solution)/shard_map/ppermute | solution.py:238
  101.3 8.0 %collective-permute-start.7 = (bf16[3,16,1024]{2,1,0:T(8,128)(2,1)S(1)}, bf16[3,16,1024]{2,1,0:T(8,128)(2,1)S(1)}, u32[]{:S(2)}, u32[]{:S(2)}) collective-permute-start(bf16[3,16,1024]{2,1,0:T(8,128)(2,1)S(1)} %get-tuple-element.37), channel_id=1, source_target_pairs={{0,12},{6,18},{12,0},{18,6},{1,13},{7,19},{13,1},{19,7},{2,14},{8,... | collective-permute-start | bytes 294920 | tf_op jit(solution)/shard_map/ppermute | solution.py:238
  110.2 15.8 %all-to-all-start.3 = ((bf16[8,11,16,128]{3,2,1,0:T(8,128)(2,1)}), bf16[8,11,16,128]{3,2,1,0:T(8,128)(2,1)S(1)}, u32[]{:S(2)}, u32[]{:S(2)}) async-start(bf16[8,11,16,128]{3,2,1,0:T(8,128)(2,1)} %total.3), calls=%async_computation.3 | async-start | bytes 720896 | tf_op jit(solution)/shard_map/all_to_all | solution.py:243
  113.6 7.1 %collective-permute-start.9 = (f32[16,1024]{1,0:T(8,128)S(1)}, f32[16,1024]{1,0:T(8,128)S(1)}, u32[]{:S(2)}, u32[]{:S(2)}) collective-permute-start(f32[16,1024]{1,0:T(8,128)S(1)} %get-tuple-element.38), channel_id=1, source_target_pairs={{0,2},{2,4},{4,0},{1,3},{3,5},{5,1},{6,8},{8,10},{10,6},{7,9},{9,1... | collective-permute-start | bytes 196616 | tf_op jit(solution)/shard_map/ppermute | solution.py:244
  115.6 6.7 %collective-permute-start.10 = (f32[16,1024]{1,0:T(8,128)S(1)}, f32[16,1024]{1,0:T(8,128)S(1)}, u32[]{:S(2)}, u32[]{:S(2)}) collective-permute-start(f32[16,1024]{1,0:T(8,128)S(1)} %get-tuple-element.39), channel_id=1, source_target_pairs={{0,4},{2,0},{4,2},{1,5},{3,1},{5,3},{6,10},{8,6},{10,8},{7,11},{9,... | collective-permute-start | bytes 196616 | tf_op jit(solution)/shard_map/ppermute | solution.py:245

commit v5 on v4

--- a/solution.py
+++ b/solution.py
@@ -82,9 +82,8 @@
     )(core, weights, mine, other)
 
 
-def grads_kernel(
-    place_ref, k_ref, above_ref, own_ref, below_ref, mine_ref, other_ref,
-    wide_ref, keep_ref, send_ref, x_ref, stack_ref,
+def wgrad_kernel(
+    place_ref, above_ref, own_ref, below_ref, mine_ref, other_ref, wide_ref, stack_ref, x_ref
 ):
     rows = own_ref.shape[0]
     slots, per = wide_ref.shape[:2]
@@ -105,8 +104,7 @@
             x,
             (((1,), (1,)), ((), ())),
             preferred_element_type=jnp.float32,
-        )
-        grad = grad.astype(jnp.bfloat16)
+        ).astype(jnp.bfloat16)
         for tap in range(9):
             for column in range(columns):
                 unit = (depth_tap * 9 + tap) * columns + column
@@ -116,9 +114,29 @@
     for unit in range(TAPS * columns, slots * per):
         wide_ref[unit // per, unit % per] = jnp.zeros((rows, LANES), jnp.bfloat16)
 
+
+def wgrad(place, above, own, below, mine, other, slots):
+    rows, cells = own.shape
+    chans = 2 * mine.shape[0] * mine.shape[1]
+    per = -(-TAPS * chans // (LANES * slots))
+    return pl.pallas_call(
+        wgrad_kernel,
+        out_shape=[
+            jax.ShapeDtypeStruct((slots, per, rows, LANES), jnp.bfloat16),
+            jax.ShapeDtypeStruct((TAPS * rows, cells), jnp.bfloat16),
+        ],
+        in_specs=merged_specs(5),
+        scratch_shapes=merged_scratch(mine),
+        compiler_params=pltpu.CompilerParams(vmem_limit_bytes=VMEM_LIMIT),
+        name="wgrad",
+    )(place, above, own, below, mine, other)
+
+
+def dgrad_kernel(place_ref, k_ref, stack_ref, keep_ref, send_ref):
+    rows = keep_ref.shape[2]
     partial = lax.dot_general(
         k_ref[...], stack_ref[...], (((0,), (0,)), ((), ())), preferred_element_type=jnp.float32
-    ).astype(jnp.bfloat16)
+    )
     first = place_ref[0] == 0
     for x_at in range(4):
         for z_at in range(3):
@@ -127,22 +145,21 @@
             at = (x_at * 3 + z_at) * 2 * rows
             even, odd = partial[at : at + rows], partial[at + rows : at + 2 * rows]
             keep_ref[x_slot, z_slot] = jnp.where(first, even, odd)
-            send_ref[x_slot, z_slot] = jnp.where(first, odd, even)
-
-
-def grads(place, k_rows, above, own, below, mine, other, slots):
-    rows, cells = own.shape
-    chans = 2 * mine.shape[0] * mine.shape[1]
-    per = -(-TAPS * chans // (LANES * slots))
-    half = jax.ShapeDtypeStruct((4, 3, rows, cells), jnp.bfloat16)
-    return pl.pallas_call(
-        grads_kernel,
-        out_shape=[jax.ShapeDtypeStruct((slots, per, rows, LANES), jnp.bfloat16), half, half],
-        in_specs=merged_specs(6),
-        scratch_shapes=merged_scratch(mine) + [pltpu.VMEM((TAPS * rows, cells), jnp.bfloat16)],
-        compiler_params=pltpu.CompilerParams(vmem_limit_bytes=VMEM_LIMIT),
-        name="grads",
-    )(place, k_rows, above, own, below, mine, other)
+            send_ref[x_slot, z_slot] = jnp.where(first, odd, even).astype(jnp.bfloat16)
+
+
+def dgrad(place, k_rows, stack):
+    shape = (4, 3, k_rows.shape[0] // TAPS, stack.shape[1])
+    return pl.pallas_call(
+        dgrad_kernel,
+        out_shape=[
+            jax.ShapeDtypeStruct(shape, jnp.float32),
+            jax.ShapeDtypeStruct(shape, jnp.bfloat16),
+        ],
+        in_specs=merged_specs(2),
+        compiler_params=pltpu.CompilerParams(vmem_limit_bytes=VMEM_LIMIT),
+        name="dgrad",
+    )(place, k_rows, stack)
 
 
 def act_kernel(mid_ref, low_ref, high_ref, cot_ref, act_ref, grad_ref):
@@ -175,6 +192,26 @@
         compiler_params=pltpu.CompilerParams(vmem_limit_bytes=VMEM_LIMIT),
         name="total",
     )(terms)
+
+
+def halve_kernel(kept_ref, came_ref, keep_ref, send_ref):
+    for at in range(keep_ref.shape[0]):
+        keep_ref[at] = kept_ref[2 * at] + came_ref[2 * at].astype(jnp.float32)
+        total = kept_ref[2 * at + 1] + came_ref[2 * at + 1].astype(jnp.float32)
+        send_ref[at] = total.astype(jnp.bfloat16)
+
+
+def halve(kept, came):
+    shape = (kept.shape[0] // 2,) + kept.shape[1:]
+    return pl.pallas_call(
+        halve_kernel,
+        out_shape=[
+            jax.ShapeDtypeStruct(shape, jnp.float32),
+            jax.ShapeDtypeStruct(shape, jnp.bfloat16),
+        ],
+        compiler_params=pltpu.CompilerParams(vmem_limit_bytes=VMEM_LIMIT),
+        name="halve",
+    )(kept, came)
 
 
 def unpack_kernel(units_ref, out_ref):
@@ -226,21 +263,20 @@
 
     grad_above = lax.ppermute(grad_pre, DEP, back)
     grad_below = lax.ppermute(grad_pre, DEP, ring)
-    ys, zs, xs = lax.axis_size("y"), lax.axis_size("zh"), lax.axis_size("x")
-    wide, keep, send = grads(place, k_rows, grad_above, grad_pre, grad_below, mine, other, ys)
+    ys, zs = lax.axis_size("y"), lax.axis_size("zh")
+    wide, stack = wgrad(place, grad_above, grad_pre, grad_below, mine, other, ys)
     scale = 1.0 / math.sqrt(UNIV * DEPTH * SIDE * SIDE)
     over_y = lax.all_to_all(wide, "y", 0, 0)
 
-    total = keep.astype(jnp.float32) + swap_cores(send).astype(jnp.float32)
-    over_y, total = lax.optimization_barrier((over_y, total))
+    keep, send = dgrad(place, k_rows, stack)
+    keep, send = halve(keep, swap_cores(send))
+    over_y, keep = lax.optimization_barrier((over_y, keep))
     over_z = lax.all_to_all(total_spread(over_y, 1.0, zs), "zh", 0, 0)
-    steps = [
-        lax.ppermute(total[away].astype(jnp.bfloat16), "x", [(i, i ^ away) for i in range(xs)])
-        for away in range(1, xs)
-    ]
-    total = total[0] + sum(step.astype(jnp.float32) for step in steps)
-    over_z, total = lax.optimization_barrier((over_z, total))
+    total = keep + lax.ppermute(send, "x", [(i, i ^ 1) for i in range(4)]).astype(jnp.float32)
+    over_z, _ = lax.optimization_barrier((over_z, total))
     units = lax.all_to_all(total_spread(over_z, scale, ys), "y", 0, 0)
+    step = lax.ppermute(total[1].astype(jnp.bfloat16), "x", [(i, i ^ 2) for i in range(4)])
+    total = total[0] + step.astype(jnp.float32)
     after = lax.ppermute(total[1], "zl", [(i, (i + 1) % 3) for i in range(3)])
     before = lax.ppermute(total[2], "zl", [(i, (i + 2) % 3) for i in range(3)])
     grad_volume = (total[0] + after + before).astype(jnp.bfloat16)

time: 128 us -> 120 us (0.938)
  the two profiles are of different devices: /device:TPU:4 before, /device:TPU:2 now
where the time goes in v5:
time: 120 us; the launch traced here: 119 us
  starting transfers between devices  74.1 us (62%)
  waiting for transfers between devices  33.7 us (28%)
  Pallas kernels  8.25 us (7%)
  local copies, waits for them, and re-layouts  1.58 us (1%)
    all_to_all x1, starting transfers between devices, body(): mine = lax.all_to_all(copies(own), CHIPS, 0, 0)  13.1 us
    all_to_all x1, waiting for transfers between devices, body(): mine = lax.all_to_all(copies(own), CHIPS, 0, 0)  8.04 us
    ppermute x1, starting transfers between devices, body(): high = lax.ppermute(down, DEP, back)  7.29 us
    ppermute x1, starting transfers between devices, body(): low = lax.ppermute(up, DEP, ring)  7.13 us
    all_to_all x1, starting transfers between devices, body(): over_y = lax.all_to_all(wide, 'y', 0, 0)  7.01 us
    all_to_all x1, waiting for transfers between devices, body(): over_z = lax.all_to_all(total_spread(over_y, 1.0, zs), 'zh', 0, 0)  6.56 us
    ppermute x1, starting transfers between devices, body(): grad_below = lax.ppermute(grad_pre, DEP, ring)  6.08 us
    all_to_all x1, starting transfers between devices, body(): over_z = lax.all_to_all(total_spread(over_y, 1.0, zs), 'zh', 0, 0)  5.59 us
  transfers between devices with their start and end apart: 14, of which 12 were waited for; matrix products, arithmetic and copies ran while one was open for 1% of the time, Pallas kernels for 2%

profile of v5, /device:TPU:2, one launch (start us, length us, event | category | flops | bytes accessed | tf_op | source)
XLA Modules:
  0.0 119.2 jit_solution(15355239118378742731)
XLA Ops:
  0.6 1.5 %broadcast_in_dim.8 = bf16[12,16,1024]{2,1,0:T(8,128)(2,1)} broadcast(bf16[16,1024]{1,0:T(8,128)(2,1)} %bitcast.40), dimensions={1,2} | broadcast | bytes 425984 | tf_op jit(solution)/shard_map/broadcast_in_dim | solution.py:252
  2.2 0.0 copy-start
  2.2 13.1 %all-to-all-start = ((bf16[12,16,1024]{2,1,0:T(8,128)(2,1)}), bf16[12,16,1024]{2,1,0:T(8,128)(2,1)S(1)}, u32[]{:S(2)}, u32[]{:S(2)}) async-start(bf16[12,16,1024]{2,1,0:T(8,128)(2,1)} %broadcast_in_dim.8), calls=%async_computation | async-start | bytes 786432 | tf_op jit(solution)/shard_map/all_to_all | solution.py:254
  15.3 0.1 pad_add_fusion.core_ref.place_ref
  15.4 8.0 %all-to-all-done.mine_ref = bf16[12,16,1024]{2,1,0:T(8,128)(2,1)S(1)} async-done(((bf16[12,16,1024]{2,1,0:T(8,128)(2,1)}), bf16[12,16,1024]{2,1,0:T(8,128)(2,1)S(1)}, u32[]{:S(2)}, u32[]{:S(2)}) %all-to-all-start) | async-done | bytes 393248 | tf_op jit(solution)/shard_map/all_to_all | solution.py:254
  23.4 0.0 copy-start.1
  23.4 2.0 %collective-permute-start = (bf16[12,16,1024]{2,1,0:T(8,128)(2,1)S(1)}, bf16[12,16,1024]{2,1,0:T(8,128)(2,1)S(1)}, u32[]{:S(2)}, u32[]{:S(2)}) collective-permute-start(bf16[12,16,1024]{2,1,0:T(8,128)(2,1)S(1)} %all-to-all-done.mine_ref), channel_id=1, source_target_pairs={{0,1},{1,0},{2,3},{3,2},{4,5},{5,4},{6,7},{7,6},{8,9},{9,8},{10,11... | collective-permute-start | bytes 1179656 | tf_op jit(solution)/shard_map/ppermute | solution.py:237
  25.5 1.7 %collective-permute-done.other_ref = bf16[12,16,1024]{2,1,0:T(8,128)(2,1)S(1)} collective-permute-done((bf16[12,16,1024]{2,1,0:T(8,128)(2,1)S(1)}, bf16[12,16,1024]{2,1,0:T(8,128)(2,1)S(1)}, u32[]{:S(2)}, u32[]{:S(2)}) %collective-permute-start) | collective-permute-done | bytes 393248 | tf_op jit(solution)/shard_map/ppermute | solution.py:237
  27.1 0.0 copy-done
  27.1 1.5 %conv.1 = (f32[16,1024]{1,0:T(8,128)S(1)}, f32[16,1024]{1,0:T(8,128)S(1)}, f32[16,1024]{1,0:T(8,128)S(1)}) custom-call(s32[3]{0:T(128)S(1)} %pad_add_fusion.core_ref.place_ref, bf16[432,384]{1,0:T(8,128)(2,1)S(1)} %bitcast.36, bf16[12,16,1024]{2,1,0:T(8,128)(2,1)S(1)} %all-to-all-done.mine_ref, bf16[12,16,1024]{2,1,0:T(8,128)(2,1)S(1)} %collective-permute-done.other_ref), custom_call_target="tpu_custom_call" | custom-call | tf_op jit(solution)/shard_map/conv/pallas_call | solution.py:75
  28.6 7.1 %collective-permute-start.1 = (f32[16,1024]{1,0:T(8,128)S(1)}, f32[16,1024]{1,0:T(8,128)S(1)}, u32[]{:S(2)}, u32[]{:S(2)}) collective-permute-start(f32[16,1024]{1,0:T(8,128)S(1)} %get-tuple-element.25), channel_id=1, source_target_pairs={{0,24},{24,48},{48,72},{72,96},{96,120},{120,144},{144,168},{168,1... | collective-permute-start | bytes 196616 | tf_op jit(solution)/shard_map/ppermute | solution.py:260
  35.8 7.3 %collective-permute-start.2 = (f32[16,1024]{1,0:T(8,128)S(1)}, f32[16,1024]{1,0:T(8,128)S(1)}, u32[]{:S(2)}, u32[]{:S(2)}) collective-permute-start(f32[16,1024]{1,0:T(8,128)S(1)} %get-tuple-element.26), channel_id=1, source_target_pairs={{24,0},{48,24},{72,48},{96,72},{120,96},{144,120},{168,144},{192,1... | collective-permute-start | bytes 196616 | tf_op jit(solution)/shard_map/ppermute | solution.py:261
  43.0 1.9 %collective-permute-done.1.low_ref = f32[16,1024]{1,0:T(8,128)S(1)} collective-permute-done((f32[16,1024]{1,0:T(8,128)S(1)}, f32[16,1024]{1,0:T(8,128)S(1)}, u32[]{:S(2)}, u32[]{:S(2)}) %collective-permute-start.1) | collective-permute-done | bytes 65568 | tf_op jit(solution)/shard_map/ppermute | solution.py:260
  45.0 1.8 %collective-permute-done.2.high_ref = f32[16,1024]{1,0:T(8,128)S(1)} collective-permute-done((f32[16,1024]{1,0:T(8,128)S(1)}, f32[16,1024]{1,0:T(8,128)S(1)}, u32[]{:S(2)}, u32[]{:S(2)}) %collective-permute-start.2) | collective-permute-done | bytes 65568 | tf_op jit(solution)/shard_map/ppermute | solution.py:261
  46.8 0.0 copy-done.1
  46.8 0.6 activate.1
  47.4 6.1 %collective-permute-start.4 = (bf16[16,1024]{1,0:T(8,128)(2,1)S(1)}, bf16[16,1024]{1,0:T(8,128)(2,1)S(1)}, u32[]{:S(2)}, u32[]{:S(2)}) collective-permute-start(bf16[16,1024]{1,0:T(8,128)(2,1)S(1)} %get-tuple-element.29.own_ref), channel_id=1, source_target_pairs={{0,24},{24,48},{48,72},{72,96},{96,120},{120,144},{144,168},{168,1... | collective-permute-start | bytes 98312 | tf_op jit(solution)/shard_map/ppermute | solution.py:265
  53.5 4.9 %collective-permute-start.3 = (bf16[16,1024]{1,0:T(8,128)(2,1)S(1)}, bf16[16,1024]{1,0:T(8,128)(2,1)S(1)}, u32[]{:S(2)}, u32[]{:S(2)}) collective-permute-start(bf16[16,1024]{1,0:T(8,128)(2,1)S(1)} %get-tuple-element.29.own_ref), channel_id=1, source_target_pairs={{24,0},{48,24},{72,48},{96,72},{120,96},{144,120},{168,144},{192,1... | collective-permute-start | bytes 98312 | tf_op jit(solution)/shard_map/ppermute | solution.py:264
  58.4 0.1 collective-permute-done.4.below_ref
  58.4 2.8 %collective-permute-done.3.above_ref = bf16[16,1024]{1,0:T(8,128)(2,1)S(1)} collective-permute-done((bf16[16,1024]{1,0:T(8,128)(2,1)S(1)}, bf16[16,1024]{1,0:T(8,128)(2,1)S(1)}, u32[]{:S(2)}, u32[]{:S(2)}) %collective-permute-start.3) | collective-permute-done | bytes 32800 | tf_op jit(solution)/shard_map/ppermute | solution.py:264
  61.2 2.5 %wgrad.1 = (bf16[8,11,16,128]{3,2,1,0:T(8,128)(2,1)}, bf16[432,1024]{1,0:T(8,128)(2,1)S(1)}) custom-call(s32[3]{0:T(128)S(1)} %pad_add_fusion.core_ref.place_ref, bf16[16,1024]{1,0:T(8,128)(2,1)S(1)} %collective-permute-done.3.above_ref, bf16[16,1024]{1,0:T(8,128)(2,1)S(1)} %get-tuple-element.29.own_ref, ...), custom_call_target="tpu_custom_call" | custom-call | tf_op jit(solution)/shard_map/wgrad/pallas_call | solution.py:122
  63.8 7.0 %all-to-all-start.1 = ((bf16[8,11,16,128]{3,2,1,0:T(8,128)(2,1)}), bf16[8,11,16,128]{3,2,1,0:T(8,128)(2,1)S(1)}, u32[]{:S(2)}, u32[]{:S(2)}) async-start(bf16[8,11,16,128]{3,2,1,0:T(8,128)(2,1)} %get-tuple-element.30), calls=%async_computation.1 | async-start | bytes 720896 | tf_op jit(solution)/shard_map/all_to_all | solution.py:269
  70.8 1.1 dgrad.1
  71.9 1.9 %collective-permute-start.5 = (bf16[4,3,16,1024]{3,2,1,0:T(8,128)(2,1)S(1)}, bf16[4,3,16,1024]{3,2,1,0:T(8,128)(2,1)S(1)}, u32[]{:S(2)}, u32[]{:S(2)}) collective-permute-start(bf16[4,3,16,1024]{3,2,1,0:T(8,128)(2,1)S(1)} %get-tuple-element.33), channel_id=1, source_target_pairs={{0,1},{1,0},{2,3},{3,2},{4,5},{5,4},{6,7},{7,6},{8,9},{9,8},{10,11... | collective-permute-start | bytes 1179656 | tf_op jit(solution)/shard_map/ppermute | solution.py:237
  73.8 1.7 %collective-permute-done.5.came_ref = bf16[4,3,16,1024]{3,2,1,0:T(8,128)(2,1)S(1)} collective-permute-done((bf16[4,3,16,1024]{3,2,1,0:T(8,128)(2,1)S(1)}, bf16[4,3,16,1024]{3,2,1,0:T(8,128)(2,1)S(1)}, u32[]{:S(2)}, u32[]{:S(2)}) %collective-permute-start.5) | collective-permute-done | bytes 393248 | tf_op jit(solution)/shard_map/ppermute | solution.py:237
  75.5 0.1 halve.1
  75.6 4.2 %collective-permute-start.6 = (bf16[2,3,16,1024]{3,2,1,0:T(8,128)(2,1)S(1)}, bf16[2,3,16,1024]{3,2,1,0:T(8,128)(2,1)S(1)}, u32[]{:S(2)}, u32[]{:S(2)}) collective-permute-start(bf16[2,3,16,1024]{3,2,1,0:T(8,128)(2,1)S(1)} %get-tuple-element.36), channel_id=1, source_target_pairs={{0,6},{6,0},{12,18},{18,12},{1,7},{7,1},{13,19},{19,13},{2,8},{8,2... | collective-permute-start | bytes 589832 | tf_op jit(solution)/shard_map/ppermute | solution.py:275
  79.8 4.0 %all-to-all-done.1.terms_ref = bf16[8,11,16,128]{3,2,1,0:T(8,128)(2,1)S(1)} async-done(((bf16[8,11,16,128]{3,2,1,0:T(8,128)(2,1)}), bf16[8,11,16,128]{3,2,1,0:T(8,128)(2,1)S(1)}, u32[]{:S(2)}, u32[]{:S(2)}) %all-to-all-start.1) | async-done | bytes 360480 | tf_op jit(solution)/shard_map/all_to_all | solution.py:269
  83.8 0.7 total.2
  84.6 5.6 %all-to-all-start.2 = ((bf16[4,11,16,128]{3,2,1,0:T(8,128)(2,1)}), bf16[4,11,16,128]{3,2,1,0:T(8,128)(2,1)S(1)}, u32[]{:S(2)}, u32[]{:S(2)}) async-start(bf16[4,11,16,128]{3,2,1,0:T(8,128)(2,1)} %total.2), calls=%async_computation.2 | async-start | bytes 360448 | tf_op jit(solution)/shard_map/all_to_all | solution.py:274
  90.2 0.0 collective-permute-done.6
  90.2 4.4 %collective-permute-start.7 = (bf16[3,16,1024]{2,1,0:T(8,128)(2,1)S(1)}, bf16[3,16,1024]{2,1,0:T(8,128)(2,1)S(1)}, u32[]{:S(2)}, u32[]{:S(2)}) collective-permute-start(bf16[3,16,1024]{2,1,0:T(8,128)(2,1)S(1)} %fusion.1), channel_id=1, source_target_pairs={{0,12},{6,18},{12,0},{18,6},{1,13},{7,19},{13,1},{19,7},{2,14},{8,... | collective-permute-start | bytes 294920 | tf_op jit(solution)/shard_map/ppermute | solution.py:278
  94.6 6.6 %all-to-all-done.2.terms_ref = bf16[4,11,16,128]{3,2,1,0:T(8,128)(2,1)S(1)} async-done(((bf16[4,11,16,128]{3,2,1,0:T(8,128)(2,1)}), bf16[4,11,16,128]{3,2,1,0:T(8,128)(2,1)S(1)}, u32[]{:S(2)}, u32[]{:S(2)}) %all-to-all-start.2) | async-done | bytes 180256 | tf_op jit(solution)/shard_map/all_to_all | solution.py:274
  101.2 0.8 total.3
  102.0 3.7 %all-to-all-start.3 = ((bf16[8,11,16,128]{3,2,1,0:T(8,128)(2,1)}), bf16[8,11,16,128]{3,2,1,0:T(8,128)(2,1)S(1)}, u32[]{:S(2)}, u32[]{:S(2)}) async-start(bf16[8,11,16,128]{3,2,1,0:T(8,128)(2,1)} %total.3), calls=%async_computation.3 | async-start | bytes 720896 | tf_op jit(solution)/shard_map/all_to_all | solution.py:277
  105.7 0.0 collective-permute-done.7
  105.8 2.4 %collective-permute-start.8 = (f32[16,1024]{1,0:T(8,128)S(1)}, f32[16,1024]{1,0:T(8,128)S(1)}, u32[]{:S(2)}, u32[]{:S(2)}) collective-permute-start(f32[16,1024]{1,0:T(8,128)S(1)} %get-tuple-element.39), channel_id=1, source_target_pairs={{0,2},{2,4},{4,0},{1,3},{3,5},{5,1},{6,8},{8,10},{10,6},{7,9},{9,1... | collective-permute-start | bytes 196616 | tf_op jit(solution)/shard_map/ppermute | solution.py:280
  108.2 4.3 %collective-permute-start.9 = (f32[16,1024]{1,0:T(8,128)S(1)}, f32[16,1024]{1,0:T(8,128)S(1)}, u32[]{:S(2)}, u32[]{:S(2)}) collective-permute-start(f32[16,1024]{1,0:T(8,128)S(1)} %get-tuple-element.40), channel_id=1, source_target_pairs={{0,4},{2,0},{4,2},{1,5},{3,1},{5,3},{6,10},{8,6},{10,8},{7,11},{9,... | collective-permute-start | bytes 196616 | tf_op jit(solution)/shard_map/ppermute | solution.py:281
  112.5 0.3 collective-permute-done.8
  112.8 1.6 %collective-permute-done.9 = f32[16,1024]{1,0:T(8,128)S(1)} collective-permute-done((f32[16,1024]{1,0:T(8,128)S(1)}, f32[16,1024]{1,0:T(8,128)S(1)}, u32[]{:S(2)}, u32[]{:S(2)}) %collective-permute-start.9) | collective-permute-done | bytes 65568 | tf_op jit(solution)/shard_map/ppermute | solution.py:281
  114.4 0.6 fusion.5
  115.0 3.3 %all-to-all-done.3.units_ref = bf16[8,11,16,128]{3,2,1,0:T(8,128)(2,1)S(1)} async-done(((bf16[8,11,16,128]{3,2,1,0:T(8,128)(2,1)}), bf16[8,11,16,128]{3,2,1,0:T(8,128)(2,1)S(1)}, u32[]{:S(2)}, u32[]{:S(2)}) %all-to-all-start.3) | async-done | bytes 360480 | tf_op jit(solution)/shard_map/all_to_all | solution.py:277
  118.3 0.9 unpack.1
  (4 shorter events, 0.1 us)
Async XLA Ops:
  2.2 25.0 %copy-start = (bf16[16,3,3,3,384]{4,0,3,2,1:T(8,128)(2,1)S(1)}, bf16[16,3,3,3,384]{4,0,3,2,1:T(8,128)(2,1)}, u32[]{:S(2)}) copy-start(bf16[16,3,3,3,384]{4,0,3,2,1:T(8,128)(2,1)} %param.4) | copy-start | bytes 995332
  2.2 21.2 %all-to-all-start = ((bf16[12,16,1024]{2,1,0:T(8,128)(2,1)}), bf16[12,16,1024]{2,1,0:T(8,128)(2,1)S(1)}, u32[]{:S(2)}, u32[]{:S(2)}) async-start(bf16[12,16,1024]{2,1,0:T(8,128)(2,1)} %broadcast_in_dim.8), calls=%async_computation | async-start | bytes 786432 | tf_op jit(solution)/shard_map/all_to_all | solution.py:254
  23.4 23.4 %copy-start.1 = (bf16[1,1,16,1024]{3,2,1,0:T(8,128)(2,1)S(1)}, bf16[1,1,16,1024]{3,2,1,0:T(8,128)(2,1)}, u32[]{:S(2)}) copy-start(bf16[1,1,16,1024]{3,2,1,0:T(8,128)(2,1)} %param.5) | copy-start | bytes 98308
  23.4 3.7 %collective-permute-start = (bf16[12,16,1024]{2,1,0:T(8,128)(2,1)S(1)}, bf16[12,16,1024]{2,1,0:T(8,128)(2,1)S(1)}, u32[]{:S(2)}, u32[]{:S(2)}) collective-permute-start(bf16[12,16,1024]{2,1,0:T(8,128)(2,1)S(1)} %all-to-all-done.mine_ref), channel_id=1, source_target_pairs={{0,1},{1,0},{2,3},{3,2},{4,5},{5,4},{6,7},{7,6},{8,9},{9,8},{10,11... | collective-permute-start | bytes 1179656 | tf_op jit(solution)/shard_map/ppermute | solution.py:237
  28.6 16.4 %collective-permute-start.1 = (f32[16,1024]{1,0:T(8,128)S(1)}, f32[16,1024]{1,0:T(8,128)S(1)}, u32[]{:S(2)}, u32[]{:S(2)}) collective-permute-start(f32[16,1024]{1,0:T(8,128)S(1)} %get-tuple-element.25), channel_id=1, source_target_pairs={{0,24},{24,48},{48,72},{72,96},{96,120},{120,144},{144,168},{168,1... | collective-permute-start | bytes 196616 | tf_op jit(solution)/shard_map/ppermute | solution.py:260
  35.8 11.0 %collective-permute-start.2 = (f32[16,1024]{1,0:T(8,128)S(1)}, f32[16,1024]{1,0:T(8,128)S(1)}, u32[]{:S(2)}, u32[]{:S(2)}) collective-permute-start(f32[16,1024]{1,0:T(8,128)S(1)} %get-tuple-element.26), channel_id=1, source_target_pairs={{24,0},{48,24},{72,48},{96,72},{120,96},{144,120},{168,144},{192,1... | collective-permute-start | bytes 196616 | tf_op jit(solution)/shard_map/ppermute | solution.py:261
  47.4 11.0 %collective-permute-start.4 = (bf16[16,1024]{1,0:T(8,128)(2,1)S(1)}, bf16[16,1024]{1,0:T(8,128)(2,1)S(1)}, u32[]{:S(2)}, u32[]{:S(2)}) collective-permute-start(bf16[16,1024]{1,0:T(8,128)(2,1)S(1)} %get-tuple-element.29.own_ref), channel_id=1, source_target_pairs={{0,24},{24,48},{48,72},{72,96},{96,120},{120,144},{144,168},{168,1... | collective-permute-start | bytes 98312 | tf_op jit(solution)/shard_map/ppermute | solution.py:265
  53.5 7.7 %collective-permute-start.3 = (bf16[16,1024]{1,0:T(8,128)(2,1)S(1)}, bf16[16,1024]{1,0:T(8,128)(2,1)S(1)}, u32[]{:S(2)}, u32[]{:S(2)}) collective-permute-start(bf16[16,1024]{1,0:T(8,128)(2,1)S(1)} %get-tuple-element.29.own_ref), channel_id=1, source_target_pairs={{24,0},{48,24},{72,48},{96,72},{120,96},{144,120},{168,144},{192,1... | collective-permute-start | bytes 98312 | tf_op jit(solution)/shard_map/ppermute | solution.py:264
  63.8 20.1 %all-to-all-start.1 = ((bf16[8,11,16,128]{3,2,1,0:T(8,128)(2,1)}), bf16[8,11,16,128]{3,2,1,0:T(8,128)(2,1)S(1)}, u32[]{:S(2)}, u32[]{:S(2)}) async-start(bf16[8,11,16,128]{3,2,1,0:T(8,128)(2,1)} %get-tuple-element.30), calls=%async_computation.1 | async-start | bytes 720896 | tf_op jit(solution)/shard_map/all_to_all | solution.py:269
  71.9 3.6 %collective-permute-start.5 = (bf16[4,3,16,1024]{3,2,1,0:T(8,128)(2,1)S(1)}, bf16[4,3,16,1024]{3,2,1,0:T(8,128)(2,1)S(1)}, u32[]{:S(2)}, u32[]{:S(2)}) collective-permute-start(bf16[4,3,16,1024]{3,2,1,0:T(8,128)(2,1)S(1)} %get-tuple-element.33), channel_id=1, source_target_pairs={{0,1},{1,0},{2,3},{3,2},{4,5},{5,4},{6,7},{7,6},{8,9},{9,8},{10,11... | collective-permute-start | bytes 1179656 | tf_op jit(solution)/shard_map/ppermute | solution.py:237
  75.6 14.5 %collective-permute-start.6 = (bf16[2,3,16,1024]{3,2,1,0:T(8,128)(2,1)S(1)}, bf16[2,3,16,1024]{3,2,1,0:T(8,128)(2,1)S(1)}, u32[]{:S(2)}, u32[]{:S(2)}) collective-permute-start(bf16[2,3,16,1024]{3,2,1,0:T(8,128)(2,1)S(1)} %get-tuple-element.36), channel_id=1, source_target_pairs={{0,6},{6,0},{12,18},{18,12},{1,7},{7,1},{13,19},{19,13},{2,8},{8,2... | collective-permute-start | bytes 589832 | tf_op jit(solution)/shard_map/ppermute | solution.py:275
  84.6 16.6 %all-to-all-start.2 = ((bf16[4,11,16,128]{3,2,1,0:T(8,128)(2,1)}), bf16[4,11,16,128]{3,2,1,0:T(8,128)(2,1)S(1)}, u32[]{:S(2)}, u32[]{:S(2)}) async-start(bf16[4,11,16,128]{3,2,1,0:T(8,128)(2,1)} %total.2), calls=%async_computation.2 | async-start | bytes 360448 | tf_op jit(solution)/shard_map/all_to_all | solution.py:274
  90.2 15.5 %collective-permute-start.7 = (bf16[3,16,1024]{2,1,0:T(8,128)(2,1)S(1)}, bf16[3,16,1024]{2,1,0:T(8,128)(2,1)S(1)}, u32[]{:S(2)}, u32[]{:S(2)}) collective-permute-start(bf16[3,16,1024]{2,1,0:T(8,128)(2,1)S(1)} %fusion.1), channel_id=1, source_target_pairs={{0,12},{6,18},{12,0},{18,6},{1,13},{7,19},{13,1},{19,7},{2,14},{8,... | collective-permute-start | bytes 294920 | tf_op jit(solution)/shard_map/ppermute | solution.py:278
  102.0 16.3 %all-to-all-start.3 = ((bf16[8,11,16,128]{3,2,1,0:T(8,128)(2,1)}), bf16[8,11,16,128]{3,2,1,0:T(8,128)(2,1)S(1)}, u32[]{:S(2)}, u32[]{:S(2)}) async-start(bf16[8,11,16,128]{3,2,1,0:T(8,128)(2,1)} %total.3), calls=%async_computation.3 | async-start | bytes 720896 | tf_op jit(solution)/shard_map/all_to_all | solution.py:277
  105.8 7.1 %collective-permute-start.8 = (f32[16,1024]{1,0:T(8,128)S(1)}, f32[16,1024]{1,0:T(8,128)S(1)}, u32[]{:S(2)}, u32[]{:S(2)}) collective-permute-start(f32[16,1024]{1,0:T(8,128)S(1)} %get-tuple-element.39), channel_id=1, source_target_pairs={{0,2},{2,4},{4,0},{1,3},{3,5},{5,1},{6,8},{8,10},{10,6},{7,9},{9,1... | collective-permute-start | bytes 196616 | tf_op jit(solution)/shard_map/ppermute | solution.py:280
  108.2 6.2 %collective-permute-start.9 = (f32[16,1024]{1,0:T(8,128)S(1)}, f32[16,1024]{1,0:T(8,128)S(1)}, u32[]{:S(2)}, u32[]{:S(2)}) collective-permute-start(f32[16,1024]{1,0:T(8,128)S(1)} %get-tuple-element.40), channel_id=1, source_target_pairs={{0,4},{2,0},{4,2},{1,5},{3,1},{5,3},{6,10},{8,6},{10,8},{7,11},{9,... | collective-permute-start | bytes 196616 | tf_op jit(solution)/shard_map/ppermute | solution.py:281

commit v6 on v5

v6 whole, which is shorter than its diff:
```python
import functools
import math

import jax
import jax.numpy as jnp
from jax import lax
from jax.experimental import pallas as pl
from jax.experimental.pallas import tpu as pltpu
from jax.sharding import Mesh
from jax.sharding import PartitionSpec as P

DEPTH = 32
SIDE = 32
UNIV = 1
TAPS = 27
LANES = 128
VMEM_LIMIT = 48 * 1024 * 1024
DEP = ("y", "zh")
CHIPS = ("x", "zl")
CHAN = ("x", "zl", "core")


def shift_cells(plane, row_step, col_step):
    cells = plane.shape[-1]
    if col_step:
        columns = lax.broadcasted_iota(jnp.int32, plane.shape, 1) % SIDE
        edge = 0 if col_step > 0 else SIDE - 1
        plain = pltpu.roll(plane, col_step % cells, 1)
        wrapped = pltpu.roll(plane, (col_step - col_step * SIDE) % cells, 1)
        plane = jnp.where(columns == edge, wrapped, plain)
    if row_step:
        plane = pltpu.roll(plane, (row_step * SIDE) % cells, 1)
    return plane


def merge_cores(core_ref, mine_ref, other_ref, x_ref):
    first = core_ref[0] == 0
    mine, other = mine_ref[...], other_ref[...]
    x_ref[:, 0] = jnp.where(first, mine, other)
    x_ref[:, 1] = jnp.where(first, other, mine)
    return x_ref[...].reshape(-1, x_ref.shape[-1])


def conv_kernel(core_ref, odd_ref, w_ref, mine_ref, other_ref, near_ref, mid_ref, far_ref, x_ref):
    rows = mid_ref.shape[0]
    x = merge_cores(core_ref, mine_ref, other_ref, x_ref)
    sums = []
    for depth_tap in range(3):
        w = w_ref[depth_tap * 9 * rows : (depth_tap + 1) * 9 * rows, :]
        product = jnp.dot(w, x, preferred_element_type=jnp.float32)
        total = None
        for col_tap in range(3):
            part = None
            for row_tap in range(3):
                at = (row_tap * 3 + col_tap) * rows
                term = shift_cells(product[at : at + rows], 1 - row_tap, 0)
                part = term if part is None else part + term
            part = shift_cells(part, 0, 1 - col_tap)
            total = part if total is None else total + part
        sums.append(total)
    up, mid, down = sums
    odd = odd_ref[0] == 1
    near_ref[...] = jnp.where(odd, down, up)
    mid_ref[...] = mid
    far_ref[...] = jnp.where(odd, up, down)


def specs(scalars, arrays):
    smem = pl.BlockSpec(memory_space=pltpu.SMEM)
    return [smem] * scalars + [pl.BlockSpec(memory_space=pltpu.VMEM)] * arrays


def merged_scratch(mine):
    return [pltpu.VMEM((mine.shape[0], 2) + mine.shape[1:], mine.dtype)]


def conv(core, odd, weights, mine, other):
    rows = weights.shape[0] // TAPS
    cells = mine.shape[-1]
    return pl.pallas_call(
        conv_kernel,
        out_shape=[jax.ShapeDtypeStruct((rows, cells), jnp.float32)] * 3,
        in_specs=specs(2, 3),
        scratch_shapes=merged_scratch(mine),
        compiler_params=pltpu.CompilerParams(vmem_limit_bytes=VMEM_LIMIT),
        name="conv",
    )(core, odd, weights, mine, other)


def stack_plane(plane, stack_ref, at):
    rows = plane.shape[0]
    plane = plane.astype(jnp.float32)
    moved = [shift_cells(plane, 0, col_tap - 1) for col_tap in range(3)]
    for row_tap in range(3):
        for col_tap in range(3):
            stack_ref[at : at + rows, :] = shift_cells(moved[col_tap], row_tap - 1, 0).astype(
                jnp.bfloat16
            )
            at += rows


def cross(stack, x):
    return lax.dot_general(
        stack, x, (((1,), (1,)), ((), ())), preferred_element_type=jnp.float32
    ).astype(jnp.bfloat16)


def own_kernel(core_ref, own_ref, mine_ref, other_ref, units_ref, stack_ref, x_ref):
    rows = own_ref.shape[0]
    x = merge_cores(core_ref, mine_ref, other_ref, x_ref)
    columns = x.shape[0] // LANES
    stack_plane(own_ref[...], stack_ref, 0)
    grad = cross(stack_ref[...], x)
    for unit in range(9 * columns):
        tap, column = divmod(unit, columns)
        units_ref[unit] = grad[
            tap * rows : (tap + 1) * rows, column * LANES : (column + 1) * LANES
        ]


def wgrad_own(core, own, mine, other):
    rows, cells = own.shape
    chans = 2 * mine.shape[0] * mine.shape[1]
    return pl.pallas_call(
        own_kernel,
        out_shape=[
            jax.ShapeDtypeStruct((9 * chans // LANES, rows, LANES), jnp.bfloat16),
            jax.ShapeDtypeStruct((9 * rows, cells), jnp.bfloat16),
            jax.ShapeDtypeStruct((mine.shape[0], 2) + mine.shape[1:], mine.dtype),
        ],
        in_specs=specs(1, 3),
        compiler_params=pltpu.CompilerParams(vmem_limit_bytes=VMEM_LIMIT),
        name="wgrad_own",
    )(core, own, mine, other)


def halo_kernel(odd_ref, near_ref, far_ref, x_ref, units_ref, wide_ref, stack_ref):
    rows = near_ref.shape[0]
    slots, per = wide_ref.shape[:2]
    x = x_ref[...].reshape(-1, x_ref.shape[-1])
    columns = x.shape[0] // LANES
    odd = odd_ref[0] == 1
    near, far = near_ref[...].astype(jnp.float32), far_ref[...].astype(jnp.float32)
    for half, plane in enumerate((jnp.where(odd, far, near), jnp.where(odd, near, far))):
        stack_plane(plane, stack_ref, half * 9 * rows)
        grad = cross(stack_ref[half * 9 * rows : (half + 1) * 9 * rows, :], x)
        for at in range(9 * columns):
            tap, column = divmod(at, columns)
            unit = 18 * half * columns + at
            wide_ref[unit // per, unit % per] = grad[
                tap * rows : (tap + 1) * rows, column * LANES : (column + 1) * LANES
            ]
    for at in range(9 * columns):
        unit = 9 * columns + at
        wide_ref[unit // per, unit % per] = units_ref[at]
    for unit in range(TAPS * columns, slots * per):
        wide_ref[unit // per, unit % per] = jnp.zeros((rows, LANES), jnp.bfloat16)


def wgrad_halo(odd, near, far, x, units, slots):
    rows, cells = near.shape
    per = -(-3 * units.shape[0] // slots)
    return pl.pallas_call(
        halo_kernel,
        out_shape=[
            jax.ShapeDtypeStruct((slots, per, rows, LANES), jnp.bfloat16),
            jax.ShapeDtypeStruct((18 * rows, cells), jnp.bfloat16),
        ],
        in_specs=specs(1, 4),
        compiler_params=pltpu.CompilerParams(vmem_limit_bytes=VMEM_LIMIT),
        name="wgrad_halo",
    )(odd, near, far, x, units)


def dgrad_kernel(core_ref, x_at_ref, z_at_ref, k_ref, own_ref, halo_ref, keep_ref, send_ref):
    rows = keep_ref.shape[2]
    n = 9 * rows
    partial = None
    for at, stack in ((0, halo_ref[:n, :]), (n, own_ref[...]), (2 * n, halo_ref[n:, :])):
        term = lax.dot_general(
            k_ref[at : at + n, :],
            stack,
            (((0,), (0,)), ((), ())),
            preferred_element_type=jnp.float32,
        )
        partial = term if partial is None else partial + term
    first = core_ref[0] == 0
    for x_at in range(4):
        for z_at in range(3):
            x_slot = x_at ^ x_at_ref[0]
            z_slot = lax.rem(z_at - z_at_ref[0] + 3, 3)
            at = (x_at * 3 + z_at) * 2 * rows
            even, odd = partial[at : at + rows], partial[at + rows : at + 2 * rows]
            keep_ref[z_slot, x_slot] = jnp.where(first, even, odd)
            send_ref[z_slot, x_slot] = jnp.where(first, odd, even).astype(jnp.bfloat16)


def dgrad(core, x_at, z_at, k_rows, own, halo):
    shape = (3, 4, k_rows.shape[0] // TAPS, own.shape[1])
    return pl.pallas_call(
        dgrad_kernel,
        out_shape=[
            jax.ShapeDtypeStruct(shape, jnp.float32),
            jax.ShapeDtypeStruct(shape, jnp.bfloat16),
        ],
        in_specs=specs(3, 3),
        compiler_params=pltpu.CompilerParams(vmem_limit_bytes=VMEM_LIMIT),
        name="dgrad",
    )(core, x_at, z_at, k_rows, own, halo)


def act_kernel(mid_ref, low_ref, high_ref, cot_ref, act_ref, grad_ref):
    preact = mid_ref[...] + low_ref[...] + high_ref[...]
    sig = jax.nn.sigmoid(preact)
    act_ref[...] = (preact * sig).astype(jnp.bfloat16)
    cot = cot_ref[...].astype(jnp.float32)
    grad_ref[...] = (cot * sig * (1.0 + preact * (1.0 - sig))).astype(jnp.bfloat16)


def activate(mid, low, high, cot):
    shape = jax.ShapeDtypeStruct(mid.shape, jnp.bfloat16)
    return pl.pallas_call(
        act_kernel,
        out_shape=[shape, shape],
        compiler_params=pltpu.CompilerParams(vmem_limit_bytes=VMEM_LIMIT),
        name="activate",
    )(mid, low, high, cot)


def total_kernel(terms_ref, out_ref, *, scale):
    total = jnp.sum(terms_ref[...].astype(jnp.float32), axis=0) * scale
    out_ref[...] = jnp.broadcast_to(total.astype(jnp.bfloat16)[None], out_ref.shape)


def total_spread(terms, scale, copies):
    return pl.pallas_call(
        functools.partial(total_kernel, scale=scale),
        out_shape=jax.ShapeDtypeStruct((copies,) + terms.shape[1:], jnp.bfloat16),
        compiler_params=pltpu.CompilerParams(vmem_limit_bytes=VMEM_LIMIT),
        name="total",
    )(terms)


def part_kernel(kept_ref, came_ref, here_ref, after_ref, before_ref):
    here_ref[...] = kept_ref[0] + came_ref[0].astype(jnp.float32)
    after_ref[...] = (kept_ref[1] + came_ref[1].astype(jnp.float32)).astype(jnp.bfloat16)
    before_ref[...] = (kept_ref[2] + came_ref[2].astype(jnp.float32)).astype(jnp.bfloat16)


def part(kept, came):
    return pl.pallas_call(
        part_kernel,
        out_shape=[
            jax.ShapeDtypeStruct(kept.shape[1:], kind)
            for kind in (jnp.float32, jnp.bfloat16, jnp.bfloat16)
        ],
        compiler_params=pltpu.CompilerParams(vmem_limit_bytes=VMEM_LIMIT),
        name="part",
    )(kept, came)


def unpack_kernel(units_ref, out_ref):
    per = units_ref.shape[1]
    columns = out_ref.shape[2] // LANES
    for tap in range(TAPS):
        for column in range(columns):
            unit = tap * columns + column
            block = units_ref[unit // per, unit % per].astype(jnp.float32)
            out_ref[tap, :, column * LANES : (column + 1) * LANES] = block


def unpack(units, chans):
    return pl.pallas_call(
        unpack_kernel,
        out_shape=jax.ShapeDtypeStruct((TAPS, units.shape[2], chans), jnp.float32),
        compiler_params=pltpu.CompilerParams(vmem_limit_bytes=VMEM_LIMIT),
        name="unpack",
    )(units)


def swap_cores(blocks):
    return lax.ppermute(blocks, "core", [(0, 1), (1, 0)])


def body(volume, kernel, cotangent):
    rows = volume.shape[2]
    cells = volume.shape[3]
    chips = lax.axis_size(CHIPS)
    depths = lax.axis_size(DEP)
    near_pairs = [(i, i ^ 1) for i in range(depths)]
    far_pairs = [(i, (i + 1 if i % 2 else i - 1) % depths) for i in range(depths)]

    def index(name):
        return lax.axis_index(name).astype(jnp.int32).reshape(1)

    core, x_at, z_at, odd = index("core"), index("x"), index("zl"), index("zh") % 2
    own = volume.reshape(rows, cells)
    cot = cotangent.reshape(rows, cells)

    def copies(block):
        return jnp.broadcast_to(block[None], (chips, rows, cells))

    mine = lax.all_to_all(copies(own), CHIPS, 0, 0)
    k_rows = jnp.transpose(kernel.reshape(rows, TAPS, -1), (1, 0, 2)).reshape(TAPS * rows, -1)
    mine, k_rows, cot, core, odd, x_at, z_at = lax.optimization_barrier(
        (mine, k_rows, cot, core, odd, x_at, z_at)
    )
    other = swap_cores(mine)

    near, mid, far = conv(core, odd, k_rows, mine, other)
    near = lax.ppermute(near, DEP, near_pairs)
    far = lax.ppermute(far, DEP, far_pairs)
    activated, grad_pre = activate(mid, near, far, cot)

    near_grad = lax.ppermute(grad_pre, DEP, near_pairs)
    far_grad = lax.ppermute(grad_pre, DEP, far_pairs)
    own_units, own_stack, x = wgrad_own(core, grad_pre, mine, other)
    ys, zs = lax.axis_size("y"), lax.axis_size("zh")
    wide, halo_stack = wgrad_halo(odd, near_grad, far_grad, x, own_units, ys)
    scale = 1.0 / math.sqrt(UNIV * DEPTH * SIDE * SIDE)
    over_y = lax.all_to_all(wide, "y", 0, 0)

    keep, send = dgrad(core, x_at, z_at, k_rows, own_stack, halo_stack)
    here, after, before = part(keep, swap_cores(send))
    over_y, here = lax.optimization_barrier((over_y, here))
    over_z = lax.all_to_all(total_spread(over_y, 1.0, zs), "zh", 0, 0)
    after = lax.ppermute(after, "zl", [(i, (i + 1) % 3) for i in range(3)])
    before = lax.ppermute(before, "zl", [(i, (i + 2) % 3) for i in range(3)])
    total = here + after.astype(jnp.float32) + before.astype(jnp.float32)
    total = total.reshape(2, 2, rows, cells)
    over_z, _ = lax.optimization_barrier((over_z, total))
    units = lax.all_to_all(total_spread(over_z, scale, ys), "y", 0, 0)
    step = lax.ppermute(total[:, 1].astype(jnp.bfloat16), "x", [(i, i ^ 1) for i in range(4)])
    total = total[:, 0] + step.astype(jnp.float32)
    step = lax.ppermute(total[1].astype(jnp.bfloat16), "x", [(i, i ^ 2) for i in range(4)])
    grad_volume = (total[0] + step.astype(jnp.float32)).astype(jnp.bfloat16)
    all_taps = unpack(units, kernel.shape[-1])
    grad_kernel = jnp.transpose(all_taps, (1, 0, 2)).reshape(kernel.shape)
    return (activated.reshape(volume.shape), grad_volume.reshape(volume.shape), grad_kernel)


def solution(mesh):
    fine = Mesh(mesh.devices.reshape(8, 4, 4, 3, 2), ("y", "zh", "x", "zl", "core"))
    field = P(None, DEP, CHAN, None)
    weight = P(CHAN, None, None, None, None)
    return jax.shard_map(
        body,
        mesh=fine,
        in_specs=(field, weight, field),
        out_specs=(field, field, weight),
        check_vma=False,
    )
```

time: 120 us -> 122 us (1.017)
  the two profiles are of different devices: /device:TPU:2 before, /device:TPU:8 now
where the time goes in v6:
time: 122 us; the launch traced here: 121 us
  starting transfers between devices  70.4 us (58%)
  waiting for transfers between devices  40.2 us (33%)
  Pallas kernels  7.04 us (6%)
  local copies, waits for them, and re-layouts  1.57 us (1%)
    all_to_all x1, waiting for transfers between devices, body(): mine = lax.all_to_all(copies(own), CHIPS, 0, 0)  10.9 us
    ppermute x1, starting transfers between devices, body(): near = lax.ppermute(near, DEP, near_pairs)  10.3 us
    all_to_all x1, waiting for transfers between devices, body(): over_z = lax.all_to_all(total_spread(over_y, 1.0, zs), 'zh', 0, 0)  10.1 us
    all_to_all x1, starting transfers between devices, body(): over_y = lax.all_to_all(wide, 'y', 0, 0)  8.76 us
    ppermute x1, starting transfers between devices, body(): far_grad = lax.ppermute(grad_pre, DEP, far_pairs)  8.29 us
    all_to_all x1, starting transfers between devices, body(): mine = lax.all_to_all(copies(own), CHIPS, 0, 0)  8.08 us
    all_to_all x1, starting transfers between devices, body(): units = lax.all_to_all(total_spread(over_z, scale, ys), 'y', 0, 0)  7.21 us
    ppermute x1, starting transfers between devices, body(): far = lax.ppermute(far, DEP, far_pairs)  7.2 us
  transfers between devices with their start and end apart: 14, of which 9 were waited for; matrix products, arithmetic and copies ran while one was open for 1% of the time, Pallas kernels for 2%

profile of v6, /device:TPU:8, one launch (start us, length us, event | category | flops | bytes accessed | tf_op | source)
XLA Modules:
  0.0 120.7 jit_solution(9821042566304440001)
XLA Ops:
  0.6 1.5 %broadcast_in_dim.8 = bf16[12,16,1024]{2,1,0:T(8,128)(2,1)} broadcast(bf16[16,1024]{1,0:T(8,128)(2,1)} %bitcast.40), dimensions={1,2} | broadcast | bytes 425984 | tf_op jit(solution)/shard_map/broadcast_in_dim | solution.py:301
  2.2 0.0 copy-start
  2.2 8.1 %all-to-all-start = ((bf16[12,16,1024]{2,1,0:T(8,128)(2,1)}), bf16[12,16,1024]{2,1,0:T(8,128)(2,1)S(1)}, u32[]{:S(2)}, u32[]{:S(2)}) async-start(bf16[12,16,1024]{2,1,0:T(8,128)(2,1)} %broadcast_in_dim.8), calls=%async_computation | async-start | bytes 786432 | tf_op jit(solution)/shard_map/all_to_all | solution.py:303
  10.3 10.9 %all-to-all-done.mine_ref = bf16[12,16,1024]{2,1,0:T(8,128)(2,1)S(1)} async-done(((bf16[12,16,1024]{2,1,0:T(8,128)(2,1)}), bf16[12,16,1024]{2,1,0:T(8,128)(2,1)S(1)}, u32[]{:S(2)}, u32[]{:S(2)}) %all-to-all-start) | async-done | bytes 393248 | tf_op jit(solution)/shard_map/all_to_all | solution.py:303
  21.2 0.0 copy-start.1
  21.2 2.0 %collective-permute-start = (bf16[12,16,1024]{2,1,0:T(8,128)(2,1)S(1)}, bf16[12,16,1024]{2,1,0:T(8,128)(2,1)S(1)}, u32[]{:S(2)}, u32[]{:S(2)}) collective-permute-start(bf16[12,16,1024]{2,1,0:T(8,128)(2,1)S(1)} %all-to-all-done.mine_ref), channel_id=1, source_target_pairs={{0,1},{1,0},{2,3},{3,2},{4,5},{5,4},{6,7},{7,6},{8,9},{9,8},{10,11... | collective-permute-start | bytes 1179656 | tf_op jit(solution)/shard_map/ppermute | solution.py:282
  23.2 1.7 %collective-permute-done.other_ref = bf16[12,16,1024]{2,1,0:T(8,128)(2,1)S(1)} collective-permute-done((bf16[12,16,1024]{2,1,0:T(8,128)(2,1)S(1)}, bf16[12,16,1024]{2,1,0:T(8,128)(2,1)S(1)}, u32[]{:S(2)}, u32[]{:S(2)}) %collective-permute-start) | collective-permute-done | bytes 393248 | tf_op jit(solution)/shard_map/ppermute | solution.py:282
  24.9 0.0 copy-done
  24.9 0.9 conv.1
  25.8 10.3 %collective-permute-start.1 = (f32[16,1024]{1,0:T(8,128)S(1)}, f32[16,1024]{1,0:T(8,128)S(1)}, u32[]{:S(2)}, u32[]{:S(2)}) collective-permute-start(f32[16,1024]{1,0:T(8,128)S(1)} %get-tuple-element.33), channel_id=1, source_target_pairs={{0,24},{24,0},{48,72},{72,48},{96,120},{120,96},{144,168},{168,144... | collective-permute-start | bytes 196616 | tf_op jit(solution)/shard_map/ppermute | solution.py:311
  36.1 7.2 %collective-permute-start.2 = (f32[16,1024]{1,0:T(8,128)S(1)}, f32[16,1024]{1,0:T(8,128)S(1)}, u32[]{:S(2)}, u32[]{:S(2)}) collective-permute-start(f32[16,1024]{1,0:T(8,128)S(1)} %get-tuple-element.34), channel_id=1, source_target_pairs={{0,744},{24,48},{48,24},{72,96},{96,72},{120,144},{144,120},{168,1... | collective-permute-start | bytes 196616 | tf_op jit(solution)/shard_map/ppermute | solution.py:312
  43.4 0.0 collective-permute-done.1.low_ref
  43.4 3.4 %collective-permute-done.2.high_ref = f32[16,1024]{1,0:T(8,128)S(1)} collective-permute-done((f32[16,1024]{1,0:T(8,128)S(1)}, f32[16,1024]{1,0:T(8,128)S(1)}, u32[]{:S(2)}, u32[]{:S(2)}) %collective-permute-start.2) | collective-permute-done | bytes 65568 | tf_op jit(solution)/shard_map/ppermute | solution.py:312
  46.8 0.0 copy-done.1
  46.8 0.6 activate.1
  47.4 8.3 %collective-permute-start.4 = (bf16[16,1024]{1,0:T(8,128)(2,1)S(1)}, bf16[16,1024]{1,0:T(8,128)(2,1)S(1)}, u32[]{:S(2)}, u32[]{:S(2)}) collective-permute-start(bf16[16,1024]{1,0:T(8,128)(2,1)S(1)} %get-tuple-element.37.own_ref), channel_id=1, source_target_pairs={{0,744},{24,48},{48,24},{72,96},{96,72},{120,144},{144,120},{168,1... | collective-permute-start | bytes 98312 | tf_op jit(solution)/shard_map/ppermute | solution.py:316
  55.7 1.9 %collective-permute-start.3 = (bf16[16,1024]{1,0:T(8,128)(2,1)S(1)}, bf16[16,1024]{1,0:T(8,128)(2,1)S(1)}, u32[]{:S(2)}, u32[]{:S(2)}) collective-permute-start(bf16[16,1024]{1,0:T(8,128)(2,1)S(1)} %get-tuple-element.37.own_ref), channel_id=1, source_target_pairs={{0,24},{24,0},{48,72},{72,48},{96,120},{120,96},{144,168},{168,144... | collective-permute-start | bytes 98312 | tf_op jit(solution)/shard_map/ppermute | solution.py:315
  57.6 0.6 wgrad_own.1
  58.2 0.0 collective-permute-done.4.far_ref
  58.2 5.4 %collective-permute-done.3.near_ref = bf16[16,1024]{1,0:T(8,128)(2,1)S(1)} collective-permute-done((bf16[16,1024]{1,0:T(8,128)(2,1)S(1)}, bf16[16,1024]{1,0:T(8,128)(2,1)S(1)}, u32[]{:S(2)}, u32[]{:S(2)}) %collective-permute-start.3) | collective-permute-done | bytes 32800 | tf_op jit(solution)/shard_map/ppermute | solution.py:315
  63.6 1.7 %wgrad_halo.1 = (bf16[8,11,16,128]{3,2,1,0:T(8,128)(2,1)}, bf16[288,1024]{1,0:T(8,128)(2,1)S(1)}) custom-call(s32[1]{0:T(128)S(6)} %select_n.7.odd_ref, bf16[16,1024]{1,0:T(8,128)(2,1)S(1)} %collective-permute-done.3.near_ref, bf16[16,1024]{1,0:T(8,128)(2,1)S(1)} %collective-permute-done.4.far_ref, bf16[12,2,16,1024]{3,2,1,0:T(8,128)(2,1)S(1)} %get-tuple-element.38.x_ref, ...), custom_call_target="tpu_custom_call" | custom-call | tf_op jit(solution)/shard_map/wgrad_halo/pallas_call | solution.py:163
  65.3 8.8 %all-to-all-start.1 = ((bf16[8,11,16,128]{3,2,1,0:T(8,128)(2,1)}), bf16[8,11,16,128]{3,2,1,0:T(8,128)(2,1)S(1)}, u32[]{:S(2)}, u32[]{:S(2)}) async-start(bf16[8,11,16,128]{3,2,1,0:T(8,128)(2,1)} %get-tuple-element.40), calls=%async_computation.1 | async-start | bytes 720896 | tf_op jit(solution)/shard_map/all_to_all | solution.py:321
  74.0 0.8 dgrad.1
  74.8 1.9 %collective-permute-start.5 = (bf16[3,4,16,1024]{3,2,1,0:T(8,128)(2,1)S(1)}, bf16[3,4,16,1024]{3,2,1,0:T(8,128)(2,1)S(1)}, u32[]{:S(2)}, u32[]{:S(2)}) collective-permute-start(bf16[3,4,16,1024]{3,2,1,0:T(8,128)(2,1)S(1)} %get-tuple-element.46), channel_id=1, source_target_pairs={{0,1},{1,0},{2,3},{3,2},{4,5},{5,4},{6,7},{7,6},{8,9},{9,8},{10,11... | collective-permute-start | bytes 1179656 | tf_op jit(solution)/shard_map/ppermute | solution.py:282
  76.8 1.7 %collective-permute-done.5.came_ref = bf16[3,4,16,1024]{3,2,1,0:T(8,128)(2,1)S(1)} collective-permute-done((bf16[3,4,16,1024]{3,2,1,0:T(8,128)(2,1)S(1)}, bf16[3,4,16,1024]{3,2,1,0:T(8,128)(2,1)S(1)}, u32[]{:S(2)}, u32[]{:S(2)}) %collective-permute-start.5) | collective-permute-done | bytes 393248 | tf_op jit(solution)/shard_map/ppermute | solution.py:282
  78.5 0.1 part.1
  78.5 2.2 %collective-permute-start.6 = (bf16[4,16,1024]{2,1,0:T(8,128)(2,1)S(1)}, bf16[4,16,1024]{2,1,0:T(8,128)(2,1)S(1)}, u32[]{:S(2)}, u32[]{:S(2)}) collective-permute-start(bf16[4,16,1024]{2,1,0:T(8,128)(2,1)S(1)} %get-tuple-element.49), channel_id=1, source_target_pairs={{0,2},{2,4},{4,0},{1,3},{3,5},{5,1},{6,8},{8,10},{10,6},{7,9},{9,1... | collective-permute-start | bytes 393224 | tf_op jit(solution)/shard_map/ppermute | solution.py:327
  80.7 4.6 %collective-permute-start.7 = (bf16[4,16,1024]{2,1,0:T(8,128)(2,1)S(1)}, bf16[4,16,1024]{2,1,0:T(8,128)(2,1)S(1)}, u32[]{:S(2)}, u32[]{:S(2)}) collective-permute-start(bf16[4,16,1024]{2,1,0:T(8,128)(2,1)S(1)} %get-tuple-element.50), channel_id=1, source_target_pairs={{0,4},{2,0},{4,2},{1,5},{3,1},{5,3},{6,10},{8,6},{10,8},{7,11},{9,... | collective-permute-start | bytes 393224 | tf_op jit(solution)/shard_map/ppermute | solution.py:328
  85.3 0.0 all-to-all-done.1.terms_ref
  85.3 0.7 total.2
  86.0 3.4 %all-to-all-start.2 = ((bf16[4,11,16,128]{3,2,1,0:T(8,128)(2,1)}), bf16[4,11,16,128]{3,2,1,0:T(8,128)(2,1)S(1)}, u32[]{:S(2)}, u32[]{:S(2)}) async-start(bf16[4,11,16,128]{3,2,1,0:T(8,128)(2,1)} %total.2), calls=%async_computation.2 | async-start | bytes 360448 | tf_op jit(solution)/shard_map/all_to_all | solution.py:326
  89.4 0.0 collective-permute-done.6
  89.4 0.4 collective-permute-done.7
  89.8 1.9 %collective-permute-start.8 = (bf16[2,16,1024]{2,1,0:T(8,128)(2,1)S(1)}, bf16[2,16,1024]{2,1,0:T(8,128)(2,1)S(1)}, u32[]{:S(2)}, u32[]{:S(2)}) collective-permute-start(bf16[2,16,1024]{2,1,0:T(8,128)(2,1)S(1)} %fusion.1), channel_id=1, source_target_pairs={{0,6},{6,0},{12,18},{18,12},{1,7},{7,1},{13,19},{19,13},{2,8},{8,2... | collective-permute-start | bytes 196616 | tf_op jit(solution)/shard_map/ppermute | solution.py:333
  91.8 10.1 %all-to-all-done.2.terms_ref = bf16[4,11,16,128]{3,2,1,0:T(8,128)(2,1)S(1)} async-done(((bf16[4,11,16,128]{3,2,1,0:T(8,128)(2,1)}), bf16[4,11,16,128]{3,2,1,0:T(8,128)(2,1)S(1)}, u32[]{:S(2)}, u32[]{:S(2)}) %all-to-all-start.2) | async-done | bytes 180256 | tf_op jit(solution)/shard_map/all_to_all | solution.py:326
  101.8 0.8 total.3
  102.6 7.2 %all-to-all-start.3 = ((bf16[8,11,16,128]{3,2,1,0:T(8,128)(2,1)}), bf16[8,11,16,128]{3,2,1,0:T(8,128)(2,1)S(1)}, u32[]{:S(2)}, u32[]{:S(2)}) async-start(bf16[8,11,16,128]{3,2,1,0:T(8,128)(2,1)} %total.3), calls=%async_computation.3 | async-start | bytes 720896 | tf_op jit(solution)/shard_map/all_to_all | solution.py:332
  109.8 0.0 collective-permute-done.8
  109.8 2.6 %collective-permute-start.9 = (bf16[16,1024]{1,0:T(8,128)(2,1)S(1)}, bf16[16,1024]{1,0:T(8,128)(2,1)S(1)}, u32[]{:S(2)}, u32[]{:S(2)}) collective-permute-start(bf16[16,1024]{1,0:T(8,128)(2,1)S(1)} %fusion.5), channel_id=1, source_target_pairs={{0,12},{6,18},{12,0},{18,6},{1,13},{7,19},{13,1},{19,7},{2,14},{8,... | collective-permute-start | bytes 98312 | tf_op jit(solution)/shard_map/ppermute | solution.py:335
  112.4 4.7 %collective-permute-done.9 = bf16[16,1024]{1,0:T(8,128)(2,1)S(1)} collective-permute-done((bf16[16,1024]{1,0:T(8,128)(2,1)S(1)}, bf16[16,1024]{1,0:T(8,128)(2,1)S(1)}, u32[]{:S(2)}, u32[]{:S(2)}) %collective-permute-start.9) | collective-permute-done | bytes 32800 | tf_op jit(solution)/shard_map/ppermute | solution.py:335
  117.2 0.6 fusion.4
  117.8 2.0 %all-to-all-done.3.units_ref = bf16[8,11,16,128]{3,2,1,0:T(8,128)(2,1)S(1)} async-done(((bf16[8,11,16,128]{3,2,1,0:T(8,128)(2,1)}), bf16[8,11,16,128]{3,2,1,0:T(8,128)(2,1)S(1)}, u32[]{:S(2)}, u32[]{:S(2)}) %all-to-all-start.3) | async-done | bytes 360480 | tf_op jit(solution)/shard_map/all_to_all | solution.py:332
  119.8 0.9 unpack.1
  (4 shorter events, 0.1 us)
Async XLA Ops:
  2.2 22.7 %copy-start = (bf16[16,3,3,3,384]{4,0,3,2,1:T(8,128)(2,1)S(1)}, bf16[16,3,3,3,384]{4,0,3,2,1:T(8,128)(2,1)}, u32[]{:S(2)}) copy-start(bf16[16,3,3,3,384]{4,0,3,2,1:T(8,128)(2,1)} %param.4) | copy-start | bytes 995332
  2.2 19.0 %all-to-all-start = ((bf16[12,16,1024]{2,1,0:T(8,128)(2,1)}), bf16[12,16,1024]{2,1,0:T(8,128)(2,1)S(1)}, u32[]{:S(2)}, u32[]{:S(2)}) async-start(bf16[12,16,1024]{2,1,0:T(8,128)(2,1)} %broadcast_in_dim.8), calls=%async_computation | async-start | bytes 786432 | tf_op jit(solution)/shard_map/all_to_all | solution.py:303
  21.2 25.6 %copy-start.1 = (bf16[1,1,16,1024]{3,2,1,0:T(8,128)(2,1)S(1)}, bf16[1,1,16,1024]{3,2,1,0:T(8,128)(2,1)}, u32[]{:S(2)}) copy-start(bf16[1,1,16,1024]{3,2,1,0:T(8,128)(2,1)} %param.5) | copy-start | bytes 98308
  21.2 3.7 %collective-permute-start = (bf16[12,16,1024]{2,1,0:T(8,128)(2,1)S(1)}, bf16[12,16,1024]{2,1,0:T(8,128)(2,1)S(1)}, u32[]{:S(2)}, u32[]{:S(2)}) collective-permute-start(bf16[12,16,1024]{2,1,0:T(8,128)(2,1)S(1)} %all-to-all-done.mine_ref), channel_id=1, source_target_pairs={{0,1},{1,0},{2,3},{3,2},{4,5},{5,4},{6,7},{7,6},{8,9},{9,8},{10,11... | collective-permute-start | bytes 1179656 | tf_op jit(solution)/shard_map/ppermute | solution.py:282
  25.8 17.5 %collective-permute-start.1 = (f32[16,1024]{1,0:T(8,128)S(1)}, f32[16,1024]{1,0:T(8,128)S(1)}, u32[]{:S(2)}, u32[]{:S(2)}) collective-permute-start(f32[16,1024]{1,0:T(8,128)S(1)} %get-tuple-element.33), channel_id=1, source_target_pairs={{0,24},{24,0},{48,72},{72,48},{96,120},{120,96},{144,168},{168,144... | collective-permute-start | bytes 196616 | tf_op jit(solution)/shard_map/ppermute | solution.py:311
  36.1 10.6 %collective-permute-start.2 = (f32[16,1024]{1,0:T(8,128)S(1)}, f32[16,1024]{1,0:T(8,128)S(1)}, u32[]{:S(2)}, u32[]{:S(2)}) collective-permute-start(f32[16,1024]{1,0:T(8,128)S(1)} %get-tuple-element.34), channel_id=1, source_target_pairs={{0,744},{24,48},{48,24},{72,96},{96,72},{120,144},{144,120},{168,1... | collective-permute-start | bytes 196616 | tf_op jit(solution)/shard_map/ppermute | solution.py:312
  47.4 10.8 %collective-permute-start.4 = (bf16[16,1024]{1,0:T(8,128)(2,1)S(1)}, bf16[16,1024]{1,0:T(8,128)(2,1)S(1)}, u32[]{:S(2)}, u32[]{:S(2)}) collective-permute-start(bf16[16,1024]{1,0:T(8,128)(2,1)S(1)} %get-tuple-element.37.own_ref), channel_id=1, source_target_pairs={{0,744},{24,48},{48,24},{72,96},{96,72},{120,144},{144,120},{168,1... | collective-permute-start | bytes 98312 | tf_op jit(solution)/shard_map/ppermute | solution.py:316
  55.7 7.9 %collective-permute-start.3 = (bf16[16,1024]{1,0:T(8,128)(2,1)S(1)}, bf16[16,1024]{1,0:T(8,128)(2,1)S(1)}, u32[]{:S(2)}, u32[]{:S(2)}) collective-permute-start(bf16[16,1024]{1,0:T(8,128)(2,1)S(1)} %get-tuple-element.37.own_ref), channel_id=1, source_target_pairs={{0,24},{24,0},{48,72},{72,48},{96,120},{120,96},{144,168},{168,144... | collective-permute-start | bytes 98312 | tf_op jit(solution)/shard_map/ppermute | solution.py:315
  65.3 20.0 %all-to-all-start.1 = ((bf16[8,11,16,128]{3,2,1,0:T(8,128)(2,1)}), bf16[8,11,16,128]{3,2,1,0:T(8,128)(2,1)S(1)}, u32[]{:S(2)}, u32[]{:S(2)}) async-start(bf16[8,11,16,128]{3,2,1,0:T(8,128)(2,1)} %get-tuple-element.40), calls=%async_computation.1 | async-start | bytes 720896 | tf_op jit(solution)/shard_map/all_to_all | solution.py:321
  74.8 3.6 %collective-permute-start.5 = (bf16[3,4,16,1024]{3,2,1,0:T(8,128)(2,1)S(1)}, bf16[3,4,16,1024]{3,2,1,0:T(8,128)(2,1)S(1)}, u32[]{:S(2)}, u32[]{:S(2)}) collective-permute-start(bf16[3,4,16,1024]{3,2,1,0:T(8,128)(2,1)S(1)} %get-tuple-element.46), channel_id=1, source_target_pairs={{0,1},{1,0},{2,3},{3,2},{4,5},{5,4},{6,7},{7,6},{8,9},{9,8},{10,11... | collective-permute-start | bytes 1179656 | tf_op jit(solution)/shard_map/ppermute | solution.py:282
  78.5 10.9 %collective-permute-start.6 = (bf16[4,16,1024]{2,1,0:T(8,128)(2,1)S(1)}, bf16[4,16,1024]{2,1,0:T(8,128)(2,1)S(1)}, u32[]{:S(2)}, u32[]{:S(2)}) collective-permute-start(bf16[4,16,1024]{2,1,0:T(8,128)(2,1)S(1)} %get-tuple-element.49), channel_id=1, source_target_pairs={{0,2},{2,4},{4,0},{1,3},{3,5},{5,1},{6,8},{8,10},{10,6},{7,9},{9,1... | collective-permute-start | bytes 393224 | tf_op jit(solution)/shard_map/ppermute | solution.py:327
  80.7 9.1 %collective-permute-start.7 = (bf16[4,16,1024]{2,1,0:T(8,128)(2,1)S(1)}, bf16[4,16,1024]{2,1,0:T(8,128)(2,1)S(1)}, u32[]{:S(2)}, u32[]{:S(2)}) collective-permute-start(bf16[4,16,1024]{2,1,0:T(8,128)(2,1)S(1)} %get-tuple-element.50), channel_id=1, source_target_pairs={{0,4},{2,0},{4,2},{1,5},{3,1},{5,3},{6,10},{8,6},{10,8},{7,11},{9,... | collective-permute-start | bytes 393224 | tf_op jit(solution)/shard_map/ppermute | solution.py:328
  86.0 15.8 %all-to-all-start.2 = ((bf16[4,11,16,128]{3,2,1,0:T(8,128)(2,1)}), bf16[4,11,16,128]{3,2,1,0:T(8,128)(2,1)S(1)}, u32[]{:S(2)}, u32[]{:S(2)}) async-start(bf16[4,11,16,128]{3,2,1,0:T(8,128)(2,1)} %total.2), calls=%async_computation.2 | async-start | bytes 360448 | tf_op jit(solution)/shard_map/all_to_all | solution.py:326
  89.8 20.0 %collective-permute-start.8 = (bf16[2,16,1024]{2,1,0:T(8,128)(2,1)S(1)}, bf16[2,16,1024]{2,1,0:T(8,128)(2,1)S(1)}, u32[]{:S(2)}, u32[]{:S(2)}) collective-permute-start(bf16[2,16,1024]{2,1,0:T(8,128)(2,1)S(1)} %fusion.1), channel_id=1, source_target_pairs={{0,6},{6,0},{12,18},{18,12},{1,7},{7,1},{13,19},{19,13},{2,8},{8,2... | collective-permute-start | bytes 196616 | tf_op jit(solution)/shard_map/ppermute | solution.py:333
  102.6 17.2 %all-to-all-start.3 = ((bf16[8,11,16,128]{3,2,1,0:T(8,128)(2,1)}), bf16[8,11,16,128]{3,2,1,0:T(8,128)(2,1)S(1)}, u32[]{:S(2)}, u32[]{:S(2)}) async-start(bf16[8,11,16,128]{3,2,1,0:T(8,128)(2,1)} %total.3), calls=%async_computation.3 | async-start | bytes 720896 | tf_op jit(solution)/shard_map/all_to_all | solution.py:332
  109.8 7.3 %collective-permute-start.9 = (bf16[16,1024]{1,0:T(8,128)(2,1)S(1)}, bf16[16,1024]{1,0:T(8,128)(2,1)S(1)}, u32[]{:S(2)}, u32[]{:S(2)}) collective-permute-start(bf16[16,1024]{1,0:T(8,128)(2,1)S(1)} %fusion.5), channel_id=1, source_target_pairs={{0,12},{6,18},{12,0},{18,6},{1,13},{7,19},{13,1},{19,7},{2,14},{8,... | collective-permute-start | bytes 98312 | tf_op jit(solution)/shard_map/ppermute | solution.py:335

commit v7 on v6

--- a/solution.py
+++ b/solution.py
@@ -41,10 +41,11 @@
     return x_ref[...].reshape(-1, x_ref.shape[-1])
 
 
-def conv_kernel(core_ref, odd_ref, w_ref, mine_ref, other_ref, near_ref, mid_ref, far_ref, x_ref):
-    rows = mid_ref.shape[0]
+def conv_kernel(
+    core_ref, w_ref, mine_ref, other_ref, own_ref, next_ref, prev_ref, next2_ref, prev2_ref, x_ref
+):
+    rows = next2_ref.shape[0]
     x = merge_cores(core_ref, mine_ref, other_ref, x_ref)
-    sums = []
     for depth_tap in range(3):
         w = w_ref[depth_tap * 9 * rows : (depth_tap + 1) * 9 * rows, :]
         product = jnp.dot(w, x, preferred_element_type=jnp.float32)
@@ -57,12 +58,16 @@
                 part = term if part is None else part + term
             part = shift_cells(part, 0, 1 - col_tap)
             total = part if total is None else total + part
-        sums.append(total)
-    up, mid, down = sums
-    odd = odd_ref[0] == 1
-    near_ref[...] = jnp.where(odd, down, up)
-    mid_ref[...] = mid
-    far_ref[...] = jnp.where(odd, up, down)
+        own_ref[depth_tap] = total
+        narrow = total.astype(jnp.bfloat16)
+        if depth_tap < 2:
+            next_ref[depth_tap] = narrow
+        if depth_tap > 0:
+            prev_ref[depth_tap - 1] = narrow
+        if depth_tap == 0:
+            next2_ref[...] = narrow
+        if depth_tap == 2:
+            prev2_ref[...] = narrow
 
 
 def specs(scalars, arrays):
@@ -70,21 +75,24 @@
     return [smem] * scalars + [pl.BlockSpec(memory_space=pltpu.VMEM)] * arrays
 
 
-def merged_scratch(mine):
-    return [pltpu.VMEM((mine.shape[0], 2) + mine.shape[1:], mine.dtype)]
-
-
-def conv(core, odd, weights, mine, other):
+def conv(core, weights, mine, other):
     rows = weights.shape[0] // TAPS
     cells = mine.shape[-1]
+    one, two = (rows, cells), (2, rows, cells)
     return pl.pallas_call(
         conv_kernel,
-        out_shape=[jax.ShapeDtypeStruct((rows, cells), jnp.float32)] * 3,
-        in_specs=specs(2, 3),
-        scratch_shapes=merged_scratch(mine),
+        out_shape=[
+            jax.ShapeDtypeStruct((3, rows, cells), jnp.float32),
+            jax.ShapeDtypeStruct(two, jnp.bfloat16),
+            jax.ShapeDtypeStruct(two, jnp.bfloat16),
+            jax.ShapeDtypeStruct(one, jnp.bfloat16),
+            jax.ShapeDtypeStruct(one, jnp.bfloat16),
+            jax.ShapeDtypeStruct((mine.shape[0], 2) + mine.shape[1:], mine.dtype),
+        ],
+        in_specs=specs(1, 3),
         compiler_params=pltpu.CompilerParams(vmem_limit_bytes=VMEM_LIMIT),
         name="conv",
-    )(core, odd, weights, mine, other)
+    )(core, weights, mine, other)
 
 
 def stack_plane(plane, stack_ref, at):
@@ -105,85 +113,58 @@
     ).astype(jnp.bfloat16)
 
 
-def own_kernel(core_ref, own_ref, mine_ref, other_ref, units_ref, stack_ref, x_ref):
-    rows = own_ref.shape[0]
-    x = merge_cores(core_ref, mine_ref, other_ref, x_ref)
-    columns = x.shape[0] // LANES
-    stack_plane(own_ref[...], stack_ref, 0)
-    grad = cross(stack_ref[...], x)
-    for unit in range(9 * columns):
-        tap, column = divmod(unit, columns)
-        units_ref[unit] = grad[
-            tap * rows : (tap + 1) * rows, column * LANES : (column + 1) * LANES
-        ]
-
-
-def wgrad_own(core, own, mine, other):
-    rows, cells = own.shape
-    chans = 2 * mine.shape[0] * mine.shape[1]
-    return pl.pallas_call(
-        own_kernel,
-        out_shape=[
-            jax.ShapeDtypeStruct((9 * chans // LANES, rows, LANES), jnp.bfloat16),
-            jax.ShapeDtypeStruct((9 * rows, cells), jnp.bfloat16),
-            jax.ShapeDtypeStruct((mine.shape[0], 2) + mine.shape[1:], mine.dtype),
-        ],
-        in_specs=specs(1, 3),
-        compiler_params=pltpu.CompilerParams(vmem_limit_bytes=VMEM_LIMIT),
-        name="wgrad_own",
-    )(core, own, mine, other)
-
-
-def halo_kernel(odd_ref, near_ref, far_ref, x_ref, units_ref, wide_ref, stack_ref):
-    rows = near_ref.shape[0]
+def grads_kernel(
+    own_ref, prev_ref, next_ref, prev2_ref, next2_ref, cot_ref, cot_prev_ref, cot_next_ref, x_ref,
+    act_ref, wide_ref, stack_ref,
+):
+    rows = act_ref.shape[0]
     slots, per = wide_ref.shape[:2]
     x = x_ref[...].reshape(-1, x_ref.shape[-1])
     columns = x.shape[0] // LANES
-    odd = odd_ref[0] == 1
-    near, far = near_ref[...].astype(jnp.float32), far_ref[...].astype(jnp.float32)
-    for half, plane in enumerate((jnp.where(odd, far, near), jnp.where(odd, near, far))):
-        stack_plane(plane, stack_ref, half * 9 * rows)
-        grad = cross(stack_ref[half * 9 * rows : (half + 1) * 9 * rows, :], x)
-        for at in range(9 * columns):
-            tap, column = divmod(at, columns)
-            unit = 18 * half * columns + at
+    f32 = jnp.float32
+    above = own_ref[0] + next_ref[0].astype(f32) + next2_ref[...].astype(f32)
+    here = own_ref[1] + prev_ref[0].astype(f32) + next_ref[1].astype(f32)
+    below = own_ref[2] + prev_ref[1].astype(f32) + prev2_ref[...].astype(f32)
+    planes = ((above, cot_next_ref), (here, cot_ref), (below, cot_prev_ref))
+    for depth_tap, (preact, cotangent_ref) in enumerate(planes):
+        sig = jax.nn.sigmoid(preact)
+        if depth_tap == 1:
+            act_ref[...] = (preact * sig).astype(jnp.bfloat16)
+        cot = cotangent_ref[...].astype(f32)
+        grad_pre = (cot * sig * (1.0 + preact * (1.0 - sig))).astype(jnp.bfloat16)
+        at = depth_tap * 9 * rows
+        stack_plane(grad_pre, stack_ref, at)
+        grad = cross(stack_ref[at : at + 9 * rows, :], x)
+        for index in range(9 * columns):
+            tap, column = divmod(index, columns)
+            unit = depth_tap * 9 * columns + index
             wide_ref[unit // per, unit % per] = grad[
                 tap * rows : (tap + 1) * rows, column * LANES : (column + 1) * LANES
             ]
-    for at in range(9 * columns):
-        unit = 9 * columns + at
-        wide_ref[unit // per, unit % per] = units_ref[at]
     for unit in range(TAPS * columns, slots * per):
         wide_ref[unit // per, unit % per] = jnp.zeros((rows, LANES), jnp.bfloat16)
 
 
-def wgrad_halo(odd, near, far, x, units, slots):
-    rows, cells = near.shape
-    per = -(-3 * units.shape[0] // slots)
-    return pl.pallas_call(
-        halo_kernel,
+def grads(sums, cots, x, slots):
+    rows, cells = cots[0].shape
+    per = -(-TAPS * 2 * x.shape[0] * rows // (LANES * slots))
+    return pl.pallas_call(
+        grads_kernel,
         out_shape=[
+            jax.ShapeDtypeStruct((rows, cells), jnp.bfloat16),
             jax.ShapeDtypeStruct((slots, per, rows, LANES), jnp.bfloat16),
-            jax.ShapeDtypeStruct((18 * rows, cells), jnp.bfloat16),
+            jax.ShapeDtypeStruct((TAPS * rows, cells), jnp.bfloat16),
         ],
-        in_specs=specs(1, 4),
-        compiler_params=pltpu.CompilerParams(vmem_limit_bytes=VMEM_LIMIT),
-        name="wgrad_halo",
-    )(odd, near, far, x, units)
-
-
-def dgrad_kernel(core_ref, x_at_ref, z_at_ref, k_ref, own_ref, halo_ref, keep_ref, send_ref):
+        compiler_params=pltpu.CompilerParams(vmem_limit_bytes=VMEM_LIMIT),
+        name="grads",
+    )(*sums, *cots, x)
+
+
+def dgrad_kernel(core_ref, x_at_ref, z_at_ref, k_ref, stack_ref, keep_ref, send_ref):
     rows = keep_ref.shape[2]
-    n = 9 * rows
-    partial = None
-    for at, stack in ((0, halo_ref[:n, :]), (n, own_ref[...]), (2 * n, halo_ref[n:, :])):
-        term = lax.dot_general(
-            k_ref[at : at + n, :],
-            stack,
-            (((0,), (0,)), ((), ())),
-            preferred_element_type=jnp.float32,
-        )
-        partial = term if partial is None else partial + term
+    partial = lax.dot_general(
+        k_ref[...], stack_ref[...], (((0,), (0,)), ((), ())), preferred_element_type=jnp.float32
+    )
     first = core_ref[0] == 0
     for x_at in range(4):
         for z_at in range(3):
@@ -195,36 +176,18 @@
             send_ref[z_slot, x_slot] = jnp.where(first, odd, even).astype(jnp.bfloat16)
 
 
-def dgrad(core, x_at, z_at, k_rows, own, halo):
-    shape = (3, 4, k_rows.shape[0] // TAPS, own.shape[1])
+def dgrad(core, x_at, z_at, k_rows, stack):
+    shape = (3, 4, k_rows.shape[0] // TAPS, stack.shape[1])
     return pl.pallas_call(
         dgrad_kernel,
         out_shape=[
             jax.ShapeDtypeStruct(shape, jnp.float32),
             jax.ShapeDtypeStruct(shape, jnp.bfloat16),
         ],
-        in_specs=specs(3, 3),
+        in_specs=specs(3, 2),
         compiler_params=pltpu.CompilerParams(vmem_limit_bytes=VMEM_LIMIT),
         name="dgrad",
-    )(core, x_at, z_at, k_rows, own, halo)
-
-
-def act_kernel(mid_ref, low_ref, high_ref, cot_ref, act_ref, grad_ref):
-    preact = mid_ref[...] + low_ref[...] + high_ref[...]
-    sig = jax.nn.sigmoid(preact)
-    act_ref[...] = (preact * sig).astype(jnp.bfloat16)
-    cot = cot_ref[...].astype(jnp.float32)
-    grad_ref[...] = (cot * sig * (1.0 + preact * (1.0 - sig))).astype(jnp.bfloat16)
-
-
-def activate(mid, low, high, cot):
-    shape = jax.ShapeDtypeStruct(mid.shape, jnp.bfloat16)
-    return pl.pallas_call(
-        act_kernel,
-        out_shape=[shape, shape],
-        compiler_params=pltpu.CompilerParams(vmem_limit_bytes=VMEM_LIMIT),
-        name="activate",
-    )(mid, low, high, cot)
+    )(core, x_at, z_at, k_rows, stack)
 
 
 def total_kernel(terms_ref, out_ref, *, scale):
@@ -287,13 +250,14 @@
     cells = volume.shape[3]
     chips = lax.axis_size(CHIPS)
     depths = lax.axis_size(DEP)
-    near_pairs = [(i, i ^ 1) for i in range(depths)]
-    far_pairs = [(i, (i + 1 if i % 2 else i - 1) % depths) for i in range(depths)]
+
+    def shift(block, step):
+        return lax.ppermute(block, DEP, [(i, (i + step) % depths) for i in range(depths)])
 
     def index(name):
         return lax.axis_index(name).astype(jnp.int32).reshape(1)
 
-    core, x_at, z_at, odd = index("core"), index("x"), index("zl"), index("zh") % 2
+    core, x_at, z_at = index("core"), index("x"), index("zl")
     own = volume.reshape(rows, cells)
     cot = cotangent.reshape(rows, cells)
 
@@ -302,25 +266,20 @@
 
     mine = lax.all_to_all(copies(own), CHIPS, 0, 0)
     k_rows = jnp.transpose(kernel.reshape(rows, TAPS, -1), (1, 0, 2)).reshape(TAPS * rows, -1)
-    mine, k_rows, cot, core, odd, x_at, z_at = lax.optimization_barrier(
-        (mine, k_rows, cot, core, odd, x_at, z_at)
+    cot_next, cot_prev = shift(cot, -1), shift(cot, 1)
+    mine, k_rows, cot, cot_next, cot_prev, core, x_at, z_at = lax.optimization_barrier(
+        (mine, k_rows, cot, cot_next, cot_prev, core, x_at, z_at)
     )
     other = swap_cores(mine)
 
-    near, mid, far = conv(core, odd, k_rows, mine, other)
-    near = lax.ppermute(near, DEP, near_pairs)
-    far = lax.ppermute(far, DEP, far_pairs)
-    activated, grad_pre = activate(mid, near, far, cot)
-
-    near_grad = lax.ppermute(grad_pre, DEP, near_pairs)
-    far_grad = lax.ppermute(grad_pre, DEP, far_pairs)
-    own_units, own_stack, x = wgrad_own(core, grad_pre, mine, other)
+    sums, to_next, to_prev, to_next2, to_prev2, x = conv(core, k_rows, mine, other)
+    sums = (sums, shift(to_next, 1), shift(to_prev, -1), shift(to_next2, 2), shift(to_prev2, -2))
     ys, zs = lax.axis_size("y"), lax.axis_size("zh")
-    wide, halo_stack = wgrad_halo(odd, near_grad, far_grad, x, own_units, ys)
+    activated, wide, stack = grads(sums, (cot, cot_prev, cot_next), x, ys)
     scale = 1.0 / math.sqrt(UNIV * DEPTH * SIDE * SIDE)
     over_y = lax.all_to_all(wide, "y", 0, 0)
 
-    keep, send = dgrad(core, x_at, z_at, k_rows, own_stack, halo_stack)
+    keep, send = dgrad(core, x_at, z_at, k_rows, stack)
     here, after, before = part(keep, swap_cores(send))
     over_y, here = lax.optimization_barrier((over_y, here))
     over_z = lax.all_to_all(total_spread(over_y, 1.0, zs), "zh", 0, 0)

time: 122 us -> 127 us (1.041)
  the two profiles are of different devices: /device:TPU:8 before, /device:TPU:2 now
where the time goes in v7:
time: 127 us; the launch traced here: 126 us
  starting transfers between devices  89.3 us (70%)
  waiting for transfers between devices  27.9 us (22%)
  Pallas kernels  6.02 us (5%)
  local copies, waits for them, and re-layouts  1.57 us (1%)
    ppermute x6, starting transfers between devices, shift(): lax.ppermute(block, DEP, [(i, (i + step) % depths) for i in range(depths)])  38.3 us
    all_to_all x1, starting transfers between devices, body(): mine = lax.all_to_all(copies(own), CHIPS, 0, 0)  13.1 us
    all_to_all x1, waiting for transfers between devices, body(): over_z = lax.all_to_all(total_spread(over_y, 1.0, zs), 'zh', 0, 0)  10.2 us
    all_to_all x1, starting transfers between devices, body(): units = lax.all_to_all(total_spread(over_z, scale, ys), 'y', 0, 0)  7.63 us
    all_to_all x1, starting transfers between devices, body(): over_y = lax.all_to_all(wide, 'y', 0, 0)  6.96 us
    all_to_all x1, starting transfers between devices, body(): over_z = lax.all_to_all(total_spread(over_y, 1.0, zs), 'zh', 0, 0)  6.33 us
    ppermute x6, waiting for transfers between devices, shift(): lax.ppermute(block, DEP, [(i, (i + step) % depths) for i in range(depths)])  6.23 us
    ppermute x1, starting transfers between devices, body(): before = lax.ppermute(before, 'zl', [(i, (i + 2) % 3) for i in range(3)])  4.82 us
  transfers between devices with their start and end apart: 16, of which 8 were waited for; matrix products, arithmetic and copies ran while one was open for 1% of the time, Pallas kernels for 2%

profile of v7, /device:TPU:2, one launch (start us, length us, event | category | flops | bytes accessed | tf_op | source)
XLA Modules:
  0.0 126.4 jit_solution(17544586105458719444)
XLA Ops:
  0.6 1.5 %broadcast_in_dim.8 = bf16[12,16,1024]{2,1,0:T(8,128)(2,1)} broadcast(bf16[16,1024]{1,0:T(8,128)(2,1)} %bitcast.41), dimensions={1,2} | broadcast | bytes 425984 | tf_op jit(solution)/shard_map/broadcast_in_dim | solution.py:265
  2.2 0.0 copy-start.1
  2.2 0.0 copy-start
  2.2 13.1 %all-to-all-start = ((bf16[12,16,1024]{2,1,0:T(8,128)(2,1)}), bf16[12,16,1024]{2,1,0:T(8,128)(2,1)S(1)}, u32[]{:S(2)}, u32[]{:S(2)}) async-start(bf16[12,16,1024]{2,1,0:T(8,128)(2,1)} %broadcast_in_dim.8), calls=%async_computation | async-start | bytes 786432 | tf_op jit(solution)/shard_map/all_to_all | solution.py:267
  15.3 0.0 copy-done.1
  15.3 4.6 %collective-permute-start.1 = (bf16[16,1024]{1,0:T(8,128)(2,1)S(1)}, bf16[16,1024]{1,0:T(8,128)(2,1)S(1)}, u32[]{:S(2)}, u32[]{:S(2)}) collective-permute-start(bf16[16,1024]{1,0:T(8,128)(2,1)S(1)} %bitcast.35), channel_id=1, source_target_pairs={{0,24},{24,48},{48,72},{72,96},{96,120},{120,144},{144,168},{168,1... | collective-permute-start | bytes 98312 | tf_op jit(solution)/shard_map/ppermute | solution.py:255
  19.9 8.5 %collective-permute-start = (bf16[16,1024]{1,0:T(8,128)(2,1)S(1)}, bf16[16,1024]{1,0:T(8,128)(2,1)S(1)}, u32[]{:S(2)}, u32[]{:S(2)}) collective-permute-start(bf16[16,1024]{1,0:T(8,128)(2,1)S(1)} %bitcast.36), channel_id=1, source_target_pairs={{0,744},{24,0},{48,24},{72,48},{96,72},{120,96},{144,120},{168,144... | collective-permute-start | bytes 98312 | tf_op jit(solution)/shard_map/ppermute | solution.py:255
  28.4 3.8 %collective-permute-done.1.cot_prev_ref = bf16[16,1024]{1,0:T(8,128)(2,1)S(1)} collective-permute-done((bf16[16,1024]{1,0:T(8,128)(2,1)S(1)}, bf16[16,1024]{1,0:T(8,128)(2,1)S(1)}, u32[]{:S(2)}, u32[]{:S(2)}) %collective-permute-start.1) | collective-permute-done | bytes 32800 | tf_op jit(solution)/shard_map/ppermute | solution.py:255
  32.2 0.0 collective-permute-done.cot_next_ref
  32.2 0.0 all-to-all-done.mine_ref
  32.2 1.9 %collective-permute-start.2 = (bf16[12,16,1024]{2,1,0:T(8,128)(2,1)S(1)}, bf16[12,16,1024]{2,1,0:T(8,128)(2,1)S(1)}, u32[]{:S(2)}, u32[]{:S(2)}) collective-permute-start(bf16[12,16,1024]{2,1,0:T(8,128)(2,1)S(1)} %all-to-all-done.mine_ref), channel_id=1, source_target_pairs={{0,1},{1,0},{2,3},{3,2},{4,5},{5,4},{6,7},{7,6},{8,9},{9,8},{10,11... | collective-permute-start | bytes 1179656 | tf_op jit(solution)/shard_map/ppermute | solution.py:245
  34.1 1.7 %collective-permute-done.2.other_ref = bf16[12,16,1024]{2,1,0:T(8,128)(2,1)S(1)} collective-permute-done((bf16[12,16,1024]{2,1,0:T(8,128)(2,1)S(1)}, bf16[12,16,1024]{2,1,0:T(8,128)(2,1)S(1)}, u32[]{:S(2)}, u32[]{:S(2)}) %collective-permute-start.2) | collective-permute-done | bytes 393248 | tf_op jit(solution)/shard_map/ppermute | solution.py:245
  35.8 0.0 copy-done
  35.8 0.9 conv.1
  36.7 3.3 %collective-permute-start.3 = (bf16[2,16,1024]{2,1,0:T(8,128)(2,1)S(1)}, bf16[2,16,1024]{2,1,0:T(8,128)(2,1)S(1)}, u32[]{:S(2)}, u32[]{:S(2)}) collective-permute-start(bf16[2,16,1024]{2,1,0:T(8,128)(2,1)S(1)} %get-tuple-element.32), channel_id=1, source_target_pairs={{0,24},{24,48},{48,72},{72,96},{96,120},{120,144},{144,168},{168,1... | collective-permute-start | bytes 196616 | tf_op jit(solution)/shard_map/ppermute | solution.py:255
  40.0 7.7 %collective-permute-start.4 = (bf16[2,16,1024]{2,1,0:T(8,128)(2,1)S(1)}, bf16[2,16,1024]{2,1,0:T(8,128)(2,1)S(1)}, u32[]{:S(2)}, u32[]{:S(2)}) collective-permute-start(bf16[2,16,1024]{2,1,0:T(8,128)(2,1)S(1)} %get-tuple-element.33), channel_id=1, source_target_pairs={{0,744},{24,0},{48,24},{72,48},{96,72},{120,96},{144,120},{168,144... | collective-permute-start | bytes 196616 | tf_op jit(solution)/shard_map/ppermute | solution.py:255
  47.7 4.5 %collective-permute-start.5 = (bf16[16,1024]{1,0:T(8,128)(2,1)S(1)}, bf16[16,1024]{1,0:T(8,128)(2,1)S(1)}, u32[]{:S(2)}, u32[]{:S(2)}) collective-permute-start(bf16[16,1024]{1,0:T(8,128)(2,1)S(1)} %get-tuple-element.34), channel_id=1, source_target_pairs={{0,48},{24,72},{48,96},{72,120},{96,144},{120,168},{144,192},{168,... | collective-permute-start | bytes 98312 | tf_op jit(solution)/shard_map/ppermute | solution.py:255
  52.2 9.8 %collective-permute-start.6 = (bf16[16,1024]{1,0:T(8,128)(2,1)S(1)}, bf16[16,1024]{1,0:T(8,128)(2,1)S(1)}, u32[]{:S(2)}, u32[]{:S(2)}) collective-permute-start(bf16[16,1024]{1,0:T(8,128)(2,1)S(1)} %get-tuple-element.35), channel_id=1, source_target_pairs={{0,720},{24,744},{48,0},{72,24},{96,48},{120,72},{144,96},{168,120... | collective-permute-start | bytes 98312 | tf_op jit(solution)/shard_map/ppermute | solution.py:255
  62.0 0.0 collective-permute-done.5.prev2_ref
  62.0 2.4 %collective-permute-done.6.next2_ref = bf16[16,1024]{1,0:T(8,128)(2,1)S(1)} collective-permute-done((bf16[16,1024]{1,0:T(8,128)(2,1)S(1)}, bf16[16,1024]{1,0:T(8,128)(2,1)S(1)}, u32[]{:S(2)}, u32[]{:S(2)}) %collective-permute-start.6) | collective-permute-done | bytes 32800 | tf_op jit(solution)/shard_map/ppermute | solution.py:255
  64.4 0.0 collective-permute-done.3.prev_ref
  64.4 0.0 collective-permute-done.4.next_ref
  64.4 2.0 %grads.1 = (bf16[16,1024]{1,0:T(8,128)(2,1)}, bf16[8,11,16,128]{3,2,1,0:T(8,128)(2,1)}, bf16[432,1024]{1,0:T(8,128)(2,1)S(1)}) custom-call(f32[3,16,1024]{2,1,0:T(8,128)S(1)} %get-tuple-element.31.own_ref, bf16[2,16,1024]{2,1,0:T(8,128)(2,1)S(1)} %collective-permute-done.3.prev_ref, bf16[2,16,1024]{2,1,0:T(8,128)(2,1)S(1)} %collective-permute-done.4.next_ref, ...), custom_call_target="tpu_custom_call" | custom-call | tf_op jit(solution)/shard_map/grads/pallas_call | solution.py:151
  66.5 7.0 %all-to-all-start.1 = ((bf16[8,11,16,128]{3,2,1,0:T(8,128)(2,1)}), bf16[8,11,16,128]{3,2,1,0:T(8,128)(2,1)S(1)}, u32[]{:S(2)}, u32[]{:S(2)}) async-start(bf16[8,11,16,128]{3,2,1,0:T(8,128)(2,1)} %get-tuple-element.41), calls=%async_computation.1 | async-start | bytes 720896 | tf_op jit(solution)/shard_map/all_to_all | solution.py:280
  73.4 0.6 dgrad.1
  74.1 1.9 %collective-permute-start.7 = (bf16[3,4,16,1024]{3,2,1,0:T(8,128)(2,1)S(1)}, bf16[3,4,16,1024]{3,2,1,0:T(8,128)(2,1)S(1)}, u32[]{:S(2)}, u32[]{:S(2)}) collective-permute-start(bf16[3,4,16,1024]{3,2,1,0:T(8,128)(2,1)S(1)} %get-tuple-element.46), channel_id=1, source_target_pairs={{0,1},{1,0},{2,3},{3,2},{4,5},{5,4},{6,7},{7,6},{8,9},{9,8},{10,11... | collective-permute-start | bytes 1179656 | tf_op jit(solution)/shard_map/ppermute | solution.py:245
  76.0 1.7 %collective-permute-done.7.came_ref = bf16[3,4,16,1024]{3,2,1,0:T(8,128)(2,1)S(1)} collective-permute-done((bf16[3,4,16,1024]{3,2,1,0:T(8,128)(2,1)S(1)}, bf16[3,4,16,1024]{3,2,1,0:T(8,128)(2,1)S(1)}, u32[]{:S(2)}, u32[]{:S(2)}) %collective-permute-start.7) | collective-permute-done | bytes 393248 | tf_op jit(solution)/shard_map/ppermute | solution.py:245
  77.7 0.1 part.1
  77.7 1.9 %collective-permute-start.8 = (bf16[4,16,1024]{2,1,0:T(8,128)(2,1)S(1)}, bf16[4,16,1024]{2,1,0:T(8,128)(2,1)S(1)}, u32[]{:S(2)}, u32[]{:S(2)}) collective-permute-start(bf16[4,16,1024]{2,1,0:T(8,128)(2,1)S(1)} %get-tuple-element.49), channel_id=1, source_target_pairs={{0,2},{2,4},{4,0},{1,3},{3,5},{5,1},{6,8},{8,10},{10,6},{7,9},{9,1... | collective-permute-start | bytes 393224 | tf_op jit(solution)/shard_map/ppermute | solution.py:286
  79.7 4.8 %collective-permute-start.9 = (bf16[4,16,1024]{2,1,0:T(8,128)(2,1)S(1)}, bf16[4,16,1024]{2,1,0:T(8,128)(2,1)S(1)}, u32[]{:S(2)}, u32[]{:S(2)}) collective-permute-start(bf16[4,16,1024]{2,1,0:T(8,128)(2,1)S(1)} %get-tuple-element.50), channel_id=1, source_target_pairs={{0,4},{2,0},{4,2},{1,5},{3,1},{5,3},{6,10},{8,6},{10,8},{7,11},{9,... | collective-permute-start | bytes 393224 | tf_op jit(solution)/shard_map/ppermute | solution.py:287
  84.5 1.2 all-to-all-done.1.terms_ref
  85.7 0.7 total.2
  86.5 6.3 %all-to-all-start.2 = ((bf16[4,11,16,128]{3,2,1,0:T(8,128)(2,1)}), bf16[4,11,16,128]{3,2,1,0:T(8,128)(2,1)S(1)}, u32[]{:S(2)}, u32[]{:S(2)}) async-start(bf16[4,11,16,128]{3,2,1,0:T(8,128)(2,1)} %total.2), calls=%async_computation.2 | async-start | bytes 360448 | tf_op jit(solution)/shard_map/all_to_all | solution.py:285
  92.8 0.0 collective-permute-done.8
  92.8 0.0 collective-permute-done.9
  92.9 2.5 %collective-permute-start.10 = (bf16[2,16,1024]{2,1,0:T(8,128)(2,1)S(1)}, bf16[2,16,1024]{2,1,0:T(8,128)(2,1)S(1)}, u32[]{:S(2)}, u32[]{:S(2)}) collective-permute-start(bf16[2,16,1024]{2,1,0:T(8,128)(2,1)S(1)} %fusion.1), channel_id=1, source_target_pairs={{0,6},{6,0},{12,18},{18,12},{1,7},{7,1},{13,19},{19,13},{2,8},{8,2... | collective-permute-start | bytes 196616 | tf_op jit(solution)/shard_map/ppermute | solution.py:292
  95.3 10.2 %all-to-all-done.2.terms_ref = bf16[4,11,16,128]{3,2,1,0:T(8,128)(2,1)S(1)} async-done(((bf16[4,11,16,128]{3,2,1,0:T(8,128)(2,1)}), bf16[4,11,16,128]{3,2,1,0:T(8,128)(2,1)S(1)}, u32[]{:S(2)}, u32[]{:S(2)}) %all-to-all-start.2) | async-done | bytes 180256 | tf_op jit(solution)/shard_map/all_to_all | solution.py:285
  105.6 0.8 total.3
  106.3 7.6 %all-to-all-start.3 = ((bf16[8,11,16,128]{3,2,1,0:T(8,128)(2,1)}), bf16[8,11,16,128]{3,2,1,0:T(8,128)(2,1)S(1)}, u32[]{:S(2)}, u32[]{:S(2)}) async-start(bf16[8,11,16,128]{3,2,1,0:T(8,128)(2,1)} %total.3), calls=%async_computation.3 | async-start | bytes 720896 | tf_op jit(solution)/shard_map/all_to_all | solution.py:291
  114.0 0.0 collective-permute-done.10
  114.0 4.0 %collective-permute-start.11 = (bf16[16,1024]{1,0:T(8,128)(2,1)S(1)}, bf16[16,1024]{1,0:T(8,128)(2,1)S(1)}, u32[]{:S(2)}, u32[]{:S(2)}) collective-permute-start(bf16[16,1024]{1,0:T(8,128)(2,1)S(1)} %fusion.5), channel_id=1, source_target_pairs={{0,12},{6,18},{12,0},{18,6},{1,13},{7,19},{13,1},{19,7},{2,14},{8,... | collective-permute-start | bytes 98312 | tf_op jit(solution)/shard_map/ppermute | solution.py:294
  118.0 3.3 %collective-permute-done.11 = bf16[16,1024]{1,0:T(8,128)(2,1)S(1)} collective-permute-done((bf16[16,1024]{1,0:T(8,128)(2,1)S(1)}, bf16[16,1024]{1,0:T(8,128)(2,1)S(1)}, u32[]{:S(2)}, u32[]{:S(2)}) %collective-permute-start.11) | collective-permute-done | bytes 32800 | tf_op jit(solution)/shard_map/ppermute | solution.py:294
  121.3 0.6 fusion.4
  121.9 3.6 %all-to-all-done.3.units_ref = bf16[8,11,16,128]{3,2,1,0:T(8,128)(2,1)S(1)} async-done(((bf16[8,11,16,128]{3,2,1,0:T(8,128)(2,1)}), bf16[8,11,16,128]{3,2,1,0:T(8,128)(2,1)S(1)}, u32[]{:S(2)}, u32[]{:S(2)}) %all-to-all-start.3) | async-done | bytes 360480 | tf_op jit(solution)/shard_map/all_to_all | solution.py:291
  125.5 0.9 unpack.1
  (4 shorter events, 0.1 us)
Async XLA Ops:
  2.2 13.1 %copy-start.1 = (bf16[1,1,16,1024]{3,2,1,0:T(8,128)(2,1)S(1)}, bf16[1,1,16,1024]{3,2,1,0:T(8,128)(2,1)}, u32[]{:S(2)}) copy-start(bf16[1,1,16,1024]{3,2,1,0:T(8,128)(2,1)} %param.5) | copy-start | bytes 98308
  2.2 33.6 %copy-start = (bf16[16,3,3,3,384]{4,0,3,2,1:T(8,128)(2,1)S(1)}, bf16[16,3,3,3,384]{4,0,3,2,1:T(8,128)(2,1)}, u32[]{:S(2)}) copy-start(bf16[16,3,3,3,384]{4,0,3,2,1:T(8,128)(2,1)} %param.4) | copy-start | bytes 995332
  2.2 30.0 %all-to-all-start = ((bf16[12,16,1024]{2,1,0:T(8,128)(2,1)}), bf16[12,16,1024]{2,1,0:T(8,128)(2,1)S(1)}, u32[]{:S(2)}, u32[]{:S(2)}) async-start(bf16[12,16,1024]{2,1,0:T(8,128)(2,1)} %broadcast_in_dim.8), calls=%async_computation | async-start | bytes 786432 | tf_op jit(solution)/shard_map/all_to_all | solution.py:267
  15.3 16.9 %collective-permute-start.1 = (bf16[16,1024]{1,0:T(8,128)(2,1)S(1)}, bf16[16,1024]{1,0:T(8,128)(2,1)S(1)}, u32[]{:S(2)}, u32[]{:S(2)}) collective-permute-start(bf16[16,1024]{1,0:T(8,128)(2,1)S(1)} %bitcast.35), channel_id=1, source_target_pairs={{0,24},{24,48},{48,72},{72,96},{96,120},{120,144},{144,168},{168,1... | collective-permute-start | bytes 98312 | tf_op jit(solution)/shard_map/ppermute | solution.py:255
  19.9 12.3 %collective-permute-start = (bf16[16,1024]{1,0:T(8,128)(2,1)S(1)}, bf16[16,1024]{1,0:T(8,128)(2,1)S(1)}, u32[]{:S(2)}, u32[]{:S(2)}) collective-permute-start(bf16[16,1024]{1,0:T(8,128)(2,1)S(1)} %bitcast.36), channel_id=1, source_target_pairs={{0,744},{24,0},{48,24},{72,48},{96,72},{120,96},{144,120},{168,144... | collective-permute-start | bytes 98312 | tf_op jit(solution)/shard_map/ppermute | solution.py:255
  32.2 3.6 %collective-permute-start.2 = (bf16[12,16,1024]{2,1,0:T(8,128)(2,1)S(1)}, bf16[12,16,1024]{2,1,0:T(8,128)(2,1)S(1)}, u32[]{:S(2)}, u32[]{:S(2)}) collective-permute-start(bf16[12,16,1024]{2,1,0:T(8,128)(2,1)S(1)} %all-to-all-done.mine_ref), channel_id=1, source_target_pairs={{0,1},{1,0},{2,3},{3,2},{4,5},{5,4},{6,7},{7,6},{8,9},{9,8},{10,11... | collective-permute-start | bytes 1179656 | tf_op jit(solution)/shard_map/ppermute | solution.py:245
  36.7 27.7 %collective-permute-start.3 = (bf16[2,16,1024]{2,1,0:T(8,128)(2,1)S(1)}, bf16[2,16,1024]{2,1,0:T(8,128)(2,1)S(1)}, u32[]{:S(2)}, u32[]{:S(2)}) collective-permute-start(bf16[2,16,1024]{2,1,0:T(8,128)(2,1)S(1)} %get-tuple-element.32), channel_id=1, source_target_pairs={{0,24},{24,48},{48,72},{72,96},{96,120},{120,144},{144,168},{168,1... | collective-permute-start | bytes 196616 | tf_op jit(solution)/shard_map/ppermute | solution.py:255
  40.0 24.4 %collective-permute-start.4 = (bf16[2,16,1024]{2,1,0:T(8,128)(2,1)S(1)}, bf16[2,16,1024]{2,1,0:T(8,128)(2,1)S(1)}, u32[]{:S(2)}, u32[]{:S(2)}) collective-permute-start(bf16[2,16,1024]{2,1,0:T(8,128)(2,1)S(1)} %get-tuple-element.33), channel_id=1, source_target_pairs={{0,744},{24,0},{48,24},{72,48},{96,72},{120,96},{144,120},{168,144... | collective-permute-start | bytes 196616 | tf_op jit(solution)/shard_map/ppermute | solution.py:255
  47.7 14.3 %collective-permute-start.5 = (bf16[16,1024]{1,0:T(8,128)(2,1)S(1)}, bf16[16,1024]{1,0:T(8,128)(2,1)S(1)}, u32[]{:S(2)}, u32[]{:S(2)}) collective-permute-start(bf16[16,1024]{1,0:T(8,128)(2,1)S(1)} %get-tuple-element.34), channel_id=1, source_target_pairs={{0,48},{24,72},{48,96},{72,120},{96,144},{120,168},{144,192},{168,... | collective-permute-start | bytes 98312 | tf_op jit(solution)/shard_map/ppermute | solution.py:255
  52.2 12.3 %collective-permute-start.6 = (bf16[16,1024]{1,0:T(8,128)(2,1)S(1)}, bf16[16,1024]{1,0:T(8,128)(2,1)S(1)}, u32[]{:S(2)}, u32[]{:S(2)}) collective-permute-start(bf16[16,1024]{1,0:T(8,128)(2,1)S(1)} %get-tuple-element.35), channel_id=1, source_target_pairs={{0,720},{24,744},{48,0},{72,24},{96,48},{120,72},{144,96},{168,120... | collective-permute-start | bytes 98312 | tf_op jit(solution)/shard_map/ppermute | solution.py:255
  66.5 19.3 %all-to-all-start.1 = ((bf16[8,11,16,128]{3,2,1,0:T(8,128)(2,1)}), bf16[8,11,16,128]{3,2,1,0:T(8,128)(2,1)S(1)}, u32[]{:S(2)}, u32[]{:S(2)}) async-start(bf16[8,11,16,128]{3,2,1,0:T(8,128)(2,1)} %get-tuple-element.41), calls=%async_computation.1 | async-start | bytes 720896 | tf_op jit(solution)/shard_map/all_to_all | solution.py:280
  74.1 3.6 %collective-permute-start.7 = (bf16[3,4,16,1024]{3,2,1,0:T(8,128)(2,1)S(1)}, bf16[3,4,16,1024]{3,2,1,0:T(8,128)(2,1)S(1)}, u32[]{:S(2)}, u32[]{:S(2)}) collective-permute-start(bf16[3,4,16,1024]{3,2,1,0:T(8,128)(2,1)S(1)} %get-tuple-element.46), channel_id=1, source_target_pairs={{0,1},{1,0},{2,3},{3,2},{4,5},{5,4},{6,7},{7,6},{8,9},{9,8},{10,11... | collective-permute-start | bytes 1179656 | tf_op jit(solution)/shard_map/ppermute | solution.py:245
  77.7 15.1 %collective-permute-start.8 = (bf16[4,16,1024]{2,1,0:T(8,128)(2,1)S(1)}, bf16[4,16,1024]{2,1,0:T(8,128)(2,1)S(1)}, u32[]{:S(2)}, u32[]{:S(2)}) collective-permute-start(bf16[4,16,1024]{2,1,0:T(8,128)(2,1)S(1)} %get-tuple-element.49), channel_id=1, source_target_pairs={{0,2},{2,4},{4,0},{1,3},{3,5},{5,1},{6,8},{8,10},{10,6},{7,9},{9,1... | collective-permute-start | bytes 393224 | tf_op jit(solution)/shard_map/ppermute | solution.py:286
  79.7 13.1 %collective-permute-start.9 = (bf16[4,16,1024]{2,1,0:T(8,128)(2,1)S(1)}, bf16[4,16,1024]{2,1,0:T(8,128)(2,1)S(1)}, u32[]{:S(2)}, u32[]{:S(2)}) collective-permute-start(bf16[4,16,1024]{2,1,0:T(8,128)(2,1)S(1)} %get-tuple-element.50), channel_id=1, source_target_pairs={{0,4},{2,0},{4,2},{1,5},{3,1},{5,3},{6,10},{8,6},{10,8},{7,11},{9,... | collective-permute-start | bytes 393224 | tf_op jit(solution)/shard_map/ppermute | solution.py:287
  86.5 19.1 %all-to-all-start.2 = ((bf16[4,11,16,128]{3,2,1,0:T(8,128)(2,1)}), bf16[4,11,16,128]{3,2,1,0:T(8,128)(2,1)S(1)}, u32[]{:S(2)}, u32[]{:S(2)}) async-start(bf16[4,11,16,128]{3,2,1,0:T(8,128)(2,1)} %total.2), calls=%async_computation.2 | async-start | bytes 360448 | tf_op jit(solution)/shard_map/all_to_all | solution.py:285
  92.9 21.1 %collective-permute-start.10 = (bf16[2,16,1024]{2,1,0:T(8,128)(2,1)S(1)}, bf16[2,16,1024]{2,1,0:T(8,128)(2,1)S(1)}, u32[]{:S(2)}, u32[]{:S(2)}) collective-permute-start(bf16[2,16,1024]{2,1,0:T(8,128)(2,1)S(1)} %fusion.1), channel_id=1, source_target_pairs={{0,6},{6,0},{12,18},{18,12},{1,7},{7,1},{13,19},{19,13},{2,8},{8,2... | collective-permute-start | bytes 196616 | tf_op jit(solution)/shard_map/ppermute | solution.py:292
  106.3 19.2 %all-to-all-start.3 = ((bf16[8,11,16,128]{3,2,1,0:T(8,128)(2,1)}), bf16[8,11,16,128]{3,2,1,0:T(8,128)(2,1)S(1)}, u32[]{:S(2)}, u32[]{:S(2)}) async-start(bf16[8,11,16,128]{3,2,1,0:T(8,128)(2,1)} %total.3), calls=%async_computation.3 | async-start | bytes 720896 | tf_op jit(solution)/shard_map/all_to_all | solution.py:291
  114.0 7.3 %collective-permute-start.11 = (bf16[16,1024]{1,0:T(8,128)(2,1)S(1)}, bf16[16,1024]{1,0:T(8,128)(2,1)S(1)}, u32[]{:S(2)}, u32[]{:S(2)}) collective-permute-start(bf16[16,1024]{1,0:T(8,128)(2,1)S(1)} %fusion.5), channel_id=1, source_target_pairs={{0,12},{6,18},{12,0},{18,6},{1,13},{7,19},{13,1},{19,7},{2,14},{8,... | collective-permute-start | bytes 98312 | tf_op jit(solution)/shard_map/ppermute | solution.py:294

commit v8 on v6

--- a/solution.py
+++ b/solution.py
@@ -41,10 +41,10 @@
     return x_ref[...].reshape(-1, x_ref.shape[-1])
 
 
-def conv_kernel(core_ref, odd_ref, w_ref, mine_ref, other_ref, near_ref, mid_ref, far_ref, x_ref):
-    rows = mid_ref.shape[0]
+def conv_kernel(core_ref, w_ref, mine_ref, other_ref, *refs):
+    outs, x_ref = refs[:3], refs[3]
+    rows = outs[0].shape[0]
     x = merge_cores(core_ref, mine_ref, other_ref, x_ref)
-    sums = []
     for depth_tap in range(3):
         w = w_ref[depth_tap * 9 * rows : (depth_tap + 1) * 9 * rows, :]
         product = jnp.dot(w, x, preferred_element_type=jnp.float32)
@@ -57,12 +57,7 @@
                 part = term if part is None else part + term
             part = shift_cells(part, 0, 1 - col_tap)
             total = part if total is None else total + part
-        sums.append(total)
-    up, mid, down = sums
-    odd = odd_ref[0] == 1
-    near_ref[...] = jnp.where(odd, down, up)
-    mid_ref[...] = mid
-    far_ref[...] = jnp.where(odd, up, down)
+        outs[depth_tap][...] = total.astype(outs[depth_tap].dtype)
 
 
 def specs(scalars, arrays):
@@ -74,17 +69,20 @@
     return [pltpu.VMEM((mine.shape[0], 2) + mine.shape[1:], mine.dtype)]
 
 
-def conv(core, odd, weights, mine, other):
+def conv(core, weights, mine, other):
     rows = weights.shape[0] // TAPS
     cells = mine.shape[-1]
     return pl.pallas_call(
         conv_kernel,
-        out_shape=[jax.ShapeDtypeStruct((rows, cells), jnp.float32)] * 3,
-        in_specs=specs(2, 3),
+        out_shape=[
+            jax.ShapeDtypeStruct((rows, cells), kind)
+            for kind in (jnp.bfloat16, jnp.float32, jnp.bfloat16)
+        ],
+        in_specs=specs(1, 3),
         scratch_shapes=merged_scratch(mine),
         compiler_params=pltpu.CompilerParams(vmem_limit_bytes=VMEM_LIMIT),
         name="conv",
-    )(core, odd, weights, mine, other)
+    )(core, weights, mine, other)
 
 
 def stack_plane(plane, stack_ref, at):
@@ -134,15 +132,13 @@
     )(core, own, mine, other)
 
 
-def halo_kernel(odd_ref, near_ref, far_ref, x_ref, units_ref, wide_ref, stack_ref):
-    rows = near_ref.shape[0]
+def halo_kernel(above_ref, below_ref, x_ref, units_ref, wide_ref, stack_ref):
+    rows = above_ref.shape[0]
     slots, per = wide_ref.shape[:2]
     x = x_ref[...].reshape(-1, x_ref.shape[-1])
     columns = x.shape[0] // LANES
-    odd = odd_ref[0] == 1
-    near, far = near_ref[...].astype(jnp.float32), far_ref[...].astype(jnp.float32)
-    for half, plane in enumerate((jnp.where(odd, far, near), jnp.where(odd, near, far))):
-        stack_plane(plane, stack_ref, half * 9 * rows)
+    for half, ref in enumerate((above_ref, below_ref)):
+        stack_plane(ref[...], stack_ref, half * 9 * rows)
         grad = cross(stack_ref[half * 9 * rows : (half + 1) * 9 * rows, :], x)
         for at in range(9 * columns):
             tap, column = divmod(at, columns)
@@ -157,8 +153,8 @@
         wide_ref[unit // per, unit % per] = jnp.zeros((rows, LANES), jnp.bfloat16)
 
 
-def wgrad_halo(odd, near, far, x, units, slots):
-    rows, cells = near.shape
+def wgrad_halo(above, below, x, units, slots):
+    rows, cells = above.shape
     per = -(-3 * units.shape[0] // slots)
     return pl.pallas_call(
         halo_kernel,
@@ -166,10 +162,9 @@
             jax.ShapeDtypeStruct((slots, per, rows, LANES), jnp.bfloat16),
             jax.ShapeDtypeStruct((18 * rows, cells), jnp.bfloat16),
         ],
-        in_specs=specs(1, 4),
         compiler_params=pltpu.CompilerParams(vmem_limit_bytes=VMEM_LIMIT),
         name="wgrad_halo",
-    )(odd, near, far, x, units)
+    )(above, below, x, units)
 
 
 def dgrad_kernel(core_ref, x_at_ref, z_at_ref, k_ref, own_ref, halo_ref, keep_ref, send_ref):
@@ -191,12 +186,12 @@
             z_slot = lax.rem(z_at - z_at_ref[0] + 3, 3)
             at = (x_at * 3 + z_at) * 2 * rows
             even, odd = partial[at : at + rows], partial[at + rows : at + 2 * rows]
-            keep_ref[z_slot, x_slot] = jnp.where(first, even, odd)
-            send_ref[z_slot, x_slot] = jnp.where(first, odd, even).astype(jnp.bfloat16)
+            keep_ref[x_slot, z_slot] = jnp.where(first, even, odd)
+            send_ref[x_slot, z_slot] = jnp.where(first, odd, even).astype(jnp.bfloat16)
 
 
 def dgrad(core, x_at, z_at, k_rows, own, halo):
-    shape = (3, 4, k_rows.shape[0] // TAPS, own.shape[1])
+    shape = (4, 3, k_rows.shape[0] // TAPS, own.shape[1])
     return pl.pallas_call(
         dgrad_kernel,
         out_shape=[
@@ -210,7 +205,7 @@
 
 
 def act_kernel(mid_ref, low_ref, high_ref, cot_ref, act_ref, grad_ref):
-    preact = mid_ref[...] + low_ref[...] + high_ref[...]
+    preact = mid_ref[...] + low_ref[...].astype(jnp.float32) + high_ref[...].astype(jnp.float32)
     sig = jax.nn.sigmoid(preact)
     act_ref[...] = (preact * sig).astype(jnp.bfloat16)
     cot = cot_ref[...].astype(jnp.float32)
@@ -241,21 +236,23 @@
     )(terms)
 
 
-def part_kernel(kept_ref, came_ref, here_ref, after_ref, before_ref):
-    here_ref[...] = kept_ref[0] + came_ref[0].astype(jnp.float32)
-    after_ref[...] = (kept_ref[1] + came_ref[1].astype(jnp.float32)).astype(jnp.bfloat16)
-    before_ref[...] = (kept_ref[2] + came_ref[2].astype(jnp.float32)).astype(jnp.bfloat16)
-
-
-def part(kept, came):
-    return pl.pallas_call(
-        part_kernel,
-        out_shape=[
-            jax.ShapeDtypeStruct(kept.shape[1:], kind)
-            for kind in (jnp.float32, jnp.bfloat16, jnp.bfloat16)
-        ],
-        compiler_params=pltpu.CompilerParams(vmem_limit_bytes=VMEM_LIMIT),
-        name="part",
+def halve_kernel(kept_ref, came_ref, keep_ref, send_ref):
+    for at in range(keep_ref.shape[0]):
+        keep_ref[at] = kept_ref[2 * at] + came_ref[2 * at].astype(jnp.float32)
+        total = kept_ref[2 * at + 1] + came_ref[2 * at + 1].astype(jnp.float32)
+        send_ref[at] = total.astype(jnp.bfloat16)
+
+
+def halve(kept, came):
+    shape = (kept.shape[0] // 2,) + kept.shape[1:]
+    return pl.pallas_call(
+        halve_kernel,
+        out_shape=[
+            jax.ShapeDtypeStruct(shape, jnp.float32),
+            jax.ShapeDtypeStruct(shape, jnp.bfloat16),
+        ],
+        compiler_params=pltpu.CompilerParams(vmem_limit_bytes=VMEM_LIMIT),
+        name="halve",
     )(kept, came)
 
 
@@ -287,13 +284,14 @@
     cells = volume.shape[3]
     chips = lax.axis_size(CHIPS)
     depths = lax.axis_size(DEP)
-    near_pairs = [(i, i ^ 1) for i in range(depths)]
-    far_pairs = [(i, (i + 1 if i % 2 else i - 1) % depths) for i in range(depths)]
+
+    def shift(block, step):
+        return lax.ppermute(block, DEP, [(i, (i + step) % depths) for i in range(depths)])
 
     def index(name):
         return lax.axis_index(name).astype(jnp.int32).reshape(1)
 
-    core, x_at, z_at, odd = index("core"), index("x"), index("zl"), index("zh") % 2
+    core, x_at, z_at = index("core"), index("x"), index("zl")
     own = volume.reshape(rows, cells)
     cot = cotangent.reshape(rows, cells)
 
@@ -302,36 +300,32 @@
 
     mine = lax.all_to_all(copies(own), CHIPS, 0, 0)
     k_rows = jnp.transpose(kernel.reshape(rows, TAPS, -1), (1, 0, 2)).reshape(TAPS * rows, -1)
-    mine, k_rows, cot, core, odd, x_at, z_at = lax.optimization_barrier(
-        (mine, k_rows, cot, core, odd, x_at, z_at)
+    mine, k_rows, cot, core, x_at, z_at = lax.optimization_barrier(
+        (mine, k_rows, cot, core, x_at, z_at)
     )
     other = swap_cores(mine)
 
-    near, mid, far = conv(core, odd, k_rows, mine, other)
-    near = lax.ppermute(near, DEP, near_pairs)
-    far = lax.ppermute(far, DEP, far_pairs)
-    activated, grad_pre = activate(mid, near, far, cot)
-
-    near_grad = lax.ppermute(grad_pre, DEP, near_pairs)
-    far_grad = lax.ppermute(grad_pre, DEP, far_pairs)
+    up, mid, down = conv(core, k_rows, mine, other)
+    activated, grad_pre = activate(mid, shift(up, 1), shift(down, -1), cot)
+
+    above, below = shift(grad_pre, -1), shift(grad_pre, 1)
     own_units, own_stack, x = wgrad_own(core, grad_pre, mine, other)
     ys, zs = lax.axis_size("y"), lax.axis_size("zh")
-    wide, halo_stack = wgrad_halo(odd, near_grad, far_grad, x, own_units, ys)
+    wide, halo_stack = wgrad_halo(above, below, x, own_units, ys)
     scale = 1.0 / math.sqrt(UNIV * DEPTH * SIDE * SIDE)
     over_y = lax.all_to_all(wide, "y", 0, 0)
 
     keep, send = dgrad(core, x_at, z_at, k_rows, own_stack, halo_stack)
-    here, after, before = part(keep, swap_cores(send))
-    over_y, here = lax.optimization_barrier((over_y, here))
+    keep, send = halve(keep, swap_cores(send))
+    over_y, keep = lax.optimization_barrier((over_y, keep))
     over_z = lax.all_to_all(total_spread(over_y, 1.0, zs), "zh", 0, 0)
+    total = keep + lax.ppermute(send, "x", [(i, i ^ 1) for i in range(4)]).astype(jnp.float32)
+    after, before = total[:, 1].astype(jnp.bfloat16), total[:, 2].astype(jnp.bfloat16)
+    over_z, _ = lax.optimization_barrier((over_z, (after, before)))
     after = lax.ppermute(after, "zl", [(i, (i + 1) % 3) for i in range(3)])
     before = lax.ppermute(before, "zl", [(i, (i + 2) % 3) for i in range(3)])
-    total = here + after.astype(jnp.float32) + before.astype(jnp.float32)
-    total = total.reshape(2, 2, rows, cells)
-    over_z, _ = lax.optimization_barrier((over_z, total))
     units = lax.all_to_all(total_spread(over_z, scale, ys), "y", 0, 0)
-    step = lax.ppermute(total[:, 1].astype(jnp.bfloat16), "x", [(i, i ^ 1) for i in range(4)])
-    total = total[:, 0] + step.astype(jnp.float32)
+    total = total[:, 0] + after.astype(jnp.float32) + before.astype(jnp.float32)
     step = lax.ppermute(total[1].astype(jnp.bfloat16), "x", [(i, i ^ 2) for i in range(4)])
     grad_volume = (total[0] + step.astype(jnp.float32)).astype(jnp.bfloat16)
     all_taps = unpack(units, kernel.shape[-1])

time: 122 us -> 116 us (0.951)
  the two profiles are of different devices: /device:TPU:8 before, /device:TPU:2 now
where the time goes in v8:
time: 116 us; the launch traced here: 115 us
  starting transfers between devices  73.6 us (63%)
  waiting for transfers between devices  31.8 us (27%)
  Pallas kernels  7.03 us (6%)
  local copies, waits for them, and re-layouts  1.57 us (1%)
    ppermute x4, starting transfers between devices, shift(): lax.ppermute(block, DEP, [(i, (i + step) % depths) for i in range(depths)])  25.8 us
    all_to_all x1, starting transfers between devices, body(): mine = lax.all_to_all(copies(own), CHIPS, 0, 0)  13.1 us
    all_to_all x1, waiting for transfers between devices, body(): mine = lax.all_to_all(copies(own), CHIPS, 0, 0)  8.12 us
    all_to_all x1, starting transfers between devices, body(): over_y = lax.all_to_all(wide, 'y', 0, 0)  7.1 us
    all_to_all x1, starting transfers between devices, body(): over_z = lax.all_to_all(total_spread(over_y, 1.0, zs), 'zh', 0, 0)  5.66 us
    ppermute x1, starting transfers between devices, body(): before = lax.ppermute(before, 'zl', [(i, (i + 2) % 3) for i in range(3)])  4.82 us
    all_to_all x1, starting transfers between devices, body(): units = lax.all_to_all(total_spread(over_z, scale, ys), 'y', 0, 0)  4.77 us
    ppermute x1, waiting for transfers between devices, body(): lax.ppermute(total[1].astype(jnp.bfloat16), 'x', [(i, i ^ 2) for i in ran...  4.4 us
  transfers between devices with their start and end apart: 14, of which 10 were waited for; matrix products, arithmetic and copies ran while one was open for 1% of the time, Pallas kernels for 3%

profile of v8, /device:TPU:2, one launch (start us, length us, event | category | flops | bytes accessed | tf_op | source)
XLA Modules:
  0.0 115.5 jit_solution(12087922695760188470)
XLA Ops:
  0.6 1.5 %broadcast_in_dim.8 = bf16[12,16,1024]{2,1,0:T(8,128)(2,1)} broadcast(bf16[16,1024]{1,0:T(8,128)(2,1)} %bitcast.44), dimensions={1,2} | broadcast | bytes 425984 | tf_op jit(solution)/shard_map/broadcast_in_dim | solution.py:299
  2.2 0.0 copy-start
  2.2 13.1 %all-to-all-start = ((bf16[12,16,1024]{2,1,0:T(8,128)(2,1)}), bf16[12,16,1024]{2,1,0:T(8,128)(2,1)S(1)}, u32[]{:S(2)}, u32[]{:S(2)}) async-start(bf16[12,16,1024]{2,1,0:T(8,128)(2,1)} %broadcast_in_dim.8), calls=%async_computation | async-start | bytes 786432 | tf_op jit(solution)/shard_map/all_to_all | solution.py:301
  15.3 8.1 %all-to-all-done.mine_ref = bf16[12,16,1024]{2,1,0:T(8,128)(2,1)S(1)} async-done(((bf16[12,16,1024]{2,1,0:T(8,128)(2,1)}), bf16[12,16,1024]{2,1,0:T(8,128)(2,1)S(1)}, u32[]{:S(2)}, u32[]{:S(2)}) %all-to-all-start) | async-done | bytes 393248 | tf_op jit(solution)/shard_map/all_to_all | solution.py:301
  23.4 0.0 copy-start.1
  23.4 2.0 %collective-permute-start = (bf16[12,16,1024]{2,1,0:T(8,128)(2,1)S(1)}, bf16[12,16,1024]{2,1,0:T(8,128)(2,1)S(1)}, u32[]{:S(2)}, u32[]{:S(2)}) collective-permute-start(bf16[12,16,1024]{2,1,0:T(8,128)(2,1)S(1)} %all-to-all-done.mine_ref), channel_id=1, source_target_pairs={{0,1},{1,0},{2,3},{3,2},{4,5},{5,4},{6,7},{7,6},{8,9},{9,8},{10,11... | collective-permute-start | bytes 1179656 | tf_op jit(solution)/shard_map/ppermute | solution.py:279
  25.5 1.7 %collective-permute-done.other_ref = bf16[12,16,1024]{2,1,0:T(8,128)(2,1)S(1)} collective-permute-done((bf16[12,16,1024]{2,1,0:T(8,128)(2,1)S(1)}, bf16[12,16,1024]{2,1,0:T(8,128)(2,1)S(1)}, u32[]{:S(2)}, u32[]{:S(2)}) %collective-permute-start) | collective-permute-done | bytes 393248 | tf_op jit(solution)/shard_map/ppermute | solution.py:279
  27.1 0.0 copy-done
  27.1 0.9 conv.1
  28.1 7.1 %collective-permute-start.1 = (bf16[16,1024]{1,0:T(8,128)(2,1)S(1)}, bf16[16,1024]{1,0:T(8,128)(2,1)S(1)}, u32[]{:S(2)}, u32[]{:S(2)}) collective-permute-start(bf16[16,1024]{1,0:T(8,128)(2,1)S(1)} %get-tuple-element.30), channel_id=1, source_target_pairs={{0,24},{24,48},{48,72},{72,96},{96,120},{120,144},{144,168},{168,1... | collective-permute-start | bytes 98312 | tf_op jit(solution)/shard_map/ppermute | solution.py:289
  35.2 7.3 %collective-permute-start.2 = (bf16[16,1024]{1,0:T(8,128)(2,1)S(1)}, bf16[16,1024]{1,0:T(8,128)(2,1)S(1)}, u32[]{:S(2)}, u32[]{:S(2)}) collective-permute-start(bf16[16,1024]{1,0:T(8,128)(2,1)S(1)} %get-tuple-element.31), channel_id=1, source_target_pairs={{0,744},{24,0},{48,24},{72,48},{96,72},{120,96},{144,120},{168,144... | collective-permute-start | bytes 98312 | tf_op jit(solution)/shard_map/ppermute | solution.py:289
  42.5 0.6 collective-permute-done.1.low_ref
  43.1 1.4 %collective-permute-done.2.high_ref = bf16[16,1024]{1,0:T(8,128)(2,1)S(1)} collective-permute-done((bf16[16,1024]{1,0:T(8,128)(2,1)S(1)}, bf16[16,1024]{1,0:T(8,128)(2,1)S(1)}, u32[]{:S(2)}, u32[]{:S(2)}) %collective-permute-start.2) | collective-permute-done | bytes 32800 | tf_op jit(solution)/shard_map/ppermute | solution.py:289
  44.5 0.0 copy-done.1
  44.5 0.6 activate.1
  45.1 6.2 %collective-permute-start.4 = (bf16[16,1024]{1,0:T(8,128)(2,1)S(1)}, bf16[16,1024]{1,0:T(8,128)(2,1)S(1)}, u32[]{:S(2)}, u32[]{:S(2)}) collective-permute-start(bf16[16,1024]{1,0:T(8,128)(2,1)S(1)} %get-tuple-element.34.own_ref), channel_id=1, source_target_pairs={{0,24},{24,48},{48,72},{72,96},{96,120},{120,144},{144,168},{168,1... | collective-permute-start | bytes 98312 | tf_op jit(solution)/shard_map/ppermute | solution.py:289
  51.4 5.1 %collective-permute-start.3 = (bf16[16,1024]{1,0:T(8,128)(2,1)S(1)}, bf16[16,1024]{1,0:T(8,128)(2,1)S(1)}, u32[]{:S(2)}, u32[]{:S(2)}) collective-permute-start(bf16[16,1024]{1,0:T(8,128)(2,1)S(1)} %get-tuple-element.34.own_ref), channel_id=1, source_target_pairs={{0,744},{24,0},{48,24},{72,48},{96,72},{120,96},{144,120},{168,144... | collective-permute-start | bytes 98312 | tf_op jit(solution)/shard_map/ppermute | solution.py:289
  56.5 0.6 wgrad_own.1
  57.1 0.0 collective-permute-done.4.below_ref
  57.1 2.1 %collective-permute-done.3.above_ref = bf16[16,1024]{1,0:T(8,128)(2,1)S(1)} collective-permute-done((bf16[16,1024]{1,0:T(8,128)(2,1)S(1)}, bf16[16,1024]{1,0:T(8,128)(2,1)S(1)}, u32[]{:S(2)}, u32[]{:S(2)}) %collective-permute-start.3) | collective-permute-done | bytes 32800 | tf_op jit(solution)/shard_map/ppermute | solution.py:289
  59.2 1.7 %wgrad_halo.1 = (bf16[8,11,16,128]{3,2,1,0:T(8,128)(2,1)}, bf16[288,1024]{1,0:T(8,128)(2,1)S(1)}) custom-call(bf16[16,1024]{1,0:T(8,128)(2,1)S(1)} %collective-permute-done.3.above_ref, bf16[16,1024]{1,0:T(8,128)(2,1)S(1)} %collective-permute-done.4.below_ref, bf16[12,2,16,1024]{3,2,1,0:T(8,128)(2,1)S(1)} %get-tuple-element.35.x_ref, ...), custom_call_target="tpu_custom_call" | custom-call | tf_op jit(solution)/shard_map/wgrad_halo/pallas_call | solution.py:159
  60.9 7.1 %all-to-all-start.1 = ((bf16[8,11,16,128]{3,2,1,0:T(8,128)(2,1)}), bf16[8,11,16,128]{3,2,1,0:T(8,128)(2,1)S(1)}, u32[]{:S(2)}, u32[]{:S(2)}) async-start(bf16[8,11,16,128]{3,2,1,0:T(8,128)(2,1)} %get-tuple-element.37), calls=%async_computation.1 | async-start | bytes 720896 | tf_op jit(solution)/shard_map/all_to_all | solution.py:316
  68.0 0.8 dgrad.1
  68.8 1.9 %collective-permute-start.5 = (bf16[4,3,16,1024]{3,2,1,0:T(8,128)(2,1)S(1)}, bf16[4,3,16,1024]{3,2,1,0:T(8,128)(2,1)S(1)}, u32[]{:S(2)}, u32[]{:S(2)}) collective-permute-start(bf16[4,3,16,1024]{3,2,1,0:T(8,128)(2,1)S(1)} %get-tuple-element.43), channel_id=1, source_target_pairs={{0,1},{1,0},{2,3},{3,2},{4,5},{5,4},{6,7},{7,6},{8,9},{9,8},{10,11... | collective-permute-start | bytes 1179656 | tf_op jit(solution)/shard_map/ppermute | solution.py:279
  70.7 1.7 %collective-permute-done.5.came_ref = bf16[4,3,16,1024]{3,2,1,0:T(8,128)(2,1)S(1)} collective-permute-done((bf16[4,3,16,1024]{3,2,1,0:T(8,128)(2,1)S(1)}, bf16[4,3,16,1024]{3,2,1,0:T(8,128)(2,1)S(1)}, u32[]{:S(2)}, u32[]{:S(2)}) %collective-permute-start.5) | collective-permute-done | bytes 393248 | tf_op jit(solution)/shard_map/ppermute | solution.py:279
  72.4 0.1 halve.1
  72.5 3.5 %collective-permute-start.6 = (bf16[2,3,16,1024]{3,2,1,0:T(8,128)(2,1)S(1)}, bf16[2,3,16,1024]{3,2,1,0:T(8,128)(2,1)S(1)}, u32[]{:S(2)}, u32[]{:S(2)}) collective-permute-start(bf16[2,3,16,1024]{3,2,1,0:T(8,128)(2,1)S(1)} %get-tuple-element.46), channel_id=1, source_target_pairs={{0,6},{6,0},{12,18},{18,12},{1,7},{7,1},{13,19},{19,13},{2,8},{8,2... | collective-permute-start | bytes 589832 | tf_op jit(solution)/shard_map/ppermute | solution.py:322
  76.0 4.0 %all-to-all-done.1.terms_ref = bf16[8,11,16,128]{3,2,1,0:T(8,128)(2,1)S(1)} async-done(((bf16[8,11,16,128]{3,2,1,0:T(8,128)(2,1)}), bf16[8,11,16,128]{3,2,1,0:T(8,128)(2,1)S(1)}, u32[]{:S(2)}, u32[]{:S(2)}) %all-to-all-start.1) | async-done | bytes 360480 | tf_op jit(solution)/shard_map/all_to_all | solution.py:316
  80.0 0.7 total.2
  80.7 5.7 %all-to-all-start.2 = ((bf16[4,11,16,128]{3,2,1,0:T(8,128)(2,1)}), bf16[4,11,16,128]{3,2,1,0:T(8,128)(2,1)S(1)}, u32[]{:S(2)}, u32[]{:S(2)}) async-start(bf16[4,11,16,128]{3,2,1,0:T(8,128)(2,1)} %total.2), calls=%async_computation.2 | async-start | bytes 360448 | tf_op jit(solution)/shard_map/all_to_all | solution.py:321
  86.4 0.0 collective-permute-done.6
  86.5 1.9 %collective-permute-start.7 = (bf16[2,16,1024]{2,1,0:T(8,128)(2,1)S(1)}, bf16[2,16,1024]{2,1,0:T(8,128)(2,1)S(1)}, u32[]{:S(2)}, u32[]{:S(2)}) collective-permute-start(bf16[2,16,1024]{2,1,0:T(8,128)(2,1)S(1)} %get-tuple-element.51), channel_id=1, source_target_pairs={{0,2},{2,4},{4,0},{1,3},{3,5},{5,1},{6,8},{8,10},{10,6},{7,9},{9,1... | collective-permute-start | bytes 196616 | tf_op jit(solution)/shard_map/ppermute | solution.py:325
  88.4 4.8 %collective-permute-start.8 = (bf16[2,16,1024]{2,1,0:T(8,128)(2,1)S(1)}, bf16[2,16,1024]{2,1,0:T(8,128)(2,1)S(1)}, u32[]{:S(2)}, u32[]{:S(2)}) collective-permute-start(bf16[2,16,1024]{2,1,0:T(8,128)(2,1)S(1)} %get-tuple-element.52), channel_id=1, source_target_pairs={{0,4},{2,0},{4,2},{1,5},{3,1},{5,3},{6,10},{8,6},{10,8},{7,11},{9,... | collective-permute-start | bytes 196616 | tf_op jit(solution)/shard_map/ppermute | solution.py:326
  93.2 4.3 %all-to-all-done.2.terms_ref = bf16[4,11,16,128]{3,2,1,0:T(8,128)(2,1)S(1)} async-done(((bf16[4,11,16,128]{3,2,1,0:T(8,128)(2,1)}), bf16[4,11,16,128]{3,2,1,0:T(8,128)(2,1)S(1)}, u32[]{:S(2)}, u32[]{:S(2)}) %all-to-all-start.2) | async-done | bytes 180256 | tf_op jit(solution)/shard_map/all_to_all | solution.py:321
  97.5 0.8 total.3
  98.3 4.8 %all-to-all-start.3 = ((bf16[8,11,16,128]{3,2,1,0:T(8,128)(2,1)}), bf16[8,11,16,128]{3,2,1,0:T(8,128)(2,1)S(1)}, u32[]{:S(2)}, u32[]{:S(2)}) async-start(bf16[8,11,16,128]{3,2,1,0:T(8,128)(2,1)} %total.3), calls=%async_computation.3 | async-start | bytes 720896 | tf_op jit(solution)/shard_map/all_to_all | solution.py:327
  103.0 0.0 collective-permute-done.7
  103.0 0.0 collective-permute-done.8
  103.1 2.9 %collective-permute-start.9 = (bf16[16,1024]{1,0:T(8,128)(2,1)S(1)}, bf16[16,1024]{1,0:T(8,128)(2,1)S(1)}, u32[]{:S(2)}, u32[]{:S(2)}) collective-permute-start(bf16[16,1024]{1,0:T(8,128)(2,1)S(1)} %fusion.5), channel_id=1, source_target_pairs={{0,12},{6,18},{12,0},{18,6},{1,13},{7,19},{13,1},{19,7},{2,14},{8,... | collective-permute-start | bytes 98312 | tf_op jit(solution)/shard_map/ppermute | solution.py:329
  106.0 4.4 %collective-permute-done.9 = bf16[16,1024]{1,0:T(8,128)(2,1)S(1)} collective-permute-done((bf16[16,1024]{1,0:T(8,128)(2,1)S(1)}, bf16[16,1024]{1,0:T(8,128)(2,1)S(1)}, u32[]{:S(2)}, u32[]{:S(2)}) %collective-permute-start.9) | collective-permute-done | bytes 32800 | tf_op jit(solution)/shard_map/ppermute | solution.py:329
  110.4 0.6 fusion.4
  111.0 3.5 %all-to-all-done.3.units_ref = bf16[8,11,16,128]{3,2,1,0:T(8,128)(2,1)S(1)} async-done(((bf16[8,11,16,128]{3,2,1,0:T(8,128)(2,1)}), bf16[8,11,16,128]{3,2,1,0:T(8,128)(2,1)S(1)}, u32[]{:S(2)}, u32[]{:S(2)}) %all-to-all-start.3) | async-done | bytes 360480 | tf_op jit(solution)/shard_map/all_to_all | solution.py:327
  114.6 0.9 unpack.1
  (4 shorter events, 0.1 us)
Async XLA Ops:
  2.2 25.0 %copy-start = (bf16[16,3,3,3,384]{4,0,3,2,1:T(8,128)(2,1)S(1)}, bf16[16,3,3,3,384]{4,0,3,2,1:T(8,128)(2,1)}, u32[]{:S(2)}) copy-start(bf16[16,3,3,3,384]{4,0,3,2,1:T(8,128)(2,1)} %param.4) | copy-start | bytes 995332
  2.2 21.2 %all-to-all-start = ((bf16[12,16,1024]{2,1,0:T(8,128)(2,1)}), bf16[12,16,1024]{2,1,0:T(8,128)(2,1)S(1)}, u32[]{:S(2)}, u32[]{:S(2)}) async-start(bf16[12,16,1024]{2,1,0:T(8,128)(2,1)} %broadcast_in_dim.8), calls=%async_computation | async-start | bytes 786432 | tf_op jit(solution)/shard_map/all_to_all | solution.py:301
  23.4 21.1 %copy-start.1 = (bf16[1,1,16,1024]{3,2,1,0:T(8,128)(2,1)S(1)}, bf16[1,1,16,1024]{3,2,1,0:T(8,128)(2,1)}, u32[]{:S(2)}) copy-start(bf16[1,1,16,1024]{3,2,1,0:T(8,128)(2,1)} %param.5) | copy-start | bytes 98308
  23.4 3.7 %collective-permute-start = (bf16[12,16,1024]{2,1,0:T(8,128)(2,1)S(1)}, bf16[12,16,1024]{2,1,0:T(8,128)(2,1)S(1)}, u32[]{:S(2)}, u32[]{:S(2)}) collective-permute-start(bf16[12,16,1024]{2,1,0:T(8,128)(2,1)S(1)} %all-to-all-done.mine_ref), channel_id=1, source_target_pairs={{0,1},{1,0},{2,3},{3,2},{4,5},{5,4},{6,7},{7,6},{8,9},{9,8},{10,11... | collective-permute-start | bytes 1179656 | tf_op jit(solution)/shard_map/ppermute | solution.py:279
  28.1 15.0 %collective-permute-start.1 = (bf16[16,1024]{1,0:T(8,128)(2,1)S(1)}, bf16[16,1024]{1,0:T(8,128)(2,1)S(1)}, u32[]{:S(2)}, u32[]{:S(2)}) collective-permute-start(bf16[16,1024]{1,0:T(8,128)(2,1)S(1)} %get-tuple-element.30), channel_id=1, source_target_pairs={{0,24},{24,48},{48,72},{72,96},{96,120},{120,144},{144,168},{168,1... | collective-permute-start | bytes 98312 | tf_op jit(solution)/shard_map/ppermute | solution.py:289
  35.2 9.3 %collective-permute-start.2 = (bf16[16,1024]{1,0:T(8,128)(2,1)S(1)}, bf16[16,1024]{1,0:T(8,128)(2,1)S(1)}, u32[]{:S(2)}, u32[]{:S(2)}) collective-permute-start(bf16[16,1024]{1,0:T(8,128)(2,1)S(1)} %get-tuple-element.31), channel_id=1, source_target_pairs={{0,744},{24,0},{48,24},{72,48},{96,72},{120,96},{144,120},{168,144... | collective-permute-start | bytes 98312 | tf_op jit(solution)/shard_map/ppermute | solution.py:289
  45.1 12.0 %collective-permute-start.4 = (bf16[16,1024]{1,0:T(8,128)(2,1)S(1)}, bf16[16,1024]{1,0:T(8,128)(2,1)S(1)}, u32[]{:S(2)}, u32[]{:S(2)}) collective-permute-start(bf16[16,1024]{1,0:T(8,128)(2,1)S(1)} %get-tuple-element.34.own_ref), channel_id=1, source_target_pairs={{0,24},{24,48},{48,72},{72,96},{96,120},{120,144},{144,168},{168,1... | collective-permute-start | bytes 98312 | tf_op jit(solution)/shard_map/ppermute | solution.py:289
  51.4 7.8 %collective-permute-start.3 = (bf16[16,1024]{1,0:T(8,128)(2,1)S(1)}, bf16[16,1024]{1,0:T(8,128)(2,1)S(1)}, u32[]{:S(2)}, u32[]{:S(2)}) collective-permute-start(bf16[16,1024]{1,0:T(8,128)(2,1)S(1)} %get-tuple-element.34.own_ref), channel_id=1, source_target_pairs={{0,744},{24,0},{48,24},{72,48},{96,72},{120,96},{144,120},{168,144... | collective-permute-start | bytes 98312 | tf_op jit(solution)/shard_map/ppermute | solution.py:289
  60.9 19.2 %all-to-all-start.1 = ((bf16[8,11,16,128]{3,2,1,0:T(8,128)(2,1)}), bf16[8,11,16,128]{3,2,1,0:T(8,128)(2,1)S(1)}, u32[]{:S(2)}, u32[]{:S(2)}) async-start(bf16[8,11,16,128]{3,2,1,0:T(8,128)(2,1)} %get-tuple-element.37), calls=%async_computation.1 | async-start | bytes 720896 | tf_op jit(solution)/shard_map/all_to_all | solution.py:316
  68.8 3.6 %collective-permute-start.5 = (bf16[4,3,16,1024]{3,2,1,0:T(8,128)(2,1)S(1)}, bf16[4,3,16,1024]{3,2,1,0:T(8,128)(2,1)S(1)}, u32[]{:S(2)}, u32[]{:S(2)}) collective-permute-start(bf16[4,3,16,1024]{3,2,1,0:T(8,128)(2,1)S(1)} %get-tuple-element.43), channel_id=1, source_target_pairs={{0,1},{1,0},{2,3},{3,2},{4,5},{5,4},{6,7},{7,6},{8,9},{9,8},{10,11... | collective-permute-start | bytes 1179656 | tf_op jit(solution)/shard_map/ppermute | solution.py:279
  72.5 13.9 %collective-permute-start.6 = (bf16[2,3,16,1024]{3,2,1,0:T(8,128)(2,1)S(1)}, bf16[2,3,16,1024]{3,2,1,0:T(8,128)(2,1)S(1)}, u32[]{:S(2)}, u32[]{:S(2)}) collective-permute-start(bf16[2,3,16,1024]{3,2,1,0:T(8,128)(2,1)S(1)} %get-tuple-element.46), channel_id=1, source_target_pairs={{0,6},{6,0},{12,18},{18,12},{1,7},{7,1},{13,19},{19,13},{2,8},{8,2... | collective-permute-start | bytes 589832 | tf_op jit(solution)/shard_map/ppermute | solution.py:322
  80.7 16.8 %all-to-all-start.2 = ((bf16[4,11,16,128]{3,2,1,0:T(8,128)(2,1)}), bf16[4,11,16,128]{3,2,1,0:T(8,128)(2,1)S(1)}, u32[]{:S(2)}, u32[]{:S(2)}) async-start(bf16[4,11,16,128]{3,2,1,0:T(8,128)(2,1)} %total.2), calls=%async_computation.2 | async-start | bytes 360448 | tf_op jit(solution)/shard_map/all_to_all | solution.py:321
  86.5 16.6 %collective-permute-start.7 = (bf16[2,16,1024]{2,1,0:T(8,128)(2,1)S(1)}, bf16[2,16,1024]{2,1,0:T(8,128)(2,1)S(1)}, u32[]{:S(2)}, u32[]{:S(2)}) collective-permute-start(bf16[2,16,1024]{2,1,0:T(8,128)(2,1)S(1)} %get-tuple-element.51), channel_id=1, source_target_pairs={{0,2},{2,4},{4,0},{1,3},{3,5},{5,1},{6,8},{8,10},{10,6},{7,9},{9,1... | collective-permute-start | bytes 196616 | tf_op jit(solution)/shard_map/ppermute | solution.py:325
  88.4 14.6 %collective-permute-start.8 = (bf16[2,16,1024]{2,1,0:T(8,128)(2,1)S(1)}, bf16[2,16,1024]{2,1,0:T(8,128)(2,1)S(1)}, u32[]{:S(2)}, u32[]{:S(2)}) collective-permute-start(bf16[2,16,1024]{2,1,0:T(8,128)(2,1)S(1)} %get-tuple-element.52), channel_id=1, source_target_pairs={{0,4},{2,0},{4,2},{1,5},{3,1},{5,3},{6,10},{8,6},{10,8},{7,11},{9,... | collective-permute-start | bytes 196616 | tf_op jit(solution)/shard_map/ppermute | solution.py:326
  98.3 16.3 %all-to-all-start.3 = ((bf16[8,11,16,128]{3,2,1,0:T(8,128)(2,1)}), bf16[8,11,16,128]{3,2,1,0:T(8,128)(2,1)S(1)}, u32[]{:S(2)}, u32[]{:S(2)}) async-start(bf16[8,11,16,128]{3,2,1,0:T(8,128)(2,1)} %total.3), calls=%async_computation.3 | async-start | bytes 720896 | tf_op jit(solution)/shard_map/all_to_all | solution.py:327
  103.1 7.3 %collective-permute-start.9 = (bf16[16,1024]{1,0:T(8,128)(2,1)S(1)}, bf16[16,1024]{1,0:T(8,128)(2,1)S(1)}, u32[]{:S(2)}, u32[]{:S(2)}) collective-permute-start(bf16[16,1024]{1,0:T(8,128)(2,1)S(1)} %fusion.5), channel_id=1, source_target_pairs={{0,12},{6,18},{12,0},{18,6},{1,13},{7,19},{13,1},{19,7},{2,14},{8,... | collective-permute-start | bytes 98312 | tf_op jit(solution)/shard_map/ppermute | solution.py:329

commit v9 on v8

--- a/solution.py
+++ b/solution.py
@@ -186,12 +186,12 @@
             z_slot = lax.rem(z_at - z_at_ref[0] + 3, 3)
             at = (x_at * 3 + z_at) * 2 * rows
             even, odd = partial[at : at + rows], partial[at + rows : at + 2 * rows]
-            keep_ref[x_slot, z_slot] = jnp.where(first, even, odd)
-            send_ref[x_slot, z_slot] = jnp.where(first, odd, even).astype(jnp.bfloat16)
+            keep_ref[z_slot, x_slot] = jnp.where(first, even, odd)
+            send_ref[z_slot, x_slot] = jnp.where(first, odd, even).astype(jnp.bfloat16)
 
 
 def dgrad(core, x_at, z_at, k_rows, own, halo):
-    shape = (4, 3, k_rows.shape[0] // TAPS, own.shape[1])
+    shape = (3, 4, k_rows.shape[0] // TAPS, own.shape[1])
     return pl.pallas_call(
         dgrad_kernel,
         out_shape=[
@@ -236,23 +236,21 @@
     )(terms)
 
 
-def halve_kernel(kept_ref, came_ref, keep_ref, send_ref):
-    for at in range(keep_ref.shape[0]):
-        keep_ref[at] = kept_ref[2 * at] + came_ref[2 * at].astype(jnp.float32)
-        total = kept_ref[2 * at + 1] + came_ref[2 * at + 1].astype(jnp.float32)
-        send_ref[at] = total.astype(jnp.bfloat16)
-
-
-def halve(kept, came):
-    shape = (kept.shape[0] // 2,) + kept.shape[1:]
-    return pl.pallas_call(
-        halve_kernel,
-        out_shape=[
-            jax.ShapeDtypeStruct(shape, jnp.float32),
-            jax.ShapeDtypeStruct(shape, jnp.bfloat16),
-        ],
-        compiler_params=pltpu.CompilerParams(vmem_limit_bytes=VMEM_LIMIT),
-        name="halve",
+def part_kernel(kept_ref, came_ref, here_ref, after_ref, before_ref):
+    here_ref[...] = kept_ref[0] + came_ref[0].astype(jnp.float32)
+    after_ref[...] = (kept_ref[1] + came_ref[1].astype(jnp.float32)).astype(jnp.bfloat16)
+    before_ref[...] = (kept_ref[2] + came_ref[2].astype(jnp.float32)).astype(jnp.bfloat16)
+
+
+def part(kept, came):
+    return pl.pallas_call(
+        part_kernel,
+        out_shape=[
+            jax.ShapeDtypeStruct(kept.shape[1:], kind)
+            for kind in (jnp.float32, jnp.bfloat16, jnp.bfloat16)
+        ],
+        compiler_params=pltpu.CompilerParams(vmem_limit_bytes=VMEM_LIMIT),
+        name="part",
     )(kept, came)
 
 
@@ -310,22 +308,21 @@
 
     above, below = shift(grad_pre, -1), shift(grad_pre, 1)
     own_units, own_stack, x = wgrad_own(core, grad_pre, mine, other)
-    ys, zs = lax.axis_size("y"), lax.axis_size("zh")
-    wide, halo_stack = wgrad_halo(above, below, x, own_units, ys)
+    wide, halo_stack = wgrad_halo(above, below, x, own_units, depths)
     scale = 1.0 / math.sqrt(UNIV * DEPTH * SIDE * SIDE)
-    over_y = lax.all_to_all(wide, "y", 0, 0)
+    terms = lax.all_to_all(wide, DEP, 0, 0)
 
     keep, send = dgrad(core, x_at, z_at, k_rows, own_stack, halo_stack)
-    keep, send = halve(keep, swap_cores(send))
-    over_y, keep = lax.optimization_barrier((over_y, keep))
-    over_z = lax.all_to_all(total_spread(over_y, 1.0, zs), "zh", 0, 0)
-    total = keep + lax.ppermute(send, "x", [(i, i ^ 1) for i in range(4)]).astype(jnp.float32)
-    after, before = total[:, 1].astype(jnp.bfloat16), total[:, 2].astype(jnp.bfloat16)
-    over_z, _ = lax.optimization_barrier((over_z, (after, before)))
+    here, after, before = part(keep, swap_cores(send))
     after = lax.ppermute(after, "zl", [(i, (i + 1) % 3) for i in range(3)])
     before = lax.ppermute(before, "zl", [(i, (i + 2) % 3) for i in range(3)])
-    units = lax.all_to_all(total_spread(over_z, scale, ys), "y", 0, 0)
-    total = total[:, 0] + after.astype(jnp.float32) + before.astype(jnp.float32)
+    total = here + after.astype(jnp.float32) + before.astype(jnp.float32)
+    total = total.reshape(2, 2, rows, cells)
+    step = total[:, 1].astype(jnp.bfloat16)
+    terms, _ = lax.optimization_barrier((terms, step))
+    units = lax.all_to_all(total_spread(terms, scale, depths), DEP, 0, 0)
+    step = lax.ppermute(step, "x", [(i, i ^ 1) for i in range(4)])
+    total = total[:, 0] + step.astype(jnp.float32)
     step = lax.ppermute(total[1].astype(jnp.bfloat16), "x", [(i, i ^ 2) for i in range(4)])
     grad_volume = (total[0] + step.astype(jnp.float32)).astype(jnp.bfloat16)
     all_taps = unpack(units, kernel.shape[-1])

time: 116 us -> 128 us (1.10)
  the two profiles are of different devices: /device:TPU:2 before, /device:TPU:136 now
where the time goes in v9:
time: 128 us
  starting transfers between devices  70.3 us (55%)
  waiting for transfers between devices  47.8 us (37%)
  Pallas kernels  6.38 us (5%)
  local copies, waits for them, and re-layouts  1.57 us (1%)
    ppermute x4, starting transfers between devices, shift(): lax.ppermute(block, DEP, [(i, (i + step) % depths) for i in range(depths)])  24.3 us
    all_to_all x1, starting transfers between devices, body(): units = lax.all_to_all(total_spread(terms, scale, depths), DEP, 0, 0)  13.6 us
    ppermute x4, waiting for transfers between devices, shift(): lax.ppermute(block, DEP, [(i, (i + step) % depths) for i in range(depths)])  9.78 us
    all_to_all x1, starting transfers between devices, body(): terms = lax.all_to_all(wide, DEP, 0, 0)  9.48 us
    all_to_all x1, waiting for transfers between devices, body(): units = lax.all_to_all(total_spread(terms, scale, depths), DEP, 0, 0)  8.67 us
    all_to_all x1, waiting for transfers between devices, body(): mine = lax.all_to_all(copies(own), CHIPS, 0, 0)  8.62 us
    all_to_all x1, starting transfers between devices, body(): mine = lax.all_to_all(copies(own), CHIPS, 0, 0)  6.79 us
    ppermute x1, starting transfers between devices, body(): after = lax.ppermute(after, 'zl', [(i, (i + 1) % 3) for i in range(3)])  5.81 us
  transfers between devices with their start and end apart: 13, of which 11 were waited for; matrix products, arithmetic and copies ran while one was open for 1% of the time, Pallas kernels for 1%

profile of v9, /device:TPU:136, one launch (start us, length us, event | category | flops | bytes accessed | tf_op | source)
XLA Modules:
  0.0 127.5 jit_solution(8411116641882398345)
XLA Ops:
  0.6 1.5 %broadcast_in_dim.8 = bf16[12,16,1024]{2,1,0:T(8,128)(2,1)} broadcast(bf16[16,1024]{1,0:T(8,128)(2,1)} %bitcast.39), dimensions={1,2} | broadcast | bytes 425984 | tf_op jit(solution)/shard_map/broadcast_in_dim | solution.py:297
  2.2 0.0 copy-start
  2.2 6.8 %all-to-all-start = ((bf16[12,16,1024]{2,1,0:T(8,128)(2,1)}), bf16[12,16,1024]{2,1,0:T(8,128)(2,1)S(1)}, u32[]{:S(2)}, u32[]{:S(2)}) async-start(bf16[12,16,1024]{2,1,0:T(8,128)(2,1)} %broadcast_in_dim.8), calls=%async_computation | async-start | bytes 786432 | tf_op jit(solution)/shard_map/all_to_all | solution.py:299
  9.0 8.6 %all-to-all-done.mine_ref = bf16[12,16,1024]{2,1,0:T(8,128)(2,1)S(1)} async-done(((bf16[12,16,1024]{2,1,0:T(8,128)(2,1)}), bf16[12,16,1024]{2,1,0:T(8,128)(2,1)S(1)}, u32[]{:S(2)}, u32[]{:S(2)}) %all-to-all-start) | async-done | bytes 393248 | tf_op jit(solution)/shard_map/all_to_all | solution.py:299
  17.6 0.0 copy-start.1
  17.6 2.0 %collective-permute-start = (bf16[12,16,1024]{2,1,0:T(8,128)(2,1)S(1)}, bf16[12,16,1024]{2,1,0:T(8,128)(2,1)S(1)}, u32[]{:S(2)}, u32[]{:S(2)}) collective-permute-start(bf16[12,16,1024]{2,1,0:T(8,128)(2,1)S(1)} %all-to-all-done.mine_ref), channel_id=1, source_target_pairs={{0,1},{1,0},{2,3},{3,2},{4,5},{5,4},{6,7},{7,6},{8,9},{9,8},{10,11... | collective-permute-start | bytes 1179656 | tf_op jit(solution)/shard_map/ppermute | solution.py:277
  19.6 1.7 %collective-permute-done.other_ref = bf16[12,16,1024]{2,1,0:T(8,128)(2,1)S(1)} collective-permute-done((bf16[12,16,1024]{2,1,0:T(8,128)(2,1)S(1)}, bf16[12,16,1024]{2,1,0:T(8,128)(2,1)S(1)}, u32[]{:S(2)}, u32[]{:S(2)}) %collective-permute-start) | collective-permute-done | bytes 393248 | tf_op jit(solution)/shard_map/ppermute | solution.py:277
  21.3 0.0 copy-done
  21.3 0.9 conv.1
  22.2 10.3 %collective-permute-start.1 = (bf16[16,1024]{1,0:T(8,128)(2,1)S(1)}, bf16[16,1024]{1,0:T(8,128)(2,1)S(1)}, u32[]{:S(2)}, u32[]{:S(2)}) collective-permute-start(bf16[16,1024]{1,0:T(8,128)(2,1)S(1)} %get-tuple-element.29), channel_id=1, source_target_pairs={{0,24},{24,48},{48,72},{72,96},{96,120},{120,144},{144,168},{168,1... | collective-permute-start | bytes 98312 | tf_op jit(solution)/shard_map/ppermute | solution.py:287
  32.6 4.3 %collective-permute-start.2 = (bf16[16,1024]{1,0:T(8,128)(2,1)S(1)}, bf16[16,1024]{1,0:T(8,128)(2,1)S(1)}, u32[]{:S(2)}, u32[]{:S(2)}) collective-permute-start(bf16[16,1024]{1,0:T(8,128)(2,1)S(1)} %get-tuple-element.30), channel_id=1, source_target_pairs={{0,744},{24,0},{48,24},{72,48},{96,72},{120,96},{144,120},{168,144... | collective-permute-start | bytes 98312 | tf_op jit(solution)/shard_map/ppermute | solution.py:287
  36.8 0.1 collective-permute-done.1.low_ref
  36.9 4.5 %collective-permute-done.2.high_ref = bf16[16,1024]{1,0:T(8,128)(2,1)S(1)} collective-permute-done((bf16[16,1024]{1,0:T(8,128)(2,1)S(1)}, bf16[16,1024]{1,0:T(8,128)(2,1)S(1)}, u32[]{:S(2)}, u32[]{:S(2)}) %collective-permute-start.2) | collective-permute-done | bytes 32800 | tf_op jit(solution)/shard_map/ppermute | solution.py:287
  41.4 0.0 copy-done.1
  41.4 0.6 activate.1
  42.0 6.7 %collective-permute-start.4 = (bf16[16,1024]{1,0:T(8,128)(2,1)S(1)}, bf16[16,1024]{1,0:T(8,128)(2,1)S(1)}, u32[]{:S(2)}, u32[]{:S(2)}) collective-permute-start(bf16[16,1024]{1,0:T(8,128)(2,1)S(1)} %get-tuple-element.35.own_ref), channel_id=1, source_target_pairs={{0,24},{24,48},{48,72},{72,96},{96,120},{120,144},{144,168},{168,1... | collective-permute-start | bytes 98312 | tf_op jit(solution)/shard_map/ppermute | solution.py:287
  48.8 3.0 %collective-permute-start.3 = (bf16[16,1024]{1,0:T(8,128)(2,1)S(1)}, bf16[16,1024]{1,0:T(8,128)(2,1)S(1)}, u32[]{:S(2)}, u32[]{:S(2)}) collective-permute-start(bf16[16,1024]{1,0:T(8,128)(2,1)S(1)} %get-tuple-element.35.own_ref), channel_id=1, source_target_pairs={{0,744},{24,0},{48,24},{72,48},{96,72},{120,96},{144,120},{168,144... | collective-permute-start | bytes 98312 | tf_op jit(solution)/shard_map/ppermute | solution.py:287
  51.8 0.6 wgrad_own.1
  52.3 0.0 collective-permute-done.4.below_ref
  52.4 5.2 %collective-permute-done.3.above_ref = bf16[16,1024]{1,0:T(8,128)(2,1)S(1)} collective-permute-done((bf16[16,1024]{1,0:T(8,128)(2,1)S(1)}, bf16[16,1024]{1,0:T(8,128)(2,1)S(1)}, u32[]{:S(2)}, u32[]{:S(2)}) %collective-permute-start.3) | collective-permute-done | bytes 32800 | tf_op jit(solution)/shard_map/ppermute | solution.py:287
  57.6 1.7 %wgrad_halo.1 = (bf16[32,3,16,128]{3,2,1,0:T(8,128)(2,1)}, bf16[288,1024]{1,0:T(8,128)(2,1)S(1)}) custom-call(bf16[16,1024]{1,0:T(8,128)(2,1)S(1)} %collective-permute-done.3.above_ref, bf16[16,1024]{1,0:T(8,128)(2,1)S(1)} %collective-permute-done.4.below_ref, bf16[12,2,16,1024]{3,2,1,0:T(8,128)(2,1)S(1)} %get-tuple-element.37.x_ref, ...), custom_call_target="tpu_custom_call" | custom-call | tf_op jit(solution)/shard_map/wgrad_halo/pallas_call | solution.py:159
  59.3 9.5 %all-to-all-start.1 = ((bf16[32,3,16,128]{3,2,1,0:T(8,128)(2,1)}), bf16[32,3,16,128]{3,2,1,0:T(8,128)(2,1)S(1)}, u32[]{:S(2)}, u32[]{:S(2)}) async-start(bf16[32,3,16,128]{3,2,1,0:T(8,128)(2,1)} %get-tuple-element.45), calls=%async_computation.1 | async-start | bytes 786432 | tf_op jit(solution)/shard_map/all_to_all | solution.py:313
  68.8 0.8 dgrad.1
  69.6 1.9 %collective-permute-start.5 = (bf16[3,4,16,1024]{3,2,1,0:T(8,128)(2,1)S(1)}, bf16[3,4,16,1024]{3,2,1,0:T(8,128)(2,1)S(1)}, u32[]{:S(2)}, u32[]{:S(2)}) collective-permute-start(bf16[3,4,16,1024]{3,2,1,0:T(8,128)(2,1)S(1)} %get-tuple-element.41), channel_id=1, source_target_pairs={{0,1},{1,0},{2,3},{3,2},{4,5},{5,4},{6,7},{7,6},{8,9},{9,8},{10,11... | collective-permute-start | bytes 1179656 | tf_op jit(solution)/shard_map/ppermute | solution.py:277
  71.5 1.7 %collective-permute-done.5.came_ref = bf16[3,4,16,1024]{3,2,1,0:T(8,128)(2,1)S(1)} collective-permute-done((bf16[3,4,16,1024]{3,2,1,0:T(8,128)(2,1)S(1)}, bf16[3,4,16,1024]{3,2,1,0:T(8,128)(2,1)S(1)}, u32[]{:S(2)}, u32[]{:S(2)}) %collective-permute-start.5) | collective-permute-done | bytes 393248 | tf_op jit(solution)/shard_map/ppermute | solution.py:277
  73.2 0.1 part.1
  73.3 5.8 %collective-permute-start.6 = (bf16[4,16,1024]{2,1,0:T(8,128)(2,1)S(1)}, bf16[4,16,1024]{2,1,0:T(8,128)(2,1)S(1)}, u32[]{:S(2)}, u32[]{:S(2)}) collective-permute-start(bf16[4,16,1024]{2,1,0:T(8,128)(2,1)S(1)} %get-tuple-element.43), channel_id=1, source_target_pairs={{0,2},{2,4},{4,0},{1,3},{3,5},{5,1},{6,8},{8,10},{10,6},{7,9},{9,1... | collective-permute-start | bytes 393224 | tf_op jit(solution)/shard_map/ppermute | solution.py:317
  79.1 1.9 %collective-permute-start.7 = (bf16[4,16,1024]{2,1,0:T(8,128)(2,1)S(1)}, bf16[4,16,1024]{2,1,0:T(8,128)(2,1)S(1)}, u32[]{:S(2)}, u32[]{:S(2)}) collective-permute-start(bf16[4,16,1024]{2,1,0:T(8,128)(2,1)S(1)} %get-tuple-element.44), channel_id=1, source_target_pairs={{0,4},{2,0},{4,2},{1,5},{3,1},{5,3},{6,10},{8,6},{10,8},{7,11},{9,... | collective-permute-start | bytes 393224 | tf_op jit(solution)/shard_map/ppermute | solution.py:318
  81.0 5.2 %collective-permute-done.6 = bf16[4,16,1024]{2,1,0:T(8,128)(2,1)S(1)} collective-permute-done((bf16[4,16,1024]{2,1,0:T(8,128)(2,1)S(1)}, bf16[4,16,1024]{2,1,0:T(8,128)(2,1)S(1)}, u32[]{:S(2)}, u32[]{:S(2)}) %collective-permute-start.6) | collective-permute-done | bytes 131104 | tf_op jit(solution)/shard_map/ppermute | solution.py:317
  86.2 3.1 %collective-permute-done.7 = bf16[4,16,1024]{2,1,0:T(8,128)(2,1)S(1)} collective-permute-done((bf16[4,16,1024]{2,1,0:T(8,128)(2,1)S(1)}, bf16[4,16,1024]{2,1,0:T(8,128)(2,1)S(1)}, u32[]{:S(2)}, u32[]{:S(2)}) %collective-permute-start.7) | collective-permute-done | bytes 131104 | tf_op jit(solution)/shard_map/ppermute | solution.py:318
  89.4 0.0 all-to-all-done.1.terms_ref
  89.4 0.8 total.1
  90.2 13.6 %all-to-all-start.2 = ((bf16[32,3,16,128]{3,2,1,0:T(8,128)(2,1)}), bf16[32,3,16,128]{3,2,1,0:T(8,128)(2,1)S(1)}, u32[]{:S(2)}, u32[]{:S(2)}) async-start(bf16[32,3,16,128]{3,2,1,0:T(8,128)(2,1)} %total.1), calls=%async_computation.2 | async-start | bytes 786432 | tf_op jit(solution)/shard_map/all_to_all | solution.py:323
  103.8 1.9 %collective-permute-start.8 = (bf16[2,16,1024]{2,1,0:T(8,128)(2,1)S(1)}, bf16[2,16,1024]{2,1,0:T(8,128)(2,1)S(1)}, u32[]{:S(2)}, u32[]{:S(2)}) collective-permute-start(bf16[2,16,1024]{2,1,0:T(8,128)(2,1)S(1)} %fusion.1), channel_id=1, source_target_pairs={{0,6},{6,0},{12,18},{18,12},{1,7},{7,1},{13,19},{19,13},{2,8},{8,2... | collective-permute-start | bytes 196616 | tf_op jit(solution)/shard_map/ppermute | solution.py:324
  105.8 4.2 %collective-permute-done.8 = bf16[2,16,1024]{2,1,0:T(8,128)(2,1)S(1)} collective-permute-done((bf16[2,16,1024]{2,1,0:T(8,128)(2,1)S(1)}, bf16[2,16,1024]{2,1,0:T(8,128)(2,1)S(1)}, u32[]{:S(2)}, u32[]{:S(2)}) %collective-permute-start.8) | collective-permute-done | bytes 65568 | tf_op jit(solution)/shard_map/ppermute | solution.py:324
  110.0 2.5 %collective-permute-start.9 = (bf16[16,1024]{1,0:T(8,128)(2,1)S(1)}, bf16[16,1024]{1,0:T(8,128)(2,1)S(1)}, u32[]{:S(2)}, u32[]{:S(2)}) collective-permute-start(bf16[16,1024]{1,0:T(8,128)(2,1)S(1)} %fusion.5), channel_id=1, source_target_pairs={{0,12},{6,18},{12,0},{18,6},{1,13},{7,19},{13,1},{19,7},{2,14},{8,... | collective-permute-start | bytes 98312 | tf_op jit(solution)/shard_map/ppermute | solution.py:326
  112.5 4.8 %collective-permute-done.9 = bf16[16,1024]{1,0:T(8,128)(2,1)S(1)} collective-permute-done((bf16[16,1024]{1,0:T(8,128)(2,1)S(1)}, bf16[16,1024]{1,0:T(8,128)(2,1)S(1)}, u32[]{:S(2)}, u32[]{:S(2)}) %collective-permute-start.9) | collective-permute-done | bytes 32800 | tf_op jit(solution)/shard_map/ppermute | solution.py:326
  117.3 0.6 fusion.4
  118.0 8.7 %all-to-all-done.2.units_ref = bf16[32,3,16,128]{3,2,1,0:T(8,128)(2,1)S(1)} async-done(((bf16[32,3,16,128]{3,2,1,0:T(8,128)(2,1)}), bf16[32,3,16,128]{3,2,1,0:T(8,128)(2,1)S(1)}, u32[]{:S(2)}, u32[]{:S(2)}) %all-to-all-start.2) | async-done | bytes 393248 | tf_op jit(solution)/shard_map/all_to_all | solution.py:323
  126.6 0.9 unpack.1
  (4 shorter events, 0.1 us)
Async XLA Ops:
  2.2 19.2 %copy-start = (bf16[16,3,3,3,384]{4,0,3,2,1:T(8,128)(2,1)S(1)}, bf16[16,3,3,3,384]{4,0,3,2,1:T(8,128)(2,1)}, u32[]{:S(2)}) copy-start(bf16[16,3,3,3,384]{4,0,3,2,1:T(8,128)(2,1)} %param.4) | copy-start | bytes 995332
  2.2 15.4 %all-to-all-start = ((bf16[12,16,1024]{2,1,0:T(8,128)(2,1)}), bf16[12,16,1024]{2,1,0:T(8,128)(2,1)S(1)}, u32[]{:S(2)}, u32[]{:S(2)}) async-start(bf16[12,16,1024]{2,1,0:T(8,128)(2,1)} %broadcast_in_dim.8), calls=%async_computation | async-start | bytes 786432 | tf_op jit(solution)/shard_map/all_to_all | solution.py:299
  17.6 23.8 %copy-start.1 = (bf16[1,1,16,1024]{3,2,1,0:T(8,128)(2,1)S(1)}, bf16[1,1,16,1024]{3,2,1,0:T(8,128)(2,1)}, u32[]{:S(2)}) copy-start(bf16[1,1,16,1024]{3,2,1,0:T(8,128)(2,1)} %param.5) | copy-start | bytes 98308
  17.6 3.7 %collective-permute-start = (bf16[12,16,1024]{2,1,0:T(8,128)(2,1)S(1)}, bf16[12,16,1024]{2,1,0:T(8,128)(2,1)S(1)}, u32[]{:S(2)}, u32[]{:S(2)}) collective-permute-start(bf16[12,16,1024]{2,1,0:T(8,128)(2,1)S(1)} %all-to-all-done.mine_ref), channel_id=1, source_target_pairs={{0,1},{1,0},{2,3},{3,2},{4,5},{5,4},{6,7},{7,6},{8,9},{9,8},{10,11... | collective-permute-start | bytes 1179656 | tf_op jit(solution)/shard_map/ppermute | solution.py:277
  22.2 14.6 %collective-permute-start.1 = (bf16[16,1024]{1,0:T(8,128)(2,1)S(1)}, bf16[16,1024]{1,0:T(8,128)(2,1)S(1)}, u32[]{:S(2)}, u32[]{:S(2)}) collective-permute-start(bf16[16,1024]{1,0:T(8,128)(2,1)S(1)} %get-tuple-element.29), channel_id=1, source_target_pairs={{0,24},{24,48},{48,72},{72,96},{96,120},{120,144},{144,168},{168,1... | collective-permute-start | bytes 98312 | tf_op jit(solution)/shard_map/ppermute | solution.py:287
  32.6 8.8 %collective-permute-start.2 = (bf16[16,1024]{1,0:T(8,128)(2,1)S(1)}, bf16[16,1024]{1,0:T(8,128)(2,1)S(1)}, u32[]{:S(2)}, u32[]{:S(2)}) collective-permute-start(bf16[16,1024]{1,0:T(8,128)(2,1)S(1)} %get-tuple-element.30), channel_id=1, source_target_pairs={{0,744},{24,0},{48,24},{72,48},{96,72},{120,96},{144,120},{168,144... | collective-permute-start | bytes 98312 | tf_op jit(solution)/shard_map/ppermute | solution.py:287
  42.0 10.3 %collective-permute-start.4 = (bf16[16,1024]{1,0:T(8,128)(2,1)S(1)}, bf16[16,1024]{1,0:T(8,128)(2,1)S(1)}, u32[]{:S(2)}, u32[]{:S(2)}) collective-permute-start(bf16[16,1024]{1,0:T(8,128)(2,1)S(1)} %get-tuple-element.35.own_ref), channel_id=1, source_target_pairs={{0,24},{24,48},{48,72},{72,96},{96,120},{120,144},{144,168},{168,1... | collective-permute-start | bytes 98312 | tf_op jit(solution)/shard_map/ppermute | solution.py:287
  48.8 8.8 %collective-permute-start.3 = (bf16[16,1024]{1,0:T(8,128)(2,1)S(1)}, bf16[16,1024]{1,0:T(8,128)(2,1)S(1)}, u32[]{:S(2)}, u32[]{:S(2)}) collective-permute-start(bf16[16,1024]{1,0:T(8,128)(2,1)S(1)} %get-tuple-element.35.own_ref), channel_id=1, source_target_pairs={{0,744},{24,0},{48,24},{72,48},{96,72},{120,96},{144,120},{168,144... | collective-permute-start | bytes 98312 | tf_op jit(solution)/shard_map/ppermute | solution.py:287
  59.3 30.1 %all-to-all-start.1 = ((bf16[32,3,16,128]{3,2,1,0:T(8,128)(2,1)}), bf16[32,3,16,128]{3,2,1,0:T(8,128)(2,1)S(1)}, u32[]{:S(2)}, u32[]{:S(2)}) async-start(bf16[32,3,16,128]{3,2,1,0:T(8,128)(2,1)} %get-tuple-element.45), calls=%async_computation.1 | async-start | bytes 786432 | tf_op jit(solution)/shard_map/all_to_all | solution.py:313
  69.6 3.6 %collective-permute-start.5 = (bf16[3,4,16,1024]{3,2,1,0:T(8,128)(2,1)S(1)}, bf16[3,4,16,1024]{3,2,1,0:T(8,128)(2,1)S(1)}, u32[]{:S(2)}, u32[]{:S(2)}) collective-permute-start(bf16[3,4,16,1024]{3,2,1,0:T(8,128)(2,1)S(1)} %get-tuple-element.41), channel_id=1, source_target_pairs={{0,1},{1,0},{2,3},{3,2},{4,5},{5,4},{6,7},{7,6},{8,9},{9,8},{10,11... | collective-permute-start | bytes 1179656 | tf_op jit(solution)/shard_map/ppermute | solution.py:277
  73.3 13.0 %collective-permute-start.6 = (bf16[4,16,1024]{2,1,0:T(8,128)(2,1)S(1)}, bf16[4,16,1024]{2,1,0:T(8,128)(2,1)S(1)}, u32[]{:S(2)}, u32[]{:S(2)}) collective-permute-start(bf16[4,16,1024]{2,1,0:T(8,128)(2,1)S(1)} %get-tuple-element.43), channel_id=1, source_target_pairs={{0,2},{2,4},{4,0},{1,3},{3,5},{5,1},{6,8},{8,10},{10,6},{7,9},{9,1... | collective-permute-start | bytes 393224 | tf_op jit(solution)/shard_map/ppermute | solution.py:317
  79.1 10.2 %collective-permute-start.7 = (bf16[4,16,1024]{2,1,0:T(8,128)(2,1)S(1)}, bf16[4,16,1024]{2,1,0:T(8,128)(2,1)S(1)}, u32[]{:S(2)}, u32[]{:S(2)}) collective-permute-start(bf16[4,16,1024]{2,1,0:T(8,128)(2,1)S(1)} %get-tuple-element.44), channel_id=1, source_target_pairs={{0,4},{2,0},{4,2},{1,5},{3,1},{5,3},{6,10},{8,6},{10,8},{7,11},{9,... | collective-permute-start | bytes 393224 | tf_op jit(solution)/shard_map/ppermute | solution.py:318
  90.2 36.5 %all-to-all-start.2 = ((bf16[32,3,16,128]{3,2,1,0:T(8,128)(2,1)}), bf16[32,3,16,128]{3,2,1,0:T(8,128)(2,1)S(1)}, u32[]{:S(2)}, u32[]{:S(2)}) async-start(bf16[32,3,16,128]{3,2,1,0:T(8,128)(2,1)} %total.1), calls=%async_computation.2 | async-start | bytes 786432 | tf_op jit(solution)/shard_map/all_to_all | solution.py:323
  103.8 6.2 %collective-permute-start.8 = (bf16[2,16,1024]{2,1,0:T(8,128)(2,1)S(1)}, bf16[2,16,1024]{2,1,0:T(8,128)(2,1)S(1)}, u32[]{:S(2)}, u32[]{:S(2)}) collective-permute-start(bf16[2,16,1024]{2,1,0:T(8,128)(2,1)S(1)} %fusion.1), channel_id=1, source_target_pairs={{0,6},{6,0},{12,18},{18,12},{1,7},{7,1},{13,19},{19,13},{2,8},{8,2... | collective-permute-start | bytes 196616 | tf_op jit(solution)/shard_map/ppermute | solution.py:324
  110.0 7.3 %collective-permute-start.9 = (bf16[16,1024]{1,0:T(8,128)(2,1)S(1)}, bf16[16,1024]{1,0:T(8,128)(2,1)S(1)}, u32[]{:S(2)}, u32[]{:S(2)}) collective-permute-start(bf16[16,1024]{1,0:T(8,128)(2,1)S(1)} %fusion.5), channel_id=1, source_target_pairs={{0,12},{6,18},{12,0},{18,6},{1,13},{7,19},{13,1},{19,7},{2,14},{8,... | collective-permute-start | bytes 98312 | tf_op jit(solution)/shard_map/ppermute | solution.py:326

commit v10 on v8

--- a/solution.py
+++ b/solution.py
@@ -236,26 +236,6 @@
     )(terms)
 
 
-def halve_kernel(kept_ref, came_ref, keep_ref, send_ref):
-    for at in range(keep_ref.shape[0]):
-        keep_ref[at] = kept_ref[2 * at] + came_ref[2 * at].astype(jnp.float32)
-        total = kept_ref[2 * at + 1] + came_ref[2 * at + 1].astype(jnp.float32)
-        send_ref[at] = total.astype(jnp.bfloat16)
-
-
-def halve(kept, came):
-    shape = (kept.shape[0] // 2,) + kept.shape[1:]
-    return pl.pallas_call(
-        halve_kernel,
-        out_shape=[
-            jax.ShapeDtypeStruct(shape, jnp.float32),
-            jax.ShapeDtypeStruct(shape, jnp.bfloat16),
-        ],
-        compiler_params=pltpu.CompilerParams(vmem_limit_bytes=VMEM_LIMIT),
-        name="halve",
-    )(kept, came)
-
-
 def unpack_kernel(units_ref, out_ref):
     per = units_ref.shape[1]
     columns = out_ref.shape[2] // LANES
@@ -316,8 +296,10 @@
     over_y = lax.all_to_all(wide, "y", 0, 0)
 
     keep, send = dgrad(core, x_at, z_at, k_rows, own_stack, halo_stack)
-    keep, send = halve(keep, swap_cores(send))
-    over_y, keep = lax.optimization_barrier((over_y, keep))
+    total = keep + swap_cores(send).astype(jnp.float32)
+    total = total.reshape(2, 2, 3, rows, cells)
+    keep, send = total[:, 0], total[:, 1].astype(jnp.bfloat16)
+    over_y, _ = lax.optimization_barrier((over_y, send))
     over_z = lax.all_to_all(total_spread(over_y, 1.0, zs), "zh", 0, 0)
     total = keep + lax.ppermute(send, "x", [(i, i ^ 1) for i in range(4)]).astype(jnp.float32)
     after, before = total[:, 1].astype(jnp.bfloat16), total[:, 2].astype(jnp.bfloat16)

time: 116 us -> 122 us (1.052)
  the two profiles are of different devices: /device:TPU:2 before, /device:TPU:8 now
where the time goes in v10:
time: 122 us
  starting transfers between devices  66.5 us (55%)
  waiting for transfers between devices  44.8 us (37%)
  Pallas kernels  6.97 us (6%)
  local copies, waits for them, and re-layouts  1.59 us (1%)
    ppermute x4, starting transfers between devices, shift(): lax.ppermute(block, DEP, [(i, (i + step) % depths) for i in range(depths)])  24.3 us
    all_to_all x1, waiting for transfers between devices, body(): mine = lax.all_to_all(copies(own), CHIPS, 0, 0)  10.9 us
    all_to_all x1, waiting for transfers between devices, body(): over_y = lax.all_to_all(wide, 'y', 0, 0)  10.7 us
    ppermute x4, waiting for transfers between devices, shift(): lax.ppermute(block, DEP, [(i, (i + step) % depths) for i in range(depths)])  8.9 us
    all_to_all x1, starting transfers between devices, body(): mine = lax.all_to_all(copies(own), CHIPS, 0, 0)  8.08 us
    all_to_all x1, starting transfers between devices, body(): over_y = lax.all_to_all(wide, 'y', 0, 0)  7.55 us
    all_to_all x1, starting transfers between devices, body(): over_z = lax.all_to_all(total_spread(over_y, 1.0, zs), 'zh', 0, 0)  6.08 us
    all_to_all x1, waiting for transfers between devices, body(): over_z = lax.all_to_all(total_spread(over_y, 1.0, zs), 'zh', 0, 0)  5.4 us
  transfers between devices with their start and end apart: 14, of which 8 were waited for; matrix products, arithmetic and copies ran while one was open for 1% of the time, Pallas kernels for 2%

profile of v10, /device:TPU:8, one launch (start us, length us, event | category | flops | bytes accessed | tf_op | source)
XLA Modules:
  0.0 121.5 jit_solution(12979505679469618217)
XLA Ops:
  0.6 1.5 %broadcast_in_dim.8 = bf16[12,16,1024]{2,1,0:T(8,128)(2,1)} broadcast(bf16[16,1024]{1,0:T(8,128)(2,1)} %bitcast.50), dimensions={1,2} | broadcast | bytes 425984 | tf_op jit(solution)/shard_map/broadcast_in_dim | solution.py:279
  2.2 0.0 copy-start
  2.2 8.1 %all-to-all-start = ((bf16[12,16,1024]{2,1,0:T(8,128)(2,1)}), bf16[12,16,1024]{2,1,0:T(8,128)(2,1)S(1)}, u32[]{:S(2)}, u32[]{:S(2)}) async-start(bf16[12,16,1024]{2,1,0:T(8,128)(2,1)} %broadcast_in_dim.8), calls=%async_computation | async-start | bytes 786432 | tf_op jit(solution)/shard_map/all_to_all | solution.py:281
  10.3 10.9 %all-to-all-done.mine_ref = bf16[12,16,1024]{2,1,0:T(8,128)(2,1)S(1)} async-done(((bf16[12,16,1024]{2,1,0:T(8,128)(2,1)}), bf16[12,16,1024]{2,1,0:T(8,128)(2,1)S(1)}, u32[]{:S(2)}, u32[]{:S(2)}) %all-to-all-start) | async-done | bytes 393248 | tf_op jit(solution)/shard_map/all_to_all | solution.py:281
  21.2 0.0 copy-start.1
  21.2 2.0 %collective-permute-start = (bf16[12,16,1024]{2,1,0:T(8,128)(2,1)S(1)}, bf16[12,16,1024]{2,1,0:T(8,128)(2,1)S(1)}, u32[]{:S(2)}, u32[]{:S(2)}) collective-permute-start(bf16[12,16,1024]{2,1,0:T(8,128)(2,1)S(1)} %all-to-all-done.mine_ref), channel_id=1, source_target_pairs={{0,1},{1,0},{2,3},{3,2},{4,5},{5,4},{6,7},{7,6},{8,9},{9,8},{10,11... | collective-permute-start | bytes 1179656 | tf_op jit(solution)/shard_map/ppermute | solution.py:259
  23.2 1.7 %collective-permute-done.other_ref = bf16[12,16,1024]{2,1,0:T(8,128)(2,1)S(1)} collective-permute-done((bf16[12,16,1024]{2,1,0:T(8,128)(2,1)S(1)}, bf16[12,16,1024]{2,1,0:T(8,128)(2,1)S(1)}, u32[]{:S(2)}, u32[]{:S(2)}) %collective-permute-start) | collective-permute-done | bytes 393248 | tf_op jit(solution)/shard_map/ppermute | solution.py:259
  24.9 0.0 copy-done
  24.9 0.9 conv.1
  25.8 10.3 %collective-permute-start.1 = (bf16[16,1024]{1,0:T(8,128)(2,1)S(1)}, bf16[16,1024]{1,0:T(8,128)(2,1)S(1)}, u32[]{:S(2)}, u32[]{:S(2)}) collective-permute-start(bf16[16,1024]{1,0:T(8,128)(2,1)S(1)} %get-tuple-element.27), channel_id=1, source_target_pairs={{0,24},{24,48},{48,72},{72,96},{96,120},{120,144},{144,168},{168,1... | collective-permute-start | bytes 98312 | tf_op jit(solution)/shard_map/ppermute | solution.py:269
  36.1 4.3 %collective-permute-start.2 = (bf16[16,1024]{1,0:T(8,128)(2,1)S(1)}, bf16[16,1024]{1,0:T(8,128)(2,1)S(1)}, u32[]{:S(2)}, u32[]{:S(2)}) collective-permute-start(bf16[16,1024]{1,0:T(8,128)(2,1)S(1)} %get-tuple-element.28), channel_id=1, source_target_pairs={{0,744},{24,0},{48,24},{72,48},{96,72},{120,96},{144,120},{168,144... | collective-permute-start | bytes 98312 | tf_op jit(solution)/shard_map/ppermute | solution.py:269
  40.4 0.0 collective-permute-done.1.low_ref
  40.4 5.2 %collective-permute-done.2.high_ref = bf16[16,1024]{1,0:T(8,128)(2,1)S(1)} collective-permute-done((bf16[16,1024]{1,0:T(8,128)(2,1)S(1)}, bf16[16,1024]{1,0:T(8,128)(2,1)S(1)}, u32[]{:S(2)}, u32[]{:S(2)}) %collective-permute-start.2) | collective-permute-done | bytes 32800 | tf_op jit(solution)/shard_map/ppermute | solution.py:269
  45.6 0.0 copy-done.1
  45.6 0.6 activate.1
  46.3 6.4 %collective-permute-start.4 = (bf16[16,1024]{1,0:T(8,128)(2,1)S(1)}, bf16[16,1024]{1,0:T(8,128)(2,1)S(1)}, u32[]{:S(2)}, u32[]{:S(2)}) collective-permute-start(bf16[16,1024]{1,0:T(8,128)(2,1)S(1)} %get-tuple-element.33.own_ref), channel_id=1, source_target_pairs={{0,24},{24,48},{48,72},{72,96},{96,120},{120,144},{144,168},{168,1... | collective-permute-start | bytes 98312 | tf_op jit(solution)/shard_map/ppermute | solution.py:269
  52.6 3.4 %collective-permute-start.3 = (bf16[16,1024]{1,0:T(8,128)(2,1)S(1)}, bf16[16,1024]{1,0:T(8,128)(2,1)S(1)}, u32[]{:S(2)}, u32[]{:S(2)}) collective-permute-start(bf16[16,1024]{1,0:T(8,128)(2,1)S(1)} %get-tuple-element.33.own_ref), channel_id=1, source_target_pairs={{0,744},{24,0},{48,24},{72,48},{96,72},{120,96},{144,120},{168,144... | collective-permute-start | bytes 98312 | tf_op jit(solution)/shard_map/ppermute | solution.py:269
  56.0 0.5 wgrad_own.1
  56.6 0.0 collective-permute-done.4.below_ref
  56.6 3.7 %collective-permute-done.3.above_ref = bf16[16,1024]{1,0:T(8,128)(2,1)S(1)} collective-permute-done((bf16[16,1024]{1,0:T(8,128)(2,1)S(1)}, bf16[16,1024]{1,0:T(8,128)(2,1)S(1)}, u32[]{:S(2)}, u32[]{:S(2)}) %collective-permute-start.3) | collective-permute-done | bytes 32800 | tf_op jit(solution)/shard_map/ppermute | solution.py:269
  60.3 1.7 %wgrad_halo.1 = (bf16[8,11,16,128]{3,2,1,0:T(8,128)(2,1)}, bf16[288,1024]{1,0:T(8,128)(2,1)S(1)}) custom-call(bf16[16,1024]{1,0:T(8,128)(2,1)S(1)} %collective-permute-done.3.above_ref, bf16[16,1024]{1,0:T(8,128)(2,1)S(1)} %collective-permute-done.4.below_ref, bf16[12,2,16,1024]{3,2,1,0:T(8,128)(2,1)S(1)} %get-tuple-element.35.x_ref, ...), custom_call_target="tpu_custom_call" | custom-call | tf_op jit(solution)/shard_map/wgrad_halo/pallas_call | solution.py:159
  62.0 0.8 dgrad.1
  62.8 1.9 %collective-permute-start.5 = (bf16[4,3,16,1024]{3,2,1,0:T(8,128)(2,1)S(1)}, bf16[4,3,16,1024]{3,2,1,0:T(8,128)(2,1)S(1)}, u32[]{:S(2)}, u32[]{:S(2)}) collective-permute-start(bf16[4,3,16,1024]{3,2,1,0:T(8,128)(2,1)S(1)} %get-tuple-element.39), channel_id=1, source_target_pairs={{0,1},{1,0},{2,3},{3,2},{4,5},{5,4},{6,7},{7,6},{8,9},{9,8},{10,11... | collective-permute-start | bytes 1179656 | tf_op jit(solution)/shard_map/ppermute | solution.py:259
  64.7 7.6 %all-to-all-start.1 = ((bf16[8,11,16,128]{3,2,1,0:T(8,128)(2,1)}), bf16[8,11,16,128]{3,2,1,0:T(8,128)(2,1)S(1)}, u32[]{:S(2)}, u32[]{:S(2)}) async-start(bf16[8,11,16,128]{3,2,1,0:T(8,128)(2,1)} %get-tuple-element.40), calls=%async_computation.1 | async-start | bytes 720896 | tf_op jit(solution)/shard_map/all_to_all | solution.py:296
  72.3 0.0 collective-permute-done.5
  72.3 0.1 convert_add_fusion
  72.4 2.3 %collective-permute-start.6 = (bf16[2,3,16,1024]{3,2,0,1:T(8,128)(2,1)S(1)}, bf16[2,3,16,1024]{3,2,0,1:T(8,128)(2,1)S(1)}, u32[]{:S(2)}, u32[]{:S(2)}) collective-permute-start(bf16[2,3,16,1024]{3,2,0,1:T(8,128)(2,1)S(1)} %fusion.1), channel_id=1, source_target_pairs={{0,6},{6,0},{12,18},{18,12},{1,7},{7,1},{13,19},{19,13},{2,8},{8,2... | collective-permute-start | bytes 589832 | tf_op jit(solution)/shard_map/ppermute | solution.py:304
  74.7 10.7 %all-to-all-done.1.terms_ref = bf16[8,11,16,128]{3,2,1,0:T(8,128)(2,1)S(1)} async-done(((bf16[8,11,16,128]{3,2,1,0:T(8,128)(2,1)}), bf16[8,11,16,128]{3,2,1,0:T(8,128)(2,1)S(1)}, u32[]{:S(2)}, u32[]{:S(2)}) %all-to-all-start.1) | async-done | bytes 360480 | tf_op jit(solution)/shard_map/all_to_all | solution.py:296
  85.5 0.7 total.2
  86.2 6.1 %all-to-all-start.2 = ((bf16[4,11,16,128]{3,2,1,0:T(8,128)(2,1)}), bf16[4,11,16,128]{3,2,1,0:T(8,128)(2,1)S(1)}, u32[]{:S(2)}, u32[]{:S(2)}) async-start(bf16[4,11,16,128]{3,2,1,0:T(8,128)(2,1)} %total.2), calls=%async_computation.2 | async-start | bytes 360448 | tf_op jit(solution)/shard_map/all_to_all | solution.py:303
  92.3 0.0 collective-permute-done.6
  92.3 0.1 fusion.8
  92.3 1.9 %collective-permute-start.7 = (bf16[2,16,1024]{2,1,0:T(8,128)(2,1)S(1)}, bf16[2,16,1024]{2,1,0:T(8,128)(2,1)S(1)}, u32[]{:S(2)}, u32[]{:S(2)}) collective-permute-start(bf16[2,16,1024]{2,1,0:T(8,128)(2,1)S(1)} %get-tuple-element.45), channel_id=1, source_target_pairs={{0,2},{2,4},{4,0},{1,3},{3,5},{5,1},{6,8},{8,10},{10,6},{7,9},{9,1... | collective-permute-start | bytes 196616 | tf_op jit(solution)/shard_map/ppermute | solution.py:307
  94.3 4.8 %collective-permute-start.8 = (bf16[2,16,1024]{2,1,0:T(8,128)(2,1)S(1)}, bf16[2,16,1024]{2,1,0:T(8,128)(2,1)S(1)}, u32[]{:S(2)}, u32[]{:S(2)}) collective-permute-start(bf16[2,16,1024]{2,1,0:T(8,128)(2,1)S(1)} %get-tuple-element.46), channel_id=1, source_target_pairs={{0,4},{2,0},{4,2},{1,5},{3,1},{5,3},{6,10},{8,6},{10,8},{7,11},{9,... | collective-permute-start | bytes 196616 | tf_op jit(solution)/shard_map/ppermute | solution.py:308
  99.1 5.4 %all-to-all-done.2.terms_ref = bf16[4,11,16,128]{3,2,1,0:T(8,128)(2,1)S(1)} async-done(((bf16[4,11,16,128]{3,2,1,0:T(8,128)(2,1)}), bf16[4,11,16,128]{3,2,1,0:T(8,128)(2,1)S(1)}, u32[]{:S(2)}, u32[]{:S(2)}) %all-to-all-start.2) | async-done | bytes 180256 | tf_op jit(solution)/shard_map/all_to_all | solution.py:303
  104.5 0.8 total.3
  105.3 4.6 %all-to-all-start.3 = ((bf16[8,11,16,128]{3,2,1,0:T(8,128)(2,1)}), bf16[8,11,16,128]{3,2,1,0:T(8,128)(2,1)S(1)}, u32[]{:S(2)}, u32[]{:S(2)}) async-start(bf16[8,11,16,128]{3,2,1,0:T(8,128)(2,1)} %total.3), calls=%async_computation.3 | async-start | bytes 720896 | tf_op jit(solution)/shard_map/all_to_all | solution.py:309
  109.9 0.0 collective-permute-done.7
  109.9 0.0 collective-permute-done.8
  109.9 2.8 %collective-permute-start.9 = (bf16[16,1024]{1,0:T(8,128)(2,1)S(1)}, bf16[16,1024]{1,0:T(8,128)(2,1)S(1)}, u32[]{:S(2)}, u32[]{:S(2)}) collective-permute-start(bf16[16,1024]{1,0:T(8,128)(2,1)S(1)} %fusion.7), channel_id=1, source_target_pairs={{0,12},{6,18},{12,0},{18,6},{1,13},{7,19},{13,1},{19,7},{2,14},{8,... | collective-permute-start | bytes 98312 | tf_op jit(solution)/shard_map/ppermute | solution.py:311
  112.8 4.5 %collective-permute-done.9 = bf16[16,1024]{1,0:T(8,128)(2,1)S(1)} collective-permute-done((bf16[16,1024]{1,0:T(8,128)(2,1)S(1)}, bf16[16,1024]{1,0:T(8,128)(2,1)S(1)}, u32[]{:S(2)}, u32[]{:S(2)}) %collective-permute-start.9) | collective-permute-done | bytes 32800 | tf_op jit(solution)/shard_map/ppermute | solution.py:311
  117.3 0.6 fusion.6
  117.9 2.8 %all-to-all-done.3.units_ref = bf16[8,11,16,128]{3,2,1,0:T(8,128)(2,1)S(1)} async-done(((bf16[8,11,16,128]{3,2,1,0:T(8,128)(2,1)}), bf16[8,11,16,128]{3,2,1,0:T(8,128)(2,1)S(1)}, u32[]{:S(2)}, u32[]{:S(2)}) %all-to-all-start.3) | async-done | bytes 360480 | tf_op jit(solution)/shard_map/all_to_all | solution.py:309
  120.6 0.9 unpack.1
  (4 shorter events, 0.1 us)
Async XLA Ops:
  2.2 22.7 %copy-start = (bf16[16,3,3,3,384]{4,0,3,2,1:T(8,128)(2,1)S(1)}, bf16[16,3,3,3,384]{4,0,3,2,1:T(8,128)(2,1)}, u32[]{:S(2)}) copy-start(bf16[16,3,3,3,384]{4,0,3,2,1:T(8,128)(2,1)} %param.4) | copy-start | bytes 995332
  2.2 19.0 %all-to-all-start = ((bf16[12,16,1024]{2,1,0:T(8,128)(2,1)}), bf16[12,16,1024]{2,1,0:T(8,128)(2,1)S(1)}, u32[]{:S(2)}, u32[]{:S(2)}) async-start(bf16[12,16,1024]{2,1,0:T(8,128)(2,1)} %broadcast_in_dim.8), calls=%async_computation | async-start | bytes 786432 | tf_op jit(solution)/shard_map/all_to_all | solution.py:281
  21.2 24.5 %copy-start.1 = (bf16[1,1,16,1024]{3,2,1,0:T(8,128)(2,1)S(1)}, bf16[1,1,16,1024]{3,2,1,0:T(8,128)(2,1)}, u32[]{:S(2)}) copy-start(bf16[1,1,16,1024]{3,2,1,0:T(8,128)(2,1)} %param.5) | copy-start | bytes 98308
  21.2 3.7 %collective-permute-start = (bf16[12,16,1024]{2,1,0:T(8,128)(2,1)S(1)}, bf16[12,16,1024]{2,1,0:T(8,128)(2,1)S(1)}, u32[]{:S(2)}, u32[]{:S(2)}) collective-permute-start(bf16[12,16,1024]{2,1,0:T(8,128)(2,1)S(1)} %all-to-all-done.mine_ref), channel_id=1, source_target_pairs={{0,1},{1,0},{2,3},{3,2},{4,5},{5,4},{6,7},{7,6},{8,9},{9,8},{10,11... | collective-permute-start | bytes 1179656 | tf_op jit(solution)/shard_map/ppermute | solution.py:259
  25.8 14.6 %collective-permute-start.1 = (bf16[16,1024]{1,0:T(8,128)(2,1)S(1)}, bf16[16,1024]{1,0:T(8,128)(2,1)S(1)}, u32[]{:S(2)}, u32[]{:S(2)}) collective-permute-start(bf16[16,1024]{1,0:T(8,128)(2,1)S(1)} %get-tuple-element.27), channel_id=1, source_target_pairs={{0,24},{24,48},{48,72},{72,96},{96,120},{120,144},{144,168},{168,1... | collective-permute-start | bytes 98312 | tf_op jit(solution)/shard_map/ppermute | solution.py:269
  36.1 9.5 %collective-permute-start.2 = (bf16[16,1024]{1,0:T(8,128)(2,1)S(1)}, bf16[16,1024]{1,0:T(8,128)(2,1)S(1)}, u32[]{:S(2)}, u32[]{:S(2)}) collective-permute-start(bf16[16,1024]{1,0:T(8,128)(2,1)S(1)} %get-tuple-element.28), channel_id=1, source_target_pairs={{0,744},{24,0},{48,24},{72,48},{96,72},{120,96},{144,120},{168,144... | collective-permute-start | bytes 98312 | tf_op jit(solution)/shard_map/ppermute | solution.py:269
  46.3 10.3 %collective-permute-start.4 = (bf16[16,1024]{1,0:T(8,128)(2,1)S(1)}, bf16[16,1024]{1,0:T(8,128)(2,1)S(1)}, u32[]{:S(2)}, u32[]{:S(2)}) collective-permute-start(bf16[16,1024]{1,0:T(8,128)(2,1)S(1)} %get-tuple-element.33.own_ref), channel_id=1, source_target_pairs={{0,24},{24,48},{48,72},{72,96},{96,120},{120,144},{144,168},{168,1... | collective-permute-start | bytes 98312 | tf_op jit(solution)/shard_map/ppermute | solution.py:269
  52.6 7.6 %collective-permute-start.3 = (bf16[16,1024]{1,0:T(8,128)(2,1)S(1)}, bf16[16,1024]{1,0:T(8,128)(2,1)S(1)}, u32[]{:S(2)}, u32[]{:S(2)}) collective-permute-start(bf16[16,1024]{1,0:T(8,128)(2,1)S(1)} %get-tuple-element.33.own_ref), channel_id=1, source_target_pairs={{0,744},{24,0},{48,24},{72,48},{96,72},{120,96},{144,120},{168,144... | collective-permute-start | bytes 98312 | tf_op jit(solution)/shard_map/ppermute | solution.py:269
  62.8 9.5 %collective-permute-start.5 = (bf16[4,3,16,1024]{3,2,1,0:T(8,128)(2,1)S(1)}, bf16[4,3,16,1024]{3,2,1,0:T(8,128)(2,1)S(1)}, u32[]{:S(2)}, u32[]{:S(2)}) collective-permute-start(bf16[4,3,16,1024]{3,2,1,0:T(8,128)(2,1)S(1)} %get-tuple-element.39), channel_id=1, source_target_pairs={{0,1},{1,0},{2,3},{3,2},{4,5},{5,4},{6,7},{7,6},{8,9},{9,8},{10,11... | collective-permute-start | bytes 1179656 | tf_op jit(solution)/shard_map/ppermute | solution.py:259
  64.7 20.7 %all-to-all-start.1 = ((bf16[8,11,16,128]{3,2,1,0:T(8,128)(2,1)}), bf16[8,11,16,128]{3,2,1,0:T(8,128)(2,1)S(1)}, u32[]{:S(2)}, u32[]{:S(2)}) async-start(bf16[8,11,16,128]{3,2,1,0:T(8,128)(2,1)} %get-tuple-element.40), calls=%async_computation.1 | async-start | bytes 720896 | tf_op jit(solution)/shard_map/all_to_all | solution.py:296
  72.4 19.8 %collective-permute-start.6 = (bf16[2,3,16,1024]{3,2,0,1:T(8,128)(2,1)S(1)}, bf16[2,3,16,1024]{3,2,0,1:T(8,128)(2,1)S(1)}, u32[]{:S(2)}, u32[]{:S(2)}) collective-permute-start(bf16[2,3,16,1024]{3,2,0,1:T(8,128)(2,1)S(1)} %fusion.1), channel_id=1, source_target_pairs={{0,6},{6,0},{12,18},{18,12},{1,7},{7,1},{13,19},{19,13},{2,8},{8,2... | collective-permute-start | bytes 589832 | tf_op jit(solution)/shard_map/ppermute | solution.py:304
  86.2 18.3 %all-to-all-start.2 = ((bf16[4,11,16,128]{3,2,1,0:T(8,128)(2,1)}), bf16[4,11,16,128]{3,2,1,0:T(8,128)(2,1)S(1)}, u32[]{:S(2)}, u32[]{:S(2)}) async-start(bf16[4,11,16,128]{3,2,1,0:T(8,128)(2,1)} %total.2), calls=%async_computation.2 | async-start | bytes 360448 | tf_op jit(solution)/shard_map/all_to_all | solution.py:303
  92.3 17.6 %collective-permute-start.7 = (bf16[2,16,1024]{2,1,0:T(8,128)(2,1)S(1)}, bf16[2,16,1024]{2,1,0:T(8,128)(2,1)S(1)}, u32[]{:S(2)}, u32[]{:S(2)}) collective-permute-start(bf16[2,16,1024]{2,1,0:T(8,128)(2,1)S(1)} %get-tuple-element.45), channel_id=1, source_target_pairs={{0,2},{2,4},{4,0},{1,3},{3,5},{5,1},{6,8},{8,10},{10,6},{7,9},{9,1... | collective-permute-start | bytes 196616 | tf_op jit(solution)/shard_map/ppermute | solution.py:307
  94.3 15.6 %collective-permute-start.8 = (bf16[2,16,1024]{2,1,0:T(8,128)(2,1)S(1)}, bf16[2,16,1024]{2,1,0:T(8,128)(2,1)S(1)}, u32[]{:S(2)}, u32[]{:S(2)}) collective-permute-start(bf16[2,16,1024]{2,1,0:T(8,128)(2,1)S(1)} %get-tuple-element.46), channel_id=1, source_target_pairs={{0,4},{2,0},{4,2},{1,5},{3,1},{5,3},{6,10},{8,6},{10,8},{7,11},{9,... | collective-permute-start | bytes 196616 | tf_op jit(solution)/shard_map/ppermute | solution.py:308
  105.3 15.4 %all-to-all-start.3 = ((bf16[8,11,16,128]{3,2,1,0:T(8,128)(2,1)}), bf16[8,11,16,128]{3,2,1,0:T(8,128)(2,1)S(1)}, u32[]{:S(2)}, u32[]{:S(2)}) async-start(bf16[8,11,16,128]{3,2,1,0:T(8,128)(2,1)} %total.3), calls=%async_computation.3 | async-start | bytes 720896 | tf_op jit(solution)/shard_map/all_to_all | solution.py:309
  109.9 7.3 %collective-permute-start.9 = (bf16[16,1024]{1,0:T(8,128)(2,1)S(1)}, bf16[16,1024]{1,0:T(8,128)(2,1)S(1)}, u32[]{:S(2)}, u32[]{:S(2)}) collective-permute-start(bf16[16,1024]{1,0:T(8,128)(2,1)S(1)} %fusion.7), channel_id=1, source_target_pairs={{0,12},{6,18},{12,0},{18,6},{1,13},{7,19},{13,1},{19,7},{2,14},{8,... | collective-permute-start | bytes 98312 | tf_op jit(solution)/shard_map/ppermute | solution.py:311

commit v11 on v8

--- a/solution.py
+++ b/solution.py
@@ -14,6 +14,7 @@
 UNIV = 1
 TAPS = 27
 LANES = 128
+HALF = 8
 VMEM_LIMIT = 48 * 1024 * 1024
 DEP = ("y", "zh")
 CHIPS = ("x", "zl")
@@ -100,81 +101,94 @@
 def cross(stack, x):
     return lax.dot_general(
         stack, x, (((1,), (1,)), ((), ())), preferred_element_type=jnp.float32
-    ).astype(jnp.bfloat16)
+    )
+
+
+def units_of(grad):
+    columns = grad.shape[1] // LANES
+    for at in range(grad.shape[0] // HALF * columns):
+        row, column = divmod(at, columns)
+        yield grad[row * HALF : (row + 1) * HALF, column * LANES : (column + 1) * LANES]
 
 
 def own_kernel(core_ref, own_ref, mine_ref, other_ref, units_ref, stack_ref, x_ref):
-    rows = own_ref.shape[0]
     x = merge_cores(core_ref, mine_ref, other_ref, x_ref)
-    columns = x.shape[0] // LANES
     stack_plane(own_ref[...], stack_ref, 0)
-    grad = cross(stack_ref[...], x)
-    for unit in range(9 * columns):
-        tap, column = divmod(unit, columns)
-        units_ref[unit] = grad[
-            tap * rows : (tap + 1) * rows, column * LANES : (column + 1) * LANES
-        ]
+    for at, unit in enumerate(units_of(cross(stack_ref[...], x))):
+        units_ref[at] = unit.astype(jnp.bfloat16)
+
+
+def plane_shapes(own, chans):
+    rows, cells = own.shape
+    return [
+        jax.ShapeDtypeStruct((9 * rows * chans // (HALF * LANES), HALF, LANES), jnp.bfloat16),
+        jax.ShapeDtypeStruct((9 * rows, cells), jnp.bfloat16),
+    ]
 
 
 def wgrad_own(core, own, mine, other):
-    rows, cells = own.shape
     chans = 2 * mine.shape[0] * mine.shape[1]
+    x = jax.ShapeDtypeStruct((mine.shape[0], 2) + mine.shape[1:], mine.dtype)
     return pl.pallas_call(
         own_kernel,
-        out_shape=[
-            jax.ShapeDtypeStruct((9 * chans // LANES, rows, LANES), jnp.bfloat16),
-            jax.ShapeDtypeStruct((9 * rows, cells), jnp.bfloat16),
-            jax.ShapeDtypeStruct((mine.shape[0], 2) + mine.shape[1:], mine.dtype),
-        ],
+        out_shape=plane_shapes(own, chans) + [x],
         in_specs=specs(1, 3),
         compiler_params=pltpu.CompilerParams(vmem_limit_bytes=VMEM_LIMIT),
         name="wgrad_own",
     )(core, own, mine, other)
 
 
-def halo_kernel(above_ref, below_ref, x_ref, units_ref, wide_ref, stack_ref):
-    rows = above_ref.shape[0]
+def below_kernel(below_ref, x_ref, units_ref, stack_ref):
+    stack_plane(below_ref[...], stack_ref, 0)
+    grad = cross(stack_ref[...], x_ref[...].reshape(-1, x_ref.shape[-1]))
+    for at, unit in enumerate(units_of(grad)):
+        units_ref[at] = unit.astype(jnp.bfloat16)
+
+
+def wgrad_below(below, x):
+    return pl.pallas_call(
+        below_kernel,
+        out_shape=plane_shapes(below, x.shape[0] * x.shape[1] * x.shape[2]),
+        compiler_params=pltpu.CompilerParams(vmem_limit_bytes=VMEM_LIMIT),
+        name="wgrad_below",
+    )(below, x)
+
+
+def above_kernel(above_ref, x_ref, own_ref, below_ref, wide_ref, stack_ref):
     slots, per = wide_ref.shape[:2]
-    x = x_ref[...].reshape(-1, x_ref.shape[-1])
-    columns = x.shape[0] // LANES
-    for half, ref in enumerate((above_ref, below_ref)):
-        stack_plane(ref[...], stack_ref, half * 9 * rows)
-        grad = cross(stack_ref[half * 9 * rows : (half + 1) * 9 * rows, :], x)
-        for at in range(9 * columns):
-            tap, column = divmod(at, columns)
-            unit = 18 * half * columns + at
-            wide_ref[unit // per, unit % per] = grad[
-                tap * rows : (tap + 1) * rows, column * LANES : (column + 1) * LANES
-            ]
-    for at in range(9 * columns):
-        unit = 9 * columns + at
-        wide_ref[unit // per, unit % per] = units_ref[at]
-    for unit in range(TAPS * columns, slots * per):
-        wide_ref[unit // per, unit % per] = jnp.zeros((rows, LANES), jnp.bfloat16)
-
-
-def wgrad_halo(above, below, x, units, slots):
-    rows, cells = above.shape
-    per = -(-3 * units.shape[0] // slots)
-    return pl.pallas_call(
-        halo_kernel,
-        out_shape=[
-            jax.ShapeDtypeStruct((slots, per, rows, LANES), jnp.bfloat16),
-            jax.ShapeDtypeStruct((18 * rows, cells), jnp.bfloat16),
-        ],
-        compiler_params=pltpu.CompilerParams(vmem_limit_bytes=VMEM_LIMIT),
-        name="wgrad_halo",
-    )(above, below, x, units)
-
-
-def dgrad_kernel(core_ref, x_at_ref, z_at_ref, k_ref, own_ref, halo_ref, keep_ref, send_ref):
+    count = own_ref.shape[0]
+    for at in range(count):
+        for unit, ref in ((count + at, own_ref), (2 * count + at, below_ref)):
+            wide_ref[unit // per, unit % per] = ref[at]
+    for unit in range(3 * count, slots * per):
+        wide_ref[unit // per, unit % per] = jnp.zeros((HALF, LANES), jnp.bfloat16)
+    stack_plane(above_ref[...], stack_ref, 0)
+    grad = cross(stack_ref[...], x_ref[...].reshape(-1, x_ref.shape[-1]))
+    for at, unit in enumerate(units_of(grad)):
+        wide_ref[at // per, at % per] = unit.astype(jnp.bfloat16)
+
+
+def wgrad_above(above, x, own_units, below_units, slots):
+    per = -(-3 * own_units.shape[0] // slots)
+    stack = plane_shapes(above, x.shape[0] * x.shape[1] * x.shape[2])[1]
+    return pl.pallas_call(
+        above_kernel,
+        out_shape=[jax.ShapeDtypeStruct((slots, per, HALF, LANES), jnp.bfloat16), stack],
+        compiler_params=pltpu.CompilerParams(vmem_limit_bytes=VMEM_LIMIT),
+        name="wgrad_above",
+    )(above, x, own_units, below_units)
+
+
+def dgrad_kernel(
+    core_ref, x_at_ref, z_at_ref, k_ref, above_ref, own_ref, below_ref, keep_ref, send_ref
+):
     rows = keep_ref.shape[2]
     n = 9 * rows
     partial = None
-    for at, stack in ((0, halo_ref[:n, :]), (n, own_ref[...]), (2 * n, halo_ref[n:, :])):
+    for at, stack_ref in ((0, above_ref), (n, own_ref), (2 * n, below_ref)):
         term = lax.dot_general(
             k_ref[at : at + n, :],
-            stack,
+            stack_ref[...],
             (((0,), (0,)), ((), ())),
             preferred_element_type=jnp.float32,
         )
@@ -190,7 +204,7 @@
             send_ref[x_slot, z_slot] = jnp.where(first, odd, even).astype(jnp.bfloat16)
 
 
-def dgrad(core, x_at, z_at, k_rows, own, halo):
+def dgrad(core, x_at, z_at, k_rows, above, own, below):
     shape = (4, 3, k_rows.shape[0] // TAPS, own.shape[1])
     return pl.pallas_call(
         dgrad_kernel,
@@ -198,10 +212,10 @@
             jax.ShapeDtypeStruct(shape, jnp.float32),
             jax.ShapeDtypeStruct(shape, jnp.bfloat16),
         ],
-        in_specs=specs(3, 3),
+        in_specs=specs(3, 4),
         compiler_params=pltpu.CompilerParams(vmem_limit_bytes=VMEM_LIMIT),
         name="dgrad",
-    )(core, x_at, z_at, k_rows, own, halo)
+    )(core, x_at, z_at, k_rows, above, own, below)
 
 
 def act_kernel(mid_ref, low_ref, high_ref, cot_ref, act_ref, grad_ref):
@@ -257,19 +271,22 @@
 
 
 def unpack_kernel(units_ref, out_ref):
+    taps, rows, chans = out_ref.shape
     per = units_ref.shape[1]
-    columns = out_ref.shape[2] // LANES
-    for tap in range(TAPS):
-        for column in range(columns):
-            unit = tap * columns + column
-            block = units_ref[unit // per, unit % per].astype(jnp.float32)
-            out_ref[tap, :, column * LANES : (column + 1) * LANES] = block
-
-
-def unpack(units, chans):
+    columns = chans // LANES
+    for at in range(taps * rows // HALF * columns):
+        row, column = divmod(at, columns)
+        tap, half = divmod(row, rows // HALF)
+        block = units_ref[at // per, at % per].astype(jnp.float32)
+        out_ref[
+            tap, half * HALF : (half + 1) * HALF, column * LANES : (column + 1) * LANES
+        ] = block
+
+
+def unpack(units, rows, chans):
     return pl.pallas_call(
         unpack_kernel,
-        out_shape=jax.ShapeDtypeStruct((TAPS, units.shape[2], chans), jnp.float32),
+        out_shape=jax.ShapeDtypeStruct((TAPS, rows, chans), jnp.float32),
         compiler_params=pltpu.CompilerParams(vmem_limit_bytes=VMEM_LIMIT),
         name="unpack",
     )(units)
@@ -311,11 +328,12 @@
     above, below = shift(grad_pre, -1), shift(grad_pre, 1)
     own_units, own_stack, x = wgrad_own(core, grad_pre, mine, other)
     ys, zs = lax.axis_size("y"), lax.axis_size("zh")
-    wide, halo_stack = wgrad_halo(above, below, x, own_units, ys)
+    below_units, below_stack = wgrad_below(below, x)
+    wide, above_stack = wgrad_above(above, x, own_units, below_units, ys)
     scale = 1.0 / math.sqrt(UNIV * DEPTH * SIDE * SIDE)
     over_y = lax.all_to_all(wide, "y", 0, 0)
 
-    keep, send = dgrad(core, x_at, z_at, k_rows, own_stack, halo_stack)
+    keep, send = dgrad(core, x_at, z_at, k_rows, above_stack, own_stack, below_stack)
     keep, send = halve(keep, swap_cores(send))
     over_y, keep = lax.optimization_barrier((over_y, keep))
     over_z = lax.all_to_all(total_spread(over_y, 1.0, zs), "zh", 0, 0)
@@ -328,7 +346,7 @@
     total = total[:, 0] + after.astype(jnp.float32) + before.astype(jnp.float32)
     step = lax.ppermute(total[1].astype(jnp.bfloat16), "x", [(i, i ^ 2) for i in range(4)])
     grad_volume = (total[0] + step.astype(jnp.float32)).astype(jnp.bfloat16)
-    all_taps = unpack(units, kernel.shape[-1])
+    all_taps = unpack(units, rows, kernel.shape[-1])
     grad_kernel = jnp.transpose(all_taps, (1, 0, 2)).reshape(kernel.shape)
     return (activated.reshape(volume.shape), grad_volume.reshape(volume.shape), grad_kernel)
 

time: 116 us -> 116 us (level)
    pallas_call x3 -> x4, Pallas kernels: 3.11 us -> 3.24 us  [the longest x1 1.27 us: wgrad_above(): pl.pallas_call(above_kernel, out_shape=[jax.ShapeDtypeStruct((slots, per,...]
where the time goes in v11:
time: 116 us; the launch traced here: 115 us
  starting transfers between devices  73.6 us (63%)
  waiting for transfers between devices  30.9 us (27%)
  Pallas kernels  7.16 us (6%)
  local copies, waits for them, and re-layouts  1.57 us (1%)
    ppermute x4, starting transfers between devices, shift(): lax.ppermute(block, DEP, [(i, (i + step) % depths) for i in range(depths)])  25.8 us
    all_to_all x1, starting transfers between devices, body(): mine = lax.all_to_all(copies(own), CHIPS, 0, 0)  13.1 us
    all_to_all x1, waiting for transfers between devices, body(): mine = lax.all_to_all(copies(own), CHIPS, 0, 0)  8.12 us
    all_to_all x1, starting transfers between devices, body(): over_y = lax.all_to_all(wide, 'y', 0, 0)  7.36 us
    all_to_all x1, starting transfers between devices, body(): over_z = lax.all_to_all(total_spread(over_y, 1.0, zs), 'zh', 0, 0)  5.69 us
    all_to_all x1, starting transfers between devices, body(): units = lax.all_to_all(total_spread(over_z, scale, ys), 'y', 0, 0)  4.9 us
    ppermute x1, starting transfers between devices, body(): before = lax.ppermute(before, 'zl', [(i, (i + 2) % 3) for i in range(3)])  4.82 us
    ppermute x1, waiting for transfers between devices, body(): lax.ppermute(total[1].astype(jnp.bfloat16), 'x', [(i, i ^ 2) for i in ran...  4.52 us
  transfers between devices with their start and end apart: 14, of which 10 were waited for; matrix products, arithmetic and copies ran while one was open for 1% of the time, Pallas kernels for 3%

profile of v11, /device:TPU:2, one launch (start us, length us, event | category | flops | bytes accessed | tf_op | source)
XLA Modules:
  0.0 114.7 jit_solution(5155920467585183396)
XLA Ops:
  0.6 1.5 %broadcast_in_dim.8 = bf16[12,16,1024]{2,1,0:T(8,128)(2,1)} broadcast(bf16[16,1024]{1,0:T(8,128)(2,1)} %bitcast.44), dimensions={1,2} | broadcast | bytes 425984 | tf_op jit(solution)/shard_map/broadcast_in_dim | solution.py:316
  2.2 0.0 copy-start
  2.2 13.1 %all-to-all-start = ((bf16[12,16,1024]{2,1,0:T(8,128)(2,1)}), bf16[12,16,1024]{2,1,0:T(8,128)(2,1)S(1)}, u32[]{:S(2)}, u32[]{:S(2)}) async-start(bf16[12,16,1024]{2,1,0:T(8,128)(2,1)} %broadcast_in_dim.8), calls=%async_computation | async-start | bytes 786432 | tf_op jit(solution)/shard_map/all_to_all | solution.py:318
  15.3 8.1 %all-to-all-done.mine_ref = bf16[12,16,1024]{2,1,0:T(8,128)(2,1)S(1)} async-done(((bf16[12,16,1024]{2,1,0:T(8,128)(2,1)}), bf16[12,16,1024]{2,1,0:T(8,128)(2,1)S(1)}, u32[]{:S(2)}, u32[]{:S(2)}) %all-to-all-start) | async-done | bytes 393248 | tf_op jit(solution)/shard_map/all_to_all | solution.py:318
  23.4 0.0 copy-start.1
  23.4 2.0 %collective-permute-start = (bf16[12,16,1024]{2,1,0:T(8,128)(2,1)S(1)}, bf16[12,16,1024]{2,1,0:T(8,128)(2,1)S(1)}, u32[]{:S(2)}, u32[]{:S(2)}) collective-permute-start(bf16[12,16,1024]{2,1,0:T(8,128)(2,1)S(1)} %all-to-all-done.mine_ref), channel_id=1, source_target_pairs={{0,1},{1,0},{2,3},{3,2},{4,5},{5,4},{6,7},{7,6},{8,9},{9,8},{10,11... | collective-permute-start | bytes 1179656 | tf_op jit(solution)/shard_map/ppermute | solution.py:296
  25.5 1.7 %collective-permute-done.other_ref = bf16[12,16,1024]{2,1,0:T(8,128)(2,1)S(1)} collective-permute-done((bf16[12,16,1024]{2,1,0:T(8,128)(2,1)S(1)}, bf16[12,16,1024]{2,1,0:T(8,128)(2,1)S(1)}, u32[]{:S(2)}, u32[]{:S(2)}) %collective-permute-start) | collective-permute-done | bytes 393248 | tf_op jit(solution)/shard_map/ppermute | solution.py:296
  27.1 0.0 copy-done
  27.1 0.9 conv.1
  28.1 7.2 %collective-permute-start.1 = (bf16[16,1024]{1,0:T(8,128)(2,1)S(1)}, bf16[16,1024]{1,0:T(8,128)(2,1)S(1)}, u32[]{:S(2)}, u32[]{:S(2)}) collective-permute-start(bf16[16,1024]{1,0:T(8,128)(2,1)S(1)} %get-tuple-element.32), channel_id=1, source_target_pairs={{0,24},{24,48},{48,72},{72,96},{96,120},{120,144},{144,168},{168,1... | collective-permute-start | bytes 98312 | tf_op jit(solution)/shard_map/ppermute | solution.py:306
  35.2 7.3 %collective-permute-start.2 = (bf16[16,1024]{1,0:T(8,128)(2,1)S(1)}, bf16[16,1024]{1,0:T(8,128)(2,1)S(1)}, u32[]{:S(2)}, u32[]{:S(2)}) collective-permute-start(bf16[16,1024]{1,0:T(8,128)(2,1)S(1)} %get-tuple-element.33), channel_id=1, source_target_pairs={{0,744},{24,0},{48,24},{72,48},{96,72},{120,96},{144,120},{168,144... | collective-permute-start | bytes 98312 | tf_op jit(solution)/shard_map/ppermute | solution.py:306
  42.5 0.6 collective-permute-done.1.low_ref
  43.1 1.4 %collective-permute-done.2.high_ref = bf16[16,1024]{1,0:T(8,128)(2,1)S(1)} collective-permute-done((bf16[16,1024]{1,0:T(8,128)(2,1)S(1)}, bf16[16,1024]{1,0:T(8,128)(2,1)S(1)}, u32[]{:S(2)}, u32[]{:S(2)}) %collective-permute-start.2) | collective-permute-done | bytes 32800 | tf_op jit(solution)/shard_map/ppermute | solution.py:306
  44.5 0.0 copy-done.1
  44.5 0.6 activate.1
  45.1 6.2 %collective-permute-start.4 = (bf16[16,1024]{1,0:T(8,128)(2,1)S(1)}, bf16[16,1024]{1,0:T(8,128)(2,1)S(1)}, u32[]{:S(2)}, u32[]{:S(2)}) collective-permute-start(bf16[16,1024]{1,0:T(8,128)(2,1)S(1)} %get-tuple-element.36.own_ref), channel_id=1, source_target_pairs={{0,24},{24,48},{48,72},{72,96},{96,120},{120,144},{144,168},{168,1... | collective-permute-start | bytes 98312 | tf_op jit(solution)/shard_map/ppermute | solution.py:306
  51.4 5.2 %collective-permute-start.3 = (bf16[16,1024]{1,0:T(8,128)(2,1)S(1)}, bf16[16,1024]{1,0:T(8,128)(2,1)S(1)}, u32[]{:S(2)}, u32[]{:S(2)}) collective-permute-start(bf16[16,1024]{1,0:T(8,128)(2,1)S(1)} %get-tuple-element.36.own_ref), channel_id=1, source_target_pairs={{0,744},{24,0},{48,24},{72,48},{96,72},{120,96},{144,120},{168,144... | collective-permute-start | bytes 98312 | tf_op jit(solution)/shard_map/ppermute | solution.py:306
  56.5 0.5 wgrad_own.1
  57.1 0.0 collective-permute-done.4.below_ref
  57.1 0.5 wgrad_below.1
  57.6 1.6 %collective-permute-done.3.above_ref = bf16[16,1024]{1,0:T(8,128)(2,1)S(1)} collective-permute-done((bf16[16,1024]{1,0:T(8,128)(2,1)S(1)}, bf16[16,1024]{1,0:T(8,128)(2,1)S(1)}, u32[]{:S(2)}, u32[]{:S(2)}) %collective-permute-start.3) | collective-permute-done | bytes 32800 | tf_op jit(solution)/shard_map/ppermute | solution.py:306
  59.2 1.3 %wgrad_above.1 = (bf16[8,21,8,128]{3,2,1,0:T(8,128)(2,1)}, bf16[144,1024]{1,0:T(8,128)(2,1)S(1)}) custom-call(bf16[16,1024]{1,0:T(8,128)(2,1)S(1)} %collective-permute-done.3.above_ref, bf16[12,2,16,1024]{3,2,1,0:T(8,128)(2,1)S(1)} %get-tuple-element.37.x_ref, bf16[54,8,128]{2,1,0:T(8,128)(2,1)S(1)} %get-tuple-element.38.own_ref, ...), custom_call_target="tpu_custom_call" | custom-call | tf_op jit(solution)/shard_map/wgrad_above/pallas_call | solution.py:174
  60.5 7.4 %all-to-all-start.1 = ((bf16[8,21,8,128]{3,2,1,0:T(8,128)(2,1)}), bf16[8,21,8,128]{3,2,1,0:T(8,128)(2,1)S(1)}, u32[]{:S(2)}, u32[]{:S(2)}) async-start(bf16[8,21,8,128]{3,2,1,0:T(8,128)(2,1)} %get-tuple-element.40), calls=%async_computation.1 | async-start | bytes 688128 | tf_op jit(solution)/shard_map/all_to_all | solution.py:334
  67.8 0.8 dgrad.1
  68.7 1.9 %collective-permute-start.5 = (bf16[4,3,16,1024]{3,2,1,0:T(8,128)(2,1)S(1)}, bf16[4,3,16,1024]{3,2,1,0:T(8,128)(2,1)S(1)}, u32[]{:S(2)}, u32[]{:S(2)}) collective-permute-start(bf16[4,3,16,1024]{3,2,1,0:T(8,128)(2,1)S(1)} %get-tuple-element.47), channel_id=1, source_target_pairs={{0,1},{1,0},{2,3},{3,2},{4,5},{5,4},{6,7},{7,6},{8,9},{9,8},{10,11... | collective-permute-start | bytes 1179656 | tf_op jit(solution)/shard_map/ppermute | solution.py:296
  70.6 1.7 %collective-permute-done.5.came_ref = bf16[4,3,16,1024]{3,2,1,0:T(8,128)(2,1)S(1)} collective-permute-done((bf16[4,3,16,1024]{3,2,1,0:T(8,128)(2,1)S(1)}, bf16[4,3,16,1024]{3,2,1,0:T(8,128)(2,1)S(1)}, u32[]{:S(2)}, u32[]{:S(2)}) %collective-permute-start.5) | collective-permute-done | bytes 393248 | tf_op jit(solution)/shard_map/ppermute | solution.py:296
  72.3 0.1 halve.1
  72.3 3.2 %collective-permute-start.6 = (bf16[2,3,16,1024]{3,2,1,0:T(8,128)(2,1)S(1)}, bf16[2,3,16,1024]{3,2,1,0:T(8,128)(2,1)S(1)}, u32[]{:S(2)}, u32[]{:S(2)}) collective-permute-start(bf16[2,3,16,1024]{3,2,1,0:T(8,128)(2,1)S(1)} %get-tuple-element.50), channel_id=1, source_target_pairs={{0,6},{6,0},{12,18},{18,12},{1,7},{7,1},{13,19},{19,13},{2,8},{8,2... | collective-permute-start | bytes 589832 | tf_op jit(solution)/shard_map/ppermute | solution.py:340
  75.6 3.7 %all-to-all-done.1.terms_ref = bf16[8,21,8,128]{3,2,1,0:T(8,128)(2,1)S(1)} async-done(((bf16[8,21,8,128]{3,2,1,0:T(8,128)(2,1)}), bf16[8,21,8,128]{3,2,1,0:T(8,128)(2,1)S(1)}, u32[]{:S(2)}, u32[]{:S(2)}) %all-to-all-start.1) | async-done | bytes 344096 | tf_op jit(solution)/shard_map/all_to_all | solution.py:334
  79.3 0.7 total.2
  80.0 5.7 %all-to-all-start.2 = ((bf16[4,21,8,128]{3,2,1,0:T(8,128)(2,1)}), bf16[4,21,8,128]{3,2,1,0:T(8,128)(2,1)S(1)}, u32[]{:S(2)}, u32[]{:S(2)}) async-start(bf16[4,21,8,128]{3,2,1,0:T(8,128)(2,1)} %total.2), calls=%async_computation.2 | async-start | bytes 344064 | tf_op jit(solution)/shard_map/all_to_all | solution.py:339
  85.7 0.0 collective-permute-done.6
  85.7 1.9 %collective-permute-start.7 = (bf16[2,16,1024]{2,1,0:T(8,128)(2,1)S(1)}, bf16[2,16,1024]{2,1,0:T(8,128)(2,1)S(1)}, u32[]{:S(2)}, u32[]{:S(2)}) collective-permute-start(bf16[2,16,1024]{2,1,0:T(8,128)(2,1)S(1)} %get-tuple-element.55), channel_id=1, source_target_pairs={{0,2},{2,4},{4,0},{1,3},{3,5},{5,1},{6,8},{8,10},{10,6},{7,9},{9,1... | collective-permute-start | bytes 196616 | tf_op jit(solution)/shard_map/ppermute | solution.py:343
  87.7 4.8 %collective-permute-start.8 = (bf16[2,16,1024]{2,1,0:T(8,128)(2,1)S(1)}, bf16[2,16,1024]{2,1,0:T(8,128)(2,1)S(1)}, u32[]{:S(2)}, u32[]{:S(2)}) collective-permute-start(bf16[2,16,1024]{2,1,0:T(8,128)(2,1)S(1)} %get-tuple-element.56), channel_id=1, source_target_pairs={{0,4},{2,0},{4,2},{1,5},{3,1},{5,3},{6,10},{8,6},{10,8},{7,11},{9,... | collective-permute-start | bytes 196616 | tf_op jit(solution)/shard_map/ppermute | solution.py:344
  92.5 4.2 %all-to-all-done.2.terms_ref = bf16[4,21,8,128]{3,2,1,0:T(8,128)(2,1)S(1)} async-done(((bf16[4,21,8,128]{3,2,1,0:T(8,128)(2,1)}), bf16[4,21,8,128]{3,2,1,0:T(8,128)(2,1)S(1)}, u32[]{:S(2)}, u32[]{:S(2)}) %all-to-all-start.2) | async-done | bytes 172064 | tf_op jit(solution)/shard_map/all_to_all | solution.py:339
  96.7 0.8 total.3
  97.5 4.9 %all-to-all-start.3 = ((bf16[8,21,8,128]{3,2,1,0:T(8,128)(2,1)}), bf16[8,21,8,128]{3,2,1,0:T(8,128)(2,1)S(1)}, u32[]{:S(2)}, u32[]{:S(2)}) async-start(bf16[8,21,8,128]{3,2,1,0:T(8,128)(2,1)} %total.3), calls=%async_computation.3 | async-start | bytes 688128 | tf_op jit(solution)/shard_map/all_to_all | solution.py:345
  102.4 0.0 collective-permute-done.7
  102.4 0.0 collective-permute-done.8
  102.4 2.8 %collective-permute-start.9 = (bf16[16,1024]{1,0:T(8,128)(2,1)S(1)}, bf16[16,1024]{1,0:T(8,128)(2,1)S(1)}, u32[]{:S(2)}, u32[]{:S(2)}) collective-permute-start(bf16[16,1024]{1,0:T(8,128)(2,1)S(1)} %fusion.5), channel_id=1, source_target_pairs={{0,12},{6,18},{12,0},{18,6},{1,13},{7,19},{13,1},{19,7},{2,14},{8,... | collective-permute-start | bytes 98312 | tf_op jit(solution)/shard_map/ppermute | solution.py:347
  105.2 4.5 %collective-permute-done.9 = bf16[16,1024]{1,0:T(8,128)(2,1)S(1)} collective-permute-done((bf16[16,1024]{1,0:T(8,128)(2,1)S(1)}, bf16[16,1024]{1,0:T(8,128)(2,1)S(1)}, u32[]{:S(2)}, u32[]{:S(2)}) %collective-permute-start.9) | collective-permute-done | bytes 32800 | tf_op jit(solution)/shard_map/ppermute | solution.py:347
  109.7 0.6 fusion.4
  110.4 3.5 %all-to-all-done.3.units_ref = bf16[8,21,8,128]{3,2,1,0:T(8,128)(2,1)S(1)} async-done(((bf16[8,21,8,128]{3,2,1,0:T(8,128)(2,1)}), bf16[8,21,8,128]{3,2,1,0:T(8,128)(2,1)S(1)}, u32[]{:S(2)}, u32[]{:S(2)}) %all-to-all-start.3) | async-done | bytes 344096 | tf_op jit(solution)/shard_map/all_to_all | solution.py:345
  113.8 0.9 unpack.1
  (4 shorter events, 0.1 us)
Async XLA Ops:
  2.2 25.0 %copy-start = (bf16[16,3,3,3,384]{4,0,3,2,1:T(8,128)(2,1)S(1)}, bf16[16,3,3,3,384]{4,0,3,2,1:T(8,128)(2,1)}, u32[]{:S(2)}) copy-start(bf16[16,3,3,3,384]{4,0,3,2,1:T(8,128)(2,1)} %param.4) | copy-start | bytes 995332
  2.2 21.2 %all-to-all-start = ((bf16[12,16,1024]{2,1,0:T(8,128)(2,1)}), bf16[12,16,1024]{2,1,0:T(8,128)(2,1)S(1)}, u32[]{:S(2)}, u32[]{:S(2)}) async-start(bf16[12,16,1024]{2,1,0:T(8,128)(2,1)} %broadcast_in_dim.8), calls=%async_computation | async-start | bytes 786432 | tf_op jit(solution)/shard_map/all_to_all | solution.py:318
  23.4 21.1 %copy-start.1 = (bf16[1,1,16,1024]{3,2,1,0:T(8,128)(2,1)S(1)}, bf16[1,1,16,1024]{3,2,1,0:T(8,128)(2,1)}, u32[]{:S(2)}) copy-start(bf16[1,1,16,1024]{3,2,1,0:T(8,128)(2,1)} %param.5) | copy-start | bytes 98308
  23.4 3.7 %collective-permute-start = (bf16[12,16,1024]{2,1,0:T(8,128)(2,1)S(1)}, bf16[12,16,1024]{2,1,0:T(8,128)(2,1)S(1)}, u32[]{:S(2)}, u32[]{:S(2)}) collective-permute-start(bf16[12,16,1024]{2,1,0:T(8,128)(2,1)S(1)} %all-to-all-done.mine_ref), channel_id=1, source_target_pairs={{0,1},{1,0},{2,3},{3,2},{4,5},{5,4},{6,7},{7,6},{8,9},{9,8},{10,11... | collective-permute-start | bytes 1179656 | tf_op jit(solution)/shard_map/ppermute | solution.py:296
  28.1 15.0 %collective-permute-start.1 = (bf16[16,1024]{1,0:T(8,128)(2,1)S(1)}, bf16[16,1024]{1,0:T(8,128)(2,1)S(1)}, u32[]{:S(2)}, u32[]{:S(2)}) collective-permute-start(bf16[16,1024]{1,0:T(8,128)(2,1)S(1)} %get-tuple-element.32), channel_id=1, source_target_pairs={{0,24},{24,48},{48,72},{72,96},{96,120},{120,144},{144,168},{168,1... | collective-permute-start | bytes 98312 | tf_op jit(solution)/shard_map/ppermute | solution.py:306
  35.2 9.3 %collective-permute-start.2 = (bf16[16,1024]{1,0:T(8,128)(2,1)S(1)}, bf16[16,1024]{1,0:T(8,128)(2,1)S(1)}, u32[]{:S(2)}, u32[]{:S(2)}) collective-permute-start(bf16[16,1024]{1,0:T(8,128)(2,1)S(1)} %get-tuple-element.33), channel_id=1, source_target_pairs={{0,744},{24,0},{48,24},{72,48},{96,72},{120,96},{144,120},{168,144... | collective-permute-start | bytes 98312 | tf_op jit(solution)/shard_map/ppermute | solution.py:306
  45.1 12.0 %collective-permute-start.4 = (bf16[16,1024]{1,0:T(8,128)(2,1)S(1)}, bf16[16,1024]{1,0:T(8,128)(2,1)S(1)}, u32[]{:S(2)}, u32[]{:S(2)}) collective-permute-start(bf16[16,1024]{1,0:T(8,128)(2,1)S(1)} %get-tuple-element.36.own_ref), channel_id=1, source_target_pairs={{0,24},{24,48},{48,72},{72,96},{96,120},{120,144},{144,168},{168,1... | collective-permute-start | bytes 98312 | tf_op jit(solution)/shard_map/ppermute | solution.py:306
  51.4 7.8 %collective-permute-start.3 = (bf16[16,1024]{1,0:T(8,128)(2,1)S(1)}, bf16[16,1024]{1,0:T(8,128)(2,1)S(1)}, u32[]{:S(2)}, u32[]{:S(2)}) collective-permute-start(bf16[16,1024]{1,0:T(8,128)(2,1)S(1)} %get-tuple-element.36.own_ref), channel_id=1, source_target_pairs={{0,744},{24,0},{48,24},{72,48},{96,72},{120,96},{144,120},{168,144... | collective-permute-start | bytes 98312 | tf_op jit(solution)/shard_map/ppermute | solution.py:306
  60.5 18.8 %all-to-all-start.1 = ((bf16[8,21,8,128]{3,2,1,0:T(8,128)(2,1)}), bf16[8,21,8,128]{3,2,1,0:T(8,128)(2,1)S(1)}, u32[]{:S(2)}, u32[]{:S(2)}) async-start(bf16[8,21,8,128]{3,2,1,0:T(8,128)(2,1)} %get-tuple-element.40), calls=%async_computation.1 | async-start | bytes 688128 | tf_op jit(solution)/shard_map/all_to_all | solution.py:334
  68.7 3.6 %collective-permute-start.5 = (bf16[4,3,16,1024]{3,2,1,0:T(8,128)(2,1)S(1)}, bf16[4,3,16,1024]{3,2,1,0:T(8,128)(2,1)S(1)}, u32[]{:S(2)}, u32[]{:S(2)}) collective-permute-start(bf16[4,3,16,1024]{3,2,1,0:T(8,128)(2,1)S(1)} %get-tuple-element.47), channel_id=1, source_target_pairs={{0,1},{1,0},{2,3},{3,2},{4,5},{5,4},{6,7},{7,6},{8,9},{9,8},{10,11... | collective-permute-start | bytes 1179656 | tf_op jit(solution)/shard_map/ppermute | solution.py:296
  72.3 13.3 %collective-permute-start.6 = (bf16[2,3,16,1024]{3,2,1,0:T(8,128)(2,1)S(1)}, bf16[2,3,16,1024]{3,2,1,0:T(8,128)(2,1)S(1)}, u32[]{:S(2)}, u32[]{:S(2)}) collective-permute-start(bf16[2,3,16,1024]{3,2,1,0:T(8,128)(2,1)S(1)} %get-tuple-element.50), channel_id=1, source_target_pairs={{0,6},{6,0},{12,18},{18,12},{1,7},{7,1},{13,19},{19,13},{2,8},{8,2... | collective-permute-start | bytes 589832 | tf_op jit(solution)/shard_map/ppermute | solution.py:340
  80.0 16.7 %all-to-all-start.2 = ((bf16[4,21,8,128]{3,2,1,0:T(8,128)(2,1)}), bf16[4,21,8,128]{3,2,1,0:T(8,128)(2,1)S(1)}, u32[]{:S(2)}, u32[]{:S(2)}) async-start(bf16[4,21,8,128]{3,2,1,0:T(8,128)(2,1)} %total.2), calls=%async_computation.2 | async-start | bytes 344064 | tf_op jit(solution)/shard_map/all_to_all | solution.py:339
  85.7 16.6 %collective-permute-start.7 = (bf16[2,16,1024]{2,1,0:T(8,128)(2,1)S(1)}, bf16[2,16,1024]{2,1,0:T(8,128)(2,1)S(1)}, u32[]{:S(2)}, u32[]{:S(2)}) collective-permute-start(bf16[2,16,1024]{2,1,0:T(8,128)(2,1)S(1)} %get-tuple-element.55), channel_id=1, source_target_pairs={{0,2},{2,4},{4,0},{1,3},{3,5},{5,1},{6,8},{8,10},{10,6},{7,9},{9,1... | collective-permute-start | bytes 196616 | tf_op jit(solution)/shard_map/ppermute | solution.py:343
  87.7 14.7 %collective-permute-start.8 = (bf16[2,16,1024]{2,1,0:T(8,128)(2,1)S(1)}, bf16[2,16,1024]{2,1,0:T(8,128)(2,1)S(1)}, u32[]{:S(2)}, u32[]{:S(2)}) collective-permute-start(bf16[2,16,1024]{2,1,0:T(8,128)(2,1)S(1)} %get-tuple-element.56), channel_id=1, source_target_pairs={{0,4},{2,0},{4,2},{1,5},{3,1},{5,3},{6,10},{8,6},{10,8},{7,11},{9,... | collective-permute-start | bytes 196616 | tf_op jit(solution)/shard_map/ppermute | solution.py:344
  97.5 16.4 %all-to-all-start.3 = ((bf16[8,21,8,128]{3,2,1,0:T(8,128)(2,1)}), bf16[8,21,8,128]{3,2,1,0:T(8,128)(2,1)S(1)}, u32[]{:S(2)}, u32[]{:S(2)}) async-start(bf16[8,21,8,128]{3,2,1,0:T(8,128)(2,1)} %total.3), calls=%async_computation.3 | async-start | bytes 688128 | tf_op jit(solution)/shard_map/all_to_all | solution.py:345
  102.4 7.3 %collective-permute-start.9 = (bf16[16,1024]{1,0:T(8,128)(2,1)S(1)}, bf16[16,1024]{1,0:T(8,128)(2,1)S(1)}, u32[]{:S(2)}, u32[]{:S(2)}) collective-permute-start(bf16[16,1024]{1,0:T(8,128)(2,1)S(1)} %fusion.5), channel_id=1, source_target_pairs={{0,12},{6,18},{12,0},{18,6},{1,13},{7,19},{13,1},{19,7},{2,14},{8,... | collective-permute-start | bytes 98312 | tf_op jit(solution)/shard_map/ppermute | solution.py:347

commit v12 on v11

--- a/solution.py
+++ b/solution.py
@@ -111,72 +111,97 @@
         yield grad[row * HALF : (row + 1) * HALF, column * LANES : (column + 1) * LANES]
 
 
-def own_kernel(core_ref, own_ref, mine_ref, other_ref, units_ref, stack_ref, x_ref):
+def put(units_ref, wide_ref, first, sem):
+    count = units_ref.shape[0]
+    copy = pltpu.make_async_copy(units_ref, wide_ref.at[pl.ds(first, count)], sem)
+    copy.start()
+    return copy
+
+
+def own_kernel(
+    core_ref, own_ref, mine_ref, other_ref, wide_ref, stack_ref, x_ref, units_ref, pad_ref, sems
+):
+    count = units_ref.shape[0]
+    pad_ref[...] = jnp.zeros_like(pad_ref)
+    pad = put(pad_ref, wide_ref, 3 * count, sems.at[0])
     x = merge_cores(core_ref, mine_ref, other_ref, x_ref)
     stack_plane(own_ref[...], stack_ref, 0)
     for at, unit in enumerate(units_of(cross(stack_ref[...], x))):
         units_ref[at] = unit.astype(jnp.bfloat16)
-
-
-def plane_shapes(own, chans):
+    put(units_ref, wide_ref, count, sems.at[1]).wait()
+    pad.wait()
+
+
+def unit_shape(count):
+    return (count, HALF, LANES)
+
+
+def wgrad_own(core, own, mine, other, slots):
     rows, cells = own.shape
-    return [
-        jax.ShapeDtypeStruct((9 * rows * chans // (HALF * LANES), HALF, LANES), jnp.bfloat16),
-        jax.ShapeDtypeStruct((9 * rows, cells), jnp.bfloat16),
-    ]
-
-
-def wgrad_own(core, own, mine, other):
     chans = 2 * mine.shape[0] * mine.shape[1]
-    x = jax.ShapeDtypeStruct((mine.shape[0], 2) + mine.shape[1:], mine.dtype)
+    count = 9 * rows * chans // (HALF * LANES)
+    full = -(-3 * count // slots) * slots
     return pl.pallas_call(
         own_kernel,
-        out_shape=plane_shapes(own, chans) + [x],
+        out_shape=[
+            jax.ShapeDtypeStruct(unit_shape(full), jnp.bfloat16),
+            jax.ShapeDtypeStruct((9 * rows, cells), jnp.bfloat16),
+            jax.ShapeDtypeStruct((mine.shape[0], 2) + mine.shape[1:], mine.dtype),
+        ],
         in_specs=specs(1, 3),
+        out_specs=[pl.BlockSpec(memory_space=pl.ANY)] + specs(0, 2),
+        scratch_shapes=[
+            pltpu.VMEM(unit_shape(count), jnp.bfloat16),
+            pltpu.VMEM(unit_shape(full - 3 * count), jnp.bfloat16),
+            pltpu.SemaphoreType.DMA((2,)),
+        ],
         compiler_params=pltpu.CompilerParams(vmem_limit_bytes=VMEM_LIMIT),
         name="wgrad_own",
     )(core, own, mine, other)
 
 
-def below_kernel(below_ref, x_ref, units_ref, stack_ref):
-    stack_plane(below_ref[...], stack_ref, 0)
+def halo_kernel(plane_ref, x_ref, before_ref, wide_ref, stack_ref, units_ref, sem, *, run):
+    del before_ref
+    count = units_ref.shape[0]
+    stack_plane(plane_ref[...], stack_ref, 0)
     grad = cross(stack_ref[...], x_ref[...].reshape(-1, x_ref.shape[-1]))
     for at, unit in enumerate(units_of(grad)):
         units_ref[at] = unit.astype(jnp.bfloat16)
-
-
-def wgrad_below(below, x):
-    return pl.pallas_call(
-        below_kernel,
-        out_shape=plane_shapes(below, x.shape[0] * x.shape[1] * x.shape[2]),
-        compiler_params=pltpu.CompilerParams(vmem_limit_bytes=VMEM_LIMIT),
-        name="wgrad_below",
-    )(below, x)
-
-
-def above_kernel(above_ref, x_ref, own_ref, below_ref, wide_ref, stack_ref):
-    slots, per = wide_ref.shape[:2]
-    count = own_ref.shape[0]
-    for at in range(count):
-        for unit, ref in ((count + at, own_ref), (2 * count + at, below_ref)):
-            wide_ref[unit // per, unit % per] = ref[at]
-    for unit in range(3 * count, slots * per):
-        wide_ref[unit // per, unit % per] = jnp.zeros((HALF, LANES), jnp.bfloat16)
-    stack_plane(above_ref[...], stack_ref, 0)
-    grad = cross(stack_ref[...], x_ref[...].reshape(-1, x_ref.shape[-1]))
-    for at, unit in enumerate(units_of(grad)):
-        wide_ref[at // per, at % per] = unit.astype(jnp.bfloat16)
-
-
-def wgrad_above(above, x, own_units, below_units, slots):
-    per = -(-3 * own_units.shape[0] // slots)
-    stack = plane_shapes(above, x.shape[0] * x.shape[1] * x.shape[2])[1]
-    return pl.pallas_call(
-        above_kernel,
-        out_shape=[jax.ShapeDtypeStruct((slots, per, HALF, LANES), jnp.bfloat16), stack],
-        compiler_params=pltpu.CompilerParams(vmem_limit_bytes=VMEM_LIMIT),
-        name="wgrad_above",
-    )(above, x, own_units, below_units)
+    put(units_ref, wide_ref, run * count, sem).wait()
+
+
+def wgrad_halo(plane, x, wide, run):
+    rows, cells = plane.shape
+    chans = x.shape[0] * x.shape[1] * x.shape[2]
+    return pl.pallas_call(
+        functools.partial(halo_kernel, run=run),
+        out_shape=[
+            jax.ShapeDtypeStruct(wide.shape, wide.dtype),
+            jax.ShapeDtypeStruct((9 * rows, cells), jnp.bfloat16),
+        ],
+        in_specs=specs(0, 2) + [pl.BlockSpec(memory_space=pl.ANY)],
+        out_specs=[pl.BlockSpec(memory_space=pl.ANY)] + specs(0, 1),
+        scratch_shapes=[
+            pltpu.VMEM(unit_shape(9 * rows * chans // (HALF * LANES)), jnp.bfloat16),
+            pltpu.SemaphoreType.DMA,
+        ],
+        input_output_aliases={2: 0},
+        compiler_params=pltpu.CompilerParams(vmem_limit_bytes=VMEM_LIMIT),
+        name="wgrad_halo",
+    )(plane, x, wide)
+
+
+def copies_kernel(block_ref, out_ref):
+    out_ref[...] = jnp.broadcast_to(block_ref[...][None], out_ref.shape)
+
+
+def copies(block, count):
+    return pl.pallas_call(
+        copies_kernel,
+        out_shape=jax.ShapeDtypeStruct((count,) + block.shape, block.dtype),
+        compiler_params=pltpu.CompilerParams(vmem_limit_bytes=VMEM_LIMIT),
+        name="copies",
+    )(block)
 
 
 def dgrad_kernel(
@@ -312,10 +337,7 @@
     own = volume.reshape(rows, cells)
     cot = cotangent.reshape(rows, cells)
 
-    def copies(block):
-        return jnp.broadcast_to(block[None], (chips, rows, cells))
-
-    mine = lax.all_to_all(copies(own), CHIPS, 0, 0)
+    mine = lax.all_to_all(copies(own, chips), CHIPS, 0, 0)
     k_rows = jnp.transpose(kernel.reshape(rows, TAPS, -1), (1, 0, 2)).reshape(TAPS * rows, -1)
     mine, k_rows, cot, core, x_at, z_at = lax.optimization_barrier(
         (mine, k_rows, cot, core, x_at, z_at)
@@ -326,10 +348,11 @@
     activated, grad_pre = activate(mid, shift(up, 1), shift(down, -1), cot)
 
     above, below = shift(grad_pre, -1), shift(grad_pre, 1)
-    own_units, own_stack, x = wgrad_own(core, grad_pre, mine, other)
     ys, zs = lax.axis_size("y"), lax.axis_size("zh")
-    below_units, below_stack = wgrad_below(below, x)
-    wide, above_stack = wgrad_above(above, x, own_units, below_units, ys)
+    wide, own_stack, x = wgrad_own(core, grad_pre, mine, other, ys)
+    wide, below_stack = wgrad_halo(below, x, wide, 2)
+    wide, above_stack = wgrad_halo(above, x, wide, 0)
+    wide = wide.reshape((ys, -1) + wide.shape[1:])
     scale = 1.0 / math.sqrt(UNIV * DEPTH * SIDE * SIDE)
     over_y = lax.all_to_all(wide, "y", 0, 0)
 

time: 116 us -> 116 us (level)
  Pallas kernels: 7.16 us -> 9.2 us
    pallas_call x3 -> x4, Pallas kernels: 2.36 us -> 4.39 us  [the longest x2 2.39 us: wgrad_halo(): pl.pallas_call(functools.partial(halo_kernel, run=run), out_shape=[jax.Sh...]
    broadcast_in_dim x1 -> x0, local copies, waits for them, and re-layouts: 1.55 us -> none  [copies(): return jnp.broadcast_to(block[None], (chips, rows, cells))]
    ppermute x4, waiting for transfers between devices: 3.56 us -> 2.21 us  [shift(): lax.ppermute(block, DEP, [(i, (i + step) % depths) for i in range(depths)])]
  transfers between devices with their start and end apart: 14 -> 14, of which waited for: 10 -> 10; matrix products, arithmetic and copies ran while one was open for 1% -> 1% of each run, Pallas kernels for 3% -> 4%
where the time goes in v12:
time: 116 us; the launch traced here: 115 us
  starting transfers between devices  73.4 us (63%)
  waiting for transfers between devices  29.8 us (26%)
  Pallas kernels  9.2 us (8%)
    ppermute x4, starting transfers between devices, shift(): lax.ppermute(block, DEP, [(i, (i + step) % depths) for i in range(depths)])  25.8 us
    all_to_all x1, starting transfers between devices, body(): mine = lax.all_to_all(copies(own, chips), CHIPS, 0, 0)  13.1 us
    all_to_all x1, waiting for transfers between devices, body(): mine = lax.all_to_all(copies(own, chips), CHIPS, 0, 0)  8.12 us
    all_to_all x1, starting transfers between devices, body(): over_y = lax.all_to_all(wide, 'y', 0, 0)  7.11 us
    all_to_all x1, starting transfers between devices, body(): over_z = lax.all_to_all(total_spread(over_y, 1.0, zs), 'zh', 0, 0)  5.45 us
    all_to_all x1, starting transfers between devices, body(): units = lax.all_to_all(total_spread(over_z, scale, ys), 'y', 0, 0)  4.93 us
    ppermute x1, starting transfers between devices, body(): before = lax.ppermute(before, 'zl', [(i, (i + 2) % 3) for i in range(3)])  4.82 us
    ppermute x1, waiting for transfers between devices, body(): lax.ppermute(total[1].astype(jnp.bfloat16), 'x', [(i, i ^ 2) for i in ran...  4.54 us
  transfers between devices with their start and end apart: 14, of which 10 were waited for; matrix products, arithmetic and copies ran while one was open for 1% of the time, Pallas kernels for 4%

profile of v12, /device:TPU:2, one launch (start us, length us, event | category | flops | bytes accessed | tf_op | source)
XLA Modules:
  0.0 114.6 jit_solution(152508419902416594)
XLA Ops:
  0.6 0.0 copy-start.2
  0.6 0.7 copy-done.2
  1.4 0.8 copies.1
  2.2 0.0 copy-start
  2.2 13.1 %all-to-all-start = ((bf16[12,16,1024]{2,1,0:T(8,128)(2,1)}), bf16[12,16,1024]{2,1,0:T(8,128)(2,1)S(1)}, u32[]{:S(2)}, u32[]{:S(2)}) async-start(bf16[12,16,1024]{2,1,0:T(8,128)(2,1)} %copies.1), calls=%async_computation | async-start | bytes 786432 | tf_op jit(solution)/shard_map/all_to_all | solution.py:340
  15.3 8.1 %all-to-all-done.mine_ref = bf16[12,16,1024]{2,1,0:T(8,128)(2,1)S(1)} async-done(((bf16[12,16,1024]{2,1,0:T(8,128)(2,1)}), bf16[12,16,1024]{2,1,0:T(8,128)(2,1)S(1)}, u32[]{:S(2)}, u32[]{:S(2)}) %all-to-all-start) | async-done | bytes 393248 | tf_op jit(solution)/shard_map/all_to_all | solution.py:340
  23.4 0.0 copy-start.1
  23.4 2.0 %collective-permute-start = (bf16[12,16,1024]{2,1,0:T(8,128)(2,1)S(1)}, bf16[12,16,1024]{2,1,0:T(8,128)(2,1)S(1)}, u32[]{:S(2)}, u32[]{:S(2)}) collective-permute-start(bf16[12,16,1024]{2,1,0:T(8,128)(2,1)S(1)} %all-to-all-done.mine_ref), channel_id=1, source_target_pairs={{0,1},{1,0},{2,3},{3,2},{4,5},{5,4},{6,7},{7,6},{8,9},{9,8},{10,11... | collective-permute-start | bytes 1179656 | tf_op jit(solution)/shard_map/ppermute | solution.py:321
  25.4 1.7 %collective-permute-done.other_ref = bf16[12,16,1024]{2,1,0:T(8,128)(2,1)S(1)} collective-permute-done((bf16[12,16,1024]{2,1,0:T(8,128)(2,1)S(1)}, bf16[12,16,1024]{2,1,0:T(8,128)(2,1)S(1)}, u32[]{:S(2)}, u32[]{:S(2)}) %collective-permute-start) | collective-permute-done | bytes 393248 | tf_op jit(solution)/shard_map/ppermute | solution.py:321
  27.1 0.0 copy-done
  27.1 0.9 conv.1
  28.1 7.1 %collective-permute-start.1 = (bf16[16,1024]{1,0:T(8,128)(2,1)S(1)}, bf16[16,1024]{1,0:T(8,128)(2,1)S(1)}, u32[]{:S(2)}, u32[]{:S(2)}) collective-permute-start(bf16[16,1024]{1,0:T(8,128)(2,1)S(1)} %get-tuple-element.32), channel_id=1, source_target_pairs={{0,24},{24,48},{48,72},{72,96},{96,120},{120,144},{144,168},{168,1... | collective-permute-start | bytes 98312 | tf_op jit(solution)/shard_map/ppermute | solution.py:331
  35.2 7.3 %collective-permute-start.2 = (bf16[16,1024]{1,0:T(8,128)(2,1)S(1)}, bf16[16,1024]{1,0:T(8,128)(2,1)S(1)}, u32[]{:S(2)}, u32[]{:S(2)}) collective-permute-start(bf16[16,1024]{1,0:T(8,128)(2,1)S(1)} %get-tuple-element.33), channel_id=1, source_target_pairs={{0,744},{24,0},{48,24},{72,48},{96,72},{120,96},{144,120},{168,144... | collective-permute-start | bytes 98312 | tf_op jit(solution)/shard_map/ppermute | solution.py:331
  42.5 0.6 collective-permute-done.1.low_ref
  43.1 1.4 %collective-permute-done.2.high_ref = bf16[16,1024]{1,0:T(8,128)(2,1)S(1)} collective-permute-done((bf16[16,1024]{1,0:T(8,128)(2,1)S(1)}, bf16[16,1024]{1,0:T(8,128)(2,1)S(1)}, u32[]{:S(2)}, u32[]{:S(2)}) %collective-permute-start.2) | collective-permute-done | bytes 32800 | tf_op jit(solution)/shard_map/ppermute | solution.py:331
  44.5 0.0 copy-done.1
  44.5 0.6 activate.1
  45.1 6.2 %collective-permute-start.4 = (bf16[16,1024]{1,0:T(8,128)(2,1)S(1)}, bf16[16,1024]{1,0:T(8,128)(2,1)S(1)}, u32[]{:S(2)}, u32[]{:S(2)}) collective-permute-start(bf16[16,1024]{1,0:T(8,128)(2,1)S(1)} %get-tuple-element.36.own_ref), channel_id=1, source_target_pairs={{0,24},{24,48},{48,72},{72,96},{96,120},{120,144},{144,168},{168,1... | collective-permute-start | bytes 98312 | tf_op jit(solution)/shard_map/ppermute | solution.py:331
  51.4 5.1 %collective-permute-start.3 = (bf16[16,1024]{1,0:T(8,128)(2,1)S(1)}, bf16[16,1024]{1,0:T(8,128)(2,1)S(1)}, u32[]{:S(2)}, u32[]{:S(2)}) collective-permute-start(bf16[16,1024]{1,0:T(8,128)(2,1)S(1)} %get-tuple-element.36.own_ref), channel_id=1, source_target_pairs={{0,744},{24,0},{48,24},{72,48},{96,72},{120,96},{144,120},{168,144... | collective-permute-start | bytes 98312 | tf_op jit(solution)/shard_map/ppermute | solution.py:331
  56.5 1.2 %wgrad_own.1 = (bf16[168,8,128]{2,1,0:T(8,128)(2,1)}, bf16[144,1024]{1,0:T(8,128)(2,1)S(1)}, bf16[12,2,16,1024]{3,2,1,0:T(8,128)(2,1)S(1)}) custom-call(s32[1]{0:T(128)} %bitcast.5.core_ref, bf16[16,1024]{1,0:T(8,128)(2,1)S(1)} %get-tuple-element.36.own_ref, bf16[12,16,1024]{2,1,0:T(8,128)(2,1)S(1)} %all-to-all-done.mine_ref, ...), custom_call_target="tpu_custom_call" | custom-call | tf_op jit(solution)/shard_map/wgrad_own/pallas_call | solution.py:144
  57.8 0.0 collective-permute-done.4.plane_ref
  57.8 1.2 %wgrad_halo.2 = (bf16[168,8,128]{2,1,0:T(8,128)(2,1)}, bf16[144,1024]{1,0:T(8,128)(2,1)S(1)}) custom-call(bf16[16,1024]{1,0:T(8,128)(2,1)S(1)} %collective-permute-done.4.plane_ref, bf16[12,2,16,1024]{3,2,1,0:T(8,128)(2,1)S(1)} %get-tuple-element.37.x_ref, bf16[168,8,128]{2,1,0:T(8,128)(2,1)} %get-tuple-element.38.before_ref), custom_call_target="tpu_custom_call", output_to_operand_aliasing={{0}: (2, {})} | custom-call | tf_op jit(solution)/shard_map/wgrad_halo/pallas_call | solution.py:176
  59.0 0.2 collective-permute-done.3.plane_ref
  59.2 1.2 %wgrad_halo.3 = (bf16[168,8,128]{2,1,0:T(8,128)(2,1)}, bf16[144,1024]{1,0:T(8,128)(2,1)S(1)}) custom-call(bf16[16,1024]{1,0:T(8,128)(2,1)S(1)} %collective-permute-done.3.plane_ref, bf16[12,2,16,1024]{3,2,1,0:T(8,128)(2,1)S(1)} %get-tuple-element.37.x_ref, bf16[168,8,128]{2,1,0:T(8,128)(2,1)} %get-tuple-element.39.before_ref), custom_call_target="tpu_custom_call", output_to_operand_aliasing={{0}: (2, {})} | custom-call | tf_op jit(solution)/shard_map/wgrad_halo/pallas_call | solution.py:176
  60.4 7.1 %all-to-all-start.1 = ((bf16[8,21,8,128]{3,2,1,0:T(8,128)(2,1)}), bf16[8,21,8,128]{3,2,1,0:T(8,128)(2,1)S(1)}, u32[]{:S(2)}, u32[]{:S(2)}) async-start(bf16[8,21,8,128]{3,2,1,0:T(8,128)(2,1)} %bitcast.9), calls=%async_computation.1 | async-start | bytes 688128 | tf_op jit(solution)/shard_map/all_to_all | solution.py:357
  67.5 0.8 dgrad.1
  68.3 1.9 %collective-permute-start.5 = (bf16[4,3,16,1024]{3,2,1,0:T(8,128)(2,1)S(1)}, bf16[4,3,16,1024]{3,2,1,0:T(8,128)(2,1)S(1)}, u32[]{:S(2)}, u32[]{:S(2)}) collective-permute-start(bf16[4,3,16,1024]{3,2,1,0:T(8,128)(2,1)S(1)} %get-tuple-element.47), channel_id=1, source_target_pairs={{0,1},{1,0},{2,3},{3,2},{4,5},{5,4},{6,7},{7,6},{8,9},{9,8},{10,11... | collective-permute-start | bytes 1179656 | tf_op jit(solution)/shard_map/ppermute | solution.py:321
  70.3 1.7 %collective-permute-done.5.came_ref = bf16[4,3,16,1024]{3,2,1,0:T(8,128)(2,1)S(1)} collective-permute-done((bf16[4,3,16,1024]{3,2,1,0:T(8,128)(2,1)S(1)}, bf16[4,3,16,1024]{3,2,1,0:T(8,128)(2,1)S(1)}, u32[]{:S(2)}, u32[]{:S(2)}) %collective-permute-start.5) | collective-permute-done | bytes 393248 | tf_op jit(solution)/shard_map/ppermute | solution.py:321
  71.9 0.1 halve.1
  72.0 3.5 %collective-permute-start.6 = (bf16[2,3,16,1024]{3,2,1,0:T(8,128)(2,1)S(1)}, bf16[2,3,16,1024]{3,2,1,0:T(8,128)(2,1)S(1)}, u32[]{:S(2)}, u32[]{:S(2)}) collective-permute-start(bf16[2,3,16,1024]{3,2,1,0:T(8,128)(2,1)S(1)} %get-tuple-element.50), channel_id=1, source_target_pairs={{0,6},{6,0},{12,18},{18,12},{1,7},{7,1},{13,19},{19,13},{2,8},{8,2... | collective-permute-start | bytes 589832 | tf_op jit(solution)/shard_map/ppermute | solution.py:363
  75.5 3.9 %all-to-all-done.1.terms_ref = bf16[8,21,8,128]{3,2,1,0:T(8,128)(2,1)S(1)} async-done(((bf16[8,21,8,128]{3,2,1,0:T(8,128)(2,1)}), bf16[8,21,8,128]{3,2,1,0:T(8,128)(2,1)S(1)}, u32[]{:S(2)}, u32[]{:S(2)}) %all-to-all-start.1) | async-done | bytes 344096 | tf_op jit(solution)/shard_map/all_to_all | solution.py:357
  79.4 0.7 total.2
  80.1 5.4 %all-to-all-start.2 = ((bf16[4,21,8,128]{3,2,1,0:T(8,128)(2,1)}), bf16[4,21,8,128]{3,2,1,0:T(8,128)(2,1)S(1)}, u32[]{:S(2)}, u32[]{:S(2)}) async-start(bf16[4,21,8,128]{3,2,1,0:T(8,128)(2,1)} %total.2), calls=%async_computation.2 | async-start | bytes 344064 | tf_op jit(solution)/shard_map/all_to_all | solution.py:362
  85.6 0.0 collective-permute-done.6
  85.7 1.9 %collective-permute-start.7 = (bf16[2,16,1024]{2,1,0:T(8,128)(2,1)S(1)}, bf16[2,16,1024]{2,1,0:T(8,128)(2,1)S(1)}, u32[]{:S(2)}, u32[]{:S(2)}) collective-permute-start(bf16[2,16,1024]{2,1,0:T(8,128)(2,1)S(1)} %get-tuple-element.55), channel_id=1, source_target_pairs={{0,2},{2,4},{4,0},{1,3},{3,5},{5,1},{6,8},{8,10},{10,6},{7,9},{9,1... | collective-permute-start | bytes 196616 | tf_op jit(solution)/shard_map/ppermute | solution.py:366
  87.6 4.8 %collective-permute-start.8 = (bf16[2,16,1024]{2,1,0:T(8,128)(2,1)S(1)}, bf16[2,16,1024]{2,1,0:T(8,128)(2,1)S(1)}, u32[]{:S(2)}, u32[]{:S(2)}) collective-permute-start(bf16[2,16,1024]{2,1,0:T(8,128)(2,1)S(1)} %get-tuple-element.56), channel_id=1, source_target_pairs={{0,4},{2,0},{4,2},{1,5},{3,1},{5,3},{6,10},{8,6},{10,8},{7,11},{9,... | collective-permute-start | bytes 196616 | tf_op jit(solution)/shard_map/ppermute | solution.py:367
  92.4 4.2 %all-to-all-done.2.terms_ref = bf16[4,21,8,128]{3,2,1,0:T(8,128)(2,1)S(1)} async-done(((bf16[4,21,8,128]{3,2,1,0:T(8,128)(2,1)}), bf16[4,21,8,128]{3,2,1,0:T(8,128)(2,1)S(1)}, u32[]{:S(2)}, u32[]{:S(2)}) %all-to-all-start.2) | async-done | bytes 172064 | tf_op jit(solution)/shard_map/all_to_all | solution.py:362
  96.6 0.8 total.3
  97.4 4.9 %all-to-all-start.3 = ((bf16[8,21,8,128]{3,2,1,0:T(8,128)(2,1)}), bf16[8,21,8,128]{3,2,1,0:T(8,128)(2,1)S(1)}, u32[]{:S(2)}, u32[]{:S(2)}) async-start(bf16[8,21,8,128]{3,2,1,0:T(8,128)(2,1)} %total.3), calls=%async_computation.3 | async-start | bytes 688128 | tf_op jit(solution)/shard_map/all_to_all | solution.py:368
  102.3 0.0 collective-permute-done.7
  102.3 0.0 collective-permute-done.8
  102.4 2.8 %collective-permute-start.9 = (bf16[16,1024]{1,0:T(8,128)(2,1)S(1)}, bf16[16,1024]{1,0:T(8,128)(2,1)S(1)}, u32[]{:S(2)}, u32[]{:S(2)}) collective-permute-start(bf16[16,1024]{1,0:T(8,128)(2,1)S(1)} %fusion.5), channel_id=1, source_target_pairs={{0,12},{6,18},{12,0},{18,6},{1,13},{7,19},{13,1},{19,7},{2,14},{8,... | collective-permute-start | bytes 98312 | tf_op jit(solution)/shard_map/ppermute | solution.py:370
  105.1 4.5 %collective-permute-done.9 = bf16[16,1024]{1,0:T(8,128)(2,1)S(1)} collective-permute-done((bf16[16,1024]{1,0:T(8,128)(2,1)S(1)}, bf16[16,1024]{1,0:T(8,128)(2,1)S(1)}, u32[]{:S(2)}, u32[]{:S(2)}) %collective-permute-start.9) | collective-permute-done | bytes 32800 | tf_op jit(solution)/shard_map/ppermute | solution.py:370
  109.7 0.6 fusion.4
  110.3 3.5 %all-to-all-done.3.units_ref = bf16[8,21,8,128]{3,2,1,0:T(8,128)(2,1)S(1)} async-done(((bf16[8,21,8,128]{3,2,1,0:T(8,128)(2,1)}), bf16[8,21,8,128]{3,2,1,0:T(8,128)(2,1)S(1)}, u32[]{:S(2)}, u32[]{:S(2)}) %all-to-all-start.3) | async-done | bytes 344096 | tf_op jit(solution)/shard_map/all_to_all | solution.py:368
  113.8 0.9 unpack.1
  (4 shorter events, 0.1 us)
Async XLA Ops:
  0.6 0.8 copy-start.2
  2.2 25.0 %copy-start = (bf16[16,3,3,3,384]{4,0,3,2,1:T(8,128)(2,1)S(1)}, bf16[16,3,3,3,384]{4,0,3,2,1:T(8,128)(2,1)}, u32[]{:S(2)}) copy-start(bf16[16,3,3,3,384]{4,0,3,2,1:T(8,128)(2,1)} %param.4) | copy-start | bytes 995332
  2.2 21.2 %all-to-all-start = ((bf16[12,16,1024]{2,1,0:T(8,128)(2,1)}), bf16[12,16,1024]{2,1,0:T(8,128)(2,1)S(1)}, u32[]{:S(2)}, u32[]{:S(2)}) async-start(bf16[12,16,1024]{2,1,0:T(8,128)(2,1)} %copies.1), calls=%async_computation | async-start | bytes 786432 | tf_op jit(solution)/shard_map/all_to_all | solution.py:340
  23.4 21.1 %copy-start.1 = (bf16[1,1,16,1024]{3,2,1,0:T(8,128)(2,1)S(1)}, bf16[1,1,16,1024]{3,2,1,0:T(8,128)(2,1)}, u32[]{:S(2)}) copy-start(bf16[1,1,16,1024]{3,2,1,0:T(8,128)(2,1)} %param.5) | copy-start | bytes 98308
  23.4 3.7 %collective-permute-start = (bf16[12,16,1024]{2,1,0:T(8,128)(2,1)S(1)}, bf16[12,16,1024]{2,1,0:T(8,128)(2,1)S(1)}, u32[]{:S(2)}, u32[]{:S(2)}) collective-permute-start(bf16[12,16,1024]{2,1,0:T(8,128)(2,1)S(1)} %all-to-all-done.mine_ref), channel_id=1, source_target_pairs={{0,1},{1,0},{2,3},{3,2},{4,5},{5,4},{6,7},{7,6},{8,9},{9,8},{10,11... | collective-permute-start | bytes 1179656 | tf_op jit(solution)/shard_map/ppermute | solution.py:321
  28.1 15.0 %collective-permute-start.1 = (bf16[16,1024]{1,0:T(8,128)(2,1)S(1)}, bf16[16,1024]{1,0:T(8,128)(2,1)S(1)}, u32[]{:S(2)}, u32[]{:S(2)}) collective-permute-start(bf16[16,1024]{1,0:T(8,128)(2,1)S(1)} %get-tuple-element.32), channel_id=1, source_target_pairs={{0,24},{24,48},{48,72},{72,96},{96,120},{120,144},{144,168},{168,1... | collective-permute-start | bytes 98312 | tf_op jit(solution)/shard_map/ppermute | solution.py:331
  35.2 9.3 %collective-permute-start.2 = (bf16[16,1024]{1,0:T(8,128)(2,1)S(1)}, bf16[16,1024]{1,0:T(8,128)(2,1)S(1)}, u32[]{:S(2)}, u32[]{:S(2)}) collective-permute-start(bf16[16,1024]{1,0:T(8,128)(2,1)S(1)} %get-tuple-element.33), channel_id=1, source_target_pairs={{0,744},{24,0},{48,24},{72,48},{96,72},{120,96},{144,120},{168,144... | collective-permute-start | bytes 98312 | tf_op jit(solution)/shard_map/ppermute | solution.py:331
  45.1 12.6 %collective-permute-start.4 = (bf16[16,1024]{1,0:T(8,128)(2,1)S(1)}, bf16[16,1024]{1,0:T(8,128)(2,1)S(1)}, u32[]{:S(2)}, u32[]{:S(2)}) collective-permute-start(bf16[16,1024]{1,0:T(8,128)(2,1)S(1)} %get-tuple-element.36.own_ref), channel_id=1, source_target_pairs={{0,24},{24,48},{48,72},{72,96},{96,120},{120,144},{144,168},{168,1... | collective-permute-start | bytes 98312 | tf_op jit(solution)/shard_map/ppermute | solution.py:331
  51.4 7.8 %collective-permute-start.3 = (bf16[16,1024]{1,0:T(8,128)(2,1)S(1)}, bf16[16,1024]{1,0:T(8,128)(2,1)S(1)}, u32[]{:S(2)}, u32[]{:S(2)}) collective-permute-start(bf16[16,1024]{1,0:T(8,128)(2,1)S(1)} %get-tuple-element.36.own_ref), channel_id=1, source_target_pairs={{0,744},{24,0},{48,24},{72,48},{96,72},{120,96},{144,120},{168,144... | collective-permute-start | bytes 98312 | tf_op jit(solution)/shard_map/ppermute | solution.py:331
  60.4 19.0 %all-to-all-start.1 = ((bf16[8,21,8,128]{3,2,1,0:T(8,128)(2,1)}), bf16[8,21,8,128]{3,2,1,0:T(8,128)(2,1)S(1)}, u32[]{:S(2)}, u32[]{:S(2)}) async-start(bf16[8,21,8,128]{3,2,1,0:T(8,128)(2,1)} %bitcast.9), calls=%async_computation.1 | async-start | bytes 688128 | tf_op jit(solution)/shard_map/all_to_all | solution.py:357
  68.3 3.6 %collective-permute-start.5 = (bf16[4,3,16,1024]{3,2,1,0:T(8,128)(2,1)S(1)}, bf16[4,3,16,1024]{3,2,1,0:T(8,128)(2,1)S(1)}, u32[]{:S(2)}, u32[]{:S(2)}) collective-permute-start(bf16[4,3,16,1024]{3,2,1,0:T(8,128)(2,1)S(1)} %get-tuple-element.47), channel_id=1, source_target_pairs={{0,1},{1,0},{2,3},{3,2},{4,5},{5,4},{6,7},{7,6},{8,9},{9,8},{10,11... | collective-permute-start | bytes 1179656 | tf_op jit(solution)/shard_map/ppermute | solution.py:321
  72.0 13.6 %collective-permute-start.6 = (bf16[2,3,16,1024]{3,2,1,0:T(8,128)(2,1)S(1)}, bf16[2,3,16,1024]{3,2,1,0:T(8,128)(2,1)S(1)}, u32[]{:S(2)}, u32[]{:S(2)}) collective-permute-start(bf16[2,3,16,1024]{3,2,1,0:T(8,128)(2,1)S(1)} %get-tuple-element.50), channel_id=1, source_target_pairs={{0,6},{6,0},{12,18},{18,12},{1,7},{7,1},{13,19},{19,13},{2,8},{8,2... | collective-permute-start | bytes 589832 | tf_op jit(solution)/shard_map/ppermute | solution.py:363
  80.1 16.5 %all-to-all-start.2 = ((bf16[4,21,8,128]{3,2,1,0:T(8,128)(2,1)}), bf16[4,21,8,128]{3,2,1,0:T(8,128)(2,1)S(1)}, u32[]{:S(2)}, u32[]{:S(2)}) async-start(bf16[4,21,8,128]{3,2,1,0:T(8,128)(2,1)} %total.2), calls=%async_computation.2 | async-start | bytes 344064 | tf_op jit(solution)/shard_map/all_to_all | solution.py:362
  85.7 16.6 %collective-permute-start.7 = (bf16[2,16,1024]{2,1,0:T(8,128)(2,1)S(1)}, bf16[2,16,1024]{2,1,0:T(8,128)(2,1)S(1)}, u32[]{:S(2)}, u32[]{:S(2)}) collective-permute-start(bf16[2,16,1024]{2,1,0:T(8,128)(2,1)S(1)} %get-tuple-element.55), channel_id=1, source_target_pairs={{0,2},{2,4},{4,0},{1,3},{3,5},{5,1},{6,8},{8,10},{10,6},{7,9},{9,1... | collective-permute-start | bytes 196616 | tf_op jit(solution)/shard_map/ppermute | solution.py:366
  87.6 14.7 %collective-permute-start.8 = (bf16[2,16,1024]{2,1,0:T(8,128)(2,1)S(1)}, bf16[2,16,1024]{2,1,0:T(8,128)(2,1)S(1)}, u32[]{:S(2)}, u32[]{:S(2)}) collective-permute-start(bf16[2,16,1024]{2,1,0:T(8,128)(2,1)S(1)} %get-tuple-element.56), channel_id=1, source_target_pairs={{0,4},{2,0},{4,2},{1,5},{3,1},{5,3},{6,10},{8,6},{10,8},{7,11},{9,... | collective-permute-start | bytes 196616 | tf_op jit(solution)/shard_map/ppermute | solution.py:367
  97.4 16.4 %all-to-all-start.3 = ((bf16[8,21,8,128]{3,2,1,0:T(8,128)(2,1)}), bf16[8,21,8,128]{3,2,1,0:T(8,128)(2,1)S(1)}, u32[]{:S(2)}, u32[]{:S(2)}) async-start(bf16[8,21,8,128]{3,2,1,0:T(8,128)(2,1)} %total.3), calls=%async_computation.3 | async-start | bytes 688128 | tf_op jit(solution)/shard_map/all_to_all | solution.py:368
  102.4 7.3 %collective-permute-start.9 = (bf16[16,1024]{1,0:T(8,128)(2,1)S(1)}, bf16[16,1024]{1,0:T(8,128)(2,1)S(1)}, u32[]{:S(2)}, u32[]{:S(2)}) collective-permute-start(bf16[16,1024]{1,0:T(8,128)(2,1)S(1)} %fusion.5), channel_id=1, source_target_pairs={{0,12},{6,18},{12,0},{18,6},{1,13},{7,19},{13,1},{19,7},{2,14},{8,... | collective-permute-start | bytes 98312 | tf_op jit(solution)/shard_map/ppermute | solution.py:370

commit v13 on v11

--- a/solution.py
+++ b/solution.py
@@ -138,45 +138,45 @@
     )(core, own, mine, other)
 
 
-def below_kernel(below_ref, x_ref, units_ref, stack_ref):
-    stack_plane(below_ref[...], stack_ref, 0)
+def first_kernel(plane_ref, x_ref, units_ref, stack_ref):
+    stack_plane(plane_ref[...], stack_ref, 0)
     grad = cross(stack_ref[...], x_ref[...].reshape(-1, x_ref.shape[-1]))
     for at, unit in enumerate(units_of(grad)):
         units_ref[at] = unit.astype(jnp.bfloat16)
 
 
-def wgrad_below(below, x):
-    return pl.pallas_call(
-        below_kernel,
-        out_shape=plane_shapes(below, x.shape[0] * x.shape[1] * x.shape[2]),
-        compiler_params=pltpu.CompilerParams(vmem_limit_bytes=VMEM_LIMIT),
-        name="wgrad_below",
-    )(below, x)
-
-
-def above_kernel(above_ref, x_ref, own_ref, below_ref, wide_ref, stack_ref):
+def wgrad_first(plane, x):
+    return pl.pallas_call(
+        first_kernel,
+        out_shape=plane_shapes(plane, x.shape[0] * x.shape[1] * x.shape[2]),
+        compiler_params=pltpu.CompilerParams(vmem_limit_bytes=VMEM_LIMIT),
+        name="wgrad_first",
+    )(plane, x)
+
+
+def last_kernel(below_ref, x_ref, above_ref, own_ref, wide_ref, stack_ref):
     slots, per = wide_ref.shape[:2]
     count = own_ref.shape[0]
     for at in range(count):
-        for unit, ref in ((count + at, own_ref), (2 * count + at, below_ref)):
+        for unit, ref in ((at, above_ref), (count + at, own_ref)):
             wide_ref[unit // per, unit % per] = ref[at]
     for unit in range(3 * count, slots * per):
         wide_ref[unit // per, unit % per] = jnp.zeros((HALF, LANES), jnp.bfloat16)
-    stack_plane(above_ref[...], stack_ref, 0)
+    stack_plane(below_ref[...], stack_ref, 0)
     grad = cross(stack_ref[...], x_ref[...].reshape(-1, x_ref.shape[-1]))
-    for at, unit in enumerate(units_of(grad)):
+    for at, unit in enumerate(units_of(grad), 2 * count):
         wide_ref[at // per, at % per] = unit.astype(jnp.bfloat16)
 
 
-def wgrad_above(above, x, own_units, below_units, slots):
+def wgrad_last(below, x, above_units, own_units, slots):
     per = -(-3 * own_units.shape[0] // slots)
-    stack = plane_shapes(above, x.shape[0] * x.shape[1] * x.shape[2])[1]
-    return pl.pallas_call(
-        above_kernel,
+    stack = plane_shapes(below, x.shape[0] * x.shape[1] * x.shape[2])[1]
+    return pl.pallas_call(
+        last_kernel,
         out_shape=[jax.ShapeDtypeStruct((slots, per, HALF, LANES), jnp.bfloat16), stack],
         compiler_params=pltpu.CompilerParams(vmem_limit_bytes=VMEM_LIMIT),
-        name="wgrad_above",
-    )(above, x, own_units, below_units)
+        name="wgrad_last",
+    )(below, x, above_units, own_units)
 
 
 def dgrad_kernel(
@@ -272,24 +272,27 @@
 
 def unpack_kernel(units_ref, out_ref):
     taps, rows, chans = out_ref.shape
-    per = units_ref.shape[1]
     columns = chans // LANES
-    for at in range(taps * rows // HALF * columns):
+    for at in range(units_ref.shape[0]):
         row, column = divmod(at, columns)
         tap, half = divmod(row, rows // HALF)
-        block = units_ref[at // per, at % per].astype(jnp.float32)
+        block = units_ref[at].astype(jnp.float32)
         out_ref[
             tap, half * HALF : (half + 1) * HALF, column * LANES : (column + 1) * LANES
         ] = block
 
 
 def unpack(units, rows, chans):
+    count = 9 * rows * chans // (HALF * LANES)
     return pl.pallas_call(
         unpack_kernel,
+        grid=(3,),
+        in_specs=[pl.BlockSpec((count, HALF, LANES), lambda i: (i, 0, 0))],
+        out_specs=pl.BlockSpec((9, rows, chans), lambda i: (i, 0, 0)),
         out_shape=jax.ShapeDtypeStruct((TAPS, rows, chans), jnp.float32),
         compiler_params=pltpu.CompilerParams(vmem_limit_bytes=VMEM_LIMIT),
         name="unpack",
-    )(units)
+    )(units.reshape(-1, HALF, LANES))
 
 
 def swap_cores(blocks):
@@ -328,8 +331,8 @@
     above, below = shift(grad_pre, -1), shift(grad_pre, 1)
     own_units, own_stack, x = wgrad_own(core, grad_pre, mine, other)
     ys, zs = lax.axis_size("y"), lax.axis_size("zh")
-    below_units, below_stack = wgrad_below(below, x)
-    wide, above_stack = wgrad_above(above, x, own_units, below_units, ys)
+    above_units, above_stack = wgrad_first(above, x)
+    wide, below_stack = wgrad_last(below, x, above_units, own_units, ys)
     scale = 1.0 / math.sqrt(UNIV * DEPTH * SIDE * SIDE)
     over_y = lax.all_to_all(wide, "y", 0, 0)
 

time: 116 us -> 118 us (1.017)
  the two profiles are of different devices: /device:TPU:2 before, /device:TPU:64 now
where the time goes in v13:
time: 118 us; the launch traced here: 117 us
  starting transfers between devices  64.1 us (54%)
  waiting for transfers between devices  41.8 us (35%)
  Pallas kernels  7.69 us (7%)
  local copies, waits for them, and re-layouts  1.57 us (1%)
    ppermute x4, starting transfers between devices, shift(): lax.ppermute(block, DEP, [(i, (i + step) % depths) for i in range(depths)])  25.8 us
    all_to_all x1, starting transfers between devices, body(): mine = lax.all_to_all(copies(own), CHIPS, 0, 0)  12.2 us
    ppermute x4, waiting for transfers between devices, shift(): lax.ppermute(block, DEP, [(i, (i + step) % depths) for i in range(depths)])  9.87 us
    all_to_all x1, waiting for transfers between devices, body(): mine = lax.all_to_all(copies(own), CHIPS, 0, 0)  8.46 us
    all_to_all x1, waiting for transfers between devices, body(): over_z = lax.all_to_all(total_spread(over_y, 1.0, zs), 'zh', 0, 0)  7.55 us
    all_to_all x1, waiting for transfers between devices, body(): over_y = lax.all_to_all(wide, 'y', 0, 0)  4.78 us
    ppermute x1, starting transfers between devices, body(): before = lax.ppermute(before, 'zl', [(i, (i + 2) % 3) for i in range(3)])  4.58 us
    ppermute x1, waiting for transfers between devices, body(): lax.ppermute(total[1].astype(jnp.bfloat16), 'x', [(i, i ^ 2) for i in ran...  4.47 us
  transfers between devices with their start and end apart: 14, of which 10 were waited for; matrix products, arithmetic and copies ran while one was open for 1% of the time, Pallas kernels for 3%

profile of v13, /device:TPU:64, one launch (start us, length us, event | category | flops | bytes accessed | tf_op | source)
XLA Modules:
  0.0 116.7 jit_solution(18177070810017454748)
XLA Ops:
  0.6 1.5 %broadcast_in_dim.8 = bf16[12,16,1024]{2,1,0:T(8,128)(2,1)} broadcast(bf16[16,1024]{1,0:T(8,128)(2,1)} %bitcast.46), dimensions={1,2} | broadcast | bytes 425984 | tf_op jit(solution)/shard_map/broadcast_in_dim | solution.py:319
  2.2 0.0 copy-start
  2.2 12.2 %all-to-all-start = ((bf16[12,16,1024]{2,1,0:T(8,128)(2,1)}), bf16[12,16,1024]{2,1,0:T(8,128)(2,1)S(1)}, u32[]{:S(2)}, u32[]{:S(2)}) async-start(bf16[12,16,1024]{2,1,0:T(8,128)(2,1)} %broadcast_in_dim.8), calls=%async_computation | async-start | bytes 786432 | tf_op jit(solution)/shard_map/all_to_all | solution.py:321
  14.4 8.5 %all-to-all-done.mine_ref = bf16[12,16,1024]{2,1,0:T(8,128)(2,1)S(1)} async-done(((bf16[12,16,1024]{2,1,0:T(8,128)(2,1)}), bf16[12,16,1024]{2,1,0:T(8,128)(2,1)S(1)}, u32[]{:S(2)}, u32[]{:S(2)}) %all-to-all-start) | async-done | bytes 393248 | tf_op jit(solution)/shard_map/all_to_all | solution.py:321
  22.9 0.0 copy-start.1
  22.9 2.0 %collective-permute-start = (bf16[12,16,1024]{2,1,0:T(8,128)(2,1)S(1)}, bf16[12,16,1024]{2,1,0:T(8,128)(2,1)S(1)}, u32[]{:S(2)}, u32[]{:S(2)}) collective-permute-start(bf16[12,16,1024]{2,1,0:T(8,128)(2,1)S(1)} %all-to-all-done.mine_ref), channel_id=1, source_target_pairs={{0,1},{1,0},{2,3},{3,2},{4,5},{5,4},{6,7},{7,6},{8,9},{9,8},{10,11... | collective-permute-start | bytes 1179656 | tf_op jit(solution)/shard_map/ppermute | solution.py:299
  24.9 1.7 %collective-permute-done.other_ref = bf16[12,16,1024]{2,1,0:T(8,128)(2,1)S(1)} collective-permute-done((bf16[12,16,1024]{2,1,0:T(8,128)(2,1)S(1)}, bf16[12,16,1024]{2,1,0:T(8,128)(2,1)S(1)}, u32[]{:S(2)}, u32[]{:S(2)}) %collective-permute-start) | collective-permute-done | bytes 393248 | tf_op jit(solution)/shard_map/ppermute | solution.py:299
  26.6 0.0 copy-done
  26.6 0.9 conv.1
  27.5 7.2 %collective-permute-start.1 = (bf16[16,1024]{1,0:T(8,128)(2,1)S(1)}, bf16[16,1024]{1,0:T(8,128)(2,1)S(1)}, u32[]{:S(2)}, u32[]{:S(2)}) collective-permute-start(bf16[16,1024]{1,0:T(8,128)(2,1)S(1)} %get-tuple-element.32), channel_id=1, source_target_pairs={{0,24},{24,48},{48,72},{72,96},{96,120},{120,144},{144,168},{168,1... | collective-permute-start | bytes 98312 | tf_op jit(solution)/shard_map/ppermute | solution.py:309
  34.7 7.3 %collective-permute-start.2 = (bf16[16,1024]{1,0:T(8,128)(2,1)S(1)}, bf16[16,1024]{1,0:T(8,128)(2,1)S(1)}, u32[]{:S(2)}, u32[]{:S(2)}) collective-permute-start(bf16[16,1024]{1,0:T(8,128)(2,1)S(1)} %get-tuple-element.33), channel_id=1, source_target_pairs={{0,744},{24,0},{48,24},{72,48},{96,72},{120,96},{144,120},{168,144... | collective-permute-start | bytes 98312 | tf_op jit(solution)/shard_map/ppermute | solution.py:309
  42.0 0.7 collective-permute-done.1.low_ref
  42.6 1.0 collective-permute-done.2.high_ref
  43.6 0.0 copy-done.1
  43.6 0.6 activate.1
  44.3 9.5 %collective-permute-start.4 = (bf16[16,1024]{1,0:T(8,128)(2,1)S(1)}, bf16[16,1024]{1,0:T(8,128)(2,1)S(1)}, u32[]{:S(2)}, u32[]{:S(2)}) collective-permute-start(bf16[16,1024]{1,0:T(8,128)(2,1)S(1)} %get-tuple-element.36.own_ref), channel_id=1, source_target_pairs={{0,744},{24,0},{48,24},{72,48},{96,72},{120,96},{144,120},{168,144... | collective-permute-start | bytes 98312 | tf_op jit(solution)/shard_map/ppermute | solution.py:309
  53.8 1.9 %collective-permute-start.3 = (bf16[16,1024]{1,0:T(8,128)(2,1)S(1)}, bf16[16,1024]{1,0:T(8,128)(2,1)S(1)}, u32[]{:S(2)}, u32[]{:S(2)}) collective-permute-start(bf16[16,1024]{1,0:T(8,128)(2,1)S(1)} %get-tuple-element.36.own_ref), channel_id=1, source_target_pairs={{0,24},{24,48},{48,72},{72,96},{96,120},{120,144},{144,168},{168,1... | collective-permute-start | bytes 98312 | tf_op jit(solution)/shard_map/ppermute | solution.py:309
  55.7 0.6 wgrad_own.1
  56.2 0.0 collective-permute-done.4.plane_ref
  56.2 0.5 wgrad_first.1
  56.8 8.2 %collective-permute-done.3.below_ref = bf16[16,1024]{1,0:T(8,128)(2,1)S(1)} collective-permute-done((bf16[16,1024]{1,0:T(8,128)(2,1)S(1)}, bf16[16,1024]{1,0:T(8,128)(2,1)S(1)}, u32[]{:S(2)}, u32[]{:S(2)}) %collective-permute-start.3) | collective-permute-done | bytes 32800 | tf_op jit(solution)/shard_map/ppermute | solution.py:309
  65.0 1.3 %wgrad_last.1 = (bf16[8,21,8,128]{3,2,1,0:T(8,128)(2,1)}, bf16[144,1024]{1,0:T(8,128)(2,1)S(1)}) custom-call(bf16[16,1024]{1,0:T(8,128)(2,1)S(1)} %collective-permute-done.3.below_ref, bf16[12,2,16,1024]{3,2,1,0:T(8,128)(2,1)S(1)} %get-tuple-element.37.x_ref, bf16[54,8,128]{2,1,0:T(8,128)(2,1)S(1)} %get-tuple-element.38.above_ref, ...), custom_call_target="tpu_custom_call" | custom-call | tf_op jit(solution)/shard_map/wgrad_last/pallas_call | solution.py:174
  66.3 4.0 %all-to-all-start.1 = ((bf16[8,21,8,128]{3,2,1,0:T(8,128)(2,1)}), bf16[8,21,8,128]{3,2,1,0:T(8,128)(2,1)S(1)}, u32[]{:S(2)}, u32[]{:S(2)}) async-start(bf16[8,21,8,128]{3,2,1,0:T(8,128)(2,1)} %get-tuple-element.40), calls=%async_computation.1 | async-start | bytes 688128 | tf_op jit(solution)/shard_map/all_to_all | solution.py:337
  70.2 0.8 dgrad.1
  71.1 1.9 %collective-permute-start.5 = (bf16[4,3,16,1024]{3,2,1,0:T(8,128)(2,1)S(1)}, bf16[4,3,16,1024]{3,2,1,0:T(8,128)(2,1)S(1)}, u32[]{:S(2)}, u32[]{:S(2)}) collective-permute-start(bf16[4,3,16,1024]{3,2,1,0:T(8,128)(2,1)S(1)} %get-tuple-element.47), channel_id=1, source_target_pairs={{0,1},{1,0},{2,3},{3,2},{4,5},{5,4},{6,7},{7,6},{8,9},{9,8},{10,11... | collective-permute-start | bytes 1179656 | tf_op jit(solution)/shard_map/ppermute | solution.py:299
  73.0 1.7 %collective-permute-done.5.came_ref = bf16[4,3,16,1024]{3,2,1,0:T(8,128)(2,1)S(1)} collective-permute-done((bf16[4,3,16,1024]{3,2,1,0:T(8,128)(2,1)S(1)}, bf16[4,3,16,1024]{3,2,1,0:T(8,128)(2,1)S(1)}, u32[]{:S(2)}, u32[]{:S(2)}) %collective-permute-start.5) | collective-permute-done | bytes 393248 | tf_op jit(solution)/shard_map/ppermute | solution.py:299
  74.7 0.1 halve.1
  74.7 2.1 %collective-permute-start.6 = (bf16[2,3,16,1024]{3,2,1,0:T(8,128)(2,1)S(1)}, bf16[2,3,16,1024]{3,2,1,0:T(8,128)(2,1)S(1)}, u32[]{:S(2)}, u32[]{:S(2)}) collective-permute-start(bf16[2,3,16,1024]{3,2,1,0:T(8,128)(2,1)S(1)} %get-tuple-element.50), channel_id=1, source_target_pairs={{0,6},{6,0},{12,18},{18,12},{1,7},{7,1},{13,19},{19,13},{2,8},{8,2... | collective-permute-start | bytes 589832 | tf_op jit(solution)/shard_map/ppermute | solution.py:343
  76.8 4.8 %all-to-all-done.1.terms_ref = bf16[8,21,8,128]{3,2,1,0:T(8,128)(2,1)S(1)} async-done(((bf16[8,21,8,128]{3,2,1,0:T(8,128)(2,1)}), bf16[8,21,8,128]{3,2,1,0:T(8,128)(2,1)S(1)}, u32[]{:S(2)}, u32[]{:S(2)}) %all-to-all-start.1) | async-done | bytes 344096 | tf_op jit(solution)/shard_map/all_to_all | solution.py:337
  81.6 0.7 total.2
  82.3 3.4 %all-to-all-start.2 = ((bf16[4,21,8,128]{3,2,1,0:T(8,128)(2,1)}), bf16[4,21,8,128]{3,2,1,0:T(8,128)(2,1)S(1)}, u32[]{:S(2)}, u32[]{:S(2)}) async-start(bf16[4,21,8,128]{3,2,1,0:T(8,128)(2,1)} %total.2), calls=%async_computation.2 | async-start | bytes 344064 | tf_op jit(solution)/shard_map/all_to_all | solution.py:342
  85.7 0.0 collective-permute-done.6
  85.8 1.9 %collective-permute-start.7 = (bf16[2,16,1024]{2,1,0:T(8,128)(2,1)S(1)}, bf16[2,16,1024]{2,1,0:T(8,128)(2,1)S(1)}, u32[]{:S(2)}, u32[]{:S(2)}) collective-permute-start(bf16[2,16,1024]{2,1,0:T(8,128)(2,1)S(1)} %get-tuple-element.55), channel_id=1, source_target_pairs={{0,2},{2,4},{4,0},{1,3},{3,5},{5,1},{6,8},{8,10},{10,6},{7,9},{9,1... | collective-permute-start | bytes 196616 | tf_op jit(solution)/shard_map/ppermute | solution.py:346
  87.7 4.6 %collective-permute-start.8 = (bf16[2,16,1024]{2,1,0:T(8,128)(2,1)S(1)}, bf16[2,16,1024]{2,1,0:T(8,128)(2,1)S(1)}, u32[]{:S(2)}, u32[]{:S(2)}) collective-permute-start(bf16[2,16,1024]{2,1,0:T(8,128)(2,1)S(1)} %get-tuple-element.56), channel_id=1, source_target_pairs={{0,4},{2,0},{4,2},{1,5},{3,1},{5,3},{6,10},{8,6},{10,8},{7,11},{9,... | collective-permute-start | bytes 196616 | tf_op jit(solution)/shard_map/ppermute | solution.py:347
  92.3 7.5 %all-to-all-done.2.terms_ref = bf16[4,21,8,128]{3,2,1,0:T(8,128)(2,1)S(1)} async-done(((bf16[4,21,8,128]{3,2,1,0:T(8,128)(2,1)}), bf16[4,21,8,128]{3,2,1,0:T(8,128)(2,1)S(1)}, u32[]{:S(2)}, u32[]{:S(2)}) %all-to-all-start.2) | async-done | bytes 172064 | tf_op jit(solution)/shard_map/all_to_all | solution.py:342
  99.8 0.8 total.3
  100.6 3.4 %all-to-all-start.3 = ((bf16[8,21,8,128]{3,2,1,0:T(8,128)(2,1)}), bf16[8,21,8,128]{3,2,1,0:T(8,128)(2,1)S(1)}, u32[]{:S(2)}, u32[]{:S(2)}) async-start(bf16[8,21,8,128]{3,2,1,0:T(8,128)(2,1)} %total.3), calls=%async_computation.3 | async-start | bytes 688128 | tf_op jit(solution)/shard_map/all_to_all | solution.py:348
  104.0 0.0 collective-permute-done.7
  104.0 0.0 collective-permute-done.8
  104.1 2.8 %collective-permute-start.9 = (bf16[16,1024]{1,0:T(8,128)(2,1)S(1)}, bf16[16,1024]{1,0:T(8,128)(2,1)S(1)}, u32[]{:S(2)}, u32[]{:S(2)}) collective-permute-start(bf16[16,1024]{1,0:T(8,128)(2,1)S(1)} %fusion.5), channel_id=1, source_target_pairs={{0,12},{6,18},{12,0},{18,6},{1,13},{7,19},{13,1},{19,7},{2,14},{8,... | collective-permute-start | bytes 98312 | tf_op jit(solution)/shard_map/ppermute | solution.py:350
  106.9 4.5 %collective-permute-done.9 = bf16[16,1024]{1,0:T(8,128)(2,1)S(1)} collective-permute-done((bf16[16,1024]{1,0:T(8,128)(2,1)S(1)}, bf16[16,1024]{1,0:T(8,128)(2,1)S(1)}, u32[]{:S(2)}, u32[]{:S(2)}) %collective-permute-start.9) | collective-permute-done | bytes 32800 | tf_op jit(solution)/shard_map/ppermute | solution.py:350
  111.4 0.6 fusion.4
  112.0 3.3 %all-to-all-done.3 = bf16[8,21,8,128]{3,2,1,0:T(8,128)(2,1)S(1)} async-done(((bf16[8,21,8,128]{3,2,1,0:T(8,128)(2,1)}), bf16[8,21,8,128]{3,2,1,0:T(8,128)(2,1)S(1)}, u32[]{:S(2)}, u32[]{:S(2)}) %all-to-all-start.3) | async-done | bytes 344096 | tf_op jit(solution)/shard_map/all_to_all | solution.py:348
  115.3 1.4 %unpack.1 = f32[27,16,384]{2,1,0:T(8,128)} custom-call(bf16[168,8,128]{2,1,0:T(8,128)(2,1)S(1)} %bitcast.41), custom_call_target="tpu_custom_call" | custom-call | tf_op jit(solution)/shard_map/unpack/pallas_call | solution.py:287
  (4 shorter events, 0.1 us)
Async XLA Ops:
  2.2 24.4 %copy-start = (bf16[16,3,3,3,384]{4,0,3,2,1:T(8,128)(2,1)S(1)}, bf16[16,3,3,3,384]{4,0,3,2,1:T(8,128)(2,1)}, u32[]{:S(2)}) copy-start(bf16[16,3,3,3,384]{4,0,3,2,1:T(8,128)(2,1)} %param.4) | copy-start | bytes 995332
  2.2 20.7 %all-to-all-start = ((bf16[12,16,1024]{2,1,0:T(8,128)(2,1)}), bf16[12,16,1024]{2,1,0:T(8,128)(2,1)S(1)}, u32[]{:S(2)}, u32[]{:S(2)}) async-start(bf16[12,16,1024]{2,1,0:T(8,128)(2,1)} %broadcast_in_dim.8), calls=%async_computation | async-start | bytes 786432 | tf_op jit(solution)/shard_map/all_to_all | solution.py:321
  22.9 20.8 %copy-start.1 = (bf16[1,1,16,1024]{3,2,1,0:T(8,128)(2,1)S(1)}, bf16[1,1,16,1024]{3,2,1,0:T(8,128)(2,1)}, u32[]{:S(2)}) copy-start(bf16[1,1,16,1024]{3,2,1,0:T(8,128)(2,1)} %param.5) | copy-start | bytes 98308
  22.9 3.7 %collective-permute-start = (bf16[12,16,1024]{2,1,0:T(8,128)(2,1)S(1)}, bf16[12,16,1024]{2,1,0:T(8,128)(2,1)S(1)}, u32[]{:S(2)}, u32[]{:S(2)}) collective-permute-start(bf16[12,16,1024]{2,1,0:T(8,128)(2,1)S(1)} %all-to-all-done.mine_ref), channel_id=1, source_target_pairs={{0,1},{1,0},{2,3},{3,2},{4,5},{5,4},{6,7},{7,6},{8,9},{9,8},{10,11... | collective-permute-start | bytes 1179656 | tf_op jit(solution)/shard_map/ppermute | solution.py:299
  27.5 15.1 %collective-permute-start.1 = (bf16[16,1024]{1,0:T(8,128)(2,1)S(1)}, bf16[16,1024]{1,0:T(8,128)(2,1)S(1)}, u32[]{:S(2)}, u32[]{:S(2)}) collective-permute-start(bf16[16,1024]{1,0:T(8,128)(2,1)S(1)} %get-tuple-element.32), channel_id=1, source_target_pairs={{0,24},{24,48},{48,72},{72,96},{96,120},{120,144},{144,168},{168,1... | collective-permute-start | bytes 98312 | tf_op jit(solution)/shard_map/ppermute | solution.py:309
  34.7 8.9 %collective-permute-start.2 = (bf16[16,1024]{1,0:T(8,128)(2,1)S(1)}, bf16[16,1024]{1,0:T(8,128)(2,1)S(1)}, u32[]{:S(2)}, u32[]{:S(2)}) collective-permute-start(bf16[16,1024]{1,0:T(8,128)(2,1)S(1)} %get-tuple-element.33), channel_id=1, source_target_pairs={{0,744},{24,0},{48,24},{72,48},{96,72},{120,96},{144,120},{168,144... | collective-permute-start | bytes 98312 | tf_op jit(solution)/shard_map/ppermute | solution.py:309
  44.3 12.0 %collective-permute-start.4 = (bf16[16,1024]{1,0:T(8,128)(2,1)S(1)}, bf16[16,1024]{1,0:T(8,128)(2,1)S(1)}, u32[]{:S(2)}, u32[]{:S(2)}) collective-permute-start(bf16[16,1024]{1,0:T(8,128)(2,1)S(1)} %get-tuple-element.36.own_ref), channel_id=1, source_target_pairs={{0,744},{24,0},{48,24},{72,48},{96,72},{120,96},{144,120},{168,144... | collective-permute-start | bytes 98312 | tf_op jit(solution)/shard_map/ppermute | solution.py:309
  53.8 11.2 %collective-permute-start.3 = (bf16[16,1024]{1,0:T(8,128)(2,1)S(1)}, bf16[16,1024]{1,0:T(8,128)(2,1)S(1)}, u32[]{:S(2)}, u32[]{:S(2)}) collective-permute-start(bf16[16,1024]{1,0:T(8,128)(2,1)S(1)} %get-tuple-element.36.own_ref), channel_id=1, source_target_pairs={{0,24},{24,48},{48,72},{72,96},{96,120},{120,144},{144,168},{168,1... | collective-permute-start | bytes 98312 | tf_op jit(solution)/shard_map/ppermute | solution.py:309
  66.3 15.3 %all-to-all-start.1 = ((bf16[8,21,8,128]{3,2,1,0:T(8,128)(2,1)}), bf16[8,21,8,128]{3,2,1,0:T(8,128)(2,1)S(1)}, u32[]{:S(2)}, u32[]{:S(2)}) async-start(bf16[8,21,8,128]{3,2,1,0:T(8,128)(2,1)} %get-tuple-element.40), calls=%async_computation.1 | async-start | bytes 688128 | tf_op jit(solution)/shard_map/all_to_all | solution.py:337
  71.1 3.6 %collective-permute-start.5 = (bf16[4,3,16,1024]{3,2,1,0:T(8,128)(2,1)S(1)}, bf16[4,3,16,1024]{3,2,1,0:T(8,128)(2,1)S(1)}, u32[]{:S(2)}, u32[]{:S(2)}) collective-permute-start(bf16[4,3,16,1024]{3,2,1,0:T(8,128)(2,1)S(1)} %get-tuple-element.47), channel_id=1, source_target_pairs={{0,1},{1,0},{2,3},{3,2},{4,5},{5,4},{6,7},{7,6},{8,9},{9,8},{10,11... | collective-permute-start | bytes 1179656 | tf_op jit(solution)/shard_map/ppermute | solution.py:299
  74.7 10.9 %collective-permute-start.6 = (bf16[2,3,16,1024]{3,2,1,0:T(8,128)(2,1)S(1)}, bf16[2,3,16,1024]{3,2,1,0:T(8,128)(2,1)S(1)}, u32[]{:S(2)}, u32[]{:S(2)}) collective-permute-start(bf16[2,3,16,1024]{3,2,1,0:T(8,128)(2,1)S(1)} %get-tuple-element.50), channel_id=1, source_target_pairs={{0,6},{6,0},{12,18},{18,12},{1,7},{7,1},{13,19},{19,13},{2,8},{8,2... | collective-permute-start | bytes 589832 | tf_op jit(solution)/shard_map/ppermute | solution.py:343
  82.3 17.5 %all-to-all-start.2 = ((bf16[4,21,8,128]{3,2,1,0:T(8,128)(2,1)}), bf16[4,21,8,128]{3,2,1,0:T(8,128)(2,1)S(1)}, u32[]{:S(2)}, u32[]{:S(2)}) async-start(bf16[4,21,8,128]{3,2,1,0:T(8,128)(2,1)} %total.2), calls=%async_computation.2 | async-start | bytes 344064 | tf_op jit(solution)/shard_map/all_to_all | solution.py:342
  85.8 18.3 %collective-permute-start.7 = (bf16[2,16,1024]{2,1,0:T(8,128)(2,1)S(1)}, bf16[2,16,1024]{2,1,0:T(8,128)(2,1)S(1)}, u32[]{:S(2)}, u32[]{:S(2)}) collective-permute-start(bf16[2,16,1024]{2,1,0:T(8,128)(2,1)S(1)} %get-tuple-element.55), channel_id=1, source_target_pairs={{0,2},{2,4},{4,0},{1,3},{3,5},{5,1},{6,8},{8,10},{10,6},{7,9},{9,1... | collective-permute-start | bytes 196616 | tf_op jit(solution)/shard_map/ppermute | solution.py:346
  87.7 16.4 %collective-permute-start.8 = (bf16[2,16,1024]{2,1,0:T(8,128)(2,1)S(1)}, bf16[2,16,1024]{2,1,0:T(8,128)(2,1)S(1)}, u32[]{:S(2)}, u32[]{:S(2)}) collective-permute-start(bf16[2,16,1024]{2,1,0:T(8,128)(2,1)S(1)} %get-tuple-element.56), channel_id=1, source_target_pairs={{0,4},{2,0},{4,2},{1,5},{3,1},{5,3},{6,10},{8,6},{10,8},{7,11},{9,... | collective-permute-start | bytes 196616 | tf_op jit(solution)/shard_map/ppermute | solution.py:347
  100.6 14.7 %all-to-all-start.3 = ((bf16[8,21,8,128]{3,2,1,0:T(8,128)(2,1)}), bf16[8,21,8,128]{3,2,1,0:T(8,128)(2,1)S(1)}, u32[]{:S(2)}, u32[]{:S(2)}) async-start(bf16[8,21,8,128]{3,2,1,0:T(8,128)(2,1)} %total.3), calls=%async_computation.3 | async-start | bytes 688128 | tf_op jit(solution)/shard_map/all_to_all | solution.py:348
  104.1 7.3 %collective-permute-start.9 = (bf16[16,1024]{1,0:T(8,128)(2,1)S(1)}, bf16[16,1024]{1,0:T(8,128)(2,1)S(1)}, u32[]{:S(2)}, u32[]{:S(2)}) collective-permute-start(bf16[16,1024]{1,0:T(8,128)(2,1)S(1)} %fusion.5), channel_id=1, source_target_pairs={{0,12},{6,18},{12,0},{18,6},{1,13},{7,19},{13,1},{19,7},{2,14},{8,... | collective-permute-start | bytes 98312 | tf_op jit(solution)/shard_map/ppermute | solution.py:350

commit v14 on v11

--- a/solution.py
+++ b/solution.py
@@ -338,14 +338,15 @@
     over_y, keep = lax.optimization_barrier((over_y, keep))
     over_z = lax.all_to_all(total_spread(over_y, 1.0, zs), "zh", 0, 0)
     total = keep + lax.ppermute(send, "x", [(i, i ^ 1) for i in range(4)]).astype(jnp.float32)
-    after, before = total[:, 1].astype(jnp.bfloat16), total[:, 2].astype(jnp.bfloat16)
-    over_z, _ = lax.optimization_barrier((over_z, (after, before)))
+    over_z, _ = lax.optimization_barrier((over_z, total))
+    units = lax.all_to_all(total_spread(over_z, scale, ys), "y", 0, 0)
+    step = lax.ppermute(total[1].astype(jnp.bfloat16), "x", [(i, i ^ 2) for i in range(4)])
+    total = total[0] + step.astype(jnp.float32)
+    after, before = total[1].astype(jnp.bfloat16), total[2].astype(jnp.bfloat16)
     after = lax.ppermute(after, "zl", [(i, (i + 1) % 3) for i in range(3)])
     before = lax.ppermute(before, "zl", [(i, (i + 2) % 3) for i in range(3)])
-    units = lax.all_to_all(total_spread(over_z, scale, ys), "y", 0, 0)
-    total = total[:, 0] + after.astype(jnp.float32) + before.astype(jnp.float32)
-    step = lax.ppermute(total[1].astype(jnp.bfloat16), "x", [(i, i ^ 2) for i in range(4)])
-    grad_volume = (total[0] + step.astype(jnp.float32)).astype(jnp.bfloat16)
+    grad_volume = total[0] + after.astype(jnp.float32) + before.astype(jnp.float32)
+    grad_volume = grad_volume.astype(jnp.bfloat16)
     all_taps = unpack(units, rows, kernel.shape[-1])
     grad_kernel = jnp.transpose(all_taps, (1, 0, 2)).reshape(kernel.shape)
     return (activated.reshape(volume.shape), grad_volume.reshape(volume.shape), grad_kernel)

time: 116 us -> 116 us (level)
    ppermute x1, waiting for transfers between devices: 4.52 us -> 0.01 us  [body(): lax.ppermute(total[1].astype(jnp.bfloat16), 'x', [(i, i ^ 2) for i in ran...]
    ppermute x1, waiting for transfers between devices: 0.01 us -> 2.57 us  [body(): before = lax.ppermute(before, 'zl', [(i, (i + 2) % 3) for i in range(3)])]
    all_to_all x1, waiting for transfers between devices: 4.19 us -> 6.71 us  [body(): over_z = lax.all_to_all(total_spread(over_y, 1.0, zs), 'zh', 0, 0)]
    ppermute x1, starting transfers between devices: 1.92 us -> 3.53 us  [body(): after = lax.ppermute(after, 'zl', [(i, (i + 1) % 3) for i in range(3)])]
    ppermute x1, starting transfers between devices: 4.82 us -> 3.22 us  [body(): before = lax.ppermute(before, 'zl', [(i, (i + 2) % 3) for i in range(3)])]
    ppermute x1, starting transfers between devices: 2.79 us -> 4.22 us  [body(): lax.ppermute(total[1].astype(jnp.bfloat16), 'x', [(i, i ^ 2) for i in ran...]
    all_to_all x1, waiting for transfers between devices: 3.47 us -> 2.3 us  [body(): units = lax.all_to_all(total_spread(over_z, scale, ys), 'y', 0, 0)]
where the time goes in v14:
time: 116 us; the launch traced here: 115 us
  starting transfers between devices  74.1 us (64%)
  waiting for transfers between devices  30.3 us (26%)
  Pallas kernels  7.16 us (6%)
  local copies, waits for them, and re-layouts  1.57 us (1%)
    ppermute x4, starting transfers between devices, shift(): lax.ppermute(block, DEP, [(i, (i + step) % depths) for i in range(depths)])  25.8 us
    all_to_all x1, starting transfers between devices, body(): mine = lax.all_to_all(copies(own), CHIPS, 0, 0)  13.1 us
    all_to_all x1, waiting for transfers between devices, body(): mine = lax.all_to_all(copies(own), CHIPS, 0, 0)  8.12 us
    all_to_all x1, starting transfers between devices, body(): over_y = lax.all_to_all(wide, 'y', 0, 0)  7.36 us
    all_to_all x1, waiting for transfers between devices, body(): over_z = lax.all_to_all(total_spread(over_y, 1.0, zs), 'zh', 0, 0)  6.71 us
    all_to_all x1, starting transfers between devices, body(): over_z = lax.all_to_all(total_spread(over_y, 1.0, zs), 'zh', 0, 0)  5.69 us
    ppermute x1, starting transfers between devices, body(): lax.ppermute(total[1].astype(jnp.bfloat16), 'x', [(i, i ^ 2) for i in ran...  4.22 us
    all_to_all x1, starting transfers between devices, body(): units = lax.all_to_all(total_spread(over_z, scale, ys), 'y', 0, 0)  4.02 us
  transfers between devices with their start and end apart: 14, of which 10 were waited for; matrix products, arithmetic and copies ran while one was open for 1% of the time, Pallas kernels for 3%

profile of v14, /device:TPU:2, one launch (start us, length us, event | category | flops | bytes accessed | tf_op | source)
XLA Modules:
  0.0 114.7 jit_solution(10416157255466250052)
XLA Ops:
  0.6 1.5 %broadcast_in_dim.8 = bf16[12,16,1024]{2,1,0:T(8,128)(2,1)} broadcast(bf16[16,1024]{1,0:T(8,128)(2,1)} %bitcast.41), dimensions={1,2} | broadcast | bytes 425984 | tf_op jit(solution)/shard_map/broadcast_in_dim | solution.py:316
  2.2 0.0 copy-start
  2.2 13.1 %all-to-all-start = ((bf16[12,16,1024]{2,1,0:T(8,128)(2,1)}), bf16[12,16,1024]{2,1,0:T(8,128)(2,1)S(1)}, u32[]{:S(2)}, u32[]{:S(2)}) async-start(bf16[12,16,1024]{2,1,0:T(8,128)(2,1)} %broadcast_in_dim.8), calls=%async_computation | async-start | bytes 786432 | tf_op jit(solution)/shard_map/all_to_all | solution.py:318
  15.3 8.1 %all-to-all-done.mine_ref = bf16[12,16,1024]{2,1,0:T(8,128)(2,1)S(1)} async-done(((bf16[12,16,1024]{2,1,0:T(8,128)(2,1)}), bf16[12,16,1024]{2,1,0:T(8,128)(2,1)S(1)}, u32[]{:S(2)}, u32[]{:S(2)}) %all-to-all-start) | async-done | bytes 393248 | tf_op jit(solution)/shard_map/all_to_all | solution.py:318
  23.4 0.0 copy-start.1
  23.4 2.0 %collective-permute-start = (bf16[12,16,1024]{2,1,0:T(8,128)(2,1)S(1)}, bf16[12,16,1024]{2,1,0:T(8,128)(2,1)S(1)}, u32[]{:S(2)}, u32[]{:S(2)}) collective-permute-start(bf16[12,16,1024]{2,1,0:T(8,128)(2,1)S(1)} %all-to-all-done.mine_ref), channel_id=1, source_target_pairs={{0,1},{1,0},{2,3},{3,2},{4,5},{5,4},{6,7},{7,6},{8,9},{9,8},{10,11... | collective-permute-start | bytes 1179656 | tf_op jit(solution)/shard_map/ppermute | solution.py:296
  25.5 1.7 %collective-permute-done.other_ref = bf16[12,16,1024]{2,1,0:T(8,128)(2,1)S(1)} collective-permute-done((bf16[12,16,1024]{2,1,0:T(8,128)(2,1)S(1)}, bf16[12,16,1024]{2,1,0:T(8,128)(2,1)S(1)}, u32[]{:S(2)}, u32[]{:S(2)}) %collective-permute-start) | collective-permute-done | bytes 393248 | tf_op jit(solution)/shard_map/ppermute | solution.py:296
  27.1 0.0 copy-done
  27.1 0.9 conv.1
  28.1 7.2 %collective-permute-start.1 = (bf16[16,1024]{1,0:T(8,128)(2,1)S(1)}, bf16[16,1024]{1,0:T(8,128)(2,1)S(1)}, u32[]{:S(2)}, u32[]{:S(2)}) collective-permute-start(bf16[16,1024]{1,0:T(8,128)(2,1)S(1)} %get-tuple-element.32), channel_id=1, source_target_pairs={{0,24},{24,48},{48,72},{72,96},{96,120},{120,144},{144,168},{168,1... | collective-permute-start | bytes 98312 | tf_op jit(solution)/shard_map/ppermute | solution.py:306
  35.2 7.3 %collective-permute-start.2 = (bf16[16,1024]{1,0:T(8,128)(2,1)S(1)}, bf16[16,1024]{1,0:T(8,128)(2,1)S(1)}, u32[]{:S(2)}, u32[]{:S(2)}) collective-permute-start(bf16[16,1024]{1,0:T(8,128)(2,1)S(1)} %get-tuple-element.33), channel_id=1, source_target_pairs={{0,744},{24,0},{48,24},{72,48},{96,72},{120,96},{144,120},{168,144... | collective-permute-start | bytes 98312 | tf_op jit(solution)/shard_map/ppermute | solution.py:306
  42.5 0.6 collective-permute-done.1.low_ref
  43.1 1.4 %collective-permute-done.2.high_ref = bf16[16,1024]{1,0:T(8,128)(2,1)S(1)} collective-permute-done((bf16[16,1024]{1,0:T(8,128)(2,1)S(1)}, bf16[16,1024]{1,0:T(8,128)(2,1)S(1)}, u32[]{:S(2)}, u32[]{:S(2)}) %collective-permute-start.2) | collective-permute-done | bytes 32800 | tf_op jit(solution)/shard_map/ppermute | solution.py:306
  44.5 0.0 copy-done.1
  44.5 0.6 activate.1
  45.1 6.2 %collective-permute-start.4 = (bf16[16,1024]{1,0:T(8,128)(2,1)S(1)}, bf16[16,1024]{1,0:T(8,128)(2,1)S(1)}, u32[]{:S(2)}, u32[]{:S(2)}) collective-permute-start(bf16[16,1024]{1,0:T(8,128)(2,1)S(1)} %get-tuple-element.36.own_ref), channel_id=1, source_target_pairs={{0,24},{24,48},{48,72},{72,96},{96,120},{120,144},{144,168},{168,1... | collective-permute-start | bytes 98312 | tf_op jit(solution)/shard_map/ppermute | solution.py:306
  51.4 5.2 %collective-permute-start.3 = (bf16[16,1024]{1,0:T(8,128)(2,1)S(1)}, bf16[16,1024]{1,0:T(8,128)(2,1)S(1)}, u32[]{:S(2)}, u32[]{:S(2)}) collective-permute-start(bf16[16,1024]{1,0:T(8,128)(2,1)S(1)} %get-tuple-element.36.own_ref), channel_id=1, source_target_pairs={{0,744},{24,0},{48,24},{72,48},{96,72},{120,96},{144,120},{168,144... | collective-permute-start | bytes 98312 | tf_op jit(solution)/shard_map/ppermute | solution.py:306
  56.5 0.5 wgrad_own.1
  57.1 0.0 collective-permute-done.4.below_ref
  57.1 0.5 wgrad_below.1
  57.6 1.6 %collective-permute-done.3.above_ref = bf16[16,1024]{1,0:T(8,128)(2,1)S(1)} collective-permute-done((bf16[16,1024]{1,0:T(8,128)(2,1)S(1)}, bf16[16,1024]{1,0:T(8,128)(2,1)S(1)}, u32[]{:S(2)}, u32[]{:S(2)}) %collective-permute-start.3) | collective-permute-done | bytes 32800 | tf_op jit(solution)/shard_map/ppermute | solution.py:306
  59.2 1.3 %wgrad_above.1 = (bf16[8,21,8,128]{3,2,1,0:T(8,128)(2,1)}, bf16[144,1024]{1,0:T(8,128)(2,1)S(1)}) custom-call(bf16[16,1024]{1,0:T(8,128)(2,1)S(1)} %collective-permute-done.3.above_ref, bf16[12,2,16,1024]{3,2,1,0:T(8,128)(2,1)S(1)} %get-tuple-element.37.x_ref, bf16[54,8,128]{2,1,0:T(8,128)(2,1)S(1)} %get-tuple-element.38.own_ref, ...), custom_call_target="tpu_custom_call" | custom-call | tf_op jit(solution)/shard_map/wgrad_above/pallas_call | solution.py:174
  60.5 7.4 %all-to-all-start.1 = ((bf16[8,21,8,128]{3,2,1,0:T(8,128)(2,1)}), bf16[8,21,8,128]{3,2,1,0:T(8,128)(2,1)S(1)}, u32[]{:S(2)}, u32[]{:S(2)}) async-start(bf16[8,21,8,128]{3,2,1,0:T(8,128)(2,1)} %get-tuple-element.40), calls=%async_computation.1 | async-start | bytes 688128 | tf_op jit(solution)/shard_map/all_to_all | solution.py:334
  67.8 0.8 dgrad.1
  68.7 1.9 %collective-permute-start.5 = (bf16[4,3,16,1024]{3,2,1,0:T(8,128)(2,1)S(1)}, bf16[4,3,16,1024]{3,2,1,0:T(8,128)(2,1)S(1)}, u32[]{:S(2)}, u32[]{:S(2)}) collective-permute-start(bf16[4,3,16,1024]{3,2,1,0:T(8,128)(2,1)S(1)} %get-tuple-element.47), channel_id=1, source_target_pairs={{0,1},{1,0},{2,3},{3,2},{4,5},{5,4},{6,7},{7,6},{8,9},{9,8},{10,11... | collective-permute-start | bytes 1179656 | tf_op jit(solution)/shard_map/ppermute | solution.py:296
  70.6 1.7 %collective-permute-done.5.came_ref = bf16[4,3,16,1024]{3,2,1,0:T(8,128)(2,1)S(1)} collective-permute-done((bf16[4,3,16,1024]{3,2,1,0:T(8,128)(2,1)S(1)}, bf16[4,3,16,1024]{3,2,1,0:T(8,128)(2,1)S(1)}, u32[]{:S(2)}, u32[]{:S(2)}) %collective-permute-start.5) | collective-permute-done | bytes 393248 | tf_op jit(solution)/shard_map/ppermute | solution.py:296
  72.3 0.1 halve.1
  72.3 3.2 %collective-permute-start.6 = (bf16[2,3,16,1024]{3,2,1,0:T(8,128)(2,1)S(1)}, bf16[2,3,16,1024]{3,2,1,0:T(8,128)(2,1)S(1)}, u32[]{:S(2)}, u32[]{:S(2)}) collective-permute-start(bf16[2,3,16,1024]{3,2,1,0:T(8,128)(2,1)S(1)} %get-tuple-element.50), channel_id=1, source_target_pairs={{0,6},{6,0},{12,18},{18,12},{1,7},{7,1},{13,19},{19,13},{2,8},{8,2... | collective-permute-start | bytes 589832 | tf_op jit(solution)/shard_map/ppermute | solution.py:340
  75.6 3.7 %all-to-all-done.1.terms_ref = bf16[8,21,8,128]{3,2,1,0:T(8,128)(2,1)S(1)} async-done(((bf16[8,21,8,128]{3,2,1,0:T(8,128)(2,1)}), bf16[8,21,8,128]{3,2,1,0:T(8,128)(2,1)S(1)}, u32[]{:S(2)}, u32[]{:S(2)}) %all-to-all-start.1) | async-done | bytes 344096 | tf_op jit(solution)/shard_map/all_to_all | solution.py:334
  79.3 0.7 total.2
  80.0 5.7 %all-to-all-start.2 = ((bf16[4,21,8,128]{3,2,1,0:T(8,128)(2,1)}), bf16[4,21,8,128]{3,2,1,0:T(8,128)(2,1)S(1)}, u32[]{:S(2)}, u32[]{:S(2)}) async-start(bf16[4,21,8,128]{3,2,1,0:T(8,128)(2,1)} %total.2), calls=%async_computation.2 | async-start | bytes 344064 | tf_op jit(solution)/shard_map/all_to_all | solution.py:339
  85.7 0.0 collective-permute-done.6
  85.7 4.2 %collective-permute-start.7 = (bf16[3,16,1024]{2,1,0:T(8,128)(2,1)S(1)}, bf16[3,16,1024]{2,1,0:T(8,128)(2,1)S(1)}, u32[]{:S(2)}, u32[]{:S(2)}) collective-permute-start(bf16[3,16,1024]{2,1,0:T(8,128)(2,1)S(1)} %fusion.1), channel_id=1, source_target_pairs={{0,12},{6,18},{12,0},{18,6},{1,13},{7,19},{13,1},{19,7},{2,14},{8,... | collective-permute-start | bytes 294920 | tf_op jit(solution)/shard_map/ppermute | solution.py:343
  90.0 6.7 %all-to-all-done.2.terms_ref = bf16[4,21,8,128]{3,2,1,0:T(8,128)(2,1)S(1)} async-done(((bf16[4,21,8,128]{3,2,1,0:T(8,128)(2,1)}), bf16[4,21,8,128]{3,2,1,0:T(8,128)(2,1)S(1)}, u32[]{:S(2)}, u32[]{:S(2)}) %all-to-all-start.2) | async-done | bytes 172064 | tf_op jit(solution)/shard_map/all_to_all | solution.py:339
  96.7 0.8 total.3
  97.4 4.0 %all-to-all-start.3 = ((bf16[8,21,8,128]{3,2,1,0:T(8,128)(2,1)}), bf16[8,21,8,128]{3,2,1,0:T(8,128)(2,1)S(1)}, u32[]{:S(2)}, u32[]{:S(2)}) async-start(bf16[8,21,8,128]{3,2,1,0:T(8,128)(2,1)} %total.3), calls=%async_computation.3 | async-start | bytes 688128 | tf_op jit(solution)/shard_map/all_to_all | solution.py:342
  101.5 0.0 collective-permute-done.7
  101.5 3.5 %collective-permute-start.8 = (bf16[16,1024]{1,0:T(8,128)(2,1)S(1)}, bf16[16,1024]{1,0:T(8,128)(2,1)S(1)}, u32[]{:S(2)}, u32[]{:S(2)}) collective-permute-start(bf16[16,1024]{1,0:T(8,128)(2,1)S(1)} %get-tuple-element.55), channel_id=1, source_target_pairs={{0,2},{2,4},{4,0},{1,3},{3,5},{5,1},{6,8},{8,10},{10,6},{7,9},{9,1... | collective-permute-start | bytes 98312 | tf_op jit(solution)/shard_map/ppermute | solution.py:346
  105.0 3.2 %collective-permute-start.9 = (bf16[16,1024]{1,0:T(8,128)(2,1)S(1)}, bf16[16,1024]{1,0:T(8,128)(2,1)S(1)}, u32[]{:S(2)}, u32[]{:S(2)}) collective-permute-start(bf16[16,1024]{1,0:T(8,128)(2,1)S(1)} %get-tuple-element.56), channel_id=1, source_target_pairs={{0,4},{2,0},{4,2},{1,5},{3,1},{5,3},{6,10},{8,6},{10,8},{7,11},{9,... | collective-permute-start | bytes 98312 | tf_op jit(solution)/shard_map/ppermute | solution.py:347
  108.3 0.0 collective-permute-done.8
  108.3 2.6 %collective-permute-done.9 = bf16[16,1024]{1,0:T(8,128)(2,1)S(1)} collective-permute-done((bf16[16,1024]{1,0:T(8,128)(2,1)S(1)}, bf16[16,1024]{1,0:T(8,128)(2,1)S(1)}, u32[]{:S(2)}, u32[]{:S(2)}) %collective-permute-start.9) | collective-permute-done | bytes 32800 | tf_op jit(solution)/shard_map/ppermute | solution.py:347
  110.9 0.6 fusion.5
  111.5 2.3 %all-to-all-done.3.units_ref = bf16[8,21,8,128]{3,2,1,0:T(8,128)(2,1)S(1)} async-done(((bf16[8,21,8,128]{3,2,1,0:T(8,128)(2,1)}), bf16[8,21,8,128]{3,2,1,0:T(8,128)(2,1)S(1)}, u32[]{:S(2)}, u32[]{:S(2)}) %all-to-all-start.3) | async-done | bytes 344096 | tf_op jit(solution)/shard_map/all_to_all | solution.py:342
  113.8 0.9 unpack.1
  (4 shorter events, 0.1 us)
Async XLA Ops:
  2.2 25.0 %copy-start = (bf16[16,3,3,3,384]{4,0,3,2,1:T(8,128)(2,1)S(1)}, bf16[16,3,3,3,384]{4,0,3,2,1:T(8,128)(2,1)}, u32[]{:S(2)}) copy-start(bf16[16,3,3,3,384]{4,0,3,2,1:T(8,128)(2,1)} %param.4) | copy-start | bytes 995332
  2.2 21.2 %all-to-all-start = ((bf16[12,16,1024]{2,1,0:T(8,128)(2,1)}), bf16[12,16,1024]{2,1,0:T(8,128)(2,1)S(1)}, u32[]{:S(2)}, u32[]{:S(2)}) async-start(bf16[12,16,1024]{2,1,0:T(8,128)(2,1)} %broadcast_in_dim.8), calls=%async_computation | async-start | bytes 786432 | tf_op jit(solution)/shard_map/all_to_all | solution.py:318
  23.4 21.1 %copy-start.1 = (bf16[1,1,16,1024]{3,2,1,0:T(8,128)(2,1)S(1)}, bf16[1,1,16,1024]{3,2,1,0:T(8,128)(2,1)}, u32[]{:S(2)}) copy-start(bf16[1,1,16,1024]{3,2,1,0:T(8,128)(2,1)} %param.5) | copy-start | bytes 98308
  23.4 3.7 %collective-permute-start = (bf16[12,16,1024]{2,1,0:T(8,128)(2,1)S(1)}, bf16[12,16,1024]{2,1,0:T(8,128)(2,1)S(1)}, u32[]{:S(2)}, u32[]{:S(2)}) collective-permute-start(bf16[12,16,1024]{2,1,0:T(8,128)(2,1)S(1)} %all-to-all-done.mine_ref), channel_id=1, source_target_pairs={{0,1},{1,0},{2,3},{3,2},{4,5},{5,4},{6,7},{7,6},{8,9},{9,8},{10,11... | collective-permute-start | bytes 1179656 | tf_op jit(solution)/shard_map/ppermute | solution.py:296
  28.1 15.0 %collective-permute-start.1 = (bf16[16,1024]{1,0:T(8,128)(2,1)S(1)}, bf16[16,1024]{1,0:T(8,128)(2,1)S(1)}, u32[]{:S(2)}, u32[]{:S(2)}) collective-permute-start(bf16[16,1024]{1,0:T(8,128)(2,1)S(1)} %get-tuple-element.32), channel_id=1, source_target_pairs={{0,24},{24,48},{48,72},{72,96},{96,120},{120,144},{144,168},{168,1... | collective-permute-start | bytes 98312 | tf_op jit(solution)/shard_map/ppermute | solution.py:306
  35.2 9.3 %collective-permute-start.2 = (bf16[16,1024]{1,0:T(8,128)(2,1)S(1)}, bf16[16,1024]{1,0:T(8,128)(2,1)S(1)}, u32[]{:S(2)}, u32[]{:S(2)}) collective-permute-start(bf16[16,1024]{1,0:T(8,128)(2,1)S(1)} %get-tuple-element.33), channel_id=1, source_target_pairs={{0,744},{24,0},{48,24},{72,48},{96,72},{120,96},{144,120},{168,144... | collective-permute-start | bytes 98312 | tf_op jit(solution)/shard_map/ppermute | solution.py:306
  45.1 12.0 %collective-permute-start.4 = (bf16[16,1024]{1,0:T(8,128)(2,1)S(1)}, bf16[16,1024]{1,0:T(8,128)(2,1)S(1)}, u32[]{:S(2)}, u32[]{:S(2)}) collective-permute-start(bf16[16,1024]{1,0:T(8,128)(2,1)S(1)} %get-tuple-element.36.own_ref), channel_id=1, source_target_pairs={{0,24},{24,48},{48,72},{72,96},{96,120},{120,144},{144,168},{168,1... | collective-permute-start | bytes 98312 | tf_op jit(solution)/shard_map/ppermute | solution.py:306
  51.4 7.8 %collective-permute-start.3 = (bf16[16,1024]{1,0:T(8,128)(2,1)S(1)}, bf16[16,1024]{1,0:T(8,128)(2,1)S(1)}, u32[]{:S(2)}, u32[]{:S(2)}) collective-permute-start(bf16[16,1024]{1,0:T(8,128)(2,1)S(1)} %get-tuple-element.36.own_ref), channel_id=1, source_target_pairs={{0,744},{24,0},{48,24},{72,48},{96,72},{120,96},{144,120},{168,144... | collective-permute-start | bytes 98312 | tf_op jit(solution)/shard_map/ppermute | solution.py:306
  60.5 18.8 %all-to-all-start.1 = ((bf16[8,21,8,128]{3,2,1,0:T(8,128)(2,1)}), bf16[8,21,8,128]{3,2,1,0:T(8,128)(2,1)S(1)}, u32[]{:S(2)}, u32[]{:S(2)}) async-start(bf16[8,21,8,128]{3,2,1,0:T(8,128)(2,1)} %get-tuple-element.40), calls=%async_computation.1 | async-start | bytes 688128 | tf_op jit(solution)/shard_map/all_to_all | solution.py:334
  68.7 3.6 %collective-permute-start.5 = (bf16[4,3,16,1024]{3,2,1,0:T(8,128)(2,1)S(1)}, bf16[4,3,16,1024]{3,2,1,0:T(8,128)(2,1)S(1)}, u32[]{:S(2)}, u32[]{:S(2)}) collective-permute-start(bf16[4,3,16,1024]{3,2,1,0:T(8,128)(2,1)S(1)} %get-tuple-element.47), channel_id=1, source_target_pairs={{0,1},{1,0},{2,3},{3,2},{4,5},{5,4},{6,7},{7,6},{8,9},{9,8},{10,11... | collective-permute-start | bytes 1179656 | tf_op jit(solution)/shard_map/ppermute | solution.py:296
  72.3 13.3 %collective-permute-start.6 = (bf16[2,3,16,1024]{3,2,1,0:T(8,128)(2,1)S(1)}, bf16[2,3,16,1024]{3,2,1,0:T(8,128)(2,1)S(1)}, u32[]{:S(2)}, u32[]{:S(2)}) collective-permute-start(bf16[2,3,16,1024]{3,2,1,0:T(8,128)(2,1)S(1)} %get-tuple-element.50), channel_id=1, source_target_pairs={{0,6},{6,0},{12,18},{18,12},{1,7},{7,1},{13,19},{19,13},{2,8},{8,2... | collective-permute-start | bytes 589832 | tf_op jit(solution)/shard_map/ppermute | solution.py:340
  80.0 16.7 %all-to-all-start.2 = ((bf16[4,21,8,128]{3,2,1,0:T(8,128)(2,1)}), bf16[4,21,8,128]{3,2,1,0:T(8,128)(2,1)S(1)}, u32[]{:S(2)}, u32[]{:S(2)}) async-start(bf16[4,21,8,128]{3,2,1,0:T(8,128)(2,1)} %total.2), calls=%async_computation.2 | async-start | bytes 344064 | tf_op jit(solution)/shard_map/all_to_all | solution.py:339
  85.7 15.7 %collective-permute-start.7 = (bf16[3,16,1024]{2,1,0:T(8,128)(2,1)S(1)}, bf16[3,16,1024]{2,1,0:T(8,128)(2,1)S(1)}, u32[]{:S(2)}, u32[]{:S(2)}) collective-permute-start(bf16[3,16,1024]{2,1,0:T(8,128)(2,1)S(1)} %fusion.1), channel_id=1, source_target_pairs={{0,12},{6,18},{12,0},{18,6},{1,13},{7,19},{13,1},{19,7},{2,14},{8,... | collective-permute-start | bytes 294920 | tf_op jit(solution)/shard_map/ppermute | solution.py:343
  97.4 16.3 %all-to-all-start.3 = ((bf16[8,21,8,128]{3,2,1,0:T(8,128)(2,1)}), bf16[8,21,8,128]{3,2,1,0:T(8,128)(2,1)S(1)}, u32[]{:S(2)}, u32[]{:S(2)}) async-start(bf16[8,21,8,128]{3,2,1,0:T(8,128)(2,1)} %total.3), calls=%async_computation.3 | async-start | bytes 688128 | tf_op jit(solution)/shard_map/all_to_all | solution.py:342
  101.5 6.8 %collective-permute-start.8 = (bf16[16,1024]{1,0:T(8,128)(2,1)S(1)}, bf16[16,1024]{1,0:T(8,128)(2,1)S(1)}, u32[]{:S(2)}, u32[]{:S(2)}) collective-permute-start(bf16[16,1024]{1,0:T(8,128)(2,1)S(1)} %get-tuple-element.55), channel_id=1, source_target_pairs={{0,2},{2,4},{4,0},{1,3},{3,5},{5,1},{6,8},{8,10},{10,6},{7,9},{9,1... | collective-permute-start | bytes 98312 | tf_op jit(solution)/shard_map/ppermute | solution.py:346
  105.0 5.8 %collective-permute-start.9 = (bf16[16,1024]{1,0:T(8,128)(2,1)S(1)}, bf16[16,1024]{1,0:T(8,128)(2,1)S(1)}, u32[]{:S(2)}, u32[]{:S(2)}) collective-permute-start(bf16[16,1024]{1,0:T(8,128)(2,1)S(1)} %get-tuple-element.56), channel_id=1, source_target_pairs={{0,4},{2,0},{4,2},{1,5},{3,1},{5,3},{6,10},{8,6},{10,8},{7,11},{9,... | collective-permute-start | bytes 98312 | tf_op jit(solution)/shard_map/ppermute | solution.py:347

commit v15 on v11

--- a/solution.py
+++ b/solution.py
@@ -154,26 +154,39 @@
     )(below, x)
 
 
-def above_kernel(above_ref, x_ref, own_ref, below_ref, wide_ref, stack_ref):
-    slots, per = wide_ref.shape[:2]
+def above_kernel(
+    above_ref, x_ref, own_ref, below_ref, wide_ref, stack_ref, units_ref, pad_ref, sems
+):
     count = own_ref.shape[0]
-    for at in range(count):
-        for unit, ref in ((count + at, own_ref), (2 * count + at, below_ref)):
-            wide_ref[unit // per, unit % per] = ref[at]
-    for unit in range(3 * count, slots * per):
-        wide_ref[unit // per, unit % per] = jnp.zeros((HALF, LANES), jnp.bfloat16)
+    pad_ref[...] = jnp.zeros_like(pad_ref)
+    moves = [
+        pltpu.make_async_copy(ref, wide_ref.at[pl.ds(run * count, ref.shape[0])], sems.at[run])
+        for run, ref in enumerate((units_ref, own_ref, below_ref, pad_ref))
+    ]
+    for move in moves[1:]:
+        move.start()
     stack_plane(above_ref[...], stack_ref, 0)
     grad = cross(stack_ref[...], x_ref[...].reshape(-1, x_ref.shape[-1]))
     for at, unit in enumerate(units_of(grad)):
-        wide_ref[at // per, at % per] = unit.astype(jnp.bfloat16)
+        units_ref[at] = unit.astype(jnp.bfloat16)
+    moves[0].start()
+    for move in moves:
+        move.wait()
 
 
 def wgrad_above(above, x, own_units, below_units, slots):
-    per = -(-3 * own_units.shape[0] // slots)
+    count = own_units.shape[0]
+    full = -(-3 * count // slots) * slots
     stack = plane_shapes(above, x.shape[0] * x.shape[1] * x.shape[2])[1]
     return pl.pallas_call(
         above_kernel,
-        out_shape=[jax.ShapeDtypeStruct((slots, per, HALF, LANES), jnp.bfloat16), stack],
+        out_shape=[jax.ShapeDtypeStruct((full, HALF, LANES), jnp.bfloat16), stack],
+        out_specs=[pl.BlockSpec(memory_space=pl.ANY), pl.BlockSpec(memory_space=pltpu.VMEM)],
+        scratch_shapes=[
+            pltpu.VMEM((count, HALF, LANES), jnp.bfloat16),
+            pltpu.VMEM((full - 3 * count, HALF, LANES), jnp.bfloat16),
+            pltpu.SemaphoreType.DMA((4,)),
+        ],
         compiler_params=pltpu.CompilerParams(vmem_limit_bytes=VMEM_LIMIT),
         name="wgrad_above",
     )(above, x, own_units, below_units)
@@ -330,6 +343,7 @@
     ys, zs = lax.axis_size("y"), lax.axis_size("zh")
     below_units, below_stack = wgrad_below(below, x)
     wide, above_stack = wgrad_above(above, x, own_units, below_units, ys)
+    wide = wide.reshape((ys, -1) + wide.shape[1:])
     scale = 1.0 / math.sqrt(UNIV * DEPTH * SIDE * SIDE)
     over_y = lax.all_to_all(wide, "y", 0, 0)
 

time: 116 us -> 116 us (level)
  no operation moved by 1% of the time
where the time goes in v15:
time: 116 us; the launch traced here: 115 us
  starting transfers between devices  73.6 us (63%)
  waiting for transfers between devices  30.9 us (27%)
  Pallas kernels  7.11 us (6%)
  local copies, waits for them, and re-layouts  1.57 us (1%)
    ppermute x4, starting transfers between devices, shift(): lax.ppermute(block, DEP, [(i, (i + step) % depths) for i in range(depths)])  25.8 us
    all_to_all x1, starting transfers between devices, body(): mine = lax.all_to_all(copies(own), CHIPS, 0, 0)  13.1 us
    all_to_all x1, waiting for transfers between devices, body(): mine = lax.all_to_all(copies(own), CHIPS, 0, 0)  8.12 us
    all_to_all x1, starting transfers between devices, body(): over_y = lax.all_to_all(wide, 'y', 0, 0)  7.37 us
    all_to_all x1, starting transfers between devices, body(): over_z = lax.all_to_all(total_spread(over_y, 1.0, zs), 'zh', 0, 0)  5.69 us
    all_to_all x1, starting transfers between devices, body(): units = lax.all_to_all(total_spread(over_z, scale, ys), 'y', 0, 0)  4.9 us
    ppermute x1, starting transfers between devices, body(): before = lax.ppermute(before, 'zl', [(i, (i + 2) % 3) for i in range(3)])  4.82 us
    ppermute x1, waiting for transfers between devices, body(): lax.ppermute(total[1].astype(jnp.bfloat16), 'x', [(i, i ^ 2) for i in ran...  4.51 us
  transfers between devices with their start and end apart: 14, of which 10 were waited for; matrix products, arithmetic and copies ran while one was open for 1% of the time, Pallas kernels for 3%

profile of v15, /device:TPU:2, one launch (start us, length us, event | category | flops | bytes accessed | tf_op | source)
XLA Modules:
  0.0 114.7 jit_solution(10741093457385573212)
XLA Ops:
  0.6 1.5 %broadcast_in_dim.8 = bf16[12,16,1024]{2,1,0:T(8,128)(2,1)} broadcast(bf16[16,1024]{1,0:T(8,128)(2,1)} %bitcast.45), dimensions={1,2} | broadcast | bytes 425984 | tf_op jit(solution)/shard_map/broadcast_in_dim | solution.py:329
  2.2 0.0 copy-start
  2.2 13.1 %all-to-all-start = ((bf16[12,16,1024]{2,1,0:T(8,128)(2,1)}), bf16[12,16,1024]{2,1,0:T(8,128)(2,1)S(1)}, u32[]{:S(2)}, u32[]{:S(2)}) async-start(bf16[12,16,1024]{2,1,0:T(8,128)(2,1)} %broadcast_in_dim.8), calls=%async_computation | async-start | bytes 786432 | tf_op jit(solution)/shard_map/all_to_all | solution.py:331
  15.3 8.1 %all-to-all-done.mine_ref = bf16[12,16,1024]{2,1,0:T(8,128)(2,1)S(1)} async-done(((bf16[12,16,1024]{2,1,0:T(8,128)(2,1)}), bf16[12,16,1024]{2,1,0:T(8,128)(2,1)S(1)}, u32[]{:S(2)}, u32[]{:S(2)}) %all-to-all-start) | async-done | bytes 393248 | tf_op jit(solution)/shard_map/all_to_all | solution.py:331
  23.4 0.0 copy-start.1
  23.4 2.0 %collective-permute-start = (bf16[12,16,1024]{2,1,0:T(8,128)(2,1)S(1)}, bf16[12,16,1024]{2,1,0:T(8,128)(2,1)S(1)}, u32[]{:S(2)}, u32[]{:S(2)}) collective-permute-start(bf16[12,16,1024]{2,1,0:T(8,128)(2,1)S(1)} %all-to-all-done.mine_ref), channel_id=1, source_target_pairs={{0,1},{1,0},{2,3},{3,2},{4,5},{5,4},{6,7},{7,6},{8,9},{9,8},{10,11... | collective-permute-start | bytes 1179656 | tf_op jit(solution)/shard_map/ppermute | solution.py:309
  25.5 1.7 %collective-permute-done.other_ref = bf16[12,16,1024]{2,1,0:T(8,128)(2,1)S(1)} collective-permute-done((bf16[12,16,1024]{2,1,0:T(8,128)(2,1)S(1)}, bf16[12,16,1024]{2,1,0:T(8,128)(2,1)S(1)}, u32[]{:S(2)}, u32[]{:S(2)}) %collective-permute-start) | collective-permute-done | bytes 393248 | tf_op jit(solution)/shard_map/ppermute | solution.py:309
  27.1 0.0 copy-done
  27.1 0.9 conv.1
  28.1 7.2 %collective-permute-start.1 = (bf16[16,1024]{1,0:T(8,128)(2,1)S(1)}, bf16[16,1024]{1,0:T(8,128)(2,1)S(1)}, u32[]{:S(2)}, u32[]{:S(2)}) collective-permute-start(bf16[16,1024]{1,0:T(8,128)(2,1)S(1)} %get-tuple-element.32), channel_id=1, source_target_pairs={{0,24},{24,48},{48,72},{72,96},{96,120},{120,144},{144,168},{168,1... | collective-permute-start | bytes 98312 | tf_op jit(solution)/shard_map/ppermute | solution.py:319
  35.2 7.3 %collective-permute-start.2 = (bf16[16,1024]{1,0:T(8,128)(2,1)S(1)}, bf16[16,1024]{1,0:T(8,128)(2,1)S(1)}, u32[]{:S(2)}, u32[]{:S(2)}) collective-permute-start(bf16[16,1024]{1,0:T(8,128)(2,1)S(1)} %get-tuple-element.33), channel_id=1, source_target_pairs={{0,744},{24,0},{48,24},{72,48},{96,72},{120,96},{144,120},{168,144... | collective-permute-start | bytes 98312 | tf_op jit(solution)/shard_map/ppermute | solution.py:319
  42.5 0.6 collective-permute-done.1.low_ref
  43.1 1.4 %collective-permute-done.2.high_ref = bf16[16,1024]{1,0:T(8,128)(2,1)S(1)} collective-permute-done((bf16[16,1024]{1,0:T(8,128)(2,1)S(1)}, bf16[16,1024]{1,0:T(8,128)(2,1)S(1)}, u32[]{:S(2)}, u32[]{:S(2)}) %collective-permute-start.2) | collective-permute-done | bytes 32800 | tf_op jit(solution)/shard_map/ppermute | solution.py:319
  44.5 0.0 copy-done.1
  44.5 0.6 activate.1
  45.1 6.2 %collective-permute-start.4 = (bf16[16,1024]{1,0:T(8,128)(2,1)S(1)}, bf16[16,1024]{1,0:T(8,128)(2,1)S(1)}, u32[]{:S(2)}, u32[]{:S(2)}) collective-permute-start(bf16[16,1024]{1,0:T(8,128)(2,1)S(1)} %get-tuple-element.36.own_ref), channel_id=1, source_target_pairs={{0,24},{24,48},{48,72},{72,96},{96,120},{120,144},{144,168},{168,1... | collective-permute-start | bytes 98312 | tf_op jit(solution)/shard_map/ppermute | solution.py:319
  51.4 5.2 %collective-permute-start.3 = (bf16[16,1024]{1,0:T(8,128)(2,1)S(1)}, bf16[16,1024]{1,0:T(8,128)(2,1)S(1)}, u32[]{:S(2)}, u32[]{:S(2)}) collective-permute-start(bf16[16,1024]{1,0:T(8,128)(2,1)S(1)} %get-tuple-element.36.own_ref), channel_id=1, source_target_pairs={{0,744},{24,0},{48,24},{72,48},{96,72},{120,96},{144,120},{168,144... | collective-permute-start | bytes 98312 | tf_op jit(solution)/shard_map/ppermute | solution.py:319
  56.5 0.5 wgrad_own.1
  57.1 0.0 collective-permute-done.4.below_ref
  57.1 0.5 wgrad_below.1
  57.6 1.6 %collective-permute-done.3.above_ref = bf16[16,1024]{1,0:T(8,128)(2,1)S(1)} collective-permute-done((bf16[16,1024]{1,0:T(8,128)(2,1)S(1)}, bf16[16,1024]{1,0:T(8,128)(2,1)S(1)}, u32[]{:S(2)}, u32[]{:S(2)}) %collective-permute-start.3) | collective-permute-done | bytes 32800 | tf_op jit(solution)/shard_map/ppermute | solution.py:319
  59.2 1.2 %wgrad_above.1 = (bf16[168,8,128]{2,1,0:T(8,128)(2,1)}, bf16[144,1024]{1,0:T(8,128)(2,1)S(1)}) custom-call(bf16[16,1024]{1,0:T(8,128)(2,1)S(1)} %collective-permute-done.3.above_ref, bf16[12,2,16,1024]{3,2,1,0:T(8,128)(2,1)S(1)} %get-tuple-element.37.x_ref, bf16[54,8,128]{2,1,0:T(8,128)(2,1)S(1)} %get-tuple-element.38.own_ref, ...), custom_call_target="tpu_custom_call" | custom-call | tf_op jit(solution)/shard_map/wgrad_above/pallas_call | solution.py:181
  60.4 7.4 %all-to-all-start.1 = ((bf16[8,21,8,128]{3,2,1,0:T(8,128)(2,1)}), bf16[8,21,8,128]{3,2,1,0:T(8,128)(2,1)S(1)}, u32[]{:S(2)}, u32[]{:S(2)}) async-start(bf16[8,21,8,128]{3,2,1,0:T(8,128)(2,1)} %bitcast.9), calls=%async_computation.1 | async-start | bytes 688128 | tf_op jit(solution)/shard_map/all_to_all | solution.py:348
  67.8 0.8 dgrad.1
  68.6 1.9 %collective-permute-start.5 = (bf16[4,3,16,1024]{3,2,1,0:T(8,128)(2,1)S(1)}, bf16[4,3,16,1024]{3,2,1,0:T(8,128)(2,1)S(1)}, u32[]{:S(2)}, u32[]{:S(2)}) collective-permute-start(bf16[4,3,16,1024]{3,2,1,0:T(8,128)(2,1)S(1)} %get-tuple-element.47), channel_id=1, source_target_pairs={{0,1},{1,0},{2,3},{3,2},{4,5},{5,4},{6,7},{7,6},{8,9},{9,8},{10,11... | collective-permute-start | bytes 1179656 | tf_op jit(solution)/shard_map/ppermute | solution.py:309
  70.6 1.7 %collective-permute-done.5.came_ref = bf16[4,3,16,1024]{3,2,1,0:T(8,128)(2,1)S(1)} collective-permute-done((bf16[4,3,16,1024]{3,2,1,0:T(8,128)(2,1)S(1)}, bf16[4,3,16,1024]{3,2,1,0:T(8,128)(2,1)S(1)}, u32[]{:S(2)}, u32[]{:S(2)}) %collective-permute-start.5) | collective-permute-done | bytes 393248 | tf_op jit(solution)/shard_map/ppermute | solution.py:309
  72.2 0.1 halve.1
  72.3 3.2 %collective-permute-start.6 = (bf16[2,3,16,1024]{3,2,1,0:T(8,128)(2,1)S(1)}, bf16[2,3,16,1024]{3,2,1,0:T(8,128)(2,1)S(1)}, u32[]{:S(2)}, u32[]{:S(2)}) collective-permute-start(bf16[2,3,16,1024]{3,2,1,0:T(8,128)(2,1)S(1)} %get-tuple-element.50), channel_id=1, source_target_pairs={{0,6},{6,0},{12,18},{18,12},{1,7},{7,1},{13,19},{19,13},{2,8},{8,2... | collective-permute-start | bytes 589832 | tf_op jit(solution)/shard_map/ppermute | solution.py:354
  75.6 3.6 %all-to-all-done.1.terms_ref = bf16[8,21,8,128]{3,2,1,0:T(8,128)(2,1)S(1)} async-done(((bf16[8,21,8,128]{3,2,1,0:T(8,128)(2,1)}), bf16[8,21,8,128]{3,2,1,0:T(8,128)(2,1)S(1)}, u32[]{:S(2)}, u32[]{:S(2)}) %all-to-all-start.1) | async-done | bytes 344096 | tf_op jit(solution)/shard_map/all_to_all | solution.py:348
  79.2 0.7 total.2
  79.9 5.7 %all-to-all-start.2 = ((bf16[4,21,8,128]{3,2,1,0:T(8,128)(2,1)}), bf16[4,21,8,128]{3,2,1,0:T(8,128)(2,1)S(1)}, u32[]{:S(2)}, u32[]{:S(2)}) async-start(bf16[4,21,8,128]{3,2,1,0:T(8,128)(2,1)} %total.2), calls=%async_computation.2 | async-start | bytes 344064 | tf_op jit(solution)/shard_map/all_to_all | solution.py:353
  85.6 0.0 collective-permute-done.6
  85.7 1.9 %collective-permute-start.7 = (bf16[2,16,1024]{2,1,0:T(8,128)(2,1)S(1)}, bf16[2,16,1024]{2,1,0:T(8,128)(2,1)S(1)}, u32[]{:S(2)}, u32[]{:S(2)}) collective-permute-start(bf16[2,16,1024]{2,1,0:T(8,128)(2,1)S(1)} %get-tuple-element.55), channel_id=1, source_target_pairs={{0,2},{2,4},{4,0},{1,3},{3,5},{5,1},{6,8},{8,10},{10,6},{7,9},{9,1... | collective-permute-start | bytes 196616 | tf_op jit(solution)/shard_map/ppermute | solution.py:357
  87.6 4.8 %collective-permute-start.8 = (bf16[2,16,1024]{2,1,0:T(8,128)(2,1)S(1)}, bf16[2,16,1024]{2,1,0:T(8,128)(2,1)S(1)}, u32[]{:S(2)}, u32[]{:S(2)}) collective-permute-start(bf16[2,16,1024]{2,1,0:T(8,128)(2,1)S(1)} %get-tuple-element.56), channel_id=1, source_target_pairs={{0,4},{2,0},{4,2},{1,5},{3,1},{5,3},{6,10},{8,6},{10,8},{7,11},{9,... | collective-permute-start | bytes 196616 | tf_op jit(solution)/shard_map/ppermute | solution.py:358
  92.5 4.2 %all-to-all-done.2.terms_ref = bf16[4,21,8,128]{3,2,1,0:T(8,128)(2,1)S(1)} async-done(((bf16[4,21,8,128]{3,2,1,0:T(8,128)(2,1)}), bf16[4,21,8,128]{3,2,1,0:T(8,128)(2,1)S(1)}, u32[]{:S(2)}, u32[]{:S(2)}) %all-to-all-start.2) | async-done | bytes 172064 | tf_op jit(solution)/shard_map/all_to_all | solution.py:353
  96.7 0.8 total.3
  97.4 4.9 %all-to-all-start.3 = ((bf16[8,21,8,128]{3,2,1,0:T(8,128)(2,1)}), bf16[8,21,8,128]{3,2,1,0:T(8,128)(2,1)S(1)}, u32[]{:S(2)}, u32[]{:S(2)}) async-start(bf16[8,21,8,128]{3,2,1,0:T(8,128)(2,1)} %total.3), calls=%async_computation.3 | async-start | bytes 688128 | tf_op jit(solution)/shard_map/all_to_all | solution.py:359
  102.3 0.0 collective-permute-done.7
  102.3 0.0 collective-permute-done.8
  102.4 2.8 %collective-permute-start.9 = (bf16[16,1024]{1,0:T(8,128)(2,1)S(1)}, bf16[16,1024]{1,0:T(8,128)(2,1)S(1)}, u32[]{:S(2)}, u32[]{:S(2)}) collective-permute-start(bf16[16,1024]{1,0:T(8,128)(2,1)S(1)} %fusion.5), channel_id=1, source_target_pairs={{0,12},{6,18},{12,0},{18,6},{1,13},{7,19},{13,1},{19,7},{2,14},{8,... | collective-permute-start | bytes 98312 | tf_op jit(solution)/shard_map/ppermute | solution.py:361
  105.2 4.5 %collective-permute-done.9 = bf16[16,1024]{1,0:T(8,128)(2,1)S(1)} collective-permute-done((bf16[16,1024]{1,0:T(8,128)(2,1)S(1)}, bf16[16,1024]{1,0:T(8,128)(2,1)S(1)}, u32[]{:S(2)}, u32[]{:S(2)}) %collective-permute-start.9) | collective-permute-done | bytes 32800 | tf_op jit(solution)/shard_map/ppermute | solution.py:361
  109.7 0.6 fusion.4
  110.3 3.5 %all-to-all-done.3.units_ref = bf16[8,21,8,128]{3,2,1,0:T(8,128)(2,1)S(1)} async-done(((bf16[8,21,8,128]{3,2,1,0:T(8,128)(2,1)}), bf16[8,21,8,128]{3,2,1,0:T(8,128)(2,1)S(1)}, u32[]{:S(2)}, u32[]{:S(2)}) %all-to-all-start.3) | async-done | bytes 344096 | tf_op jit(solution)/shard_map/all_to_all | solution.py:359
  113.8 0.9 unpack.1
  (4 shorter events, 0.1 us)
Async XLA Ops:
  2.2 25.0 %copy-start = (bf16[16,3,3,3,384]{4,0,3,2,1:T(8,128)(2,1)S(1)}, bf16[16,3,3,3,384]{4,0,3,2,1:T(8,128)(2,1)}, u32[]{:S(2)}) copy-start(bf16[16,3,3,3,384]{4,0,3,2,1:T(8,128)(2,1)} %param.4) | copy-start | bytes 995332
  2.2 21.2 %all-to-all-start = ((bf16[12,16,1024]{2,1,0:T(8,128)(2,1)}), bf16[12,16,1024]{2,1,0:T(8,128)(2,1)S(1)}, u32[]{:S(2)}, u32[]{:S(2)}) async-start(bf16[12,16,1024]{2,1,0:T(8,128)(2,1)} %broadcast_in_dim.8), calls=%async_computation | async-start | bytes 786432 | tf_op jit(solution)/shard_map/all_to_all | solution.py:331
  23.4 21.1 %copy-start.1 = (bf16[1,1,16,1024]{3,2,1,0:T(8,128)(2,1)S(1)}, bf16[1,1,16,1024]{3,2,1,0:T(8,128)(2,1)}, u32[]{:S(2)}) copy-start(bf16[1,1,16,1024]{3,2,1,0:T(8,128)(2,1)} %param.5) | copy-start | bytes 98308
  23.4 3.7 %collective-permute-start = (bf16[12,16,1024]{2,1,0:T(8,128)(2,1)S(1)}, bf16[12,16,1024]{2,1,0:T(8,128)(2,1)S(1)}, u32[]{:S(2)}, u32[]{:S(2)}) collective-permute-start(bf16[12,16,1024]{2,1,0:T(8,128)(2,1)S(1)} %all-to-all-done.mine_ref), channel_id=1, source_target_pairs={{0,1},{1,0},{2,3},{3,2},{4,5},{5,4},{6,7},{7,6},{8,9},{9,8},{10,11... | collective-permute-start | bytes 1179656 | tf_op jit(solution)/shard_map/ppermute | solution.py:309
  28.1 15.0 %collective-permute-start.1 = (bf16[16,1024]{1,0:T(8,128)(2,1)S(1)}, bf16[16,1024]{1,0:T(8,128)(2,1)S(1)}, u32[]{:S(2)}, u32[]{:S(2)}) collective-permute-start(bf16[16,1024]{1,0:T(8,128)(2,1)S(1)} %get-tuple-element.32), channel_id=1, source_target_pairs={{0,24},{24,48},{48,72},{72,96},{96,120},{120,144},{144,168},{168,1... | collective-permute-start | bytes 98312 | tf_op jit(solution)/shard_map/ppermute | solution.py:319
  35.2 9.3 %collective-permute-start.2 = (bf16[16,1024]{1,0:T(8,128)(2,1)S(1)}, bf16[16,1024]{1,0:T(8,128)(2,1)S(1)}, u32[]{:S(2)}, u32[]{:S(2)}) collective-permute-start(bf16[16,1024]{1,0:T(8,128)(2,1)S(1)} %get-tuple-element.33), channel_id=1, source_target_pairs={{0,744},{24,0},{48,24},{72,48},{96,72},{120,96},{144,120},{168,144... | collective-permute-start | bytes 98312 | tf_op jit(solution)/shard_map/ppermute | solution.py:319
  45.1 12.0 %collective-permute-start.4 = (bf16[16,1024]{1,0:T(8,128)(2,1)S(1)}, bf16[16,1024]{1,0:T(8,128)(2,1)S(1)}, u32[]{:S(2)}, u32[]{:S(2)}) collective-permute-start(bf16[16,1024]{1,0:T(8,128)(2,1)S(1)} %get-tuple-element.36.own_ref), channel_id=1, source_target_pairs={{0,24},{24,48},{48,72},{72,96},{96,120},{120,144},{144,168},{168,1... | collective-permute-start | bytes 98312 | tf_op jit(solution)/shard_map/ppermute | solution.py:319
  51.4 7.8 %collective-permute-start.3 = (bf16[16,1024]{1,0:T(8,128)(2,1)S(1)}, bf16[16,1024]{1,0:T(8,128)(2,1)S(1)}, u32[]{:S(2)}, u32[]{:S(2)}) collective-permute-start(bf16[16,1024]{1,0:T(8,128)(2,1)S(1)} %get-tuple-element.36.own_ref), channel_id=1, source_target_pairs={{0,744},{24,0},{48,24},{72,48},{96,72},{120,96},{144,120},{168,144... | collective-permute-start | bytes 98312 | tf_op jit(solution)/shard_map/ppermute | solution.py:319
  60.4 18.8 %all-to-all-start.1 = ((bf16[8,21,8,128]{3,2,1,0:T(8,128)(2,1)}), bf16[8,21,8,128]{3,2,1,0:T(8,128)(2,1)S(1)}, u32[]{:S(2)}, u32[]{:S(2)}) async-start(bf16[8,21,8,128]{3,2,1,0:T(8,128)(2,1)} %bitcast.9), calls=%async_computation.1 | async-start | bytes 688128 | tf_op jit(solution)/shard_map/all_to_all | solution.py:348
  68.6 3.6 %collective-permute-start.5 = (bf16[4,3,16,1024]{3,2,1,0:T(8,128)(2,1)S(1)}, bf16[4,3,16,1024]{3,2,1,0:T(8,128)(2,1)S(1)}, u32[]{:S(2)}, u32[]{:S(2)}) collective-permute-start(bf16[4,3,16,1024]{3,2,1,0:T(8,128)(2,1)S(1)} %get-tuple-element.47), channel_id=1, source_target_pairs={{0,1},{1,0},{2,3},{3,2},{4,5},{5,4},{6,7},{7,6},{8,9},{9,8},{10,11... | collective-permute-start | bytes 1179656 | tf_op jit(solution)/shard_map/ppermute | solution.py:309
  72.3 13.3 %collective-permute-start.6 = (bf16[2,3,16,1024]{3,2,1,0:T(8,128)(2,1)S(1)}, bf16[2,3,16,1024]{3,2,1,0:T(8,128)(2,1)S(1)}, u32[]{:S(2)}, u32[]{:S(2)}) collective-permute-start(bf16[2,3,16,1024]{3,2,1,0:T(8,128)(2,1)S(1)} %get-tuple-element.50), channel_id=1, source_target_pairs={{0,6},{6,0},{12,18},{18,12},{1,7},{7,1},{13,19},{19,13},{2,8},{8,2... | collective-permute-start | bytes 589832 | tf_op jit(solution)/shard_map/ppermute | solution.py:354
  79.9 16.7 %all-to-all-start.2 = ((bf16[4,21,8,128]{3,2,1,0:T(8,128)(2,1)}), bf16[4,21,8,128]{3,2,1,0:T(8,128)(2,1)S(1)}, u32[]{:S(2)}, u32[]{:S(2)}) async-start(bf16[4,21,8,128]{3,2,1,0:T(8,128)(2,1)} %total.2), calls=%async_computation.2 | async-start | bytes 344064 | tf_op jit(solution)/shard_map/all_to_all | solution.py:353
  85.7 16.6 %collective-permute-start.7 = (bf16[2,16,1024]{2,1,0:T(8,128)(2,1)S(1)}, bf16[2,16,1024]{2,1,0:T(8,128)(2,1)S(1)}, u32[]{:S(2)}, u32[]{:S(2)}) collective-permute-start(bf16[2,16,1024]{2,1,0:T(8,128)(2,1)S(1)} %get-tuple-element.55), channel_id=1, source_target_pairs={{0,2},{2,4},{4,0},{1,3},{3,5},{5,1},{6,8},{8,10},{10,6},{7,9},{9,1... | collective-permute-start | bytes 196616 | tf_op jit(solution)/shard_map/ppermute | solution.py:357
  87.6 14.7 %collective-permute-start.8 = (bf16[2,16,1024]{2,1,0:T(8,128)(2,1)S(1)}, bf16[2,16,1024]{2,1,0:T(8,128)(2,1)S(1)}, u32[]{:S(2)}, u32[]{:S(2)}) collective-permute-start(bf16[2,16,1024]{2,1,0:T(8,128)(2,1)S(1)} %get-tuple-element.56), channel_id=1, source_target_pairs={{0,4},{2,0},{4,2},{1,5},{3,1},{5,3},{6,10},{8,6},{10,8},{7,11},{9,... | collective-permute-start | bytes 196616 | tf_op jit(solution)/shard_map/ppermute | solution.py:358
  97.4 16.4 %all-to-all-start.3 = ((bf16[8,21,8,128]{3,2,1,0:T(8,128)(2,1)}), bf16[8,21,8,128]{3,2,1,0:T(8,128)(2,1)S(1)}, u32[]{:S(2)}, u32[]{:S(2)}) async-start(bf16[8,21,8,128]{3,2,1,0:T(8,128)(2,1)} %total.3), calls=%async_computation.3 | async-start | bytes 688128 | tf_op jit(solution)/shard_map/all_to_all | solution.py:359
  102.4 7.3 %collective-permute-start.9 = (bf16[16,1024]{1,0:T(8,128)(2,1)S(1)}, bf16[16,1024]{1,0:T(8,128)(2,1)S(1)}, u32[]{:S(2)}, u32[]{:S(2)}) collective-permute-start(bf16[16,1024]{1,0:T(8,128)(2,1)S(1)} %fusion.5), channel_id=1, source_target_pairs={{0,12},{6,18},{12,0},{18,6},{1,13},{7,19},{13,1},{19,7},{2,14},{8,... | collective-permute-start | bytes 98312 | tf_op jit(solution)/shard_map/ppermute | solution.py:361
